TPU v7x, 32 devices: a whole 2x2x4 slice. The times are simulated.
32 devices in a mesh: cell: 4 (over x, core), head: 4 (over z), ctx: 2 (over y).
Axes of the slice: x: 2, y: 2, z: 4, core: 2. Of those that a mesh axis runs over, the one named last changes fastest.
Arguments:
- inputs: bfloat16 [4, 2048, 1120], P('cell', ('head', 'ctx')), may hold values from -6 to 6
- dataset_ids: int32 [4], P('cell'), may hold values from 0 to 19
- lengths: int32 [4], P('cell'), may hold values from 1024 to 2048, as said below
- dataset_table: bfloat16 [20, 1120], replicated, may hold values from -3 to 3
- attn_gain: float32 [1120], replicated, may hold values from 0.5 to 1.5
- attn_shift: float32 [1120], replicated, may hold values from -1.5 to 1.5
- qkv_weight: bfloat16 [1120, 3360], replicated, may hold values from -0.1875 to 0.1875
- query_bias: float32 [1120], replicated, may hold values from -1.5 to 1.5
- value_bias: float32 [1120], replicated, may hold values from -1.5 to 1.5
- out_weight: bfloat16 [1120, 1120], replicated, may hold values from -3 to 3
- out_bias: float32 [1120], replicated, may hold values from -1.5 to 1.5
- mlp_gain: float32 [1120], replicated, may hold values from 0.5 to 1.5
- mlp_shift: float32 [1120], replicated, may hold values from -1.5 to 1.5
- fc_weight: bfloat16 [1120, 4480], replicated, may hold values from -0.1875 to 0.1875
- fc_bias: float32 [4480], replicated, may hold values from -1.5 to 1.5
- proj_weight: bfloat16 [4480, 1120], replicated, may hold values from -0.09375 to 0.09375
- proj_bias: float32 [1120], replicated, may hold values from -1.5 to 1.5
- cotangent: bfloat16 [4, 2048, 1120], P('cell', ('head', 'ctx')), may hold values from -6 to 6
Outputs:
- block_out: bfloat16 [4, 2048, 1120], P('cell', ('head', 'ctx'))
- input_grad: bfloat16 [4, 2048, 1120], P('cell', ('head', 'ctx'))
- table_grad: float32 [20, 1120], P(None, 'cell')
- attn_gain_grad: float32 [1120], P('cell')
- attn_shift_grad: float32 [1120], P('cell')
- qkv_weight_grad: float32 [1120, 3360], P('cell', ('head', 'ctx'))
- query_bias_grad: float32 [1120], P('cell')
- value_bias_grad: float32 [1120], P('cell')
- out_weight_grad: float32 [1120, 1120], P('cell', ('head', 'ctx'))
- out_bias_grad: float32 [1120], P('cell')
- mlp_gain_grad: float32 [1120], P('cell')
- mlp_shift_grad: float32 [1120], P('cell')
- fc_weight_grad: float32 [1120, 4480], P('cell', ('head', 'ctx'))
- fc_bias_grad: float32 [4480], P('cell')
- proj_weight_grad: float32 [4480, 1120], P('cell', ('head', 'ctx'))
- proj_bias_grad: float32 [1120], P('cell')
Inputs may be any that keep to these rules, and one draw needn't show every extreme that they name: `lengths`: each cell has 1024 to 2048 valid positions at the start of its 2048; some cell fills all 2048.
All inputs are finite; a program needn't handle non-finite values.
Results may differ from a plain program's by a relative error of at most 0.015.
Values may be sent and summed in bfloat16 or wider, within the bound.
No kernel may reach another device: no remote copies, remote signals or barrier semaphores. Data moves between devices by JAX's collectives and lax.ppermute only.
A program may use at most 192 MiB of HBM per device.

v0:
```python
import math

import jax
import jax.numpy as jnp
from jax import lax
from jax.sharding import PartitionSpec as P

HEADS = 20
HD = 56


epsilon = 1e-05


def layer_norm(values, gain_row, shift_row):
    center = values - jnp.mean(values, axis=-1, keepdims=True)
    spread = jnp.mean(center * center, axis=-1, keepdims=True)
    return center * lax.rsqrt(spread + epsilon) * gain_row + shift_row


def gelu_tanh(values):
    return jax.nn.gelu(values, approximate=True)


def global_place(local_rows, source_rows, halves, half_index):
    return (
        local_rows // source_rows * halves + half_index
    ) * source_rows + local_rows % source_rows


def body(
    inputs,
    dataset_ids,
    lengths,
    dataset_table,
    attn_gain,
    attn_shift,
    qkv_weight,
    query_bias,
    value_bias,
    out_weight,
    out_bias,
    mlp_gain,
    mlp_shift,
    fc_weight,
    fc_bias,
    proj_weight,
    proj_bias,
    cotangent,
):
    cell_count, row_count, model_width = inputs.shape
    groups = lax.axis_size("head")
    halves = lax.axis_size("ctx")
    half_index = lax.axis_index("ctx")
    head_count = HEADS // groups
    head_width = head_count * HD
    token_count = cell_count * row_count
    score_scale = 1.0 / math.sqrt(HD)
    one_hot = (
        dataset_ids[:, None] == jnp.arange(dataset_table.shape[0], dtype=jnp.int32)[None, :]
    ).astype(jnp.bfloat16)
    embedded = jnp.dot(one_hot, dataset_table, preferred_element_type=jnp.float32)
    residual = (inputs.astype(jnp.float32) + embedded[:, None, :]).reshape(token_count, model_width)
    normed = layer_norm(residual, attn_gain, attn_shift).astype(jnp.bfloat16)
    mixed_qkv = jnp.dot(normed, qkv_weight, preferred_element_type=jnp.float32)
    bias_row = jnp.concatenate([query_bias, jnp.zeros_like(query_bias), value_bias])
    mixed_qkv = (
        (mixed_qkv + bias_row)
        .astype(jnp.bfloat16)
        .reshape(cell_count, row_count, 3, groups, head_width)
    )
    query, keys_here, values_here = (
        lax.all_to_all(mixed_qkv[:, :, 0], "head", split_axis=2, concat_axis=1, tiled=True),
        lax.all_to_all(mixed_qkv[:, :, 1], "head", split_axis=2, concat_axis=1, tiled=True),
        lax.all_to_all(mixed_qkv[:, :, 2], "head", split_axis=2, concat_axis=1, tiled=True),
    )
    ctx_rows = groups * row_count
    query = query.reshape(cell_count, ctx_rows, head_count, HD)
    keys_here = keys_here.reshape(cell_count, ctx_rows, head_count, HD)
    values_here = values_here.reshape(cell_count, ctx_rows, head_count, HD)
    all_keys, all_values = (
        lax.all_gather(keys_here, "ctx", axis=1, tiled=True),
        lax.all_gather(values_here, "ctx", axis=1, tiled=True),
    )
    key_rows = halves * ctx_rows
    query_pos = global_place(jnp.arange(ctx_rows, dtype=jnp.int32), row_count, halves, half_index)
    key_index = jnp.arange(key_rows, dtype=jnp.int32)
    key_pos = global_place(key_index % ctx_rows, row_count, halves, key_index // ctx_rows)
    block_rows = min(512, ctx_rows)
    block_count = ctx_rows // block_rows
    block_ids = jnp.arange(block_count, dtype=jnp.int32)

    def masked_scores(queries, offset, cell_keys, seq_len):
        scores = (
            jnp.einsum("qhd,khd->hqk", queries, cell_keys, preferred_element_type=jnp.float32)
            * score_scale
        )
        block_pos = lax.dynamic_slice_in_dim(query_pos, offset, block_rows, 0)
        allowed = (key_pos[None, :] <= block_pos[:, None]) & (key_pos[None, :] < seq_len)
        return jnp.where(allowed[None], scores, -1e30)

    def attend_cell(cell_items):
        cell_query, cell_keys, cell_values, seq_len = cell_items

        def attend_block(block_index):
            offset = block_index * block_rows
            queries = lax.dynamic_slice_in_dim(cell_query, offset, block_rows, 0)
            scores = masked_scores(queries, offset, cell_keys, seq_len)
            row_max = jnp.max(scores, axis=-1, keepdims=True)
            powers = jnp.exp(scores - row_max)
            row_sum = jnp.sum(powers, axis=-1, keepdims=True)
            weights = (powers / row_sum).astype(jnp.bfloat16)
            result = jnp.einsum(
                "hqk,khd->qhd", weights, cell_values, preferred_element_type=jnp.float32
            )
            return (result.astype(jnp.bfloat16), row_max[..., 0], row_sum[..., 0])

        block_outs, maxima, row_sums = lax.map(attend_block, block_ids)
        return (block_outs.reshape(ctx_rows, head_count, HD), maxima, row_sums)

    attended, maxima, row_sums = lax.map(attend_cell, (query, all_keys, all_values, lengths))
    attended_rows = lax.all_to_all(
        attended.reshape(cell_count, ctx_rows, 1, head_width),
        "head",
        split_axis=1,
        concat_axis=2,
        tiled=True,
    )
    attended_rows = attended_rows.reshape(token_count, model_width)
    attn_out = jnp.dot(attended_rows, out_weight, preferred_element_type=jnp.float32) + out_bias
    middle = residual + attn_out
    mlp_normed = layer_norm(middle, mlp_gain, mlp_shift).astype(jnp.bfloat16)
    hidden = jnp.dot(mlp_normed, fc_weight, preferred_element_type=jnp.float32) + fc_bias
    active = gelu_tanh(hidden).astype(jnp.bfloat16)
    branch = jnp.dot(active, proj_weight, preferred_element_type=jnp.float32) + proj_bias
    block_out = (middle + branch).astype(jnp.bfloat16).reshape(cell_count, row_count, model_width)
    grad_low = cotangent.reshape(token_count, model_width)
    grad_top = grad_low.astype(jnp.float32)
    proj_weight_grad = jnp.einsum("nf,nd->fd", active, grad_low, preferred_element_type=jnp.float32)
    proj_bias_grad = jnp.sum(grad_top, axis=0)
    active_grad = jnp.einsum("nd,fd->nf", grad_low, proj_weight, preferred_element_type=jnp.float32)
    gelu_pull = jax.vjp(gelu_tanh, hidden)[1]
    hidden_grad = gelu_pull(active_grad)[0].astype(jnp.bfloat16)
    fc_weight_grad = jnp.einsum(
        "nd,nf->df", mlp_normed, hidden_grad, preferred_element_type=jnp.float32
    )
    fc_bias_grad = jnp.sum(hidden_grad, axis=0, dtype=jnp.float32)
    normed_grad = jnp.einsum(
        "nf,df->nd", hidden_grad, fc_weight, preferred_element_type=jnp.float32
    )
    mlp_pull = jax.vjp(layer_norm, middle, mlp_gain, mlp_shift)[1]
    middle_part, mlp_gain_grad, mlp_shift_grad = mlp_pull(normed_grad)
    middle_grad = grad_top + middle_part
    middle_low = middle_grad.astype(jnp.bfloat16)
    out_weight_grad = jnp.einsum(
        "nd,ne->de", attended_rows, middle_low, preferred_element_type=jnp.float32
    )
    out_bias_grad = jnp.sum(middle_low, axis=0, dtype=jnp.float32)
    attended_grad = jnp.einsum(
        "ne,de->nd", middle_low, out_weight, preferred_element_type=jnp.float32
    ).astype(jnp.bfloat16)
    attended_grad = lax.all_to_all(
        attended_grad.reshape(cell_count, row_count, groups, head_width),
        "head",
        split_axis=2,
        concat_axis=1,
        tiled=True,
    )
    attended_grad = attended_grad.reshape(cell_count, ctx_rows, head_count, HD)

    def back_cell(cell_items):
        cell_query, cell_keys, cell_values, cell_grad, seq_len, cell_max, cell_sum = cell_items

        def back_block(accums, block_index):
            key_acc, value_acc = accums
            offset = block_index * block_rows
            queries = lax.dynamic_slice_in_dim(cell_query, offset, block_rows, 0)
            out_grad = lax.dynamic_slice_in_dim(cell_grad, offset, block_rows, 0)
            scores = masked_scores(queries, offset, cell_keys, seq_len)
            row_max = cell_max[block_index][..., None]
            row_sum = cell_sum[block_index][..., None]
            weights = jnp.exp(scores - row_max) / row_sum
            weights_low = weights.astype(jnp.bfloat16)
            prob_grad = jnp.einsum(
                "qhd,khd->hqk", out_grad, cell_values, preferred_element_type=jnp.float32
            )
            score_grad = weights * (
                prob_grad - jnp.sum(weights * prob_grad, axis=-1, keepdims=True)
            )
            score_low = score_grad.astype(jnp.bfloat16)
            query_part = (
                jnp.einsum("hqk,khd->qhd", score_low, cell_keys, preferred_element_type=jnp.float32)
                * score_scale
            )
            key_acc = (
                key_acc
                + jnp.einsum("hqk,qhd->khd", score_low, queries, preferred_element_type=jnp.float32)
                * score_scale
            )
            value_acc = value_acc + jnp.einsum(
                "hqk,qhd->khd", weights_low, out_grad, preferred_element_type=jnp.float32
            )
            return ((key_acc, value_acc), query_part.astype(jnp.bfloat16))

        zero_acc = jnp.zeros((key_rows, head_count, HD), jnp.float32)
        (key_grad, value_grad), query_grad = lax.scan(back_block, (zero_acc, zero_acc), block_ids)
        return (query_grad.reshape(ctx_rows, head_count, HD), key_grad, value_grad)

    query_grad, key_grad, value_grad = lax.map(
        back_cell, (query, all_keys, all_values, attended_grad, lengths, maxima, row_sums)
    )
    key_grad, value_grad = (
        lax.psum_scatter(key_grad, "ctx", scatter_dimension=1, tiled=True),
        lax.psum_scatter(value_grad, "ctx", scatter_dimension=1, tiled=True),
    )
    shape_back = (cell_count, ctx_rows, 1, head_width)
    query_grad, key_grad, value_grad = (
        lax.all_to_all(
            query_grad.reshape(shape_back), "head", split_axis=1, concat_axis=2, tiled=True
        ),
        lax.all_to_all(
            key_grad.astype(jnp.bfloat16).reshape(shape_back),
            "head",
            split_axis=1,
            concat_axis=2,
            tiled=True,
        ),
        lax.all_to_all(
            value_grad.astype(jnp.bfloat16).reshape(shape_back),
            "head",
            split_axis=1,
            concat_axis=2,
            tiled=True,
        ),
    )
    qkv_grad = jnp.stack([query_grad, key_grad, value_grad], axis=2).reshape(
        token_count, 3 * model_width
    )
    qkv_weight_grad = jnp.einsum("nd,ne->de", normed, qkv_grad, preferred_element_type=jnp.float32)
    column_sums = jnp.sum(qkv_grad, axis=0, dtype=jnp.float32)
    query_bias_grad = column_sums[:model_width]
    value_bias_grad = column_sums[2 * model_width :]
    normed_back = jnp.einsum("ne,de->nd", qkv_grad, qkv_weight, preferred_element_type=jnp.float32)
    attn_pull = jax.vjp(layer_norm, residual, attn_gain, attn_shift)[1]
    residual_part, attn_gain_grad, attn_shift_grad = attn_pull(normed_back)
    residual_grad = middle_grad + residual_part
    input_grad = residual_grad.astype(jnp.bfloat16).reshape(cell_count, row_count, model_width)
    cell_totals = jnp.sum(residual_grad.reshape(cell_count, row_count, model_width), axis=1)
    table_grad = jnp.dot(
        one_hot.astype(jnp.float32).T, cell_totals, precision=lax.Precision.HIGHEST
    )
    (
        qkv_weight_grad,
        out_weight_grad,
        fc_weight_grad,
        proj_weight_grad,
        table_grad,
        attn_gain_grad,
        attn_shift_grad,
        query_bias_grad,
        value_bias_grad,
        out_bias_grad,
        mlp_gain_grad,
        mlp_shift_grad,
        fc_bias_grad,
        proj_bias_grad,
    ) = (
        lax.psum_scatter(
            qkv_weight_grad.astype(jnp.bfloat16), "cell", scatter_dimension=0, tiled=True
        ).astype(jnp.float32),
        lax.psum_scatter(
            out_weight_grad.astype(jnp.bfloat16), "cell", scatter_dimension=0, tiled=True
        ).astype(jnp.float32),
        lax.psum_scatter(
            fc_weight_grad.astype(jnp.bfloat16), "cell", scatter_dimension=0, tiled=True
        ).astype(jnp.float32),
        lax.psum_scatter(
            proj_weight_grad.astype(jnp.bfloat16), "cell", scatter_dimension=0, tiled=True
        ).astype(jnp.float32),
        lax.psum_scatter(
            table_grad.astype(jnp.bfloat16), "cell", scatter_dimension=1, tiled=True
        ).astype(jnp.float32),
        lax.psum_scatter(
            attn_gain_grad.astype(jnp.bfloat16), "cell", scatter_dimension=0, tiled=True
        ).astype(jnp.float32),
        lax.psum_scatter(
            attn_shift_grad.astype(jnp.bfloat16), "cell", scatter_dimension=0, tiled=True
        ).astype(jnp.float32),
        lax.psum_scatter(
            query_bias_grad.astype(jnp.bfloat16), "cell", scatter_dimension=0, tiled=True
        ).astype(jnp.float32),
        lax.psum_scatter(
            value_bias_grad.astype(jnp.bfloat16), "cell", scatter_dimension=0, tiled=True
        ).astype(jnp.float32),
        lax.psum_scatter(
            out_bias_grad.astype(jnp.bfloat16), "cell", scatter_dimension=0, tiled=True
        ).astype(jnp.float32),
        lax.psum_scatter(
            mlp_gain_grad.astype(jnp.bfloat16), "cell", scatter_dimension=0, tiled=True
        ).astype(jnp.float32),
        lax.psum_scatter(
            mlp_shift_grad.astype(jnp.bfloat16), "cell", scatter_dimension=0, tiled=True
        ).astype(jnp.float32),
        lax.psum_scatter(
            fc_bias_grad.astype(jnp.bfloat16), "cell", scatter_dimension=0, tiled=True
        ).astype(jnp.float32),
        lax.psum_scatter(
            proj_bias_grad.astype(jnp.bfloat16), "cell", scatter_dimension=0, tiled=True
        ).astype(jnp.float32),
    )
    qkv_weight_grad, out_weight_grad, fc_weight_grad, proj_weight_grad = (
        lax.psum_scatter(
            qkv_weight_grad.astype(jnp.bfloat16), ("head", "ctx"), scatter_dimension=1, tiled=True
        ).astype(jnp.float32),
        lax.psum_scatter(
            out_weight_grad.astype(jnp.bfloat16), ("head", "ctx"), scatter_dimension=1, tiled=True
        ).astype(jnp.float32),
        lax.psum_scatter(
            fc_weight_grad.astype(jnp.bfloat16), ("head", "ctx"), scatter_dimension=1, tiled=True
        ).astype(jnp.float32),
        lax.psum_scatter(
            proj_weight_grad.astype(jnp.bfloat16), ("head", "ctx"), scatter_dimension=1, tiled=True
        ).astype(jnp.float32),
    )
    (
        table_grad,
        attn_gain_grad,
        attn_shift_grad,
        query_bias_grad,
        value_bias_grad,
        out_bias_grad,
        mlp_gain_grad,
        mlp_shift_grad,
        fc_bias_grad,
        proj_bias_grad,
    ) = lax.psum(
        (
            table_grad,
            attn_gain_grad,
            attn_shift_grad,
            query_bias_grad,
            value_bias_grad,
            out_bias_grad,
            mlp_gain_grad,
            mlp_shift_grad,
            fc_bias_grad,
            proj_bias_grad,
        ),
        ("head", "ctx"),
    )
    return (
        block_out,
        input_grad,
        table_grad,
        attn_gain_grad,
        attn_shift_grad,
        qkv_weight_grad,
        query_bias_grad,
        value_bias_grad,
        out_weight_grad,
        out_bias_grad,
        mlp_gain_grad,
        mlp_shift_grad,
        fc_weight_grad,
        fc_bias_grad,
        proj_weight_grad,
        proj_bias_grad,
    )


def solution(mesh):
    in_specs = (
        P("cell", ("head", "ctx"), None),
        P("cell"),
        P("cell"),
        P(),
        P(),
        P(),
        P(),
        P(),
        P(),
        P(),
        P(),
        P(),
        P(),
        P(),
        P(),
        P(),
        P(),
        P("cell", ("head", "ctx"), None),
    )
    out_specs = (
        P("cell", ("head", "ctx"), None),
        P("cell", ("head", "ctx"), None),
        P(None, "cell"),
        P("cell"),
        P("cell"),
        P("cell", ("head", "ctx")),
        P("cell"),
        P("cell"),
        P("cell", ("head", "ctx")),
        P("cell"),
        P("cell"),
        P("cell"),
        P("cell", ("head", "ctx")),
        P("cell"),
        P("cell", ("head", "ctx")),
        P("cell"),
    )
    return jax.shard_map(body, mesh=mesh, in_specs=in_specs, out_specs=out_specs, check_vma=False)
```

profile of v0, /device:TPU:0, one launch (start us, length us, event | category | flops | bytes accessed | tf_op | source)
XLA Modules:
  0.0 1091.5 jit_solution(7670386799444710307)
XLA Ops:
  13.0 7.4 fusion.73
  21.4 21.7 %all_to_all.120 = bf16[1,256,4,280]{1,3,0,2:T(8,128)(2,1)S(1)} all-to-all(bf16[1,256,4,280]{1,3,0,2:T(8,128)(2,1)S(1)} %get-tuple-element.532), channel_id=1, replica_groups=mesh['cell'=4,'head'=4,'ctx'=2] {'head'}, dimensions={2} | all-to-all | bytes 1146880 | tf_op jit(solution)/shard_map/all_to_all | solution.py:74
  46.5 17.4 %all_to_all.121 = bf16[1,256,4,280]{1,3,0,2:T(8,128)(2,1)S(1)} all-to-all(bf16[1,256,4,280]{1,3,0,2:T(8,128)(2,1)S(1)} %get-tuple-element.531), channel_id=1, replica_groups=mesh['cell'=4,'head'=4,'ctx'=2] {'head'}, dimensions={2} | all-to-all | bytes 1146880 | tf_op jit(solution)/shard_map/all_to_all | solution.py:75
  65.4 3.7 all-to-all-start
  69.1 14.8 %all-to-all-done = bf16[1,256,4,280]{1,3,0,2:T(8,128)(2,1)S(1)} async-done(((bf16[1,256,4,280]{1,3,0,2:T(8,128)(2,1)}), bf16[1,256,4,280]{1,3,0,2:T(8,128)(2,1)S(1)}, u32[]{:S(2)}, u32[]{:S(2)}) %all-to-all-start) | async-done | bytes 573472 | tf_op jit(solution)/shard_map/all_to_all | solution.py:73
  86.5 6.1 all-gather.5.cloned.1.call-done
  93.5 52.4 %while.54 = (s32[]{:T(128)}, bf16[2,512,5,56]{1,3,2,0:T(8,128)(2,1)}, f32[2,5,512]{2,1,0:T(8,128)S(1)}, f32[2,5,512]{2,1,0:T(8,128)S(1)}, s32[2]{0:T(128)S(1)}, ...) while((s32[]{:T(128)}, ...), condition=%wide.region_5.6_spmd.clone.clone, body=%wide.region_2.5_spmd.clone.clone.sunk | while | flops 1239700480 | bytes 158593792 | solution.py:118
  96.2 5.5 fusion.179
  101.8 5.9 fusion.180
  109.1 10.6 fusion.181
  122.4 5.5 fusion.179
  127.9 5.9 fusion.180
  135.3 10.6 fusion.181
  151.0 4.7 copy.83
  156.2 7.4 reduce.12
  163.7 3.6 reshape.400
  167.3 20.1 %all_to_all.122 = bf16[4,2,35840]{2,1,0:T(2,128)(2,1)} all-to-all(bf16[4,2,35840]{2,1,0:T(2,128)(2,1)} %reshape.400), channel_id=1, replica_groups=mesh['cell'=4,'head'=4,'ctx'=2] {'head'}, dimensions={0} | all-to-all | bytes 1146880 | tf_op jit(solution)/shard_map/all_to_all | solution.py:122
  187.3 4.3 reshape.401
  191.6 4.6 copy.84
  202.8 6.8 convolution_add_fusion
  209.6 12.4 %fusion.131 = (bf16[4480]{0:T(1024)(128)(2,1)}, bf16[256,4480]{1,0:T(8,128)(2,1)S(1)}) fusion(f32[256,4480]{1,0:T(8,128)S(1)} %convolution_add_fusion, bf16[4480,1120]{0,1:T(8,128)(2,1)} %param.37, bf16[1,256,1120]{1,2,0:T(8,128)(2,1)S(1)} %copy-done.13), kind=kOutput, calls=%fused_computation.215 | convolution fusion | flops 2593091072 | bytes 17498880 | tf_op jit(solution)/shard_map/nd,fd->nf/dot_general | solution.py:141
  222.1 3.8 multiply_reduce_fusion.1
  229.0 4.2 all-to-all-start.4
  233.2 14.9 %all-to-all-done.4 = bf16[1,256,4,280]{1,3,0,2:T(8,128)(2,1)} async-done(((bf16[1,256,4,280]{1,3,0,2:T(8,128)(2,1)}), bf16[1,256,4,280]{1,3,0,2:T(8,128)(2,1)}, u32[]{:S(2)}, u32[]{:S(2)}) %all-to-all-start.4) | async-done | bytes 573472 | tf_op jit(solution)/shard_map/all_to_all | solution.py:162
  253.5 157.0 %while.55 = (s32[]{:T(128)}, f32[2048,5,56]{0,2,1:T(8,128)S(1)}, f32[2048,5,56]{0,2,1:T(8,128)}, bf16[2,512,5,56]{1,3,2,0:T(8,128)(2,1)}, s32[2]{0:T(128)S(1)}, ...) while((s32[]{:T(128)}, f32[2048,5,56]{0,2,1:T(8,128)S(1)}, ...), condition=%wide.region_12.13_spmd.clone.clone, body=%wide.region_10.12_spmd.clone.clone.sunk | while | flops 2993835520 | bytes 185022880 | solution.py:206
  254.8 11.3 %fusion.191 = f32[5,512,2048]{2,1,0:T(8,128)} fusion(bf16[2048,5,56]{0,2,1:T(8,128)(2,1)} %get-tuple-element.796, bf16[1024,5,56]{0,2,1:T(8,128)(2,1)} %get-tuple-element.795, s32[]{:T(128)S(6)} %select_n.573), kind=kOutput, calls=%fused_computation.63.clone.1 | convolution fusion | flops 587202560 | bytes 22405124 | tf_op jit(solution)/shard_map/while/body/eval_jaxpr/while/body/eval_jaxpr/qhd,khd->hqk/dot_general | solution.py:184
  270.6 18.3 %multiply_reduce_fusion.8 = (f32[5,512]{1,0:T(8,128)S(1)}, f32[5,512,2048]{2,1,0:T(8,128)}) fusion(f32[5,512,2048]{2,1,0:T(8,128)} %fusion.191, f32[5,512]{1,0:T(8,128)S(1)} %get-tuple-element.702, f32[5,512]{1,0:T(8,128)S(1)} %get-tuple-element.703, bf16[2048,5,56]{0,2,1:T(8,128)(2,1)} %get-tuple-element.792, ...), kind=kOutput, calls=%fused_computation.48.clone.1 | convolution fusion | flops 618657280 | bytes 44468228 | tf_op jit(solution)/shard_map/while/body/eval_jaxpr/while/body/eval_jaxpr/qhd,khd->hqk/dot_general | solution.py:95
  288.9 18.0 %multiply_convert_fusion.6 = bf16[5,512,2048]{2,1,0:T(8,128)(2,1)} fusion(f32[5,512,2048]{2,1,0:T(8,128)} %get-tuple-element.704, f32[5,512,2048]{2,1,0:T(8,128)} %fusion.191, f32[5,512]{1,0:T(8,128)S(1)} %get-tuple-element.705), kind=kLoop, calls=%fused_computation.47.clone.1 | loop fusion | flops 15728640 | bytes 52439040 | tf_op jit(solution)/shard_map/while/body/eval_jaxpr/while/body/eval_jaxpr/convert_element_type | solution.py:190
  306.9 6.2 fusion.193
  313.1 7.4 fusion.195
  321.4 10.3 fusion.194
  333.0 11.3 %fusion.191 = f32[5,512,2048]{2,1,0:T(8,128)} fusion(bf16[2048,5,56]{0,2,1:T(8,128)(2,1)} %get-tuple-element.796, bf16[1024,5,56]{0,2,1:T(8,128)(2,1)} %get-tuple-element.795, s32[]{:T(128)S(6)} %select_n.573), kind=kOutput, calls=%fused_computation.63.clone.1 | convolution fusion | flops 587202560 | bytes 22405124 | tf_op jit(solution)/shard_map/while/body/eval_jaxpr/while/body/eval_jaxpr/qhd,khd->hqk/dot_general | solution.py:184
  348.7 18.3 %multiply_reduce_fusion.8 = (f32[5,512]{1,0:T(8,128)S(1)}, f32[5,512,2048]{2,1,0:T(8,128)}) fusion(f32[5,512,2048]{2,1,0:T(8,128)} %fusion.191, f32[5,512]{1,0:T(8,128)S(1)} %get-tuple-element.702, f32[5,512]{1,0:T(8,128)S(1)} %get-tuple-element.703, bf16[2048,5,56]{0,2,1:T(8,128)(2,1)} %get-tuple-element.792, ...), kind=kOutput, calls=%fused_computation.48.clone.1 | convolution fusion | flops 618657280 | bytes 44468228 | tf_op jit(solution)/shard_map/while/body/eval_jaxpr/while/body/eval_jaxpr/qhd,khd->hqk/dot_general | solution.py:95
  367.0 18.0 %multiply_convert_fusion.6 = bf16[5,512,2048]{2,1,0:T(8,128)(2,1)} fusion(f32[5,512,2048]{2,1,0:T(8,128)} %get-tuple-element.704, f32[5,512,2048]{2,1,0:T(8,128)} %fusion.191, f32[5,512]{1,0:T(8,128)S(1)} %get-tuple-element.705), kind=kLoop, calls=%fused_computation.47.clone.1 | loop fusion | flops 15728640 | bytes 52439040 | tf_op jit(solution)/shard_map/while/body/eval_jaxpr/while/body/eval_jaxpr/convert_element_type | solution.py:190
  385.0 6.2 fusion.193
  391.2 7.4 fusion.195
  399.4 10.9 %fusion.194 = f32[2048,5,56]{0,2,1:T(8,128)} fusion(f32[5,512,2048]{2,1,0:T(8,128)} %get-tuple-element.704, f32[2048,5,56]{0,2,1:T(8,128)} %get-tuple-element.768, pred[]{:T(512)S(6)} %compare.12, bf16[1024,5,56]{0,2,1:T(8,128)(2,1)S(1)} %copy-done.8, s32[]{:T(128)S(6)} %select_n.573), kind=kOutput, calls=%fused_computation.57.clone.1 | convolution fusion | flops 593592320 | bytes 25845764 | tf_op jit(solution)/shard_map/while/body/eval_jaxpr/while/body/eval_jaxpr/hqk,qhd->khd/dot_general | solution.py:200
  413.2 7.3 convolution_convert_fusion.1
  424.3 10.4 convolution_convert_fusion
  436.5 3.3 copy.89
  439.8 6.6 reduce.15
  448.5 3.9 all-to-all-start.5
  457.0 6.6 reduce.14
  467.5 4.3 all-to-all-start.6
  471.8 8.8 reduce-scatter.22.cloned.1.call-done
  484.9 6.6 reduce.13
  493.6 4.6 all-to-all-start.7
  501.5 3.7 copy.90
  505.6 4.3 reshape.405
  509.9 4.6 copy.92
  516.4 4.3 reshape.403
  520.7 4.6 copy.94
  531.7 4.9 convolution_convert_fusion.2
  539.2 6.7 fusion.124
  550.5 26.4 %reduce-scatter.32.cloned.1.call-done = bf16[280,4480]{1,0:T(8,128)(2,1)} async-done(((bf16[1120,4480]{1,0:T(8,128)(2,1)}), bf16[280,4480]{1,0:T(8,128)(2,1)}) %reduce-scatter.32.cloned.1.call-update) | async-done | bytes 2508816
  576.9 4.6 copy.106
  581.9 32.8 %reduce-scatter.30.cloned.1.call-done = bf16[280,1120]{1,0:T(8,128)(2,1)} async-done(((bf16[1120,1120]{1,0:T(8,128)(2,1)}), bf16[280,1120]{1,0:T(8,128)(2,1)}) %reduce-scatter.30.cloned.1.call-update) | async-done | bytes 627216
  614.7 86.0 %reduce-scatter.24.cloned.1.call-done = bf16[1120,1120]{1,0:T(8,128)(2,1)} async-done(((bf16[4480,1120]{1,0:T(8,128)(2,1)}), bf16[1120,1120]{1,0:T(8,128)(2,1)}) %reduce-scatter.24.cloned.1.call-update) | async-done | bytes 2508816 | tf_op jit(solution)/shard_map/reduce_scatter | solution.py:277
  700.7 71.8 %reduce-scatter.28.cloned.1.call-done = bf16[280,3360]{1,0:T(8,128)(2,1)} async-done(((bf16[1120,3360]{1,0:T(8,128)(2,1)}), bf16[280,3360]{1,0:T(8,128)(2,1)}) %reduce-scatter.28.cloned.1.call-update) | async-done | bytes 1881616
  777.0 9.1 fusion.84
  786.1 23.4 %all-reduce.24.cloned.1.call-done = (bf16[20,1120]{1,0:T(8,128)(2,1)}, bf16[1120]{0:T(1024)(128)(2,1)}, bf16[1120]{0:T(1024)(128)(2,1)}, bf16[1120]{0:T(1024)(12...) async-done(((bf16[20,1120]{1,0:T(8,128)(2,1)}, ...) | async-done | bytes 71696
  814.0 39.6 %all-reduce.16 = (f32[20,280]{1,0:T(8,128)}, f32[280]{0:T(512)}, f32[280]{0:T(512)}, f32[280]{0:T(512)}, f32[280]{0:T(512)}, /*index=5*/f32[280]{0:T(512)}, f32[...) all-reduce(f32[20,280]{1,0:T(8,128)S(1)} %dynamic-slice_convert_fus, ...), channel_id=1, replica_groups=mesh['cell'=4,'head'=4,'ctx'=2] {'head','ctx'}, use_global_device_ids=true, to_apply=%region_19.20 | all-reduce | flops 8960 | bytes 71680 | tf_op jit(solution)/shard_map/psum | solution.py:336
  853.6 37.5 %reduce-scatter.26.cloned.1.call-done = bf16[560,280]{1,0:T(8,128)(2,1)} async-done(((bf16[4480,280]{1,0:T(8,128)(2,1)}), bf16[560,280]{1,0:T(8,128)(2,1)}) %reduce-scatter.26.cloned.1.call-update) | async-done | bytes 313616
  893.3 182.6 %all-reduce.22.cloned.1.call-done = (bf16[280,3360]{1,0:T(8,128)(2,1)}, bf16[280,1120]{1,0:T(8,128)(2,1)}, bf16[1120,1120]{1,0:T(8,128)(2,1)}) async-done(((bf16[280,3360]{1,0:T(8,128)(2,1)}, bf16[280,1120]{1,0:T(8,128)(2,1)}, bf16[1120,1120]{1,0:T(8,128)(2,1)}), (bf16[280,3360]{1,0:T(8,128)(2,1)}, bf16[280,1120]{1,0:T(8,128)(2,1)}, bf16[1120,1120]{1,0:T(8,128)(2,1)})) %all-reduce.22.cloned.1.call-update) | async-done | bytes 5017616
  (252 shorter events, 111.6 us)
Async XLA Ops:
  7.2 192.6 %copy-start = (bf16[1120,1120]{1,0:T(8,128)(2,1)S(1)}, bf16[1120,1120]{1,0:T(8,128)(2,1)}, u32[]{:S(2)}) copy-start(bf16[1120,1120]{1,0:T(8,128)(2,1)} %param.31) | copy-start | bytes 7526404
  7.2 79.3 %all-gather.3.cloned.1.call-start = ((), (), s32[]{:S(2)}) async-start(), calls=%async_computation.15 | async-start | bytes 1720320 | tf_op jit(solution)/shard_map/all_gather | solution.py:82
  9.0 11.4 %copy-start.24 = (f32[1120]{0:T(1024)}, f32[1120]{0:T(1024)S(1)}, u32[]{:S(2)}) copy-start(f32[1120]{0:T(1024)S(1)} %convolution_reduce_fusion) | copy-start | bytes 13444
  10.3 10.1 copy-start.36
  12.2 8.2 copy-start.39
  46.4 46.2 %all-gather.5.cloned.1.call-start = ((), (), s32[]{:S(2)}) async-start(), calls=%async_computation.16 | async-start | bytes 1720320 | tf_op jit(solution)/shard_map/all_gather | solution.py:83
  65.4 18.5 %all-to-all-start = ((bf16[1,256,4,280]{1,3,0,2:T(8,128)(2,1)}), bf16[1,256,4,280]{1,3,0,2:T(8,128)(2,1)S(1)}, u32[]{:S(2)}, u32[]{:S(2)}) async-start(bf16[1,256,4,280]{1,3,0,2:T(8,128)(2,1)} %get-tuple-element.533), calls=%async_computation | async-start | bytes 1146880 | tf_op jit(solution)/shard_map/all_to_all | solution.py:73
  101.7 7.3 copy-start.2
  101.7 7.3 copy-start.5
  127.9 7.3 copy-start.2
  127.9 7.3 copy-start.5
  191.6 8.2 copy-start.25
  191.6 8.2 copy-start.46
  199.8 2.7 copy-start.16
  199.9 2.9 copy-start.27
  199.9 2.8 copy-start.30
  199.9 2.8 copy-start.41
  202.5 23.4 %copy-start.6 = (f32[256,1120]{0,1:T(8,128)}, f32[256,1120]{0,1:T(8,128)S(1)}, u32[]{:S(2)}) copy-start(f32[256,1120]{0,1:T(8,128)S(1)} %get-tuple-element.537) | copy-start | bytes 3440644
  202.5 23.4 %copy-start.32 = (f32[256]{0:T(256)}, f32[256]{0:T(256)S(1)}, u32[]{:S(2)}) copy-start(f32[256]{0:T(256)S(1)} %broadcast_multiply_fusion) | copy-start | bytes 3076
  202.7 23.2 %copy-start.34 = (f32[256]{0:T(256)}, f32[256]{0:T(256)S(1)}, u32[]{:S(2)}) copy-start(f32[256]{0:T(256)S(1)} %fusion.121) | copy-start | bytes 3076
  202.7 6.9 copy-start.13
  202.8 19.3 %slice-start = ((s8[10035200]{0:T(1024)(128)(4,1)}), s8[4194304]{0:T(1024)(128)(4,1)S(1)}, s32[]{:S(2)}) async-start(s8[10035200]{0:T(1024)(128)(4,1)} %bitcast.232), calls=%async_computation.26 | async-start | bytes 8388608
  209.6 12.4 %copy-start.15 = (f32[256,4480]{1,0:T(8,128)}, f32[256,4480]{1,0:T(8,128)S(1)}, u32[]{:S(2)}) copy-start(f32[256,4480]{1,0:T(8,128)S(1)} %convolution_add_fusion) | copy-start | bytes 13762564
  209.6 12.4 %slice-start.1 = ((s8[10035200]{0:T(1024)(128)(4,1)}), s8[4194304]{0:T(1024)(128)(4,1)S(1)}, s32[]{:S(2)}) async-start(s8[10035200]{0:T(1024)(128)(4,1)} %bitcast.232), calls=%async_computation.27 | async-start | bytes 8388608
  209.6 12.4 %slice-start.2 = ((s8[10035200]{0:T(1024)(128)(4,1)}), s8[1646592]{0:T(1024)(128)(4,1)S(1)}, s32[]{:S(2)}) async-start(s8[10035200]{0:T(1024)(128)(4,1)} %bitcast.232), calls=%async_computation.28 | async-start | bytes 3293184
  222.0 3.9 copy-start.23
  226.3 2.7 copy-start.10
  226.3 2.7 copy-start.42
  227.2 1.7 copy-start.18
  229.0 19.1 %all-to-all-start.4 = ((bf16[1,256,4,280]{1,3,0,2:T(8,128)(2,1)}), bf16[1,256,4,280]{1,3,0,2:T(8,128)(2,1)}, u32[]{:S(2)}, u32[]{:S(2)}) async-start(bf16[1,256,4,280]{1,3,0,2:T(8,128)(2,1)} %bitcast.256), calls=%async_computation.4 | async-start | bytes 1146880 | tf_op jit(solution)/shard_map/all_to_all | solution.py:162
  233.1 219.3 %reduce-scatter.20.cloned.1.call-start = ((), (), s32[]{:S(2)}) async-start(), calls=%async_computation.17 | async-start | bytes 3440640 | tf_op jit(solution)/shard_map/reduce_scatter | solution.py:213
  306.9 6.2 copy-start.4
  306.9 6.2 copy-start.20
  313.1 8.2 copy-start.8
  385.0 6.2 copy-start.4
  385.0 6.2 copy-start.20
  391.2 8.2 copy-start.8
  410.6 2.1 copy-start.28
  410.6 2.1 copy-start.31
  410.6 2.1 copy-start.33
  410.6 2.1 copy-start.35
  412.0 68.6 %reduce-scatter.22.cloned.1.call-start = ((), (), s32[]{:S(2)}) async-start(), calls=%async_computation.18 | async-start | bytes 3440640 | tf_op jit(solution)/shard_map/reduce_scatter | solution.py:214
  412.6 164.3 %reduce-scatter.32.cloned.1.call-start = ((), (), s32[]{:S(2)}) async-start(), calls=%async_computation.23 | async-start | bytes 12544000
  420.6 3.7 copy-start.14
  420.6 194.1 %reduce-scatter.30.cloned.1.call-start = ((), (), s32[]{:S(2)}) async-start(), calls=%async_computation.22 | async-start | bytes 3225600
  424.2 276.5 %reduce-scatter.24.cloned.1.call-start = ((), (), s32[]{:S(2)}) async-start(), calls=%async_computation.19 | async-start | bytes 12902400 | tf_op jit(solution)/shard_map/reduce_scatter | solution.py:277
  448.5 19.0 %all-to-all-start.5 = ((bf16[4,2,35840]{2,1,0:T(2,128)(2,1)}), bf16[4,2,35840]{2,1,0:T(2,128)(2,1)S(1)}, u32[]{:S(2)}, u32[]{:S(2)}) async-start(bf16[4,2,35840]{2,1,0:T(2,128)(2,1)} %reshape.406), calls=%async_computation.5 | async-start | bytes 1146880 | tf_op jit(solution)/shard_map/all_to_all | solution.py:218
  467.5 26.2 %all-to-all-start.6 = ((bf16[4,2,35840]{2,1,0:T(2,128)(2,1)}), bf16[4,2,35840]{2,1,0:T(2,128)(2,1)}, u32[]{:S(2)}, u32[]{:S(2)}) async-start(bf16[4,2,35840]{2,1,0:T(2,128)(2,1)} %reshape.404), calls=%async_computation.7 | async-start | bytes 1146880 | tf_op jit(solution)/shard_map/all_to_all | solution.py:221
  493.6 22.7 %all-to-all-start.7 = ((bf16[4,2,35840]{2,1,0:T(2,128)(2,1)}), bf16[4,2,35840]{2,1,0:T(2,128)(2,1)}, u32[]{:S(2)}, u32[]{:S(2)}) async-start(bf16[4,2,35840]{2,1,0:T(2,128)(2,1)} %reshape.402), calls=%async_computation.9 | async-start | bytes 1146880 | tf_op jit(solution)/shard_map/all_to_all | solution.py:228
  498.2 274.3 %reduce-scatter.28.cloned.1.call-start = ((), (), s32[]{:S(2)}) async-start(), calls=%async_computation.21 | async-start | bytes 9676800
  530.2 1.5 copy-start.9
  530.2 1.5 copy-start.26
  530.2 1.5 copy-start.29
  530.2 1.5 copy-start.37
  530.2 1.5 copy-start.38
  536.7 272.7 %all-reduce.24.cloned.1.call-start = ((), (), s32[]{:S(2)}) async-start(), calls=%async_computation.25 | async-start | bytes 196608
  539.2 6.7 copy-start.45
  539.2 7.1 copy-start.43
  545.9 1.6 copy-start.11
  550.4 340.7 %reduce-scatter.26.cloned.1.call-start = ((), (), s32[]{:S(2)}) async-start(), calls=%async_computation.20 | async-start | bytes 3870720
  581.5 494.4 %all-reduce.22.cloned.1.call-start = ((), (), s32[]{:S(2)}) async-start(), calls=%async_computation.24 | async-start | bytes 10321920
  772.6 2.5 copy-start.48
  772.6 4.4 copy-start.47
  1075.9 8.8 copy-start.1
  (11 other events, 11.5 us)
Sparse Core Ops, SparseCore 0:
  46.6 21.4 all-gather.2
  70.2 22.3 all-gather.4
  412.1 32.1 reduce-scatter.19
  446.5 34.0 reduce-scatter.21
  483.0 93.8 reduce-scatter.31
  579.3 35.3 reduce-scatter.29
  617.3 83.3 reduce-scatter.23
  703.3 69.2 reduce-scatter.27
  776.7 32.6 all-reduce.23
  812.9 78.1 reduce-scatter.25
  895.1 180.7 all-reduce.21
where the time goes:
time: 1100 us; the launch traced here: 1090 us
  waiting for transfers between devices  508 us (46%)
  matrix products  216 us (20%)
  local copies, waits for them, and re-layouts  115 us (10%)
  other arithmetic  107 us (10%)
  blocking collectives  98.8 us (9%)
  starting transfers between devices  21.3 us (2%)
  between operations  18.3 us (2%)
    unnamed x17, waiting for transfers between devices  375 us
    reduce_scatter x1, waiting for transfers between devices, body(): lax.psum_scatter(proj_weight_grad.astype(jnp.bfloat16), 'cell', scatter_d...  86 us
    dot_general x4, matrix products, masked_scores(): jnp.einsum('qhd,khd->hqk', queries, cell_keys, preferred_element_type=jnp...  47.6 us
    unnamed x109, local copies, waits for them, and re-layouts  44.8 us
    psum x1, blocking collectives, body(): lax.psum((table_grad, attn_gain_grad, attn_shift_grad, query_bias_grad, v...  39.6 us
    convert_element_type x2, other arithmetic, back_block(): score_low = score_grad.astype(jnp.bfloat16)  35.9 us
    unnamed x7, other arithmetic  27.1 us
    dot_general x2, matrix products, back_block(): jnp.einsum('qhd,khd->hqk', out_grad, cell_values, preferred_element_type=...  22.5 us
  transfers between devices with their start and end apart: 16, of which 12 were waited for; matrix products, arithmetic and copies ran while one was open for 12% of the time, Pallas kernels for 0%

commit v1 on v0

v1 whole, which is shorter than its diff:
```python
import math

import jax
import jax.numpy as jnp
from jax import lax
from jax.experimental import pallas as pl
from jax.experimental.pallas import tpu as pltpu
from jax.sharding import PartitionSpec as P

HEADS = 20
HD = 56


epsilon = 1e-05
MASKED = -1e30
LOG2E = math.log2(math.e)


def layer_norm(values, gain_row, shift_row):
    center = values - jnp.mean(values, axis=-1, keepdims=True)
    spread = jnp.mean(center * center, axis=-1, keepdims=True)
    return center * lax.rsqrt(spread + epsilon) * gain_row + shift_row


def gelu_tanh(values):
    return jax.nn.gelu(values, approximate=True)


def swap(values, axis, bit):
    return lax.ppermute(values, axis, [(i, i ^ bit) for i in range(lax.axis_size(axis))])


def bits_of(axis):
    size, bit, found = lax.axis_size(axis), 1, []
    while bit < size:
        found.append((axis, bit))
        bit *= 2
    return found


def nn(a, b):
    return jnp.dot(a, b, preferred_element_type=jnp.float32)


def nt(a, b):
    return lax.dot_general(a, b, (((1,), (1,)), ((), ())), preferred_element_type=jnp.float32)


def weight_blocks(pairs, left_ids, right_ids):
    count = left_ids.shape[0]
    pair_count = len(pairs)
    rows = pairs[0][0].shape[1]
    cols = sum(r.shape[2] for _, r in pairs)

    def kernel(li, ri, *refs):
        i = pl.program_id(0)
        out = refs[-1]
        parts = []
        for p in range(pair_count):
            parts.append(nn(refs[2 * p][li[i]], refs[2 * p + 1][ri[i]]))
        whole = parts[0] if pair_count == 1 else jnp.concatenate(parts, axis=-1)
        out[0] = whole.astype(jnp.bfloat16)

    flat = [x for pair in pairs for x in pair]
    return pl.pallas_call(
        kernel,
        out_shape=jax.ShapeDtypeStruct((count, rows, cols), jnp.bfloat16),
        grid_spec=pltpu.PrefetchScalarGridSpec(
            num_scalar_prefetch=2,
            grid=(count,),
            in_specs=[
                pl.BlockSpec(x.shape, lambda i, li, ri: (0, 0, 0), pipeline_mode=pl.Buffered(1))
                for x in flat
            ],
            out_specs=pl.BlockSpec((1, rows, cols), lambda i, li, ri: (i, 0, 0)),
        ),
        name="weight_blocks",
    )(left_ids, right_ids, *flat)


def relative_ids(steps):
    count = 1
    for axis, _ in steps:
        count *= 2
    places = jnp.arange(count, dtype=jnp.int32)
    rel = {"cell": jnp.zeros_like(places), "head": jnp.zeros_like(places), "ctx": jnp.zeros_like(places)}
    for s, (axis, bit) in enumerate(steps):
        on = (places >> (len(steps) - 1 - s)) & 1
        rel[axis] = rel[axis] + on * bit
    cell_ids = rel["cell"] ^ lax.axis_index("cell")
    part_ids = (rel["head"] ^ lax.axis_index("head")) * lax.axis_size("ctx") + (
        rel["ctx"] ^ lax.axis_index("ctx")
    )
    return cell_ids, part_ids


def add_up(kept, got):
    return kept.astype(jnp.float32) + got.astype(jnp.float32)


def scatter_sum(kept, sent, steps):
    total = None
    for s, (axis, bit) in enumerate(steps):
        if s:
            total = total.astype(jnp.bfloat16)
            half = total.shape[0] // 2
            kept, sent = total[:half], total[half:]
        total = add_up(kept, swap(sent, axis, bit))
    return total[0]


def head_dims(qkv_ref):
    width = qkv_ref.shape[-1] // 3
    return width, width // HD


def chunk_mask(start, seq_len, query_start, rows, cols):
    key_pos = start + lax.broadcasted_iota(jnp.int32, (rows, cols), 0)
    if query_start is None:
        return key_pos < seq_len
    query_pos = query_start + lax.broadcasted_iota(jnp.int32, (rows, cols), 1)
    return (key_pos < seq_len) & (key_pos <= query_pos)


def sweep(i, half, seq_len, rows, visit, blocks):
    def own(j, carry):
        visit(j, (2 * j + half) * rows, False)
        return carry

    def other(j, carry):
        visit(blocks + j, (2 * j + 1 - half) * rows, False)
        return carry

    span = 2 * rows
    own_count = jnp.minimum(i, (seq_len - half * rows + span - 1) // span)
    other_count = jnp.minimum(i + half, (seq_len - (1 - half) * rows + span - 1) // span)
    lax.fori_loop(0, other_count, other, 0)
    lax.fori_loop(0, own_count, own, 0)
    visit(i, (2 * i + half) * rows, True)


def attend_kernel(info, qkv, kv_other, out, out_t, logs, q_t, k_n, v_t, acc, m_ref, l_ref):
    width, heads = head_dims(qkv)
    blocks, rows = q_t.shape[0], q_t.shape[-1]
    seq_len, half = info[0], info[1]
    factor = LOG2E / math.sqrt(HD)

    def prepare(b, carry):
        at = pl.ds(pl.multiple_of(b * rows, rows), rows)
        mine = qkv[at, :]
        mine_t = mine.astype(jnp.float32).T
        theirs = kv_other[at, :]
        theirs_t = theirs[:, width:].astype(jnp.float32).T
        for h in range(heads):
            lo, hi = h * HD, (h + 1) * HD
            q_t[b, h] = mine_t[lo:hi].astype(jnp.bfloat16)
            v_t[b, h] = mine_t[2 * width + lo : 2 * width + hi].astype(jnp.bfloat16)
            k_n[b, h] = mine[:, width + lo : width + hi]
            v_t[blocks + b, h] = theirs_t[lo:hi].astype(jnp.bfloat16)
            k_n[blocks + b, h] = theirs[:, lo:hi]
        return carry

    lax.fori_loop(0, blocks, prepare, 0)

    def block(i, carry):
        acc[...] = jnp.zeros_like(acc)
        m_ref[...] = jnp.full_like(m_ref, MASKED)
        l_ref[...] = jnp.zeros_like(l_ref)

        def visit(j, start, diagonal):
            query_start = (2 * i + half) * rows if diagonal else None
            allowed = chunk_mask(start, seq_len, query_start, rows, rows)
            for h in range(heads):
                s = nn(k_n[j, h], q_t[i, h]) * factor
                s = jnp.where(allowed, s, MASKED)
                old = m_ref[h]
                new = jnp.maximum(old, jnp.max(s, axis=0, keepdims=True))
                shrink = jnp.exp2(old - new)
                p = jnp.exp2(s - new)
                l_ref[h] = l_ref[h] * shrink + jnp.sum(p, axis=0, keepdims=True)
                acc[h] = acc[h] * shrink + nn(v_t[j, h], p.astype(jnp.bfloat16))
                m_ref[h] = new

        sweep(i, half, seq_len, rows, visit, blocks)
        at = pl.ds(pl.multiple_of(i * rows, rows), rows)
        for h in range(heads):
            out_t[i, h * HD : (h + 1) * HD, :] = acc[h] / l_ref[h]
            logs[i, h] = m_ref[h] + jnp.log2(l_ref[h])
        out[at, :] = out_t[i].T.astype(jnp.bfloat16)
        return carry

    lax.fori_loop(0, blocks, block, 0)


def vmem_specs(count):
    return [pl.BlockSpec(memory_space=pltpu.VMEM)] * count


def attend(info, qkv, kv_other, blocks):
    rows_all, wide = qkv.shape
    width = wide // 3
    heads, rows = width // HD, rows_all // blocks
    bf, f32 = jnp.bfloat16, jnp.float32
    pairs = blocks * rows * rows * (blocks + 1)
    return pl.pallas_call(
        attend_kernel,
        out_shape=(
            jax.ShapeDtypeStruct((rows_all, width), bf),
            jax.ShapeDtypeStruct((blocks, width, rows), f32),
            jax.ShapeDtypeStruct((blocks, heads, 1, rows), f32),
        ),
        in_specs=[pl.BlockSpec(memory_space=pltpu.SMEM)] + vmem_specs(2),
        out_specs=tuple(vmem_specs(3)),
        scratch_shapes=[
            pltpu.VMEM((blocks, heads, HD, rows), bf),
            pltpu.VMEM((2 * blocks, heads, rows, HD), bf),
            pltpu.VMEM((2 * blocks, heads, HD, rows), bf),
            pltpu.VMEM((heads, HD, rows), f32),
            pltpu.VMEM((heads, 1, rows), f32),
            pltpu.VMEM((heads, 1, rows), f32),
        ],
        cost_estimate=pl.CostEstimate(
            flops=20 * 1024 * 1024 * 1024, transcendentals=pairs * heads, bytes_accessed=8 * 1024 * 1024
        ),
        name="attend",
    )(info, qkv, kv_other)


def back_kernel(
    info, qkv, kv_other, grad, out_t, logs,
    dq, dkv, dkv_other,
    q_t, g_t, k_n, k_t, v_n, dq_t, dk_t, dv_t, delta,
):
    width, heads = head_dims(qkv)
    blocks, rows = q_t.shape[0], q_t.shape[-1]
    seq_len, half = info[0], info[1]
    scale = 1.0 / math.sqrt(HD)
    factor = LOG2E * scale

    def prepare(b, carry):
        at = pl.ds(pl.multiple_of(b * rows, rows), rows)
        mine = qkv[at, :]
        mine_t = mine[:, : 2 * width].astype(jnp.float32).T
        grad_t = grad[at, :].astype(jnp.float32).T
        theirs = kv_other[at, :]
        theirs_t = theirs[:, :width].astype(jnp.float32).T
        for h in range(heads):
            lo, hi = h * HD, (h + 1) * HD
            q_t[b, h] = mine_t[lo:hi].astype(jnp.bfloat16)
            g_t[b, h] = grad_t[lo:hi].astype(jnp.bfloat16)
            delta[b, h] = jnp.sum(grad_t[lo:hi] * out_t[b, lo:hi], axis=0, keepdims=True)
            k_t[b, h] = mine_t[width + lo : width + hi].astype(jnp.bfloat16)
            k_n[b, h] = mine[:, width + lo : width + hi]
            v_n[b, h] = mine[:, 2 * width + lo : 2 * width + hi]
            k_t[blocks + b, h] = theirs_t[lo:hi].astype(jnp.bfloat16)
            k_n[blocks + b, h] = theirs[:, lo:hi]
            v_n[blocks + b, h] = theirs[:, width + lo : width + hi]
        return carry

    lax.fori_loop(0, blocks, prepare, 0)
    dk_t[...] = jnp.zeros_like(dk_t)
    dv_t[...] = jnp.zeros_like(dv_t)

    def block(i, carry):
        dq_t[...] = jnp.zeros_like(dq_t)

        def visit(j, start, diagonal):
            query_start = (2 * i + half) * rows if diagonal else None
            allowed = chunk_mask(start, seq_len, query_start, rows, rows)
            for h in range(heads):
                at = slice(h * HD, (h + 1) * HD)
                s = nn(k_n[j, h], q_t[i, h]) * factor - logs[i, h]
                p = jnp.exp2(jnp.where(allowed, s, MASKED))
                dv_t[j, at] += nt(g_t[i, h], p.astype(jnp.bfloat16))
                dp = nn(v_n[j, h], g_t[i, h])
                ds = (p * (dp - delta[i, h])).astype(jnp.bfloat16)
                dq_t[at] += nn(k_t[j, h], ds)
                dk_t[j, at] += nt(q_t[i, h], ds)

        sweep(i, half, seq_len, rows, visit, blocks)
        at = pl.ds(pl.multiple_of(i * rows, rows), rows)
        dq[at, :] = (dq_t[...] * scale).T.astype(dq.dtype)
        return carry

    lax.fori_loop(0, blocks, block, 0)

    def finish(b, carry):
        at = pl.ds(pl.multiple_of(b * rows, rows), rows)
        dkv[at, :width] = (dk_t[b] * scale).T.astype(dkv.dtype)
        dkv[at, width:] = dv_t[b].T.astype(dkv.dtype)
        dkv_other[at, :width] = (dk_t[blocks + b] * scale).T.astype(dkv_other.dtype)
        dkv_other[at, width:] = dv_t[blocks + b].T.astype(dkv_other.dtype)
        return carry

    lax.fori_loop(0, blocks, finish, 0)


def attend_back(info, qkv, kv_other, grad, out_t, logs, blocks):
    rows_all, wide = qkv.shape
    width = wide // 3
    heads, rows = width // HD, rows_all // blocks
    bf, f32 = jnp.bfloat16, jnp.float32
    pairs = blocks * rows * rows * (blocks + 1)
    return pl.pallas_call(
        back_kernel,
        out_shape=(
            jax.ShapeDtypeStruct((rows_all, width), bf),
            jax.ShapeDtypeStruct((rows_all, 2 * width), bf),
            jax.ShapeDtypeStruct((rows_all, 2 * width), bf),
        ),
        in_specs=[pl.BlockSpec(memory_space=pltpu.SMEM)] + vmem_specs(5),
        out_specs=tuple(vmem_specs(3)),
        scratch_shapes=[
            pltpu.VMEM((blocks, heads, HD, rows), bf),
            pltpu.VMEM((blocks, heads, HD, rows), bf),
            pltpu.VMEM((2 * blocks, heads, rows, HD), bf),
            pltpu.VMEM((2 * blocks, heads, HD, rows), bf),
            pltpu.VMEM((2 * blocks, heads, rows, HD), bf),
            pltpu.VMEM((width, rows), f32),
            pltpu.VMEM((2 * blocks, width, rows), f32),
            pltpu.VMEM((2 * blocks, width, rows), f32),
            pltpu.VMEM((blocks, heads, 1, rows), f32),
        ],
        cost_estimate=pl.CostEstimate(
            flops=60 * 1024 * 1024 * 1024, transcendentals=pairs * heads, bytes_accessed=8 * 1024 * 1024
        ),
        name="attend_back",
    )(info, qkv, kv_other, grad, out_t, logs)


def column_blocks(values, count):
    return values.reshape(values.shape[0], count, -1).transpose(1, 0, 2)


def row_blocks(values, count):
    return values.reshape(values.shape[0], count, -1).transpose(1, 2, 0)


def block_sum(pairs, by_cell_left, steps):
    cell_ids, part_ids = relative_ids(steps)
    left, right = (cell_ids, part_ids) if by_cell_left else (part_ids, cell_ids)
    half = left.shape[0] // 2
    sent = weight_blocks(pairs, left[half:], right[half:])
    kept = weight_blocks(pairs, left[:half], right[:half])
    return kept, sent


def body(
    inputs,
    dataset_ids,
    lengths,
    dataset_table,
    attn_gain,
    attn_shift,
    qkv_weight,
    query_bias,
    value_bias,
    out_weight,
    out_bias,
    mlp_gain,
    mlp_shift,
    fc_weight,
    fc_bias,
    proj_weight,
    proj_bias,
    cotangent,
):
    cell_count, row_count, model_width = inputs.shape
    cells = lax.axis_size("cell")
    groups = lax.axis_size("head")
    halves = lax.axis_size("ctx")
    parts = groups * halves
    half_index = lax.axis_index("ctx")
    head_width = HEADS // groups * HD
    token_count = cell_count * row_count
    ctx_rows = groups * row_count
    cell_steps, ctx_steps, head_steps = bits_of("cell"), bits_of("ctx"), bits_of("head")[::-1]
    steps_x = cell_steps + ctx_steps + head_steps
    steps_y = cell_steps[:1] + ctx_steps + cell_steps[1:] + head_steps
    one_hot = (
        dataset_ids[:, None] == jnp.arange(dataset_table.shape[0], dtype=jnp.int32)[None, :]
    ).astype(jnp.bfloat16)
    embedded = jnp.dot(one_hot, dataset_table, preferred_element_type=jnp.float32)
    residual = (inputs.astype(jnp.float32) + embedded[:, None, :]).reshape(token_count, model_width)
    normed = layer_norm(residual, attn_gain, attn_shift).astype(jnp.bfloat16)
    mixed_qkv = jnp.dot(normed, qkv_weight, preferred_element_type=jnp.float32)
    bias_row = jnp.concatenate([query_bias, jnp.zeros_like(query_bias), value_bias])
    mixed_qkv = (mixed_qkv + bias_row).astype(jnp.bfloat16)

    def to_heads(values):
        sections = values.shape[1] // model_width
        values = values.reshape(cell_count, row_count, sections, groups, head_width)
        values = values.transpose(3, 0, 1, 2, 4).reshape(groups, cell_count, row_count, -1)
        values = lax.all_to_all(values, "head", split_axis=0, concat_axis=0, tiled=True)
        return values.transpose(1, 0, 2, 3).reshape(cell_count, ctx_rows, -1)

    def to_rows(values):
        sections = values.shape[-1] // head_width
        values = values.reshape(cell_count, groups, row_count, -1).transpose(1, 0, 2, 3)
        values = lax.all_to_all(values, "head", split_axis=0, concat_axis=0, tiled=True)
        values = values.reshape(groups, cell_count, row_count, sections, head_width)
        return values.transpose(1, 2, 3, 0, 4).reshape(token_count, sections * model_width)

    qkv_heads = to_heads(mixed_qkv)
    kv_other = swap(qkv_heads[:, :, head_width:], "ctx", 1)
    infos = [jnp.stack([lengths[n], half_index.astype(jnp.int32)]) for n in range(cell_count)]
    runs = [attend(infos[n], qkv_heads[n], kv_other[n], groups) for n in range(cell_count)]
    attended = jnp.stack([r[0] for r in runs])
    attended_rows = to_rows(attended)
    attn_out = jnp.dot(attended_rows, out_weight, preferred_element_type=jnp.float32) + out_bias
    middle = residual + attn_out
    mlp_normed = layer_norm(middle, mlp_gain, mlp_shift).astype(jnp.bfloat16)
    hidden = jnp.dot(mlp_normed, fc_weight, preferred_element_type=jnp.float32) + fc_bias
    active = gelu_tanh(hidden).astype(jnp.bfloat16)
    branch = jnp.dot(active, proj_weight, preferred_element_type=jnp.float32) + proj_bias
    block_out = (middle + branch).astype(jnp.bfloat16).reshape(cell_count, row_count, model_width)
    grad_low = cotangent.reshape(token_count, model_width)
    grad_top = grad_low.astype(jnp.float32)
    proj_bias_grad = jnp.sum(grad_top, axis=0)
    active_grad = jnp.einsum("nd,fd->nf", grad_low, proj_weight, preferred_element_type=jnp.float32)
    gelu_pull = jax.vjp(gelu_tanh, hidden)[1]
    hidden_grad = gelu_pull(active_grad)[0].astype(jnp.bfloat16)
    fc_bias_grad = jnp.sum(hidden_grad, axis=0, dtype=jnp.float32)
    normed_grad = jnp.einsum(
        "nf,df->nd", hidden_grad, fc_weight, preferred_element_type=jnp.float32
    )
    mlp_pull = jax.vjp(layer_norm, middle, mlp_gain, mlp_shift)[1]
    middle_part, mlp_gain_grad, mlp_shift_grad = mlp_pull(normed_grad)
    middle_grad = grad_top + middle_part
    middle_low = middle_grad.astype(jnp.bfloat16)
    out_bias_grad = jnp.sum(middle_low, axis=0, dtype=jnp.float32)
    attended_grad = jnp.einsum(
        "ne,de->nd", middle_low, out_weight, preferred_element_type=jnp.float32
    ).astype(jnp.bfloat16)
    grad_heads = to_heads(attended_grad)

    fc_kept, fc_sent = block_sum(
        [(row_blocks(mlp_normed, cells), column_blocks(hidden_grad, parts))], True, steps_x
    )
    po_kept, po_sent = block_sum(
        [
            (row_blocks(grad_low, parts), column_blocks(active, cells)),
            (row_blocks(middle_low, parts), column_blocks(attended_rows, cells)),
        ],
        False,
        steps_y,
    )
    grad_heads, fc_kept, fc_sent, po_kept, po_sent = lax.optimization_barrier(
        (grad_heads, fc_kept, fc_sent, po_kept, po_sent)
    )
    fc_weight_grad = scatter_sum(fc_kept, fc_sent, steps_x)
    po_grad = scatter_sum(po_kept, po_sent, steps_y)
    proj_rows = active.shape[1] // cells
    proj_weight_grad = po_grad[:, :proj_rows].T
    out_weight_grad = po_grad[:, proj_rows:].T

    backs = [
        attend_back(
            infos[n], qkv_heads[n], kv_other[n], grad_heads[n], runs[n][1], runs[n][2], groups
        )
        for n in range(cell_count)
    ]
    dq = jnp.stack([b[0] for b in backs])
    dkv = jnp.stack([b[1] for b in backs])
    dkv_got = swap(jnp.stack([b[2] for b in backs]), "ctx", 1)
    dkv = add_up(dkv, dkv_got).astype(jnp.bfloat16)
    qkv_grad = to_rows(jnp.concatenate([dq, dkv], axis=-1))
    qkv_kept, qkv_sent = block_sum(
        [(row_blocks(normed, cells), column_blocks(qkv_grad, parts))], True, steps_x
    )
    qkv_weight_grad = scatter_sum(qkv_kept, qkv_sent, steps_x)
    column_sums = jnp.sum(qkv_grad, axis=0, dtype=jnp.float32)
    query_bias_grad = column_sums[:model_width]
    value_bias_grad = column_sums[2 * model_width :]
    normed_back = jnp.einsum("ne,de->nd", qkv_grad, qkv_weight, preferred_element_type=jnp.float32)
    attn_pull = jax.vjp(layer_norm, residual, attn_gain, attn_shift)[1]
    residual_part, attn_gain_grad, attn_shift_grad = attn_pull(normed_back)
    residual_grad = middle_grad + residual_part
    input_grad = residual_grad.astype(jnp.bfloat16).reshape(cell_count, row_count, model_width)
    cell_totals = jnp.sum(residual_grad.reshape(cell_count, row_count, model_width), axis=1)
    table_grad = jnp.dot(
        one_hot.astype(jnp.float32).T, cell_totals, precision=lax.Precision.HIGHEST
    )

    width = model_width // cells
    vectors = [
        attn_gain_grad,
        attn_shift_grad,
        query_bias_grad,
        value_bias_grad,
        out_bias_grad,
        mlp_gain_grad,
        mlp_shift_grad,
        proj_bias_grad,
    ]
    fc_rows = fc_bias_grad.shape[0] // model_width
    packed = jnp.concatenate(
        [table_grad.reshape(-1, cells, width).transpose(1, 0, 2)]
        + [v.reshape(cells, 1, width) for v in vectors]
        + [fc_bias_grad.reshape(cells, fc_rows, width)],
        axis=1,
    )
    cell_index = lax.axis_index("cell")
    for axis, bit in cell_steps[::-1]:
        on = (cell_index // bit) % 2
        half = packed.shape[0] // 2
        kept = lax.dynamic_slice_in_dim(packed, on * half, half, 0)
        sent = lax.dynamic_slice_in_dim(packed, (1 - on) * half, half, 0)
        packed = kept + swap(sent, axis, bit)
    for axis, bit in ctx_steps + head_steps:
        packed = packed + swap(packed, axis, bit)
    packed = packed[0]
    datasets = dataset_table.shape[0]
    table_grad = packed[:datasets]
    (
        attn_gain_grad,
        attn_shift_grad,
        query_bias_grad,
        value_bias_grad,
        out_bias_grad,
        mlp_gain_grad,
        mlp_shift_grad,
        proj_bias_grad,
    ) = [packed[datasets + n] for n in range(len(vectors))]
    fc_bias_grad = packed[datasets + len(vectors) :].reshape(-1)
    return (
        block_out,
        input_grad,
        table_grad,
        attn_gain_grad,
        attn_shift_grad,
        qkv_weight_grad,
        query_bias_grad,
        value_bias_grad,
        out_weight_grad,
        out_bias_grad,
        mlp_gain_grad,
        mlp_shift_grad,
        fc_weight_grad,
        fc_bias_grad,
        proj_weight_grad,
        proj_bias_grad,
    )


def solution(mesh):
    in_specs = (
        P("cell", ("head", "ctx"), None),
        P("cell"),
        P("cell"),
        P(),
        P(),
        P(),
        P(),
        P(),
        P(),
        P(),
        P(),
        P(),
        P(),
        P(),
        P(),
        P(),
        P(),
        P("cell", ("head", "ctx"), None),
    )
    out_specs = (
        P("cell", ("head", "ctx"), None),
        P("cell", ("head", "ctx"), None),
        P(None, "cell"),
        P("cell"),
        P("cell"),
        P("cell", ("head", "ctx")),
        P("cell"),
        P("cell"),
        P("cell", ("head", "ctx")),
        P("cell"),
        P("cell"),
        P("cell"),
        P("cell", ("head", "ctx")),
        P("cell"),
        P("cell", ("head", "ctx")),
        P("cell"),
    )
    return jax.shard_map(body, mesh=mesh, in_specs=in_specs, out_specs=out_specs, check_vma=False)
```

time: 1100 us -> 698 us (0.63)
  waiting for transfers between devices: 508 us -> 287 us
  matrix products: 216 us -> 56.2 us
  Pallas kernels: 0 us -> 130 us
  other arithmetic: 107 us -> 50.4 us
  blocking collectives: 98.8 us -> 46.3 us
  local copies, waits for them, and re-layouts: 115 us -> 72.2 us
  starting transfers between devices: 21.3 us -> 41.8 us
  between operations: 18.3 us -> 3.45 us
    unnamed x17 -> x0, waiting for transfers between devices: 375 us -> none
    ppermute x0 -> x22, waiting for transfers between devices: none -> 238 us  [swap(): lax.ppermute(values, axis, [(i, i ^ bit) for i in range(lax.axis_size(axi...]
    dot_general x18 -> x0, matrix products: 165 us -> none  [the longest x4 47.6 us: masked_scores(): jnp.einsum('qhd,khd->hqk', queries, cell_keys, preferred_element_type=jnp...]
    pallas_call x0 -> x8, Pallas kernels: none -> 130 us  [the longest x6 68.5 us: weight_blocks(): pl.pallas_call(kernel, out_shape=jax.ShapeDtypeStruct((count, rows, cols)...]
    reduce_scatter x3 -> x0, waiting for transfers between devices: 94.8 us -> none  [the longest x1 86 us: body(): lax.psum_scatter(proj_weight_grad.astype(jnp.bfloat16), 'cell', scatter_d...]
    psum x1 -> x0, blocking collectives: 39.6 us -> none  [body(): lax.psum((table_grad, attn_gain_grad, attn_shift_grad, query_bias_grad, v...]
    unnamed x109 -> x98, local copies, waits for them, and re-layouts: 44.8 us -> 6 us
    ppermute x0 -> x22, starting transfers between devices: none -> 28.4 us  [swap(): lax.ppermute(values, axis, [(i, i ^ bit) for i in range(lax.axis_size(axi...]
  transfers between devices with their start and end apart: 16 -> 25, of which waited for: 12 -> 14; matrix products, arithmetic and copies ran while one was open for 12% -> 15% of each run, Pallas kernels for 0% -> 15%
where the time goes in v1:
time: 698 us; the launch traced here: 687 us
  waiting for transfers between devices  287 us (41%)
  Pallas kernels  130 us (19%)
  local copies, waits for them, and re-layouts  72.2 us (10%)
  matrix products  56.2 us (8%)
  other arithmetic  50.4 us (7%)
  blocking collectives  46.3 us (7%)
  starting transfers between devices  41.8 us (6%)
    ppermute x22, waiting for transfers between devices, swap(): lax.ppermute(values, axis, [(i, i ^ bit) for i in range(lax.axis_size(axi...  238 us
    pallas_call x6, Pallas kernels, weight_blocks(): pl.pallas_call(kernel, out_shape=jax.ShapeDtypeStruct((count, rows, cols)...  68.5 us
    all_to_all x2, waiting for transfers between devices, to_rows(): lax.all_to_all(values, 'head', split_axis=0, concat_axis=0, tiled=True)  48.8 us
    all_to_all x1, blocking collectives, to_heads(): lax.all_to_all(values, 'head', split_axis=0, concat_axis=0, tiled=True)  46.3 us
    convert_element_type x12, other arithmetic, scatter_sum(): total = total.astype(jnp.bfloat16)  34.5 us
    pallas_call x1, Pallas kernels, attend_back(): pl.pallas_call(back_kernel, out_shape=(jax.ShapeDtypeStruct((rows_all, wi...  32.4 us
    pallas_call x1, Pallas kernels, attend(): pl.pallas_call(attend_kernel, out_shape=(jax.ShapeDtypeStruct((rows_all,...  28.8 us
    ppermute x22, starting transfers between devices, swap(): lax.ppermute(values, axis, [(i, i ^ bit) for i in range(lax.axis_size(axi...  28.4 us
  transfers between devices with their start and end apart: 25, of which 14 were waited for; matrix products, arithmetic and copies ran while one was open for 15% of the time, Pallas kernels for 15%

profile of v1, /device:TPU:0, one launch (start us, length us, event | category | flops | bytes accessed | tf_op | source)
XLA Modules:
  0.0 686.8 jit_solution(12670788029023272829)
XLA Ops:
  2.5 2.3 convert_add_fusion.2
  5.8 7.2 %fusion = bf16[256,3360]{0,1:T(8,128)(2,1)S(1)} fusion(bf16[1120,3360]{1,0:T(8,128)(2,1)} %param.24, f32[3360]{0:T(1024)S(1)} %concatenate.14, bf16[1,256,1120]{1,2,0:T(8,128)(2,1)S(1)} %copy-done.14, f32[1120]{0:T(1024)S(1)} %copy-done.36, f32[1120]{0:T(1024)S(1)} %copy-done.24, f32[256]{0:T(256)S(1)} %fusion.28, f32[256]{0:T(256)S(1)} %broadcast_multiply_fusion.1, ...), kind=kOutput, calls=%fused_computation.9 | convolution fusion | flops 1930485760 | bytes 9849088 | tf_op jit(solution)/shard_map/dot_general | solution.py:386
  13.2 46.3 %all_to_all.20 = bf16[4,1,256,840]{2,3,1,0:T(8,128)(2,1)S(1)} all-to-all(bf16[4,1,256,840]{2,3,1,0:T(8,128)(2,1)S(1)} %bitcast.155), channel_id=1, replica_groups=mesh['cell'=4,'head'=4,'ctx'=2] {'head'}, dimensions={0} | all-to-all | bytes 3440640 | tf_op jit(solution)/shard_map/all_to_all | solution.py:394
  64.5 3.5 copy.79
  68.0 20.2 %collective-permute-done = bf16[1,1024,560]{1,2,0:T(8,128)(2,1)} collective-permute-done((bf16[1,1024,560]{1,2,0:T(8,128)(2,1)}, bf16[1,1024,560]{1,2,0:T(8,128)(2,1)}, u32[]{:S(2)}, u32[]{:S(2)}) %collective-permute-start) | collective-permute-done | bytes 1146912 | tf_op jit(solution)/shard_map/ppermute | solution.py:30
  88.3 2.4 copy.81
  90.7 28.8 %attend.1 = (bf16[1024,280]{1,0:T(8,128)(2,1)}, f32[4,280,256]{2,1,0:T(8,128)}, f32[4,5,1,256]{3,2,1,0:T(1,128)}) custom-call(s32[2]{0:T(128)} %pad_add_fusion.info, bf16[1024,840]{1,0:T(8,128)(2,1)} %bitcast.165, bf16[1024,560]{1,0:T(8,128)(2,1)} %bitcast.168), custom_call_target="tpu_custom_call" | custom-call | flops 21474836480 | bytes 8388608 | tf_op jit(solution)/shard_map/attend/pallas_call | solution.py:205
  119.5 2.3 copy.82
  121.8 4.4 all-to-all-start.1
  127.1 13.0 %all-to-all-done.1 = bf16[4,1,256,280]{2,3,1,0:T(8,128)(2,1)} async-done(((bf16[4,1,256,280]{2,3,1,0:T(8,128)(2,1)}), bf16[4,1,256,280]{2,3,1,0:T(8,128)(2,1)}, u32[]{:S(2)}, u32[]{:S(2)}) %all-to-all-start.1) | async-done | bytes 573472 | tf_op jit(solution)/shard_map/all_to_all | solution.py:400
  142.7 2.6 fusion.49
  146.1 9.9 %multiply_convert_fusion = (bf16[256,4480]{1,0:T(8,128)(2,1)}, f32[256,4480]{1,0:T(8,128)S(1)}) fusion(f32[4480]{0:T(1024)S(1)} %copy-done.38, bf16[256,1120]{0,1:T(8,128)(2,1)S(1)} %add_convert_fusion.13, bf16[1120,4480]{1,0:T(8,128)(2,1)} %param.31), kind=kOutput, calls=%fused_computation.19 | convolution fusion | flops 2580480000 | bytes 17507840 | tf_op jit(solution)/shard_map/dot_general | solution.py:413
  156.0 20.7 %convert_reduce_fusion = (f32[4480]{0:T(1024)S(1)}, bf16[256,4480]{1,0:T(8,128)(2,1)S(1)}) fusion(f32[256,4480]{1,0:T(8,128)S(1)} %get-tuple-element.74, bf16[4480,1120]{0,1:T(8,128)(2,1)} %param.33, bf16[1,256,1120]{1,2,0:T(8,128)(2,1)S(1)} %copy-done.18), kind=kOutput, calls=%fused_computation.18 | convolution fusion | flops 2594237952 | bytes 17507840 | tf_op jit(solution)/shard_map/nd,fd->nf/dot_general | solution.py:420
  176.7 3.3 multiply_reduce_fusion
  180.6 1.7 convolution_convert_fusion
  182.4 3.5 all-to-all-start.2
  188.2 3.2 copy.86
  191.4 2.0 reshape.284
  193.4 2.6 copy.87
  195.9 3.2 copy.88
  199.1 2.6 copy.89
  201.7 11.2 %weight_blocks.6 = bf16[16,280,560]{2,1,0:T(8,128)(2,1)} custom-call(s32[16]{0:T(128)} %get-tuple-element.70.li, s32[16]{0:T(128)} %get-tuple-element.68.ri, bf16[4,280,256]{2,1,0:T(8,128)(2,1)} %bitcast.161, bf16[8,256,560]{2,1,0:T(8,128)(2,1)} %bitcast.140), custom_call_target="tpu_custom_call" | custom-call | tf_op jit(solution)/shard_map/weight_blocks/pallas_call | solution.py:65
  212.9 11.2 %weight_blocks.7 = bf16[16,280,560]{2,1,0:T(8,128)(2,1)} custom-call(s32[16]{0:T(128)} %get-tuple-element.69.li, s32[16]{0:T(128)} %get-tuple-element.67.ri, bf16[4,280,256]{2,1,0:T(8,128)(2,1)} %bitcast.162, bf16[8,256,560]{2,1,0:T(8,128)(2,1)} %bitcast.141), custom_call_target="tpu_custom_call" | custom-call | tf_op jit(solution)/shard_map/weight_blocks/pallas_call | solution.py:65
  224.1 12.6 %weight_blocks.8 = bf16[16,140,1400]{2,1,0:T(8,128)(2,1)} custom-call(s32[16]{0:T(128)} %get-tuple-element.66.li, s32[16]{0:T(128)} %get-tuple-element.64.ri, bf16[8,140,256]{2,1,0:T(8,128)(2,1)} %bitcast.156, bf16[4,256,1120]{2,1,0:T(8,128)(2,1)} %bitcast.142, bf16[8,140,256]{2,1,0:T(8,128)(2,1)} %bitcast.158, bf16[4,256,280]{2,1,0:T(8,128)(2,1)} %bitcast.150), custom_call_target="tpu_custom_call" | custom-call | tf_op jit(solution)/shard_map/weight_blocks/pallas_call | solution.py:65
  236.6 12.5 %weight_blocks.9 = bf16[16,140,1400]{2,1,0:T(8,128)(2,1)} custom-call(s32[16]{0:T(128)} %get-tuple-element.65.li, s32[16]{0:T(128)} %get-tuple-element.63.ri, bf16[8,140,256]{2,1,0:T(8,128)(2,1)} %bitcast.157, bf16[4,256,1120]{2,1,0:T(8,128)(2,1)} %bitcast.143, bf16[8,140,256]{2,1,0:T(8,128)(2,1)} %bitcast.159, bf16[4,256,280]{2,1,0:T(8,128)(2,1)} %bitcast.151), custom_call_target="tpu_custom_call" | custom-call | tf_op jit(solution)/shard_map/weight_blocks/pallas_call | solution.py:65
  250.4 6.7 copy.97
  257.0 32.4 %attend_back.1 = (bf16[1024,280]{1,0:T(8,128)(2,1)}, bf16[1024,560]{1,0:T(8,128)(2,1)}, bf16[1024,560]{1,0:T(8,128)(2,1)}) custom-call(s32[2]{0:T(128)} %pad_add_fusion.info, bf16[1024,840]{1,0:T(8,128)(2,1)} %bitcast.166, bf16[1024,560]{1,0:T(8,128)(2,1)} %bitcast.169, bf16[1024,280]{1,0:T(8,128)(2,1)} %bitcast.171, ...), custom_call_target="tpu_custom_call" | custom-call | flops 64424509440 | bytes 8388608 | tf_op jit(solution)/shard_map/attend_back/pallas_call | solution.py:304
  291.1 11.2 %collective-permute-start.1 = (bf16[1,1024,560]{1,2,0:T(8,128)(2,1)S(1)}, bf16[1,1024,560]{1,2,0:T(8,128)(2,1)}, u32[]{:S(2)}, u32[]{:S(2)}) collective-permute-start(bf16[1,1024,560]{1,2,0:T(8,128)(2,1)S(1)} %copy.90), channel_id=1, source_target_pairs={{0,1},{1,0},{2,3},{3,2},{4,5},{5,4},{6,7},{7,6},{8,9},{9,8},{10,11... | collective-permute-start | bytes 3440648 | tf_op jit(solution)/shard_map/ppermute | solution.py:30
  302.7 24.3 %collective-permute-done.1 = bf16[1,1024,560]{1,2,0:T(8,128)(2,1)} collective-permute-done((bf16[1,1024,560]{1,2,0:T(8,128)(2,1)S(1)}, bf16[1,1024,560]{1,2,0:T(8,128)(2,1)}, u32[]{:S(2)}, u32[]{:S(2)}) %collective-permute-start.1) | collective-permute-done | bytes 1146912 | tf_op jit(solution)/shard_map/ppermute | solution.py:30
  328.7 2.8 fusion.10
  334.4 5.4 all-to-all-start.3
  340.1 2.4 fusion.15.refs_0_
  342.9 35.8 %all-to-all-done.3 = bf16[4,1,256,840]{2,3,1,0:T(8,128)(2,1)S(1)} async-done(((bf16[4,1,256,840]{2,3,1,0:T(8,128)(2,1)}), bf16[4,1,256,840]{2,3,1,0:T(8,128)(2,1)S(1)}, u32[]{:S(2)}, u32[]{:S(2)}) %all-to-all-start.3) | async-done | bytes 1720352 | tf_op jit(solution)/shard_map/all_to_all | solution.py:400
  380.1 2.5 reshape_reshape.11
  382.7 3.8 copy.96
  386.4 10.5 %weight_blocks.11 = bf16[16,280,420]{2,1,0:T(8,128)(2,1)} custom-call(s32[16]{0:T(128)} %get-tuple-element.69.li, s32[16]{0:T(128)} %get-tuple-element.67.ri, bf16[4,280,256]{2,1,0:T(8,128)(2,1)} %fusion.15.refs_0_, bf16[8,256,420]{2,1,0:T(8,128)(2,1)} %bitcast.144), custom_call_target="tpu_custom_call" | custom-call | tf_op jit(solution)/shard_map/weight_blocks/pallas_call | solution.py:65
  396.9 6.1 fusion.42
  403.5 9.0 %add_convert_fusion = bf16[16,140,1400]{2,1,0:T(8,128)(2,1)} fusion(bf16[16,140,1400]{2,1,0:T(8,128)(2,1)} %weight_blocks.8, bf16[16,140,1400]{2,0,1:T(8,128)(2,1)} %collective-permute-done.12), kind=kLoop, calls=%fused_computation | loop fusion | flops 12544000 | bytes 18816000 | tf_op jit(solution)/shard_map/convert_element_type | solution.py:105
  412.5 1.9 slice-done.2
  414.4 2.3 copy.99
  418.2 5.8 add_convert_fusion.1
  424.0 1.9 slice.246
  427.4 1.8 multiply_reduce_fusion.1
  430.5 2.1 collective-permute-start.2
  432.5 61.4 %collective-permute-done.2 = f32[2,32,280]{2,1,0:T(8,128)S(1)} collective-permute-done((f32[2,32,280]{2,1,0:T(8,128)S(1)}, f32[2,32,280]{2,1,0:T(8,128)S(1)}, u32[]{:S(2)}, u32[]{:S(2)}) %collective-permute-start.2) | collective-permute-done | bytes 71712 | tf_op jit(solution)/shard_map/ppermute | solution.py:30
  495.9 3.5 collective-permute-done.4
  499.6 10.5 %weight_blocks.10 = bf16[16,280,420]{2,1,0:T(8,128)(2,1)} custom-call(s32[16]{0:T(128)} %get-tuple-element.70.li, s32[16]{0:T(128)} %get-tuple-element.68.ri, bf16[4,280,256]{2,1,0:T(8,128)(2,1)} %fusion.15.refs_0_, bf16[8,256,420]{2,1,0:T(8,128)(2,1)} %bitcast.145), custom_call_target="tpu_custom_call" | custom-call | tf_op jit(solution)/shard_map/weight_blocks/pallas_call | solution.py:65
  510.1 2.1 collective-permute-start.6
  512.2 5.0 add_convert_fusion.2
  518.8 1.8 copy-done.3
  520.9 3.8 add_convert_fusion.4
  526.9 3.3 add_convert_fusion.3
  530.4 1.8 copy.101
  534.2 3.7 fusion.12
  539.3 34.4 %collective-permute-done.8 = bf16[8,280,420]{2,1,0:T(8,128)(2,1)} collective-permute-done((bf16[8,280,420]{2,1,0:T(8,128)(2,1)}, bf16[8,280,420]{2,1,0:T(8,128)(2,1)}, u32[]{:S(2)}, u32[]{:S(2)}) %collective-permute-start.8) | collective-permute-done | bytes 1881632 | tf_op jit(solution)/shard_map/ppermute | solution.py:30
  573.7 3.1 add_convert_fusion.5
  577.5 1.9 add_convert_fusion.7
  580.6 24.3 %collective-permute-done.14 = bf16[4,140,1400]{2,0,1:T(4,128)(2,1)} collective-permute-done((bf16[4,140,1400]{2,0,1:T(4,128)(2,1)}, bf16[4,140,1400]{2,0,1:T(4,128)(2,1)}, u32[]{:S(2)}, u32[]{:S(2)}) %collective-permute-start.14) | collective-permute-done | bytes 1568032 | tf_op jit(solution)/shard_map/ppermute | solution.py:30
  608.9 1.8 collective-permute-start.10
  611.3 23.4 %collective-permute-done.20 = bf16[2,280,560]{2,1,0:T(8,128)(2,1)S(1)} collective-permute-done((bf16[2,280,560]{2,1,0:T(8,128)(2,1)S(1)}, bf16[2,280,560]{2,1,0:T(8,128)(2,1)S(1)}, u32[]{:S(2)}, u32[]{:S(2)}) %collective-permute-start.20) | collective-permute-done | bytes 627232 | tf_op jit(solution)/shard_map/ppermute | solution.py:30
  635.0 31.9 %collective-permute-done.10 = bf16[2,280,420]{2,1,0:T(8,128)(2,1)S(1)} collective-permute-done((bf16[2,280,420]{2,1,0:T(8,128)(2,1)S(1)}, bf16[2,280,420]{2,1,0:T(8,128)(2,1)S(1)}, u32[]{:S(2)}, u32[]{:S(2)}) %collective-permute-start.10) | collective-permute-done | bytes 470432 | tf_op jit(solution)/shard_map/ppermute | solution.py:30
  667.4 2.1 collective-permute-start.16
  670.5 6.4 collective-permute-done.11
  677.8 6.8 collective-permute-done.16
  (215 shorter events, 48.6 us)
Async XLA Ops:
  0.6 142.0 %copy-start = (bf16[1120,1120]{1,0:T(8,128)(2,1)S(1)}, bf16[1120,1120]{1,0:T(8,128)(2,1)}, u32[]{:S(2)}) copy-start(bf16[1120,1120]{1,0:T(8,128)(2,1)} %param.27) | copy-start | bytes 7526404
  0.7 4.2 copy-start.14
  0.7 5.0 copy-start.34
  0.7 5.0 copy-start.35
  0.7 5.1 copy-start.36
  0.7 5.1 copy-start.24
  4.9 8.2 %copy-start.27 = (f32[256]{0:T(256)}, f32[256]{0:T(256)S(1)}, u32[]{:S(2)}) copy-start(f32[256]{0:T(256)S(1)} %broadcast_multiply_fusion.1) | copy-start | bytes 3076
  5.7 7.3 %copy-start.29 = (f32[256]{0:T(256)}, f32[256]{0:T(256)S(1)}, u32[]{:S(2)}) copy-start(f32[256]{0:T(256)S(1)} %fusion.28) | copy-start | bytes 3076
  61.7 26.5 %collective-permute-start = (bf16[1,1024,560]{1,2,0:T(8,128)(2,1)}, bf16[1,1024,560]{1,2,0:T(8,128)(2,1)}, u32[]{:S(2)}, u32[]{:S(2)}) collective-permute-start(bf16[1,1024,560]{1,2,0:T(8,128)(2,1)} %slice.217), channel_id=1, source_target_pairs={{0,1},{1,0},{2,3},{3,2},{4,5},{5,4},{6,7},{7,6},{8,9},{9,8},{10,11... | collective-permute-start | bytes 3440648 | tf_op jit(solution)/shard_map/ppermute | solution.py:30
  119.5 6.7 copy-start.17
  121.8 18.4 %all-to-all-start.1 = ((bf16[4,1,256,280]{2,3,1,0:T(8,128)(2,1)}), bf16[4,1,256,280]{2,3,1,0:T(8,128)(2,1)}, u32[]{:S(2)}, u32[]{:S(2)}) async-start(bf16[4,1,256,280]{2,3,1,0:T(8,128)(2,1)} %copy.82), calls=%async_computation.1 | async-start | bytes 1146880 | tf_op jit(solution)/shard_map/all_to_all | solution.py:400
  126.2 16.5 %copy-start.39 = (f32[1120]{0:T(1024)S(1)}, f32[1120]{0:T(1024)}, u32[]{:S(2)}) copy-start(f32[1120]{0:T(1024)} %param.28) | copy-start | bytes 13444
  141.6 3.7 copy-start.7
  145.3 34.7 %copy-start.10 = (f32[256,1120]{0,1:T(8,128)}, f32[256,1120]{0,1:T(8,128)S(1)}, u32[]{:S(2)}) copy-start(f32[256,1120]{0,1:T(8,128)S(1)} %get-tuple-element.72) | copy-start | bytes 3440644
  146.0 10.0 %copy-start.16 = (bf16[256,1120]{0,1:T(8,128)(2,1)}, bf16[256,1120]{0,1:T(8,128)(2,1)S(1)}, u32[]{:S(2)}) copy-start(bf16[256,1120]{0,1:T(8,128)(2,1)S(1)} %add_convert_fusion.13) | copy-start | bytes 1720324
  146.1 10.0 %copy-start.18 = (bf16[1,256,1120]{1,2,0:T(8,128)(2,1)S(1)}, bf16[1,256,1120]{1,2,0:T(8,128)(2,1)}, u32[]{:S(2)}) copy-start(bf16[1,256,1120]{1,2,0:T(8,128)(2,1)} %param.35) | copy-start | bytes 1720324
  146.1 30.6 %slice-start.3 = ((s8[10035200]{0:T(1024)(128)(4,1)}), s8[4194304]{0:T(1024)(128)(4,1)S(1)}, s32[]{:S(2)}) async-start(s8[10035200]{0:T(1024)(128)(4,1)} %bitcast.176), calls=%async_computation.7 | async-start | bytes 8388608
  146.1 30.6 %slice-start.4 = ((s8[10035200]{0:T(1024)(128)(4,1)}), s8[4194304]{0:T(1024)(128)(4,1)S(1)}, s32[]{:S(2)}) async-start(s8[10035200]{0:T(1024)(128)(4,1)} %bitcast.176), calls=%async_computation.8 | async-start | bytes 8388608
  156.0 20.7 %slice-start.5 = ((s8[10035200]{0:T(1024)(128)(4,1)}), s8[1646592]{0:T(1024)(128)(4,1)S(1)}, s32[]{:S(2)}) async-start(s8[10035200]{0:T(1024)(128)(4,1)} %bitcast.176), calls=%async_computation.9 | async-start | bytes 3293184
  182.4 66.8 %all-to-all-start.2 = ((bf16[4,1,256,280]{2,3,1,0:T(8,128)(2,1)}), bf16[4,1,256,280]{2,3,1,0:T(8,128)(2,1)S(1)}, u32[]{:S(2)}, u32[]{:S(2)}) async-start(bf16[4,1,256,280]{2,3,1,0:T(8,128)(2,1)} %bitcast.174), calls=%async_computation.2 | async-start | bytes 1146880 | tf_op jit(solution)/shard_map/all_to_all | solution.py:394
  257.0 146.4 %collective-permute-start.12 = (bf16[16,140,1400]{2,0,1:T(8,128)(2,1)}, bf16[16,140,1400]{2,0,1:T(8,128)(2,1)}, u32[]{:S(2)}, u32[]{:S(2)}) collective-permute-start(bf16[16,140,1400]{2,0,1:T(8,128)(2,1)} %copy.97), channel_id=1, source_target_pairs={{0,8},{8,0},{16,24},{24,16},{1,9},{9,1},{17,25},{25,17},{2,10},{10... | collective-permute-start | bytes 18816008 | tf_op jit(solution)/shard_map/ppermute | solution.py:30
  289.5 12.8 %copy-start.23 = (bf16[1024,280]{1,0:T(8,128)(2,1)S(1)}, bf16[1024,280]{1,0:T(8,128)(2,1)}, u32[]{:S(2)}) copy-start(bf16[1024,280]{1,0:T(8,128)(2,1)} %get-tuple-element.31) | copy-start | bytes 1720324
  291.1 35.9 %collective-permute-start.1 = (bf16[1,1024,560]{1,2,0:T(8,128)(2,1)S(1)}, bf16[1,1024,560]{1,2,0:T(8,128)(2,1)}, u32[]{:S(2)}, u32[]{:S(2)}) collective-permute-start(bf16[1,1024,560]{1,2,0:T(8,128)(2,1)S(1)} %copy.90), channel_id=1, source_target_pairs={{0,1},{1,0},{2,3},{3,2},{4,5},{5,4},{6,7},{7,6},{8,9},{9,8},{10,11... | collective-permute-start | bytes 3440648 | tf_op jit(solution)/shard_map/ppermute | solution.py:30
  302.6 115.6 %collective-permute-start.17 = (bf16[16,280,560]{2,1,0:T(8,128)(2,1)}, bf16[16,280,560]{2,1,0:T(8,128)(2,1)}, u32[]{:S(2)}, u32[]{:S(2)}) collective-permute-start(bf16[16,280,560]{2,1,0:T(8,128)(2,1)} %weight_blocks.7), channel_id=1, source_target_pairs={{0,8},{8,0},{16,24},{24,16},{1,9},{9,1},{17,25},{25,17},{2,10},{10... | collective-permute-start | bytes 15052808 | tf_op jit(solution)/shard_map/ppermute | solution.py:30
  334.4 5.5 copy-start.37
  334.4 5.6 copy-start.25
  334.4 5.6 copy-start.28
  334.4 5.7 copy-start.30
  334.4 44.3 %all-to-all-start.3 = ((bf16[4,1,256,840]{2,3,1,0:T(8,128)(2,1)}), bf16[4,1,256,840]{2,3,1,0:T(8,128)(2,1)S(1)}, u32[]{:S(2)}, u32[]{:S(2)}) async-start(bf16[4,1,256,840]{2,3,1,0:T(8,128)(2,1)} %pad_maximum_fusion), calls=%async_computation.3 | async-start | bytes 3440640 | tf_op jit(solution)/shard_map/all_to_all | solution.py:400
  386.4 10.5 %copy-start.15 = (bf16[1,256,1120]{1,2,0:T(8,128)(2,1)S(1)}, bf16[1,256,1120]{1,2,0:T(8,128)(2,1)}, u32[]{:S(2)}) copy-start(bf16[1,256,1120]{1,2,0:T(8,128)(2,1)} %param.18) | copy-start | bytes 1720324
  396.9 115.3 %collective-permute-start.7 = (bf16[16,280,420]{2,1,0:T(8,128)(2,1)}, bf16[16,280,420]{2,1,0:T(8,128)(2,1)}, u32[]{:S(2)}, u32[]{:S(2)}) collective-permute-start(bf16[16,280,420]{2,1,0:T(8,128)(2,1)} %weight_blocks.11), channel_id=1, source_target_pairs={{0,8},{8,0},{16,24},{24,16},{1,9},{9,1},{17,25},{25,17},{2,10},{10... | collective-permute-start | bytes 11289608 | tf_op jit(solution)/shard_map/ppermute | solution.py:30
  396.9 6.1 copy-start.32
  416.7 110.2 %collective-permute-start.13 = (bf16[8,140,1400]{2,0,1:T(8,128)(2,1)}, bf16[8,140,1400]{2,0,1:T(8,128)(2,1)}, u32[]{:S(2)}, u32[]{:S(2)}) collective-permute-start(bf16[8,140,1400]{2,0,1:T(8,128)(2,1)} %copy.99), channel_id=1, source_target_pairs={{0,1},{1,0},{2,3},{3,2},{4,5},{5,4},{6,7},{7,6},{8,9},{9,8},{10,11... | collective-permute-start | bytes 9408008 | tf_op jit(solution)/shard_map/ppermute | solution.py:30
  424.0 3.4 copy-start.2
  424.0 3.4 copy-start.13
  424.0 3.4 copy-start.19
  427.4 93.5 %collective-permute-start.18 = (bf16[8,280,560]{2,1,0:T(8,128)(2,1)}, bf16[8,280,560]{2,1,0:T(8,128)(2,1)}, u32[]{:S(2)}, u32[]{:S(2)}) collective-permute-start(bf16[8,280,560]{2,1,0:T(8,128)(2,1)} %slice.246), channel_id=1, source_target_pairs={{0,16},{8,24},{16,0},{24,8},{1,17},{9,25},{17,1},{25,9},{2,18},{10... | collective-permute-start | bytes 7526408 | tf_op jit(solution)/shard_map/ppermute | solution.py:30
  430.5 63.5 %collective-permute-start.2 = (f32[2,32,280]{2,1,0:T(8,128)S(1)}, f32[2,32,280]{2,1,0:T(8,128)S(1)}, u32[]{:S(2)}, u32[]{:S(2)}) collective-permute-start(f32[2,32,280]{2,1,0:T(8,128)S(1)} %constant_dynamic-slice_fusion.1), channel_id=1, source_target_pairs={{0,16},{8,24},{16,0},{24,8},{1,17},{9,25},{17,1},{25,9},{2,18},{10... | collective-permute-start | bytes 215048 | tf_op jit(solution)/shard_map/ppermute | solution.py:30
  494.0 1.3 collective-permute-start.3
  495.3 4.2 collective-permute-start.4
  499.5 10.6 %collective-permute-start.5 = (f32[1,32,280]{2,1,0:T(8,128)S(1)}, f32[1,32,280]{2,1,0:T(8,128)S(1)}, u32[]{:S(2)}, u32[]{:S(2)}) collective-permute-start(f32[1,32,280]{2,1,0:T(8,128)S(1)} %add.246), channel_id=1, source_target_pairs={{0,4},{2,6},{4,0},{6,2},{1,5},{3,7},{5,1},{7,3},{8,12},{10,14},{12... | collective-permute-start | bytes 107528 | tf_op jit(solution)/shard_map/ppermute | solution.py:30
  510.1 27.8 %collective-permute-start.6 = (f32[1,32,280]{2,1,0:T(8,128)S(1)}, f32[1,32,280]{2,1,0:T(8,128)S(1)}, u32[]{:S(2)}, u32[]{:S(2)}) collective-permute-start(f32[1,32,280]{2,1,0:T(8,128)S(1)} %add.247), channel_id=1, source_target_pairs={{0,2},{2,0},{4,6},{6,4},{1,3},{3,1},{5,7},{7,5},{8,10},{10,8},{12,... | collective-permute-start | bytes 107528 | tf_op jit(solution)/shard_map/ppermute | solution.py:30
  517.2 3.4 copy-start.3
  517.2 9.7 %slice-start = ((s8[6488064]{0:T(1024)(128)(4,1)}), s8[4194304]{0:T(1024)(128)(4,1)S(1)}, s32[]{:S(2)}) async-start(s8[6488064]{0:T(1024)(128)(4,1)} %bitcast.138), calls=%async_computation.4 | async-start | bytes 8388608
  520.6 6.3 slice-start.1
  520.6 53.0 %collective-permute-start.8 = (bf16[8,280,420]{2,1,0:T(8,128)(2,1)}, bf16[8,280,420]{2,1,0:T(8,128)(2,1)}, u32[]{:S(2)}, u32[]{:S(2)}) collective-permute-start(bf16[8,280,420]{2,1,0:T(8,128)(2,1)} %slice.224), channel_id=1, source_target_pairs={{0,16},{8,24},{16,0},{24,8},{1,17},{9,25},{17,1},{25,9},{2,18},{10... | collective-permute-start | bytes 5644808 | tf_op jit(solution)/shard_map/ppermute | solution.py:30
  520.9 13.3 %slice-start.6 = ((s8[10035200]{0:T(1024)(128)(4,1)}), s8[4194304]{0:T(1024)(128)(4,1)S(1)}, s32[]{:S(2)}) async-start(s8[10035200]{0:T(1024)(128)(4,1)} %bitcast.178), calls=%async_computation.10 | async-start | bytes 8388608
  524.7 9.5 %slice-start.7 = ((s8[10035200]{0:T(1024)(128)(4,1)}), s8[4194304]{0:T(1024)(128)(4,1)S(1)}, s32[]{:S(2)}) async-start(s8[10035200]{0:T(1024)(128)(4,1)} %bitcast.178), calls=%async_computation.11 | async-start | bytes 8388608
  525.9 8.2 %slice-start.8 = ((s8[10035200]{0:T(1024)(128)(4,1)}), s8[1646592]{0:T(1024)(128)(4,1)S(1)}, s32[]{:S(2)}) async-start(s8[10035200]{0:T(1024)(128)(4,1)} %bitcast.178), calls=%async_computation.12 | async-start | bytes 3293184
  525.9 51.6 %collective-permute-start.19 = (bf16[4,280,560]{2,1,0:T(8,128)(2,1)}, bf16[4,280,560]{2,1,0:T(8,128)(2,1)}, u32[]{:S(2)}, u32[]{:S(2)}) collective-permute-start(bf16[4,280,560]{2,1,0:T(8,128)(2,1)} %slice.248), channel_id=1, source_target_pairs={{0,1},{1,0},{2,3},{3,2},{4,5},{5,4},{6,7},{7,6},{8,9},{9,8},{10,11... | collective-permute-start | bytes 3763208 | tf_op jit(solution)/shard_map/ppermute | solution.py:30
  530.2 4.0 copy-start.20
  530.4 3.8 copy-start.11
  530.4 3.8 copy-start.40
  532.7 72.2 %collective-permute-start.14 = (bf16[4,140,1400]{2,0,1:T(4,128)(2,1)}, bf16[4,140,1400]{2,0,1:T(4,128)(2,1)}, u32[]{:S(2)}, u32[]{:S(2)}) collective-permute-start(bf16[4,140,1400]{2,0,1:T(4,128)(2,1)} %copy.101), channel_id=1, source_target_pairs={{0,16},{8,24},{16,0},{24,8},{1,17},{9,25},{17,1},{25,9},{2,18},{10... | collective-permute-start | bytes 4704008 | tf_op jit(solution)/shard_map/ppermute | solution.py:30
  573.7 3.9 copy-start.9
  576.9 31.7 %collective-permute-start.9 = (bf16[4,280,420]{2,1,0:T(8,128)(2,1)S(1)}, bf16[4,280,420]{2,1,0:T(8,128)(2,1)S(1)}, u32[]{:S(2)}, u32[]{:S(2)}) collective-permute-start(bf16[4,280,420]{2,1,0:T(8,128)(2,1)S(1)} %slice.226), channel_id=1, source_target_pairs={{0,1},{1,0},{2,3},{3,2},{4,5},{5,4},{6,7},{7,6},{8,9},{9,8},{10,11... | collective-permute-start | bytes 2822408 | tf_op jit(solution)/shard_map/ppermute | solution.py:30
  577.5 27.4 %copy-start.6 = (bf16[8,140,1400]{2,1,0:T(8,128)(2,1)S(1)}, bf16[8,140,1400]{2,1,0:T(8,128)(2,1)}, u32[]{:S(2)}) copy-start(bf16[8,140,1400]{2,1,0:T(8,128)(2,1)} %copy-done.5) | copy-start | bytes 9408004
  579.5 55.2 %collective-permute-start.20 = (bf16[2,280,560]{2,1,0:T(8,128)(2,1)S(1)}, bf16[2,280,560]{2,1,0:T(8,128)(2,1)S(1)}, u32[]{:S(2)}, u32[]{:S(2)}) collective-permute-start(bf16[2,280,560]{2,1,0:T(8,128)(2,1)S(1)} %slice.250), channel_id=1, source_target_pairs={{0,4},{2,6},{4,0},{6,2},{1,5},{3,7},{5,1},{7,3},{8,12},{10,14},{12... | collective-permute-start | bytes 1881608 | tf_op jit(solution)/shard_map/ppermute | solution.py:30
  607.3 59.9 %collective-permute-start.15 = (bf16[2,140,1400]{2,0,1:T(2,128)(2,1)S(1)}, bf16[2,140,1400]{2,0,1:T(2,128)(2,1)S(1)}, u32[]{:S(2)}, u32[]{:S(2)}) collective-permute-start(bf16[2,140,1400]{2,0,1:T(2,128)(2,1)S(1)} %copy.103), channel_id=1, source_target_pairs={{0,4},{2,6},{4,0},{6,2},{1,5},{3,7},{5,1},{7,3},{8,12},{10,14},{12... | collective-permute-start | bytes 2352008 | tf_op jit(solution)/shard_map/ppermute | solution.py:30
  608.9 58.0 %collective-permute-start.10 = (bf16[2,280,420]{2,1,0:T(8,128)(2,1)S(1)}, bf16[2,280,420]{2,1,0:T(8,128)(2,1)S(1)}, u32[]{:S(2)}, u32[]{:S(2)}) collective-permute-start(bf16[2,280,420]{2,1,0:T(8,128)(2,1)S(1)} %slice.228), channel_id=1, source_target_pairs={{0,4},{2,6},{4,0},{6,2},{1,5},{3,7},{5,1},{7,3},{8,12},{10,14},{12... | collective-permute-start | bytes 1411208 | tf_op jit(solution)/shard_map/ppermute | solution.py:30
  635.0 34.6 %collective-permute-start.21 = (bf16[1,280,560]{2,1,0:T(8,128)(2,1)S(1)}, bf16[1,280,560]{2,1,0:T(8,128)(2,1)S(1)}, u32[]{:S(2)}, u32[]{:S(2)}) collective-permute-start(bf16[1,280,560]{2,1,0:T(8,128)(2,1)S(1)} %slice.252), channel_id=1, source_target_pairs={{0,2},{2,0},{4,6},{6,4},{1,3},{3,1},{5,7},{7,5},{8,10},{10,8},{12,... | collective-permute-start | bytes 940808 | tf_op jit(solution)/shard_map/ppermute | solution.py:30
  667.1 9.8 %collective-permute-start.11 = (bf16[1,280,420]{2,1,0:T(8,128)(2,1)S(1)}, bf16[1,280,420]{2,1,0:T(8,128)(2,1)S(1)}, u32[]{:S(2)}, u32[]{:S(2)}) collective-permute-start(bf16[1,280,420]{2,1,0:T(8,128)(2,1)S(1)} %slice.230), channel_id=1, source_target_pairs={{0,2},{2,0},{4,6},{6,4},{1,3},{3,1},{5,7},{7,5},{8,10},{10,8},{12,... | collective-permute-start | bytes 705608 | tf_op jit(solution)/shard_map/ppermute | solution.py:30
  667.4 17.2 %collective-permute-start.16 = (bf16[1,140,1400]{2,1,0:T(8,128)(2,1)S(1)}, bf16[1,140,1400]{2,1,0:T(8,128)(2,1)S(1)}, u32[]{:S(2)}, u32[]{:S(2)}) collective-permute-start(bf16[1,140,1400]{2,1,0:T(8,128)(2,1)S(1)} %slice.240), channel_id=1, source_target_pairs={{0,2},{2,0},{4,6},{6,4},{1,3},{3,1},{5,7},{7,5},{8,10},{10,8},{12,... | collective-permute-start | bytes 1176008 | tf_op jit(solution)/shard_map/ppermute | solution.py:30
  676.9 9.5 %copy-start.1 = (bf16[1120,1120]{1,0:T(8,128)(2,1)S(1)}, bf16[1120,1120]{1,0:T(8,128)(2,1)}, u32[]{:S(2)}) copy-start(bf16[1120,1120]{1,0:T(8,128)(2,1)} %param.27) | copy-start | bytes 7526404
  (11 other events, 21.8 us)

commit v2 on v1

--- a/solution.py
+++ b/solution.py
@@ -6,6 +6,8 @@
 from jax.experimental import pallas as pl
 from jax.experimental.pallas import tpu as pltpu
 from jax.sharding import PartitionSpec as P
+import numpy as np
+
 
 HEADS = 20
 HD = 56
@@ -46,52 +48,55 @@
     return lax.dot_general(a, b, (((1,), (1,)), ((), ())), preferred_element_type=jnp.float32)
 
 
-def weight_blocks(pairs, left_ids, right_ids):
-    count = left_ids.shape[0]
-    pair_count = len(pairs)
-    rows = pairs[0][0].shape[1]
-    cols = sum(r.shape[2] for _, r in pairs)
-
-    def kernel(li, ri, *refs):
-        i = pl.program_id(0)
-        out = refs[-1]
-        parts = []
-        for p in range(pair_count):
-            parts.append(nn(refs[2 * p][li[i]], refs[2 * p + 1][ri[i]]))
-        whole = parts[0] if pair_count == 1 else jnp.concatenate(parts, axis=-1)
-        out[0] = whole.astype(jnp.bfloat16)
-
-    flat = [x for pair in pairs for x in pair]
-    return pl.pallas_call(
+def weight_blocks(left, right, by_cell_left, y_first):
+    cells, groups, halves = lax.axis_size("cell"), lax.axis_size("head"), lax.axis_size("ctx")
+    parts, half_cells = groups * halves, cells // 2
+    steps = bits_of("cell")
+    rel = np.zeros((cells,), np.int32)
+    for s, (_, bit) in enumerate(steps):
+        rel += ((np.arange(cells) >> (len(steps) - 1 - s)) & 1).astype(np.int32) * bit
+    cell_ids = jnp.asarray(rel) ^ lax.axis_index("cell")
+    places = jnp.arange(parts, dtype=jnp.int32)
+    part_ids = ((places % groups) ^ lax.axis_index("head")) * halves + (
+        (places // groups) ^ lax.axis_index("ctx")
+    )
+    rows, cols = left.shape[1], right.shape[2]
+
+    def kernel(ci, pi, left_ref, right_ref, kept, sent):
+        part = pi[pl.program_id(0)]
+        for n in range(cells):
+            cell = ci[n]
+            out, at = (kept, n) if n < half_cells else (sent, n - half_cells)
+            if by_cell_left:
+                block = nn(left_ref[cell], right_ref[part])
+            else:
+                block = nn(left_ref[part], right_ref[cell])
+            if y_first:
+                out[0, at, 0] = block.astype(jnp.bfloat16)
+            else:
+                out[at, 0] = block.astype(jnp.bfloat16)
+
+    if y_first:
+        shape = (halves, half_cells, groups, rows, cols)
+        spec = pl.BlockSpec(
+            (1, half_cells, 1, rows, cols), lambda i, ci, pi: (i // groups, 0, i % groups, 0, 0)
+        )
+    else:
+        shape = (half_cells, parts, rows, cols)
+        spec = pl.BlockSpec((half_cells, 1, rows, cols), lambda i, ci, pi: (0, i, 0, 0))
+    whole = [
+        pl.BlockSpec(x.shape, lambda i, ci, pi: (0, 0, 0), pipeline_mode=pl.Buffered(1))
+        for x in (left, right)
+    ]
+    kept, sent = pl.pallas_call(
         kernel,
-        out_shape=jax.ShapeDtypeStruct((count, rows, cols), jnp.bfloat16),
+        out_shape=[jax.ShapeDtypeStruct(shape, jnp.bfloat16)] * 2,
         grid_spec=pltpu.PrefetchScalarGridSpec(
-            num_scalar_prefetch=2,
-            grid=(count,),
-            in_specs=[
-                pl.BlockSpec(x.shape, lambda i, li, ri: (0, 0, 0), pipeline_mode=pl.Buffered(1))
-                for x in flat
-            ],
-            out_specs=pl.BlockSpec((1, rows, cols), lambda i, li, ri: (i, 0, 0)),
+            num_scalar_prefetch=2, grid=(parts,), in_specs=whole, out_specs=[spec, spec]
         ),
         name="weight_blocks",
-    )(left_ids, right_ids, *flat)
-
-
-def relative_ids(steps):
-    count = 1
-    for axis, _ in steps:
-        count *= 2
-    places = jnp.arange(count, dtype=jnp.int32)
-    rel = {"cell": jnp.zeros_like(places), "head": jnp.zeros_like(places), "ctx": jnp.zeros_like(places)}
-    for s, (axis, bit) in enumerate(steps):
-        on = (places >> (len(steps) - 1 - s)) & 1
-        rel[axis] = rel[axis] + on * bit
-    cell_ids = rel["cell"] ^ lax.axis_index("cell")
-    part_ids = (rel["head"] ^ lax.axis_index("head")) * lax.axis_size("ctx") + (
-        rel["ctx"] ^ lax.axis_index("ctx")
-    )
-    return cell_ids, part_ids
+    )(cell_ids, part_ids, left, right)
+    return kept.reshape(-1, rows, cols), sent.reshape(-1, rows, cols)
 
 
 def add_up(kept, got):
@@ -105,7 +110,8 @@
             total = total.astype(jnp.bfloat16)
             half = total.shape[0] // 2
             kept, sent = total[:half], total[half:]
-        total = add_up(kept, swap(sent, axis, bit))
+        got = swap(sent, axis, bit)
+        total = add_up(kept, got)
     return total[0]
 
 
@@ -336,13 +342,25 @@
     return values.reshape(values.shape[0], count, -1).transpose(1, 2, 0)
 
 
-def block_sum(pairs, by_cell_left, steps):
-    cell_ids, part_ids = relative_ids(steps)
-    left, right = (cell_ids, part_ids) if by_cell_left else (part_ids, cell_ids)
-    half = left.shape[0] // 2
-    sent = weight_blocks(pairs, left[half:], right[half:])
-    kept = weight_blocks(pairs, left[:half], right[:half])
-    return kept, sent
+def head_columns(groups, halves, sections, units):
+    local, owned = units // groups, sections * units // (groups * halves)
+    send = [[[[] for _ in range(groups)] for _ in range(halves)] for _ in range(groups)]
+    take = np.zeros((groups, halves, owned, 2), np.int32)
+    for u in range(sections * units):
+        section, inside = divmod(u, units)
+        source, offset = divmod(inside, local)
+        owner, place = divmod(u, owned)
+        head, ctx = divmod(owner, halves)
+        slots = send[source][ctx][head]
+        take[head, ctx, place] = (source, len(slots))
+        slots.append(section * local + offset)
+    width = max(len(x) for a in send for b in a for x in b)
+    table = np.zeros((groups, halves, groups, width), np.int32)
+    for a in range(groups):
+        for b in range(halves):
+            for c in range(groups):
+                table[a, b, c, : len(send[a][b][c])] = send[a][b][c]
+    return table, take
 
 
 def body(
@@ -403,6 +421,10 @@
 
     qkv_heads = to_heads(mixed_qkv)
     kv_other = swap(qkv_heads[:, :, head_width:], "ctx", 1)
+    normed_near = normed.reshape(cell_count, 1, row_count, model_width)
+    normed_near = lax.all_gather(normed_near, "head", axis=1, tiled=True)
+    normed_near = normed_near.reshape(cell_count * ctx_rows, model_width)
+    normed_far = swap(normed_near, "ctx", 1)
     infos = [jnp.stack([lengths[n], half_index.astype(jnp.int32)]) for n in range(cell_count)]
     runs = [attend(infos[n], qkv_heads[n], kv_other[n], groups) for n in range(cell_count)]
     attended = jnp.stack([r[0] for r in runs])
@@ -415,6 +437,11 @@
     branch = jnp.dot(active, proj_weight, preferred_element_type=jnp.float32) + proj_bias
     block_out = (middle + branch).astype(jnp.bfloat16).reshape(cell_count, row_count, model_width)
     grad_low = cotangent.reshape(token_count, model_width)
+    proj_kept, proj_sent = weight_blocks(
+        row_blocks(grad_low, parts), column_blocks(active, cells), False, False
+    )
+    grad_low, proj_kept, proj_sent = lax.optimization_barrier((grad_low, proj_kept, proj_sent))
+    proj_weight_grad = scatter_sum(proj_kept, proj_sent, steps_x).T
     grad_top = grad_low.astype(jnp.float32)
     proj_bias_grad = jnp.sum(grad_top, axis=0)
     active_grad = jnp.einsum("nd,fd->nf", grad_low, proj_weight, preferred_element_type=jnp.float32)
@@ -434,41 +461,64 @@
     ).astype(jnp.bfloat16)
     grad_heads = to_heads(attended_grad)
 
-    fc_kept, fc_sent = block_sum(
-        [(row_blocks(mlp_normed, cells), column_blocks(hidden_grad, parts))], True, steps_x
-    )
-    po_kept, po_sent = block_sum(
-        [
-            (row_blocks(grad_low, parts), column_blocks(active, cells)),
-            (row_blocks(middle_low, parts), column_blocks(attended_rows, cells)),
-        ],
-        False,
-        steps_y,
-    )
-    grad_heads, fc_kept, fc_sent, po_kept, po_sent = lax.optimization_barrier(
-        (grad_heads, fc_kept, fc_sent, po_kept, po_sent)
+    fc_kept, fc_sent = weight_blocks(
+        row_blocks(mlp_normed, cells), column_blocks(hidden_grad, parts), True, False
+    )
+    out_kept, out_sent = weight_blocks(
+        row_blocks(middle_low, parts), column_blocks(attended_rows, cells), False, True
+    )
+    grad_heads, fc_kept, fc_sent, out_kept, out_sent = lax.optimization_barrier(
+        (grad_heads, fc_kept, fc_sent, out_kept, out_sent)
     )
     fc_weight_grad = scatter_sum(fc_kept, fc_sent, steps_x)
-    po_grad = scatter_sum(po_kept, po_sent, steps_y)
-    proj_rows = active.shape[1] // cells
-    proj_weight_grad = po_grad[:, :proj_rows].T
-    out_weight_grad = po_grad[:, proj_rows:].T
+    out_weight_grad = scatter_sum(out_kept, out_sent, steps_y).T
 
     backs = [
-        attend_back(
-            infos[n], qkv_heads[n], kv_other[n], grad_heads[n], runs[n][1], runs[n][2], groups
-        )
-        for n in range(cell_count)
+      attend_back(
+        infos[n], qkv_heads[n], kv_other[n], grad_heads[n], runs[n][1], runs[n][2], groups
+      )
+      for n in range(cell_count)
     ]
     dq = jnp.stack([b[0] for b in backs])
     dkv = jnp.stack([b[1] for b in backs])
-    dkv_got = swap(jnp.stack([b[2] for b in backs]), "ctx", 1)
+    dkv_far = jnp.stack([b[2] for b in backs])
+
+    def tall(values):
+        return values.reshape(cell_count * ctx_rows, -1)
+
+    def over_tokens(a, b):
+        return jnp.einsum("nd,ne->de", a, b, preferred_element_type=jnp.float32)
+
+    qkv_part = jnp.concatenate(
+        [
+            over_tokens(normed_near, tall(dq)),
+            over_tokens(normed_near, tall(dkv)) + over_tokens(normed_far, tall(dkv_far)),
+        ],
+        axis=1,
+    ).astype(jnp.bfloat16)
+    units = 2 * groups
+    local_units = 3 * units // groups
+    qkv_part = qkv_part.reshape(cells, model_width // cells, local_units, -1).transpose(0, 2, 1, 3)
+    cell_index = lax.axis_index("cell")
+    for axis, bit in cell_steps[::-1]:
+        on = (cell_index // bit) % 2
+        half = qkv_part.shape[0] // 2
+        kept = lax.dynamic_slice_in_dim(qkv_part, on * half, half, 0)
+        sent = lax.dynamic_slice_in_dim(qkv_part, (1 - on) * half, half, 0)
+        qkv_part = add_up(kept, swap(sent, axis, bit)).astype(jnp.bfloat16)
+    qkv_part = add_up(qkv_part, swap(qkv_part, "ctx", 1)).astype(jnp.bfloat16)[0]
+    send_table, take_table = head_columns(groups, halves, 3, units)
+    head_index = lax.axis_index("head")
+    sent = qkv_part[jnp.asarray(send_table)[head_index, half_index]]
+    got = lax.all_to_all(sent, "head", split_axis=0, concat_axis=0, tiled=True)
+    taken = jnp.asarray(take_table)[head_index, half_index]
+    qkv_weight_grad = jnp.concatenate(
+        [got[taken[n, 0], taken[n, 1]] for n in range(take_table.shape[2])], axis=-1
+    ).astype(jnp.float32)
+
+    dkv_got = swap(dkv_far, "ctx", 1)
     dkv = add_up(dkv, dkv_got).astype(jnp.bfloat16)
     qkv_grad = to_rows(jnp.concatenate([dq, dkv], axis=-1))
-    qkv_kept, qkv_sent = block_sum(
-        [(row_blocks(normed, cells), column_blocks(qkv_grad, parts))], True, steps_x
-    )
-    qkv_weight_grad = scatter_sum(qkv_kept, qkv_sent, steps_x)
     column_sums = jnp.sum(qkv_grad, axis=0, dtype=jnp.float32)
     query_bias_grad = column_sums[:model_width]
     value_bias_grad = column_sums[2 * model_width :]
@@ -500,7 +550,6 @@
         + [fc_bias_grad.reshape(cells, fc_rows, width)],
         axis=1,
     )
-    cell_index = lax.axis_index("cell")
     for axis, bit in cell_steps[::-1]:
         on = (cell_index // bit) % 2
         half = packed.shape[0] // 2

time: 698 us -> 678 us (0.971)
  waiting for transfers between devices: 287 us -> 226 us
  Pallas kernels: 130 us -> 88.4 us
  local copies, waits for them, and re-layouts: 72.2 us -> 103 us
  between operations: 3.45 us -> 28.4 us
  starting transfers between devices: 41.8 us -> 55.8 us
  matrix products: 56.2 us -> 63.4 us
    pallas_call x6 -> x3, Pallas kernels: 68.5 us -> 27.2 us  [weight_blocks(): pl.pallas_call(kernel, out_shape=[jax.ShapeDtypeStruct(shape, jnp.bfloat1...]
    all_to_all x2, waiting for transfers between devices: 48.8 us -> 7.86 us  [to_rows(): lax.all_to_all(values, 'head', split_axis=0, concat_axis=0, tiled=True)]
    ppermute x22 -> x26, waiting for transfers between devices: 238 us -> 218 us  [swap(): lax.ppermute(values, axis, [(i, i ^ bit) for i in range(lax.axis_size(axi...]
    dot_general x1, matrix products: 20.7 us -> 11.6 us  [body(): jnp.einsum('nd,fd->nf', grad_low, proj_weight, preferred_element_type=jnp...]
    ppermute x22 -> x26, starting transfers between devices: 28.4 us -> 37.3 us  [swap(): lax.ppermute(values, axis, [(i, i ^ bit) for i in range(lax.axis_size(axi...]
    unnamed x98 -> x106, local copies, waits for them, and re-layouts: 6 us -> 13.7 us
    dot_general x0 -> x3, matrix products: none -> 7.51 us  [over_tokens(): return jnp.einsum('nd,ne->de', a, b, preferred_element_type=jnp.float32)]
  transfers between devices with their start and end apart: 25 -> 31, of which waited for: 14 -> 11; matrix products, arithmetic and copies ran while one was open for 15% -> 29% of each run, Pallas kernels for 15% -> 9%
where the time goes in v2:
time: 678 us; the launch traced here: 666 us
  waiting for transfers between devices  226 us (33%)
  local copies, waits for them, and re-layouts  103 us (15%)
  Pallas kernels  88.4 us (13%)
  matrix products  63.4 us (9%)
  starting transfers between devices  55.8 us (8%)
  other arithmetic  53.7 us (8%)
  blocking collectives  46.3 us (7%)
  between operations  28.4 us (4%)
    ppermute x26, waiting for transfers between devices, swap(): lax.ppermute(values, axis, [(i, i ^ bit) for i in range(lax.axis_size(axi...  218 us
    all_to_all x1, blocking collectives, to_heads(): lax.all_to_all(values, 'head', split_axis=0, concat_axis=0, tiled=True)  46.3 us
    ppermute x26, starting transfers between devices, swap(): lax.ppermute(values, axis, [(i, i ^ bit) for i in range(lax.axis_size(axi...  37.3 us
    pallas_call x1, Pallas kernels, attend_back(): pl.pallas_call(back_kernel, out_shape=(jax.ShapeDtypeStruct((rows_all, wi...  32.4 us
    pallas_call x1, Pallas kernels, attend(): pl.pallas_call(attend_kernel, out_shape=(jax.ShapeDtypeStruct((rows_all,...  28.8 us
    convert_element_type x12, other arithmetic, scatter_sum(): total = total.astype(jnp.bfloat16)  27.9 us
    pallas_call x3, Pallas kernels, weight_blocks(): pl.pallas_call(kernel, out_shape=[jax.ShapeDtypeStruct(shape, jnp.bfloat1...  27.2 us
    unnamed x106, local copies, waits for them, and re-layouts  13.7 us
  transfers between devices with their start and end apart: 31, of which 11 were waited for; matrix products, arithmetic and copies ran while one was open for 29% of the time, Pallas kernels for 9%

profile of v2, /device:TPU:0, one launch (start us, length us, event | category | flops | bytes accessed | tf_op | source)
XLA Modules:
  0.0 665.7 jit_solution(18181597315349320961)
XLA Ops:
  12.9 7.4 %fusion = bf16[256,3360]{0,1:T(8,128)(2,1)S(1)} fusion(bf16[1120,3360]{1,0:T(8,128)(2,1)} %param.29, f32[3360]{0:T(1024)S(1)} %concatenate.21, bf16[1,256,1120]{1,2,0:T(8,128)(2,1)} %param.23, f32[1120]{0:T(1024)} %param.28, f32[1120]{0:T(1024)} %param.27, f32[256]{0:T(256)S(1)} %fusion.36, f32[256]{0:T(256)S(1)} %broadcast_multiply_fusion.1, ...), kind=kOutput, calls=%fused_computation.8 | convolution fusion | flops 1930485760 | bytes 9849088 | tf_op jit(solution)/shard_map/dot_general | solution.py:404
  20.5 46.3 %all_to_all.25 = bf16[4,1,256,840]{2,3,1,0:T(8,128)(2,1)S(1)} all-to-all(bf16[4,1,256,840]{2,3,1,0:T(8,128)(2,1)S(1)} %bitcast.192), channel_id=1, replica_groups=mesh['cell'=4,'head'=4,'ctx'=2] {'head'}, dimensions={0} | all-to-all | bytes 3440640 | tf_op jit(solution)/shard_map/all_to_all | solution.py:412
  71.8 3.5 copy.125
  75.3 20.3 %collective-permute-done = bf16[1,1024,560]{1,2,0:T(8,128)(2,1)} collective-permute-done((bf16[1,1024,560]{1,2,0:T(8,128)(2,1)}, bf16[1,1024,560]{1,2,0:T(8,128)(2,1)}, u32[]{:S(2)}, u32[]{:S(2)}) %collective-permute-start) | collective-permute-done | bytes 1146912 | tf_op jit(solution)/shard_map/ppermute | solution.py:32
  95.6 2.4 copy.127
  98.0 28.8 %attend.1 = (bf16[1024,280]{1,0:T(8,128)(2,1)}, f32[4,280,256]{2,1,0:T(8,128)}, f32[4,5,1,256]{3,2,1,0:T(1,128)}) custom-call(s32[2]{0:T(128)} %pad_add_fusion.info, bf16[1024,840]{1,0:T(8,128)(2,1)} %bitcast.207, bf16[1024,560]{1,0:T(8,128)(2,1)} %bitcast.213), custom_call_target="tpu_custom_call" | custom-call | flops 21474836480 | bytes 8388608 | tf_op jit(solution)/shard_map/attend/pallas_call | solution.py:211
  126.8 2.3 copy.128
  129.1 4.2 all-to-all-start.1
  135.2 2.0 reshape_reshape.6
  138.3 7.9 %all-to-all-done.1 = bf16[4,1,256,280]{2,3,1,0:T(8,128)(2,1)} async-done(((bf16[4,1,256,280]{2,3,1,0:T(8,128)(2,1)}), bf16[4,1,256,280]{2,3,1,0:T(8,128)(2,1)}, u32[]{:S(2)}, u32[]{:S(2)}) %all-to-all-start.1) | async-done | bytes 573472 | tf_op jit(solution)/shard_map/all_to_all | solution.py:418
  146.1 2.3 copy.129
  148.4 2.3 copy.130
  150.7 2.5 fusion.51
  154.5 10.5 %multiply_convert_fusion = (bf16[256,4480]{1,0:T(8,128)(2,1)}, f32[256,4480]{1,0:T(8,128)}) fusion(f32[4480]{0:T(1024)S(1)} %copy-done.45, bf16[256,1120]{0,1:T(8,128)(2,1)S(1)} %add_convert_fusion.12, bf16[1120,4480]{1,0:T(8,128)(2,1)} %param.36), kind=kOutput, calls=%fused_computation.18 | convolution fusion | flops 2580480000 | bytes 17507840 | tf_op jit(solution)/shard_map/dot_general | solution.py:435
  165.0 4.2 copy.131
  169.2 4.3 copy.132
  173.5 10.0 %weight_blocks.3 = (bf16[2,8,140,1120]{3,2,1,0:T(8,128)(2,1)}, bf16[2,8,140,1120]{3,2,1,0:T(8,128)(2,1)}) custom-call(s32[4]{0:T(128)} %broadcast_xor_fusion.ci, s32[8]{0:T(128)} %fusion.40.pi, bf16[8,140,256]{2,1,0:T(8,128)(2,1)} %bitcast.205, bf16[4,256,1120]{2,1,0:T(8,128)(2,1)} %bitcast.187), custom_call_target="tpu_custom_call" | custom-call | tf_op jit(solution)/shard_map/weight_blocks/pallas_call | solution.py:91
  183.5 11.6 %convert_reduce_fusion = (f32[4480]{0:T(1024)S(1)}, bf16[256,4480]{1,0:T(8,128)(2,1)S(1)}) fusion(f32[256,4480]{1,0:T(8,128)} %get-tuple-element.127, bf16[256,1120]{0,1:T(8,128)(2,1)} %bitcast.199, bf16[4480,1120]{0,1:T(8,128)(2,1)} %param.38), kind=kOutput, calls=%fused_computation.17 | convolution fusion | flops 2594237952 | bytes 17507840 | tf_op jit(solution)/shard_map/nd,fd->nf/dot_general | solution.py:447
  195.1 7.9 %multiply_reduce_fusion = (f32[1120]{0:T(1024)S(1)}, f32[256]{0:T(256)S(1)}, f32[1120]{0:T(1024)S(1)}, f32[256,1120]{0,1:T(8,128)S(1)}) fusion(f32[256,1120]{0,1:T(8,128)S(1)} %copy-done.11, f32[256]{0:T(256)S(1)} %fusion.37, f32[256]{0:T(256)S(1)} %broadcast_multiply_fusion, f32[1120]{0:T(1024)S(1)} %copy-done.38, ...), kind=kOutput, calls=%fused_computation.55 | convolution fusion | flops 2571302656 | bytes 14639232 | tf_op jit(solution)/shard_map/nf,df->nd/dot_general | solution.py:451
  206.1 4.4 all-to-all-start.2
  210.5 3.0 copy.142
  213.5 2.5 copy.143
  216.1 5.6 collective-permute-start.7
  221.6 2.0 reshape.421
  223.6 4.2 copy.134
  227.8 4.4 copy.135
  232.2 6.9 %weight_blocks.5 = (bf16[2,2,4,140,280]{4,3,2,1,0:T(8,128)(2,1)}, bf16[2,2,4,140,280]{4,3,2,1,0:T(8,128)(2,1)}) custom-call(s32[4]{0:T(128)} %broadcast_xor_fusion.ci, s32[8]{0:T(128)} %fusion.40.pi, bf16[8,140,256]{2,1,0:T(8,128)(2,1)} %bitcast.204, bf16[4,256,280]{2,1,0:T(8,128)(2,1)} %bitcast.191), custom_call_target="tpu_custom_call" | custom-call | tf_op jit(solution)/shard_map/weight_blocks/pallas_call | solution.py:91
  239.0 10.4 %weight_blocks.4 = (bf16[2,8,280,560]{3,2,1,0:T(8,128)(2,1)}, bf16[2,8,280,560]{3,2,1,0:T(8,128)(2,1)}) custom-call(s32[4]{0:T(128)} %broadcast_xor_fusion.ci, s32[8]{0:T(128)} %fusion.40.pi, bf16[4,280,256]{2,1,0:T(8,128)(2,1)} %bitcast.206, bf16[8,256,560]{2,1,0:T(8,128)(2,1)} %bitcast.183), custom_call_target="tpu_custom_call" | custom-call | tf_op jit(solution)/shard_map/weight_blocks/pallas_call | solution.py:91
  249.4 2.3 copy.133
  251.6 32.4 %attend_back.1 = (bf16[1024,280]{1,0:T(8,128)(2,1)}, bf16[1024,560]{1,0:T(8,128)(2,1)}, bf16[1024,560]{1,0:T(8,128)(2,1)}) custom-call(s32[2]{0:T(128)} %pad_add_fusion.info, bf16[1024,840]{1,0:T(8,128)(2,1)} %bitcast.208, bf16[1024,560]{1,0:T(8,128)(2,1)} %bitcast.214, bf16[1024,280]{1,0:T(8,128)(2,1)} %bitcast.217, ...), custom_call_target="tpu_custom_call" | custom-call | flops 64424509440 | bytes 8388608 | tf_op jit(solution)/shard_map/attend_back/pallas_call | solution.py:310
  284.0 2.4 copy.136
  286.4 5.5 collective-permute-start.1
  291.9 2.2 convolution_convert_fusion
  294.1 3.5 fusion.52
  300.9 5.4 convert_element_type.249
  306.3 4.1 dynamic-slice_bitcast_fusion
  310.4 3.0 collective-permute-start.8
  315.0 5.8 copy.154
  324.0 2.7 fusion.12
  329.6 5.1 all-to-all-start.3
  334.6 7.8 %collective-permute-done.8 = bf16[2,6,280,140]{2,0,3,1:T(2,128)(2,1)} collective-permute-done((bf16[2,6,280,140]{2,0,3,1:T(2,128)(2,1)}, bf16[2,6,280,140]{2,0,3,1:T(2,128)(2,1)}, u32[]{:S(2)}, u32[]{:S(2)}) %collective-permute-start.8) | collective-permute-done | bytes 940832 | tf_op jit(solution)/shard_map/ppermute | solution.py:32
  342.4 2.1 fusion.11
  345.8 1.9 add_convert_fusion.4
  362.6 2.4 add_convert_fusion.10
  366.8 4.4 collective-permute-done.12
  375.4 7.6 %fusion.14 = bf16[1,256,1120]{1,2,0:T(8,128)(2,1)} fusion(f32[256,1120]{0,1:T(8,128)S(1)} %copy-done.12, bf16[256,4480]{1,0:T(8,128)(2,1)S(1)} %copy-done.26, bf16[4480,1120]{0,1:T(8,128)(2,1)} %param.38, f32[1120]{0:T(1024)S(1)} %copy-done.47), kind=kOutput, calls=%fused_computation.36 | convolution fusion | flops 2569871360 | bytes 14053760 | tf_op jit(solution)/shard_map/dot_general | solution.py:437
  387.7 2.8 copy.147
  392.5 2.6 collective-permute-start.14
  395.2 4.4 all-to-all-start.4
  399.7 5.8 fusion.46
  406.5 3.8 add_convert_fusion.1
  417.6 5.8 add_convert_fusion
  423.4 2.0 slice.219
  430.5 2.0 collective-permute-start.15
  432.5 102.1 %collective-permute-done.2 = f32[2,32,280]{2,1,0:T(8,128)S(1)} collective-permute-done((f32[2,32,280]{2,1,0:T(8,128)S(1)}, f32[2,32,280]{2,1,0:T(8,128)S(1)}, u32[]{:S(2)}, u32[]{:S(2)}) %collective-permute-start.2) | collective-permute-done | bytes 71712 | tf_op jit(solution)/shard_map/ppermute | solution.py:32
  534.8 3.1 add_convert_fusion.3
  544.7 27.1 %collective-permute-done.4 = f32[1,32,280]{2,1,0:T(8,128)S(1)} collective-permute-done((f32[1,32,280]{2,1,0:T(8,128)S(1)}, f32[1,32,280]{2,1,0:T(8,128)S(1)}, u32[]{:S(2)}, u32[]{:S(2)}) %collective-permute-start.4) | collective-permute-done | bytes 35872 | tf_op jit(solution)/shard_map/ppermute | solution.py:32
  571.8 2.6 collective-permute-start.5
  574.5 3.6 add_convert_fusion.2
  581.3 2.0 add_convert_fusion.6
  587.4 2.1 copy.157
  590.1 22.2 %collective-permute-done.18 = bf16[4,280,560]{2,1,0:T(8,128)(2,1)} collective-permute-done((bf16[4,280,560]{2,1,0:T(8,128)(2,1)}, bf16[4,280,560]{2,1,0:T(8,128)(2,1)}, u32[]{:S(2)}, u32[]{:S(2)}) %collective-permute-start.18) | collective-permute-done | bytes 1254432 | tf_op jit(solution)/shard_map/ppermute | solution.py:32
  621.9 25.0 %collective-permute-done.19 = bf16[2,280,560]{2,1,0:T(8,128)(2,1)S(1)} collective-permute-done((bf16[2,280,560]{2,1,0:T(8,128)(2,1)S(1)}, bf16[2,280,560]{2,1,0:T(8,128)(2,1)S(1)}, u32[]{:S(2)}, u32[]{:S(2)}) %collective-permute-start.19) | collective-permute-done | bytes 627232 | tf_op jit(solution)/shard_map/ppermute | solution.py:32
  651.1 6.6 collective-permute-done.20
  (242 shorter events, 87.5 us)
Async XLA Ops:
  7.2 143.5 %copy-start = (bf16[1120,1120]{1,0:T(8,128)(2,1)S(1)}, bf16[1120,1120]{1,0:T(8,128)(2,1)}, u32[]{:S(2)}) copy-start(bf16[1120,1120]{1,0:T(8,128)(2,1)} %param.32) | copy-start | bytes 7526404
  12.1 121.7 %copy-start.39 = (f32[256]{0:T(256)}, f32[256]{0:T(256)S(1)}, u32[]{:S(2)}) copy-start(f32[256]{0:T(256)S(1)} %fusion.36) | copy-start | bytes 3076
  69.0 26.5 %collective-permute-start = (bf16[1,1024,560]{1,2,0:T(8,128)(2,1)}, bf16[1,1024,560]{1,2,0:T(8,128)(2,1)}, u32[]{:S(2)}, u32[]{:S(2)}) collective-permute-start(bf16[1,1024,560]{1,2,0:T(8,128)(2,1)} %slice.199), channel_id=1, source_target_pairs={{0,1},{1,0},{2,3},{3,2},{4,5},{5,4},{6,7},{7,6},{8,9},{9,8},{10,11... | collective-permute-start | bytes 3440648 | tf_op jit(solution)/shard_map/ppermute | solution.py:32
  126.8 7.1 %copy-start.5 = (bf16[1,256,1120]{1,2,0:T(8,128)(2,1)S(1)}, bf16[1,256,1120]{1,2,0:T(8,128)(2,1)}, u32[]{:S(2)}) copy-start(bf16[1,256,1120]{1,2,0:T(8,128)(2,1)} %param.23) | copy-start | bytes 1720324
  126.8 7.1 %copy-start.37 = (f32[1120]{0:T(1024)S(1)}, f32[1120]{0:T(1024)}, u32[]{:S(2)}) copy-start(f32[1120]{0:T(1024)} %param.27) | copy-start | bytes 13444
  126.8 7.1 %copy-start.43 = (f32[1120]{0:T(1024)S(1)}, f32[1120]{0:T(1024)}, u32[]{:S(2)}) copy-start(f32[1120]{0:T(1024)} %param.28) | copy-start | bytes 13444
  129.1 17.0 %all-to-all-start.1 = ((bf16[4,1,256,280]{2,3,1,0:T(8,128)(2,1)}), bf16[4,1,256,280]{2,3,1,0:T(8,128)(2,1)}, u32[]{:S(2)}, u32[]{:S(2)}) async-start(bf16[4,1,256,280]{2,3,1,0:T(8,128)(2,1)} %copy.128), calls=%async_computation.1 | async-start | bytes 1146880 | tf_op jit(solution)/shard_map/all_to_all | solution.py:418
  133.3 4.5 copy-start.48
  133.3 77.3 %all-gather.2.cloned.1.call-start = ((), (), s32[]{:S(2)}) async-start(), calls=%async_computation.5 | async-start | bytes 2867200 | tf_op jit(solution)/shard_map/all_gather | solution.py:425
  135.2 15.4 %copy-start.46 = (f32[1120]{0:T(1024)S(1)}, f32[1120]{0:T(1024)}, u32[]{:S(2)}) copy-start(f32[1120]{0:T(1024)} %param.33) | copy-start | bytes 13444
  150.7 3.5 copy-start.38
  150.7 3.5 copy-start.44
  154.5 10.5 %copy-start.28 = (bf16[256,1120]{0,1:T(8,128)(2,1)}, bf16[256,1120]{0,1:T(8,128)(2,1)S(1)}, u32[]{:S(2)}) copy-start(bf16[256,1120]{0,1:T(8,128)(2,1)S(1)} %add_convert_fusion.12) | copy-start | bytes 1720324
  183.5 11.6 %copy-start.11 = (f32[256,1120]{0,1:T(8,128)S(1)}, f32[256,1120]{0,1:T(8,128)}, u32[]{:S(2)}) copy-start(f32[256,1120]{0,1:T(8,128)} %copy-done.10) | copy-start | bytes 3440644
  195.1 7.9 %copy-start.27 = (bf16[256,4480]{1,0:T(8,128)(2,1)}, bf16[256,4480]{1,0:T(8,128)(2,1)S(1)}, u32[]{:S(2)}) copy-start(bf16[256,4480]{1,0:T(8,128)(2,1)S(1)} %get-tuple-element.105) | copy-start | bytes 6881284
  206.1 43.3 %all-to-all-start.2 = ((bf16[4,1,256,280]{2,3,1,0:T(8,128)(2,1)}), bf16[4,1,256,280]{2,3,1,0:T(8,128)(2,1)}, u32[]{:S(2)}, u32[]{:S(2)}) async-start(bf16[4,1,256,280]{2,3,1,0:T(8,128)(2,1)} %bitcast.220), calls=%async_computation.2 | async-start | bytes 1146880 | tf_op jit(solution)/shard_map/all_to_all | solution.py:412
  216.1 78.1 %collective-permute-start.7 = (bf16[1024,1120]{0,1:T(8,128)(2,1)}, bf16[1024,1120]{0,1:T(8,128)(2,1)}, u32[]{:S(2)}, u32[]{:S(2)}) collective-permute-start(bf16[1024,1120]{0,1:T(8,128)(2,1)} %copy.143), channel_id=1, source_target_pairs={{0,1},{1,0},{2,3},{3,2},{4,5},{5,4},{6,7},{7,6},{8,9},{9,8},{10,11... | collective-permute-start | bytes 6881288 | tf_op jit(solution)/shard_map/ppermute | solution.py:32
  286.4 35.9 %collective-permute-start.1 = (bf16[1,1024,560]{1,2,0:T(8,128)(2,1)}, bf16[1,1024,560]{1,2,0:T(8,128)(2,1)}, u32[]{:S(2)}, u32[]{:S(2)}) collective-permute-start(bf16[1,1024,560]{1,2,0:T(8,128)(2,1)} %copy.136), channel_id=1, source_target_pairs={{0,1},{1,0},{2,3},{3,2},{4,5},{5,4},{6,7},{7,6},{8,9},{9,8},{10,11... | collective-permute-start | bytes 3440648 | tf_op jit(solution)/shard_map/ppermute | solution.py:32
  294.1 3.6 copy-start.35
  306.3 7.1 %copy-start.31 = (bf16[2,2,4,140,280]{4,3,2,1,0:T(8,128)(2,1)S(1)}, bf16[2,2,4,140,280]{4,3,2,1,0:T(8,128)(2,1)}, u32[]{:S(2)}) copy-start(bf16[2,2,4,140,280]{4,3,2,1,0:T(8,128)(2,1)} %get-tuple-element.43) | copy-start | bytes 3763204
  310.4 32.0 %collective-permute-start.8 = (bf16[2,6,280,140]{2,0,3,1:T(2,128)(2,1)}, bf16[2,6,280,140]{2,0,3,1:T(2,128)(2,1)}, u32[]{:S(2)}, u32[]{:S(2)}) collective-permute-start(bf16[2,6,280,140]{2,0,3,1:T(2,128)(2,1)} %get-tuple-element.111), channel_id=1, source_target_pairs={{0,16},{8,24},{16,0},{24,8},{1,17},{9,25},{17,1},{25,9},{2,18},{10... | collective-permute-start | bytes 2822408 | tf_op jit(solution)/shard_map/ppermute | solution.py:32
  315.0 30.8 %collective-permute-start.11 = (bf16[16,140,280]{2,0,1:T(8,128)(2,1)}, bf16[16,140,280]{2,0,1:T(8,128)(2,1)}, u32[]{:S(2)}, u32[]{:S(2)}) collective-permute-start(bf16[16,140,280]{2,0,1:T(8,128)(2,1)} %copy.152), channel_id=1, source_target_pairs={{0,8},{8,0},{16,24},{24,16},{1,9},{9,1},{17,25},{25,17},{2,10},{10... | collective-permute-start | bytes 3763208 | tf_op jit(solution)/shard_map/ppermute | solution.py:32
  315.0 7.0 %copy-start.36 = (bf16[1024,280]{1,0:T(8,128)(2,1)S(1)}, bf16[1024,280]{1,0:T(8,128)(2,1)}, u32[]{:S(2)}) copy-start(bf16[1024,280]{1,0:T(8,128)(2,1)} %get-tuple-element.47) | copy-start | bytes 1720324
  320.8 85.7 %collective-permute-start.21 = (bf16[16,140,1120]{2,0,1:T(8,128)(2,1)}, bf16[16,140,1120]{2,0,1:T(8,128)(2,1)}, u32[]{:S(2)}, u32[]{:S(2)}) collective-permute-start(bf16[16,140,1120]{2,0,1:T(8,128)(2,1)} %copy.154), channel_id=1, source_target_pairs={{0,8},{8,0},{16,24},{24,16},{1,9},{9,1},{17,25},{25,17},{2,10},{10... | collective-permute-start | bytes 15052808 | tf_op jit(solution)/shard_map/ppermute | solution.py:32
  329.6 65.6 %all-to-all-start.3 = ((bf16[4,1,256,840]{2,3,1,0:T(8,128)(2,1)}), bf16[4,1,256,840]{2,3,1,0:T(8,128)(2,1)S(1)}, u32[]{:S(2)}, u32[]{:S(2)}) async-start(bf16[4,1,256,840]{2,3,1,0:T(8,128)(2,1)} %pad_maximum_fusion.1), calls=%async_computation.3 | async-start | bytes 3440640 | tf_op jit(solution)/shard_map/all_to_all | solution.py:418
  342.4 3.4 copy-start.30
  345.5 17.1 %collective-permute-start.9 = (bf16[1,6,280,140]{2,3,1,0:T(8,128)(2,1)}, bf16[1,6,280,140]{2,3,1,0:T(8,128)(2,1)}, u32[]{:S(2)}, u32[]{:S(2)}) collective-permute-start(bf16[1,6,280,140]{2,3,1,0:T(8,128)(2,1)} %constant_dynamic-slice_fusion.5), channel_id=1, source_target_pairs={{0,8},{8,0},{16,24},{24,16},{1,9},{9,1},{17,25},{25,17},{2,10},{10... | collective-permute-start | bytes 1411208 | tf_op jit(solution)/shard_map/ppermute | solution.py:32
  349.0 22.2 %collective-permute-start.12 = (bf16[8,140,280]{2,0,1:T(8,128)(2,1)S(1)}, bf16[8,140,280]{2,0,1:T(8,128)(2,1)}, u32[]{:S(2)}, u32[]{:S(2)}) collective-permute-start(bf16[8,140,280]{2,0,1:T(8,128)(2,1)S(1)} %slice.208), channel_id=1, source_target_pairs={{0,1},{1,0},{2,3},{3,2},{4,5},{5,4},{6,7},{7,6},{8,9},{9,8},{10,11... | collective-permute-start | bytes 1881608 | tf_op jit(solution)/shard_map/ppermute | solution.py:32
  362.5 8.7 %copy-start.14 = (bf16[16,140,280]{2,0,1:T(8,128)(2,1)S(1)}, bf16[16,140,280]{2,0,1:T(8,128)(2,1)}, u32[]{:S(2)}) copy-start(bf16[16,140,280]{2,0,1:T(8,128)(2,1)} %copy-done.13) | copy-start | bytes 3763204
  362.5 55.0 %collective-permute-start.16 = (bf16[16,280,560]{2,1,0:T(8,128)(2,1)}, bf16[16,280,560]{2,1,0:T(8,128)(2,1)}, u32[]{:S(2)}, u32[]{:S(2)}) collective-permute-start(bf16[16,280,560]{2,1,0:T(8,128)(2,1)} %bitcast.224), channel_id=1, source_target_pairs={{0,8},{8,0},{16,24},{24,16},{1,9},{9,1},{17,25},{25,17},{2,10},{10... | collective-permute-start | bytes 15052808 | tf_op jit(solution)/shard_map/ppermute | solution.py:32
  362.6 12.7 %copy-start.47 = (f32[1120]{0:T(1024)S(1)}, f32[1120]{0:T(1024)}, u32[]{:S(2)}) copy-start(f32[1120]{0:T(1024)} %param.39) | copy-start | bytes 13444
  365.0 10.3 %copy-start.12 = (f32[256,1120]{0,1:T(8,128)S(1)}, f32[256,1120]{0,1:T(8,128)}, u32[]{:S(2)}) copy-start(f32[256,1120]{0,1:T(8,128)} %copy-done.10) | copy-start | bytes 3440644
  365.0 10.3 %copy-start.26 = (bf16[256,4480]{1,0:T(8,128)(2,1)S(1)}, bf16[256,4480]{1,0:T(8,128)(2,1)}, u32[]{:S(2)}) copy-start(bf16[256,4480]{1,0:T(8,128)(2,1)} %get-tuple-element.126) | copy-start | bytes 6881284
  365.0 19.6 %collective-permute-start.10 = (bf16[1,6,280,140]{2,3,1,0:T(8,128)(2,1)}, bf16[1,6,280,140]{2,3,1,0:T(8,128)(2,1)}, u32[]{:S(2)}, u32[]{:S(2)}) collective-permute-start(bf16[1,6,280,140]{2,3,1,0:T(8,128)(2,1)} %add_convert_fusion.10), channel_id=1, source_target_pairs={{0,1},{1,0},{2,3},{3,2},{4,5},{5,4},{6,7},{7,6},{8,9},{9,8},{10,11... | collective-permute-start | bytes 1411208 | tf_op jit(solution)/shard_map/ppermute | solution.py:32
  372.6 10.4 %copy-start.24 = (bf16[8,140,280]{2,0,1:T(8,128)(2,1)}, bf16[8,140,280]{2,0,1:T(8,128)(2,1)S(1)}, u32[]{:S(2)}) copy-start(bf16[8,140,280]{2,0,1:T(8,128)(2,1)S(1)} %add_convert_fusion.7) | copy-start | bytes 1881604
  373.6 16.9 %collective-permute-start.13 = (bf16[4,140,280]{2,0,1:T(4,128)(2,1)}, bf16[4,140,280]{2,0,1:T(4,128)(2,1)}, u32[]{:S(2)}, u32[]{:S(2)}) collective-permute-start(bf16[4,140,280]{2,0,1:T(4,128)(2,1)} %slice.210), channel_id=1, source_target_pairs={{0,16},{8,24},{16,0},{24,8},{1,17},{9,25},{17,1},{25,9},{2,18},{10... | collective-permute-start | bytes 940808 | tf_op jit(solution)/shard_map/ppermute | solution.py:32
  392.5 37.5 %collective-permute-start.14 = (bf16[2,140,280]{2,0,1:T(2,128)(2,1)S(1)}, bf16[2,140,280]{2,0,1:T(2,128)(2,1)S(1)}, u32[]{:S(2)}, u32[]{:S(2)}) collective-permute-start(bf16[2,140,280]{2,0,1:T(2,128)(2,1)S(1)} %slice.212), channel_id=1, source_target_pairs={{0,4},{2,6},{4,0},{6,2},{1,5},{3,7},{5,1},{7,3},{8,12},{10,14},{12... | collective-permute-start | bytes 470408 | tf_op jit(solution)/shard_map/ppermute | solution.py:32
  395.2 147.7 %all-to-all-start.4 = ((bf16[4,2,280,140]{2,1,3,0:T(2,128)(2,1)}), bf16[4,2,280,140]{2,1,3,0:T(2,128)(2,1)}, u32[]{:S(2)}, u32[]{:S(2)}) async-start(bf16[4,2,280,140]{2,1,3,0:T(2,128)(2,1)} %copy.147), calls=%async_computation.4 | async-start | bytes 1720320 | tf_op jit(solution)/shard_map/all_to_all | solution.py:513
  399.7 6.8 %slice-start = ((s8[5308416]{0:T(1024)(128)(4,1)}), s8[4194304]{0:T(1024)(128)(4,1)S(1)}, s32[]{:S(2)}) async-start(s8[5308416]{0:T(1024)(128)(4,1)} %bitcast.195), calls=%async_computation.6 | async-start | bytes 8388608
  399.7 5.8 copy-start.42
  399.7 5.8 copy-start.40
  399.7 6.8 %slice-start.1 = ((s8[5308416]{0:T(1024)(128)(4,1)}), s8[1114112]{0:T(1024)(128)(4,1)S(1)}, s32[]{:S(2)}) async-start(s8[5308416]{0:T(1024)(128)(4,1)} %bitcast.195), calls=%async_computation.7 | async-start | bytes 2228224
  410.3 3.5 copy-start.3
  410.3 5.3 copy-start.9
  410.4 5.3 copy-start.21
  410.4 5.3 copy-start.23
  413.9 120.9 %collective-permute-start.22 = (bf16[8,140,1120]{2,0,1:T(8,128)(2,1)}, bf16[8,140,1120]{2,0,1:T(8,128)(2,1)}, u32[]{:S(2)}, u32[]{:S(2)}) collective-permute-start(bf16[8,140,1120]{2,0,1:T(8,128)(2,1)} %slice.228), channel_id=1, source_target_pairs={{0,16},{8,24},{16,0},{24,8},{1,17},{9,25},{17,1},{25,9},{2,18},{10... | collective-permute-start | bytes 7526408 | tf_op jit(solution)/shard_map/ppermute | solution.py:32
  423.4 3.5 copy-start.2
  426.8 147.6 %collective-permute-start.17 = (bf16[8,280,560]{2,1,0:T(8,128)(2,1)}, bf16[8,280,560]{2,1,0:T(8,128)(2,1)}, u32[]{:S(2)}, u32[]{:S(2)}) collective-permute-start(bf16[8,280,560]{2,1,0:T(8,128)(2,1)} %slice.219), channel_id=1, source_target_pairs={{0,16},{8,24},{16,0},{24,8},{1,17},{9,25},{17,1},{25,9},{2,18},{10... | collective-permute-start | bytes 7526408 | tf_op jit(solution)/shard_map/ppermute | solution.py:32
  428.3 106.4 %collective-permute-start.2 = (f32[2,32,280]{2,1,0:T(8,128)S(1)}, f32[2,32,280]{2,1,0:T(8,128)S(1)}, u32[]{:S(2)}, u32[]{:S(2)}) collective-permute-start(f32[2,32,280]{2,1,0:T(8,128)S(1)} %constant_dynamic-slice_fusion.8), channel_id=1, source_target_pairs={{0,16},{8,24},{16,0},{24,8},{1,17},{9,25},{17,1},{25,9},{2,18},{10... | collective-permute-start | bytes 215048 | tf_op jit(solution)/shard_map/ppermute | solution.py:32
  430.5 109.6 %collective-permute-start.15 = (bf16[1,140,280]{2,0,1:T(2,128)(2,1)S(1)}, bf16[1,140,280]{2,0,1:T(2,128)(2,1)S(1)}, u32[]{:S(2)}, u32[]{:S(2)}) collective-permute-start(bf16[1,140,280]{2,0,1:T(2,128)(2,1)S(1)} %slice.214), channel_id=1, source_target_pairs={{0,2},{2,0},{4,6},{6,4},{1,3},{3,1},{5,7},{7,5},{8,10},{10,8},{12,... | collective-permute-start | bytes 235208 | tf_op jit(solution)/shard_map/ppermute | solution.py:32
  534.7 6.5 collective-permute-start.3
  539.8 41.5 %collective-permute-start.23 = (bf16[4,140,1120]{2,0,1:T(4,128)(2,1)}, bf16[4,140,1120]{2,0,1:T(4,128)(2,1)}, u32[]{:S(2)}, u32[]{:S(2)}) collective-permute-start(bf16[4,140,1120]{2,0,1:T(4,128)(2,1)} %slice.230), channel_id=1, source_target_pairs={{0,1},{1,0},{2,3},{3,2},{4,5},{5,4},{6,7},{7,6},{8,9},{9,8},{10,11... | collective-permute-start | bytes 3763208 | tf_op jit(solution)/shard_map/ppermute | solution.py:32
  541.2 30.6 %collective-permute-start.4 = (f32[1,32,280]{2,1,0:T(8,128)S(1)}, f32[1,32,280]{2,1,0:T(8,128)S(1)}, u32[]{:S(2)}, u32[]{:S(2)}) collective-permute-start(f32[1,32,280]{2,1,0:T(8,128)S(1)} %dynamic-slice_add_fusion.1), channel_id=1, source_target_pairs={{0,1},{1,0},{2,3},{3,2},{4,5},{5,4},{6,7},{7,6},{8,9},{9,8},{10,11... | collective-permute-start | bytes 107528 | tf_op jit(solution)/shard_map/ppermute | solution.py:32
  571.8 8.0 %collective-permute-start.5 = (f32[1,32,280]{2,1,0:T(8,128)S(1)}, f32[1,32,280]{2,1,0:T(8,128)S(1)}, u32[]{:S(2)}, u32[]{:S(2)}) collective-permute-start(f32[1,32,280]{2,1,0:T(8,128)S(1)} %add.298), channel_id=1, source_target_pairs={{0,4},{2,6},{4,0},{6,2},{1,5},{3,7},{5,1},{7,3},{8,12},{10,14},{12... | collective-permute-start | bytes 107528 | tf_op jit(solution)/shard_map/ppermute | solution.py:32
  579.3 33.0 %collective-permute-start.18 = (bf16[4,280,560]{2,1,0:T(8,128)(2,1)}, bf16[4,280,560]{2,1,0:T(8,128)(2,1)}, u32[]{:S(2)}, u32[]{:S(2)}) collective-permute-start(bf16[4,280,560]{2,1,0:T(8,128)(2,1)} %slice.221), channel_id=1, source_target_pairs={{0,1},{1,0},{2,3},{3,2},{4,5},{5,4},{6,7},{7,6},{8,9},{9,8},{10,11... | collective-permute-start | bytes 3763208 | tf_op jit(solution)/shard_map/ppermute | solution.py:32
  579.8 9.7 %collective-permute-start.6 = (f32[1,32,280]{2,1,0:T(8,128)S(1)}, f32[1,32,280]{2,1,0:T(8,128)S(1)}, u32[]{:S(2)}, u32[]{:S(2)}) collective-permute-start(f32[1,32,280]{2,1,0:T(8,128)S(1)} %add.299), channel_id=1, source_target_pairs={{0,2},{2,0},{4,6},{6,4},{1,3},{3,1},{5,7},{7,5},{8,10},{10,8},{12,... | collective-permute-start | bytes 107528 | tf_op jit(solution)/shard_map/ppermute | solution.py:32
  585.9 30.3 %collective-permute-start.24 = (bf16[2,140,1120]{2,0,1:T(2,128)(2,1)}, bf16[2,140,1120]{2,0,1:T(2,128)(2,1)}, u32[]{:S(2)}, u32[]{:S(2)}) collective-permute-start(bf16[2,140,1120]{2,0,1:T(2,128)(2,1)} %slice.232), channel_id=1, source_target_pairs={{0,4},{2,6},{4,0},{6,2},{1,5},{3,7},{5,1},{7,3},{8,12},{10,14},{12... | collective-permute-start | bytes 1881608 | tf_op jit(solution)/shard_map/ppermute | solution.py:32
  614.0 4.6 copy-start.16
  614.1 32.8 %collective-permute-start.19 = (bf16[2,280,560]{2,1,0:T(8,128)(2,1)S(1)}, bf16[2,280,560]{2,1,0:T(8,128)(2,1)S(1)}, u32[]{:S(2)}, u32[]{:S(2)}) collective-permute-start(bf16[2,280,560]{2,1,0:T(8,128)(2,1)S(1)} %slice.223), channel_id=1, source_target_pairs={{0,4},{2,6},{4,0},{6,2},{1,5},{3,7},{5,1},{7,3},{8,12},{10,14},{12... | collective-permute-start | bytes 1881608 | tf_op jit(solution)/shard_map/ppermute | solution.py:32
  617.9 30.3 %copy-start.15 = (bf16[2,140,1120]{2,0,1:T(2,128)(2,1)}, bf16[2,140,1120]{2,0,1:T(2,128)(2,1)S(1)}, u32[]{:S(2)}) copy-start(bf16[2,140,1120]{2,0,1:T(2,128)(2,1)S(1)} %add_convert_fusion.11) | copy-start | bytes 1881604
  619.4 28.9 %collective-permute-start.25 = (bf16[1,140,1120]{2,1,0:T(8,128)(2,1)}, bf16[1,140,1120]{2,1,0:T(8,128)(2,1)S(1)}, u32[]{:S(2)}, u32[]{:S(2)}) collective-permute-start(bf16[1,140,1120]{2,1,0:T(8,128)(2,1)} %copy.155), channel_id=1, source_target_pairs={{0,2},{2,0},{4,6},{6,4},{1,3},{3,1},{5,7},{7,5},{8,10},{10,8},{12,... | collective-permute-start | bytes 940808 | tf_op jit(solution)/shard_map/ppermute | solution.py:32
  648.3 9.4 %collective-permute-start.20 = (bf16[1,280,560]{2,1,0:T(8,128)(2,1)S(1)}, bf16[1,280,560]{2,1,0:T(8,128)(2,1)S(1)}, u32[]{:S(2)}, u32[]{:S(2)}) collective-permute-start(bf16[1,280,560]{2,1,0:T(8,128)(2,1)S(1)} %slice.225), channel_id=1, source_target_pairs={{0,2},{2,0},{4,6},{6,4},{1,3},{3,1},{5,7},{7,5},{8,10},{10,8},{12,... | collective-permute-start | bytes 940808 | tf_op jit(solution)/shard_map/ppermute | solution.py:32
  648.3 10.3 %copy-start.1 = (bf16[1120,1120]{1,0:T(8,128)(2,1)S(1)}, bf16[1120,1120]{1,0:T(8,128)(2,1)}, u32[]{:S(2)}) copy-start(bf16[1120,1120]{1,0:T(8,128)(2,1)} %param.32) | copy-start | bytes 7526404
  (18 other events, 31.9 us)
Sparse Core Ops, SparseCore 0:
  136.2 54.8 all-gather.1

commit v3 on v2

--- a/solution.py
+++ b/solution.py
@@ -48,55 +48,109 @@
     return lax.dot_general(a, b, (((1,), (1,)), ((), ())), preferred_element_type=jnp.float32)
 
 
+def relative_order(count, axis_bits):
+    rel = np.zeros((count,), np.int32)
+    for s, bit in enumerate(axis_bits):
+        rel += ((np.arange(count) >> (len(axis_bits) - 1 - s)) & 1).astype(np.int32) * bit
+    return jnp.asarray(rel)
+
+
+def padded_rows(values, multiple=16):
+    extra = -values.shape[1] % multiple
+    return jnp.pad(values, ((0, 0), (0, extra), (0, 0))) if extra else values
+
+
 def weight_blocks(left, right, by_cell_left, y_first):
     cells, groups, halves = lax.axis_size("cell"), lax.axis_size("head"), lax.axis_size("ctx")
     parts, half_cells = groups * halves, cells // 2
-    steps = bits_of("cell")
-    rel = np.zeros((cells,), np.int32)
-    for s, (_, bit) in enumerate(steps):
-        rel += ((np.arange(cells) >> (len(steps) - 1 - s)) & 1).astype(np.int32) * bit
-    cell_ids = jnp.asarray(rel) ^ lax.axis_index("cell")
+    cell_ids = relative_order(cells, [b for _, b in bits_of("cell")]) ^ lax.axis_index("cell")
     places = jnp.arange(parts, dtype=jnp.int32)
     part_ids = ((places % groups) ^ lax.axis_index("head")) * halves + (
         (places // groups) ^ lax.axis_index("ctx")
     )
+    left_ids, right_ids = (cell_ids, part_ids) if by_cell_left else (part_ids, cell_ids)
+    left = padded_rows(left[left_ids])
     rows, cols = left.shape[1], right.shape[2]
-
-    def kernel(ci, pi, left_ref, right_ref, kept, sent):
-        part = pi[pl.program_id(0)]
-        for n in range(cells):
-            cell = ci[n]
-            out, at = (kept, n) if n < half_cells else (sent, n - half_cells)
-            if by_cell_left:
-                block = nn(left_ref[cell], right_ref[part])
-            else:
-                block = nn(left_ref[part], right_ref[cell])
-            if y_first:
-                out[0, at, 0] = block.astype(jnp.bfloat16)
-            else:
-                out[at, 0] = block.astype(jnp.bfloat16)
-
-    if y_first:
+    tall = left.reshape(-1, left.shape[2])
+    right_count = right.shape[0]
+
+    def put(out, index, values):
+        out[index] = values.astype(jnp.bfloat16)
+
+    def kernel(ids, left_ref, right_ref, kept, sent):
+        i = pl.program_id(0)
+        if by_cell_left:
+            block = nn(left_ref[...], right_ref[ids[i]])
+            for n in range(cells):
+                out, at = (kept, n) if n < half_cells else (sent, n - half_cells)
+                put(out, (at, 0), block[n * rows : (n + 1) * rows])
+        else:
+            block = nn(left_ref[...], right_ref[ids[(i + half_cells) % cells]])
+
+            def fill(out):
+                for n in range(parts):
+                    at = (n // groups, 0, n % groups) if y_first else (0, n)
+                    put(out, at, block[n * rows : (n + 1) * rows])
+
+            pl.when(i < half_cells)(lambda: fill(sent))
+            pl.when(i >= half_cells)(lambda: fill(kept))
+
+    last = half_cells - 1
+    if by_cell_left:
+        shape = (half_cells, parts, rows, cols)
+        specs = [pl.BlockSpec((half_cells, 1, rows, cols), lambda i, ids: (0, i, 0, 0))] * 2
+    elif y_first:
         shape = (halves, half_cells, groups, rows, cols)
-        spec = pl.BlockSpec(
-            (1, half_cells, 1, rows, cols), lambda i, ci, pi: (i // groups, 0, i % groups, 0, 0)
-        )
+        block_shape = (halves, 1, groups, rows, cols)
+        specs = [
+            pl.BlockSpec(block_shape, lambda i, ids: (0, jnp.maximum(i - last - 1, 0), 0, 0, 0)),
+            pl.BlockSpec(block_shape, lambda i, ids: (0, jnp.minimum(i, last), 0, 0, 0)),
+        ]
     else:
         shape = (half_cells, parts, rows, cols)
-        spec = pl.BlockSpec((half_cells, 1, rows, cols), lambda i, ci, pi: (0, i, 0, 0))
-    whole = [
-        pl.BlockSpec(x.shape, lambda i, ci, pi: (0, 0, 0), pipeline_mode=pl.Buffered(1))
-        for x in (left, right)
-    ]
+        block_shape = (1, parts, rows, cols)
+        specs = [
+            pl.BlockSpec(block_shape, lambda i, ids: (jnp.maximum(i - last - 1, 0), 0, 0, 0)),
+            pl.BlockSpec(block_shape, lambda i, ids: (jnp.minimum(i, last), 0, 0, 0)),
+        ]
     kept, sent = pl.pallas_call(
         kernel,
         out_shape=[jax.ShapeDtypeStruct(shape, jnp.bfloat16)] * 2,
         grid_spec=pltpu.PrefetchScalarGridSpec(
-            num_scalar_prefetch=2, grid=(parts,), in_specs=whole, out_specs=[spec, spec]
+            num_scalar_prefetch=1,
+            grid=(right_count,),
+            in_specs=[
+                pl.BlockSpec(tall.shape, lambda i, ids: (0, 0), pipeline_mode=pl.Buffered(1)),
+                pl.BlockSpec(right.shape, lambda i, ids: (0, 0, 0), pipeline_mode=pl.Buffered(1)),
+            ],
+            out_specs=specs,
         ),
         name="weight_blocks",
-    )(cell_ids, part_ids, left, right)
+    )(right_ids, tall, right)
     return kept.reshape(-1, rows, cols), sent.reshape(-1, rows, cols)
+
+
+def line_gather(values):
+    groups, halves = lax.axis_size("head"), lax.axis_size("ctx")
+    index = lax.axis_index("head")
+
+    def across(piece, heads):
+        pairs = [(h * halves + c, h * halves + (c ^ 1)) for h in heads for c in range(halves)]
+        return lax.ppermute(piece, ("head", "ctx"), pairs)
+
+    near, far = {0: values}, {0: across(values, range(groups))}
+    rising = falling = values
+    for k in range(1, groups):
+        rising = lax.ppermute(rising, "head", [(i, i + 1) for i in range(k - 1, groups - 1)])
+        falling = lax.ppermute(falling, "head", [(i + 1, i) for i in range(groups - k)])
+        near[-k], near[k] = rising, falling
+        far[-k], far[k] = across(rising, range(k, groups)), across(falling, range(groups - k))
+
+    def ordered(found):
+        line = jnp.stack([found[k] for k in range(1 - groups, groups)])
+        return lax.dynamic_slice_in_dim(line, groups - 1 - index, groups, 0)
+
+    return ordered(near), ordered(far)
 
 
 def add_up(kept, got):
@@ -401,9 +455,23 @@
     embedded = jnp.dot(one_hot, dataset_table, preferred_element_type=jnp.float32)
     residual = (inputs.astype(jnp.float32) + embedded[:, None, :]).reshape(token_count, model_width)
     normed = layer_norm(residual, attn_gain, attn_shift).astype(jnp.bfloat16)
-    mixed_qkv = jnp.dot(normed, qkv_weight, preferred_element_type=jnp.float32)
+    normed_near, normed_far = line_gather(normed.reshape(cell_count, row_count, model_width))
+    normed_near = normed_near.transpose(1, 0, 2, 3).reshape(cell_count * ctx_rows, model_width)
+    normed_far = normed_far.transpose(1, 0, 2, 3).reshape(cell_count * ctx_rows, model_width)
+    head_index = lax.axis_index("head")
+
+    def own_columns(values):
+        values = values.reshape(values.shape[0], 3, groups, head_width)
+        values = lax.dynamic_index_in_dim(values, head_index, 2, keepdims=False)
+        return values.reshape(values.shape[0], 3 * head_width)
+
+    own_weight = own_columns(qkv_weight)
     bias_row = jnp.concatenate([query_bias, jnp.zeros_like(query_bias), value_bias])
-    mixed_qkv = (mixed_qkv + bias_row).astype(jnp.bfloat16)
+    own_bias = own_columns(bias_row[None])
+    qkv_heads = (nn(normed_near, own_weight) + own_bias).astype(jnp.bfloat16)
+    qkv_heads = qkv_heads.reshape(cell_count, ctx_rows, -1)
+    kv_other = nn(normed_far, own_weight[:, head_width:]) + own_bias[:, head_width:]
+    kv_other = kv_other.astype(jnp.bfloat16).reshape(cell_count, ctx_rows, -1)
 
     def to_heads(values):
         sections = values.shape[1] // model_width
@@ -419,12 +487,6 @@
         values = values.reshape(groups, cell_count, row_count, sections, head_width)
         return values.transpose(1, 2, 3, 0, 4).reshape(token_count, sections * model_width)
 
-    qkv_heads = to_heads(mixed_qkv)
-    kv_other = swap(qkv_heads[:, :, head_width:], "ctx", 1)
-    normed_near = normed.reshape(cell_count, 1, row_count, model_width)
-    normed_near = lax.all_gather(normed_near, "head", axis=1, tiled=True)
-    normed_near = normed_near.reshape(cell_count * ctx_rows, model_width)
-    normed_far = swap(normed_near, "ctx", 1)
     infos = [jnp.stack([lengths[n], half_index.astype(jnp.int32)]) for n in range(cell_count)]
     runs = [attend(infos[n], qkv_heads[n], kv_other[n], groups) for n in range(cell_count)]
     attended = jnp.stack([r[0] for r in runs])
@@ -440,8 +502,8 @@
     proj_kept, proj_sent = weight_blocks(
         row_blocks(grad_low, parts), column_blocks(active, cells), False, False
     )
-    grad_low, proj_kept, proj_sent = lax.optimization_barrier((grad_low, proj_kept, proj_sent))
-    proj_weight_grad = scatter_sum(proj_kept, proj_sent, steps_x).T
+    part_columns = model_width // parts
+    proj_weight_grad = scatter_sum(proj_kept, proj_sent, steps_x)[:part_columns].T
     grad_top = grad_low.astype(jnp.float32)
     proj_bias_grad = jnp.sum(grad_top, axis=0)
     active_grad = jnp.einsum("nd,fd->nf", grad_low, proj_weight, preferred_element_type=jnp.float32)
@@ -467,11 +529,9 @@
     out_kept, out_sent = weight_blocks(
         row_blocks(middle_low, parts), column_blocks(attended_rows, cells), False, True
     )
-    grad_heads, fc_kept, fc_sent, out_kept, out_sent = lax.optimization_barrier(
-        (grad_heads, fc_kept, fc_sent, out_kept, out_sent)
-    )
-    fc_weight_grad = scatter_sum(fc_kept, fc_sent, steps_x)
-    out_weight_grad = scatter_sum(out_kept, out_sent, steps_y).T
+    cell_rows = model_width // cells
+    fc_weight_grad = scatter_sum(fc_kept, fc_sent, steps_x)[:cell_rows]
+    out_weight_grad = scatter_sum(out_kept, out_sent, steps_y)[:part_columns].T
 
     backs = [
       attend_back(
@@ -489,6 +549,8 @@
     def over_tokens(a, b):
         return jnp.einsum("nd,ne->de", a, b, preferred_element_type=jnp.float32)
 
+    dkv_got = swap(dkv_far, "ctx", 1)
+    dq_rows = to_rows(dq)
     qkv_part = jnp.concatenate(
         [
             over_tokens(normed_near, tall(dq)),
@@ -508,7 +570,6 @@
         qkv_part = add_up(kept, swap(sent, axis, bit)).astype(jnp.bfloat16)
     qkv_part = add_up(qkv_part, swap(qkv_part, "ctx", 1)).astype(jnp.bfloat16)[0]
     send_table, take_table = head_columns(groups, halves, 3, units)
-    head_index = lax.axis_index("head")
     sent = qkv_part[jnp.asarray(send_table)[head_index, half_index]]
     got = lax.all_to_all(sent, "head", split_axis=0, concat_axis=0, tiled=True)
     taken = jnp.asarray(take_table)[head_index, half_index]
@@ -516,9 +577,9 @@
         [got[taken[n, 0], taken[n, 1]] for n in range(take_table.shape[2])], axis=-1
     ).astype(jnp.float32)
 
-    dkv_got = swap(dkv_far, "ctx", 1)
     dkv = add_up(dkv, dkv_got).astype(jnp.bfloat16)
-    qkv_grad = to_rows(jnp.concatenate([dq, dkv], axis=-1))
+    dkv, dq_rows = lax.optimization_barrier((dkv, dq_rows))
+    qkv_grad = jnp.concatenate([dq_rows, to_rows(dkv)], axis=-1)
     column_sums = jnp.sum(qkv_grad, axis=0, dtype=jnp.float32)
     query_bias_grad = column_sums[:model_width]
     value_bias_grad = column_sums[2 * model_width :]

time: 678 us -> 754 us (1.11)
  waiting for transfers between devices: 226 us -> 319 us
  blocking collectives: 46.3 us -> 15.2 us
  starting transfers between devices: 55.8 us -> 77 us
  between operations: 28.4 us -> 15.2 us
  local copies, waits for them, and re-layouts: 103 us -> 115 us
    ppermute x26 -> x24, waiting for transfers between devices: 218 us -> 272 us  [swap(): lax.ppermute(values, axis, [(i, i ^ bit) for i in range(lax.axis_size(axi...]
    ppermute x0 -> x13, waiting for transfers between devices: none -> 46.8 us  [the longest x3 21.3 us: line_gather(): lax.ppermute(falling, 'head', [(i + 1, i) for i in range(groups - k)])]
    all_to_all x1, blocking collectives: 46.3 us -> 15.2 us  [to_rows(): lax.all_to_all(values, 'head', split_axis=0, concat_axis=0, tiled=True)]
    ppermute x0 -> x13, starting transfers between devices: none -> 26.7 us  [the longest x7 14.1 us: across(): return lax.ppermute(piece, ('head', 'ctx'), pairs)]
    unnamed x106 -> x122, local copies, waits for them, and re-layouts: 13.7 us -> 32.3 us
    dynamic_slice x0 -> x6, local copies, waits for them, and re-layouts: none -> 14.7 us  [the longest x4 11.6 us: ordered(): return lax.dynamic_slice_in_dim(line, groups - 1 - index, groups, 0)]
    all_to_all x2, waiting for transfers between devices: 7.86 us -> 0.01 us  [to_rows(): lax.all_to_all(values, 'head', split_axis=0, concat_axis=0, tiled=True)]
    ppermute x26 -> x24, starting transfers between devices: 37.3 us -> 31.5 us  [swap(): lax.ppermute(values, axis, [(i, i ^ bit) for i in range(lax.axis_size(axi...]
  transfers between devices with their start and end apart: 31 -> 41, of which waited for: 11 -> 14; matrix products, arithmetic and copies ran while one was open for 29% -> 23% of each run, Pallas kernels for 9% -> 8%
where the time goes in v3:
time: 754 us; the launch traced here: 745 us
  waiting for transfers between devices  319 us (42%)
  local copies, waits for them, and re-layouts  115 us (15%)
  Pallas kernels  87.8 us (12%)
  starting transfers between devices  77 us (10%)
  matrix products  61.6 us (8%)
  other arithmetic  54.5 us (7%)
  blocking collectives  15.2 us (2%)
  between operations  15.2 us (2%)
    ppermute x24, waiting for transfers between devices, swap(): lax.ppermute(values, axis, [(i, i ^ bit) for i in range(lax.axis_size(axi...  272 us
    pallas_call x1, Pallas kernels, attend_back(): pl.pallas_call(back_kernel, out_shape=(jax.ShapeDtypeStruct((rows_all, wi...  32.6 us
    unnamed x122, local copies, waits for them, and re-layouts  32.3 us
    ppermute x24, starting transfers between devices, swap(): lax.ppermute(values, axis, [(i, i ^ bit) for i in range(lax.axis_size(axi...  31.5 us
    convert_element_type x12, other arithmetic, scatter_sum(): total = total.astype(jnp.bfloat16)  28.8 us
    pallas_call x1, Pallas kernels, attend(): pl.pallas_call(attend_kernel, out_shape=(jax.ShapeDtypeStruct((rows_all,...  28.8 us
    pallas_call x3, Pallas kernels, weight_blocks(): pl.pallas_call(kernel, out_shape=[jax.ShapeDtypeStruct(shape, jnp.bfloat1...  26.4 us
    ppermute x3, waiting for transfers between devices, line_gather(): lax.ppermute(falling, 'head', [(i + 1, i) for i in range(groups - k)])  21.3 us
  transfers between devices with their start and end apart: 41, of which 14 were waited for; matrix products, arithmetic and copies ran while one was open for 23% of the time, Pallas kernels for 8%

profile of v3, /device:TPU:0, one launch (start us, length us, event | category | flops | bytes accessed | tf_op | source)
XLA Modules:
  0.0 745.5 jit_solution(3116821860071533599)
XLA Ops:
  5.1 2.4 add_convert_fusion.12
  7.5 5.8 collective-permute-start
  14.6 10.4 %collective-permute-done = bf16[1,256,1120]{1,2,0:T(8,128)(2,1)} collective-permute-done((bf16[1,256,1120]{1,2,0:T(8,128)(2,1)}, bf16[1,256,1120]{1,2,0:T(8,128)(2,1)}, u32[]{:S(2)}, u32[]{:S(2)}) %collective-permute-start) | collective-permute-done | bytes 573472 | tf_op jit(solution)/shard_map/ppermute | solution.py:144
  26.5 3.4 collective-permute-done.3
  35.3 11.4 %copy.87 = bf16[1120,3360]{0,1:T(8,128)(2,1)} copy(bf16[1120,3360]{1,0:T(8,128)(2,1)} %param.29) | data formatting | bytes 15052800 | tf_op args[6]
  47.3 3.0 constant_dynamic-slice_fusion.10
  52.0 2.4 collective-permute-start.10
  63.2 17.9 %collective-permute-done.5 = bf16[1,256,1120]{1,2,0:T(8,128)(2,1)S(1)} collective-permute-done((bf16[1,256,1120]{1,2,0:T(8,128)(2,1)}, bf16[1,256,1120]{1,2,0:T(8,128)(2,1)S(1)}, u32[]{:S(2)}, u32[]{:S(2)}) %collective-permute-start.5) | collective-permute-done | bytes 573472 | tf_op jit(solution)/shard_map/ppermute | solution.py:145
  83.5 4.3 copy.86
  88.5 6.4 add_convert_fusion.2.qkv
  94.9 2.4 collective-permute-start.11
  97.4 4.0 collective-permute-start.12
  105.8 7.1 collective-permute-done.11
  112.9 8.0 %collective-permute-done.12 = bf16[1,256,1120]{1,2,0:T(8,128)(2,1)S(1)} collective-permute-done((bf16[1,256,1120]{1,2,0:T(8,128)(2,1)S(1)}, bf16[1,256,1120]{1,2,0:T(8,128)(2,1)S(1)}, u32[]{:S(2)}, u32[]{:S(2)}) %collective-permute-start.12) | collective-permute-done | bytes 573472 | tf_op jit(solution)/shard_map/ppermute | solution.py:139
  122.5 4.2 copy.89
  126.7 5.3 add_convert_fusion.5.kv_other
  132.0 28.8 %attend.1 = (bf16[1024,280]{1,0:T(8,128)(2,1)}, f32[4,280,256]{2,1,0:T(8,128)}, f32[4,5,1,256]{3,2,1,0:T(1,128)}) custom-call(s32[2]{0:T(128)} %pad_add_fusion.info, bf16[1024,840]{1,0:T(8,128)(2,1)} %add_convert_fusion.2.qkv, bf16[1024,560]{1,0:T(8,128)(2,1)} %add_convert_fusion.5.kv_other), custom_call_target="tpu_custom_call" | custom-call | flops 21474836480 | bytes 8388608 | tf_op jit(solution)/shard_map/attend/pallas_call | solution.py:265
  160.8 2.2 copy.91
  163.0 15.2 %all_to_all.25 = bf16[4,1,256,280]{2,3,1,0:T(8,128)(2,1)} all-to-all(bf16[4,1,256,280]{2,3,1,0:T(8,128)(2,1)} %copy.91), channel_id=1, replica_groups=mesh['cell'=4,'head'=4,'ctx'=2] {'head'}, dimensions={0} | all-to-all | bytes 1146880 | tf_op jit(solution)/shard_map/all_to_all | solution.py:486
  178.1 2.2 copy.92
  180.4 2.2 copy.93
  182.6 2.4 fusion.60
  185.8 9.9 %multiply_convert_fusion = (bf16[256,4480]{1,0:T(8,128)(2,1)}, f32[256,4480]{1,0:T(8,128)S(1)}) fusion(f32[4480]{0:T(1024)S(1)} %copy-done.46, bf16[256,1120]{0,1:T(8,128)(2,1)S(1)} %add_convert_fusion.11, bf16[1120,4480]{1,0:T(8,128)(2,1)} %param.36), kind=kOutput, calls=%fused_computation.21 | convolution fusion | flops 2580480000 | bytes 17507840 | tf_op jit(solution)/shard_map/dot_general | solution.py:497
  195.7 10.5 %convert_reduce_fusion = (f32[4480]{0:T(1024)S(1)}, bf16[256,4480]{1,0:T(8,128)(2,1)S(1)}) fusion(f32[256,4480]{1,0:T(8,128)S(1)} %get-tuple-element.105, bf16[4480,1120]{0,1:T(8,128)(2,1)} %param.38, bf16[1,256,1120]{1,2,0:T(8,128)(2,1)S(1)} %copy-done.16), kind=kOutput, calls=%fused_computation.20 | convolution fusion | flops 2594237952 | bytes 17507840 | tf_op jit(solution)/shard_map/nd,fd->nf/dot_general | solution.py:509
  206.3 3.3 multiply_reduce_fusion
  212.0 4.2 all-to-all-start.1
  219.2 3.2 copy.107
  222.4 2.5 gather_fusion.1
  226.8 5.8 weight_blocks.3
  232.6 2.5 gather_fusion.2
  237.0 2.6 copy.108
  239.6 10.3 %weight_blocks.4 = (bf16[2,8,288,560]{3,2,1,0:T(8,128)(2,1)}, bf16[2,8,288,560]{3,2,1,0:T(8,128)(2,1)}) custom-call(s32[8]{0:T(128)} %fusion.45.ids, bf16[1152,256]{1,0:T(8,128)(2,1)} %bitcast.238, bf16[8,256,560]{2,1,0:T(8,128)(2,1)} %bitcast.218), custom_call_target="tpu_custom_call" | custom-call | tf_op jit(solution)/shard_map/weight_blocks/pallas_call | solution.py:116
  250.4 2.2 copy.94
  252.6 32.6 %attend_back.1 = (bf16[1024,280]{1,0:T(8,128)(2,1)}, bf16[1024,560]{1,0:T(8,128)(2,1)}, bf16[1024,560]{1,0:T(8,128)(2,1)}) custom-call(s32[2]{0:T(128)} %pad_add_fusion.info, bf16[1024,840]{1,0:T(8,128)(2,1)} %add_convert_fusion.2.qkv, bf16[1024,560]{1,0:T(8,128)(2,1)} %add_convert_fusion.5.kv_other, bf16[1024,280]{1,0:T(8,128)(2,1)} %bitcast.244, ...), custom_call_target="tpu_custom_call" | custom-call | flops 64424509440 | bytes 8388608 | tf_op jit(solution)/shard_map/attend_back/pallas_call | solution.py:364
  285.2 3.1 fusion.61
  293.6 5.1 convert_element_type.267
  298.8 4.2 dynamic-slice_bitcast_fusion
  303.0 2.5 collective-permute-start.19
  308.8 3.2 copy.109
  312.0 2.6 copy.110
  314.5 10.3 %weight_blocks.5 = (bf16[2,8,144,1120]{3,2,1,0:T(8,128)(2,1)}, bf16[2,8,144,1120]{3,2,1,0:T(8,128)(2,1)}) custom-call(s32[4]{0:T(128)} %get-tuple-element.101.ids, bf16[1152,256]{1,0:T(8,128)(2,1)} %bitcast.237, bf16[4,256,1120]{2,1,0:T(8,128)(2,1)} %bitcast.219), custom_call_target="tpu_custom_call" | custom-call | tf_op jit(solution)/shard_map/weight_blocks/pallas_call | solution.py:116
  339.4 11.2 %collective-permute-start.13 = (bf16[1,1024,560]{1,2,0:T(8,128)(2,1)}, bf16[1,1024,560]{1,2,0:T(8,128)(2,1)}, u32[]{:S(2)}, u32[]{:S(2)}) collective-permute-start(bf16[1,1024,560]{1,2,0:T(8,128)(2,1)} %copy.95), channel_id=1, source_target_pairs={{0,1},{1,0},{2,3},{3,2},{4,5},{5,4},{6,7},{7,6},{8,9},{9,8},{10,11... | collective-permute-start | bytes 3440648 | tf_op jit(solution)/shard_map/ppermute | solution.py:32
  350.6 2.5 fusion.9
  355.6 5.0 all-to-all-start.2
  363.6 31.7 %collective-permute-done.23 = bf16[8,144,280]{2,1,0:T(8,128)(2,1)} collective-permute-done((bf16[8,144,280]{2,1,0:T(8,128)(2,1)}, bf16[8,144,280]{2,1,0:T(8,128)(2,1)}, u32[]{:S(2)}, u32[]{:S(2)}) %collective-permute-start.23) | collective-permute-done | bytes 645152 | tf_op jit(solution)/shard_map/ppermute | solution.py:32
  398.1 2.4 copy.96
  404.1 5.2 all-to-all-start.3
  409.3 8.2 %fusion.16 = bf16[1,256,1120]{1,2,0:T(8,128)(2,1)} fusion(f32[256,1120]{0,1:T(8,128)S(1)} %copy-done.10, bf16[256,4480]{1,0:T(8,128)(2,1)} %get-tuple-element.104, bf16[4480,1120]{0,1:T(8,128)(2,1)} %param.38, f32[1120]{0:T(1024)S(1)} %copy-done.48), kind=kOutput, calls=%fused_computation.42 | convolution fusion | flops 2569871360 | bytes 14053760 | tf_op jit(solution)/shard_map/dot_general | solution.py:499
  419.2 3.0 collective-permute-start.25
  426.1 19.8 %collective-permute-done.25 = bf16[2,144,280]{2,1,0:T(8,128)(2,1)S(1)} collective-permute-done((bf16[2,144,280]{2,1,0:T(8,128)(2,1)S(1)}, bf16[2,144,280]{2,1,0:T(8,128)(2,1)S(1)}, u32[]{:S(2)}, u32[]{:S(2)}) %collective-permute-start.25) | collective-permute-done | bytes 161312 | tf_op jit(solution)/shard_map/ppermute | solution.py:32
  446.2 7.0 fusion.52
  453.1 5.9 fusion
  464.2 5.4 fusion.1
  483.7 4.5 all-to-all-start.4
  488.2 98.4 %collective-permute-done.14 = f32[2,32,280]{2,1,0:T(8,128)S(1)} collective-permute-done((f32[2,32,280]{2,1,0:T(8,128)S(1)}, f32[2,32,280]{2,1,0:T(8,128)S(1)}, u32[]{:S(2)}, u32[]{:S(2)}) %collective-permute-start.14) | collective-permute-done | bytes 71712 | tf_op jit(solution)/shard_map/ppermute | solution.py:32
  586.7 3.6 add_convert_fusion
  593.1 2.4 add_convert_fusion.1
  602.9 53.0 %collective-permute-done.16 = f32[1,32,280]{2,1,0:T(8,128)S(1)} collective-permute-done((f32[1,32,280]{2,1,0:T(8,128)S(1)}, f32[1,32,280]{2,1,0:T(8,128)S(1)}, u32[]{:S(2)}, u32[]{:S(2)}) %collective-permute-start.16) | collective-permute-done | bytes 35872 | tf_op jit(solution)/shard_map/ppermute | solution.py:32
  656.6 4.6 collective-permute-done.17
  671.1 2.4 collective-permute-start.35
  674.8 40.3 %collective-permute-done.30 = bf16[2,288,560]{2,1,0:T(8,128)(2,1)S(1)} collective-permute-done((bf16[2,288,560]{2,1,0:T(8,128)(2,1)S(1)}, bf16[2,288,560]{2,1,0:T(8,128)(2,1)S(1)}, u32[]{:S(2)}, u32[]{:S(2)}) %collective-permute-start.30) | collective-permute-done | bytes 645152 | tf_op jit(solution)/shard_map/ppermute | solution.py:32
  716.6 12.9 %collective-permute-done.35 = bf16[2,144,1120]{2,1,0:T(8,128)(2,1)} collective-permute-done((bf16[2,144,1120]{2,1,0:T(8,128)(2,1)S(1)}, bf16[2,144,1120]{2,1,0:T(8,128)(2,1)}, u32[]{:S(2)}, u32[]{:S(2)}) %collective-permute-start.35) | collective-permute-done | bytes 645152 | tf_op jit(solution)/shard_map/ppermute | solution.py:32
  731.7 5.6 collective-permute-done.31
  738.2 6.1 collective-permute-done.36
  (292 shorter events, 117.4 us)
Async XLA Ops:
  0.6 181.9 %copy-start = (bf16[1120,1120]{1,0:T(8,128)(2,1)S(1)}, bf16[1120,1120]{1,0:T(8,128)(2,1)}, u32[]{:S(2)}) copy-start(bf16[1120,1120]{1,0:T(8,128)(2,1)} %param.32) | copy-start | bytes 7526404
  0.7 33.6 %copy-start.43 = (f32[1120]{0:T(1024)S(1)}, f32[1120]{0:T(1024)}, u32[]{:S(2)}) copy-start(f32[1120]{0:T(1024)} %param.30) | copy-start | bytes 13444
  0.7 33.5 %copy-start.44 = (f32[1120]{0:T(1024)S(1)}, f32[1120]{0:T(1024)}, u32[]{:S(2)}) copy-start(f32[1120]{0:T(1024)} %param.31) | copy-start | bytes 13444
  3.7 56.7 %copy-start.34 = (f32[256]{0:T(256)}, f32[256]{0:T(256)S(1)}, u32[]{:S(2)}) copy-start(f32[256]{0:T(256)S(1)} %broadcast_multiply_fusion.1) | copy-start | bytes 3076
  5.1 29.1 %copy-start.40 = (f32[256]{0:T(256)}, f32[256]{0:T(256)S(1)}, u32[]{:S(2)}) copy-start(f32[256]{0:T(256)S(1)} %multiply_reduce_fusion.5) | copy-start | bytes 3076
  5.1 55.4 %copy-start.38 = (f32[256]{0:T(256)}, f32[256]{0:T(256)S(1)}, u32[]{:S(2)}) copy-start(f32[256]{0:T(256)S(1)} %fusion.36) | copy-start | bytes 3076
  7.5 17.5 %collective-permute-start = (bf16[1,256,1120]{1,2,0:T(8,128)(2,1)}, bf16[1,256,1120]{1,2,0:T(8,128)(2,1)}, u32[]{:S(2)}, u32[]{:S(2)}) collective-permute-start(bf16[1,256,1120]{1,2,0:T(8,128)(2,1)} %add_convert_fusion.12), channel_id=1, source_target_pairs={{0,2},{2,4},{4,6},{1,3},{3,5},{5,7},{8,10},{10,12},{12,14},{9,11},... | collective-permute-start | bytes 1720328 | tf_op jit(solution)/shard_map/ppermute | solution.py:144
  13.3 16.6 %collective-permute-start.3 = (bf16[1,256,1120]{1,2,0:T(8,128)(2,1)}, bf16[1,256,1120]{1,2,0:T(8,128)(2,1)}, u32[]{:S(2)}, u32[]{:S(2)}) collective-permute-start(bf16[1,256,1120]{1,2,0:T(8,128)(2,1)} %add_convert_fusion.12), channel_id=1, source_target_pairs={{2,0},{4,2},{6,4},{3,1},{5,3},{7,5},{10,8},{12,10},{14,12},{11,9},... | collective-permute-start | bytes 1720328 | tf_op jit(solution)/shard_map/ppermute | solution.py:145
  25.0 6.2 collective-permute-start.1
  29.9 24.5 %collective-permute-start.4 = (bf16[1,256,1120]{1,2,0:T(8,128)(2,1)}, bf16[1,256,1120]{1,2,0:T(8,128)(2,1)}, u32[]{:S(2)}, u32[]{:S(2)}) collective-permute-start(bf16[1,256,1120]{1,2,0:T(8,128)(2,1)} %collective-permute-done.3), channel_id=1, source_target_pairs={{2,0},{4,2},{3,1},{5,3},{10,8},{12,10},{11,9},{13,11},{18,16},{20,... | collective-permute-start | bytes 1720328 | tf_op jit(solution)/shard_map/ppermute | solution.py:145
  31.2 24.6 %collective-permute-start.2 = (bf16[1,256,1120]{1,2,0:T(8,128)(2,1)}, bf16[1,256,1120]{1,2,0:T(8,128)(2,1)}, u32[]{:S(2)}, u32[]{:S(2)}) collective-permute-start(bf16[1,256,1120]{1,2,0:T(8,128)(2,1)} %collective-permute-done.1), channel_id=1, source_target_pairs={{4,6},{5,7},{12,14},{13,15},{20,22},{21,23},{28,30},{29,31}} | collective-permute-start | bytes 1720328 | tf_op jit(solution)/shard_map/ppermute | solution.py:144
  32.7 70.9 %collective-permute-start.9 = (bf16[1,256,1120]{1,2,0:T(8,128)(2,1)}, bf16[1,256,1120]{1,2,0:T(8,128)(2,1)}, u32[]{:S(2)}, u32[]{:S(2)}) collective-permute-start(bf16[1,256,1120]{1,2,0:T(8,128)(2,1)} %add_convert_fusion.12), channel_id=1, source_target_pairs={{0,1},{1,0},{2,3},{3,2},{4,5},{5,4},{6,7},{7,6},{8,9},{9,8},{10,11... | collective-permute-start | bytes 1720328 | tf_op jit(solution)/shard_map/ppermute | solution.py:139
  50.3 10.2 %copy-start.4 = (bf16[1,256,1120]{1,2,0:T(8,128)(2,1)S(1)}, bf16[1,256,1120]{1,2,0:T(8,128)(2,1)}, u32[]{:S(2)}) copy-start(bf16[1,256,1120]{1,2,0:T(8,128)(2,1)} %param.23) | copy-start | bytes 1720324
  50.3 10.2 %copy-start.32 = (f32[1120]{0:T(1024)S(1)}, f32[1120]{0:T(1024)}, u32[]{:S(2)}) copy-start(f32[1120]{0:T(1024)} %param.27) | copy-start | bytes 13444
  50.3 10.2 %copy-start.36 = (f32[1120]{0:T(1024)S(1)}, f32[1120]{0:T(1024)}, u32[]{:S(2)}) copy-start(f32[1120]{0:T(1024)} %param.28) | copy-start | bytes 13444
  50.3 52.1 %collective-permute-start.8 = (bf16[1,256,1120]{1,2,0:T(8,128)(2,1)}, bf16[1,256,1120]{1,2,0:T(8,128)(2,1)}, u32[]{:S(2)}, u32[]{:S(2)}) collective-permute-start(bf16[1,256,1120]{1,2,0:T(8,128)(2,1)} %collective-permute-done), channel_id=1, source_target_pairs={{2,3},{3,2},{4,5},{5,4},{6,7},{7,6},{10,11},{11,10},{12,13},{13,12... | collective-permute-start | bytes 1720328 | tf_op jit(solution)/shard_map/ppermute | solution.py:139
  52.0 52.7 %collective-permute-start.10 = (bf16[1,256,1120]{1,2,0:T(8,128)(2,1)}, bf16[1,256,1120]{1,2,0:T(8,128)(2,1)}, u32[]{:S(2)}, u32[]{:S(2)}) collective-permute-start(bf16[1,256,1120]{1,2,0:T(8,128)(2,1)} %collective-permute-done.3), channel_id=1, source_target_pairs={{0,1},{1,0},{2,3},{3,2},{4,5},{5,4},{8,9},{9,8},{10,11},{11,10},{1... | collective-permute-start | bytes 1720328 | tf_op jit(solution)/shard_map/ppermute | solution.py:139
  54.4 43.0 %collective-permute-start.7 = (bf16[1,256,1120]{1,2,0:T(8,128)(2,1)}, bf16[1,256,1120]{1,2,0:T(8,128)(2,1)}, u32[]{:S(2)}, u32[]{:S(2)}) collective-permute-start(bf16[1,256,1120]{1,2,0:T(8,128)(2,1)} %collective-permute-done.1), channel_id=1, source_target_pairs={{4,5},{5,4},{6,7},{7,6},{12,13},{13,12},{14,15},{15,14},{20,21},{2... | collective-permute-start | bytes 1720328 | tf_op jit(solution)/shard_map/ppermute | solution.py:139
  55.9 25.2 %collective-permute-start.5 = (bf16[1,256,1120]{1,2,0:T(8,128)(2,1)}, bf16[1,256,1120]{1,2,0:T(8,128)(2,1)S(1)}, u32[]{:S(2)}, u32[]{:S(2)}) collective-permute-start(bf16[1,256,1120]{1,2,0:T(8,128)(2,1)} %collective-permute-done.4), channel_id=1, source_target_pairs={{2,0},{3,1},{10,8},{11,9},{18,16},{19,17},{26,24},{27,25}} | collective-permute-start | bytes 1720328 | tf_op jit(solution)/shard_map/ppermute | solution.py:145
  87.8 7.1 collective-permute-start.6
  94.9 17.9 %collective-permute-start.11 = (bf16[1,256,1120]{1,2,0:T(8,128)(2,1)}, bf16[1,256,1120]{1,2,0:T(8,128)(2,1)S(1)}, u32[]{:S(2)}, u32[]{:S(2)}) collective-permute-start(bf16[1,256,1120]{1,2,0:T(8,128)(2,1)} %collective-permute-done.4), channel_id=1, source_target_pairs={{0,1},{1,0},{2,3},{3,2},{8,9},{9,8},{10,11},{11,10},{16,17},{17,16... | collective-permute-start | bytes 1720328 | tf_op jit(solution)/shard_map/ppermute | solution.py:139
  97.4 23.5 %collective-permute-start.12 = (bf16[1,256,1120]{1,2,0:T(8,128)(2,1)S(1)}, bf16[1,256,1120]{1,2,0:T(8,128)(2,1)S(1)}, u32[]{:S(2)}, u32[]{:S(2)}) collective-permute-start(bf16[1,256,1120]{1,2,0:T(8,128)(2,1)S(1)} %copy-done.31), channel_id=1, source_target_pairs={{0,1},{1,0},{8,9},{9,8},{16,17},{17,16},{24,25},{25,24}} | collective-permute-start | bytes 1720328 | tf_op jit(solution)/shard_map/ppermute | solution.py:139
  163.0 19.6 %copy-start.47 = (f32[1120]{0:T(1024)S(1)}, f32[1120]{0:T(1024)}, u32[]{:S(2)}) copy-start(f32[1120]{0:T(1024)} %param.33) | copy-start | bytes 13444
  185.0 24.6 %copy-start.9 = (f32[256,1120]{0,1:T(8,128)}, f32[256,1120]{0,1:T(8,128)S(1)}, u32[]{:S(2)}) copy-start(f32[256,1120]{0,1:T(8,128)S(1)} %get-tuple-element.103) | copy-start | bytes 3440644
  185.8 9.9 %copy-start.24 = (bf16[256,1120]{0,1:T(8,128)(2,1)}, bf16[256,1120]{0,1:T(8,128)(2,1)S(1)}, u32[]{:S(2)}) copy-start(bf16[256,1120]{0,1:T(8,128)(2,1)S(1)} %add_convert_fusion.11) | copy-start | bytes 1720324
  185.8 9.9 %copy-start.16 = (bf16[1,256,1120]{1,2,0:T(8,128)(2,1)S(1)}, bf16[1,256,1120]{1,2,0:T(8,128)(2,1)}, u32[]{:S(2)}) copy-start(bf16[1,256,1120]{1,2,0:T(8,128)(2,1)} %param.40) | copy-start | bytes 1720324
  185.8 20.5 %slice-start.2 = ((s8[10035200]{0:T(1024)(128)(4,1)}), s8[4194304]{0:T(1024)(128)(4,1)S(1)}, s32[]{:S(2)}) async-start(s8[10035200]{0:T(1024)(128)(4,1)} %bitcast.249), calls=%async_computation.7 | async-start | bytes 8388608
  185.8 20.5 %slice-start.3 = ((s8[10035200]{0:T(1024)(128)(4,1)}), s8[4194304]{0:T(1024)(128)(4,1)S(1)}, s32[]{:S(2)}) async-start(s8[10035200]{0:T(1024)(128)(4,1)} %bitcast.249), calls=%async_computation.8 | async-start | bytes 8388608
  195.7 10.6 %slice-start.4 = ((s8[10035200]{0:T(1024)(128)(4,1)}), s8[1646592]{0:T(1024)(128)(4,1)S(1)}, s32[]{:S(2)}) async-start(s8[10035200]{0:T(1024)(128)(4,1)} %bitcast.249), calls=%async_computation.9 | async-start | bytes 3293184
  212.0 38.4 %all-to-all-start.1 = ((bf16[4,1,256,280]{2,3,1,0:T(8,128)(2,1)}), bf16[4,1,256,280]{2,3,1,0:T(8,128)(2,1)}, u32[]{:S(2)}, u32[]{:S(2)}) async-start(bf16[4,1,256,280]{2,3,1,0:T(8,128)(2,1)} %bitcast.246), calls=%async_computation.1 | async-start | bytes 1146880 | tf_op jit(solution)/shard_map/all_to_all | solution.py:480
  232.6 118.0 %collective-permute-start.22 = (bf16[16,144,280]{2,1,0:T(8,128)(2,1)}, bf16[16,144,280]{2,1,0:T(8,128)(2,1)}, u32[]{:S(2)}, u32[]{:S(2)}) collective-permute-start(bf16[16,144,280]{2,1,0:T(8,128)(2,1)} %bitcast.253), channel_id=1, source_target_pairs={{0,8},{8,0},{16,24},{24,16},{1,9},{9,1},{17,25},{25,17},{2,10},{10... | collective-permute-start | bytes 3870728 | tf_op jit(solution)/shard_map/ppermute | solution.py:32
  249.9 203.3 %collective-permute-start.27 = (bf16[16,288,560]{2,1,0:T(8,128)(2,1)}, bf16[16,288,560]{2,1,0:T(8,128)(2,1)}, u32[]{:S(2)}, u32[]{:S(2)}) collective-permute-start(bf16[16,288,560]{2,1,0:T(8,128)(2,1)} %bitcast.251), channel_id=1, source_target_pairs={{0,8},{8,0},{16,24},{24,16},{1,9},{9,1},{17,25},{25,17},{2,10},{10... | collective-permute-start | bytes 15482888 | tf_op jit(solution)/shard_map/ppermute | solution.py:32
  252.6 32.6 %copy-start.21 = (bf16[4,1,256,1120]{3,2,0,1:T(8,128)(2,1)S(1)}, bf16[4,1,256,1120]{3,2,0,1:T(8,128)(2,1)}, u32[]{:S(2)}) copy-start(bf16[4,1,256,1120]{3,2,0,1:T(8,128)(2,1)} %copy.86) | copy-start | bytes 6881284
  303.0 57.6 %collective-permute-start.19 = (bf16[2,6,280,140]{2,0,3,1:T(2,128)(2,1)}, bf16[2,6,280,140]{2,0,3,1:T(2,128)(2,1)}, u32[]{:S(2)}, u32[]{:S(2)}) collective-permute-start(bf16[2,6,280,140]{2,0,3,1:T(2,128)(2,1)} %get-tuple-element.81), channel_id=1, source_target_pairs={{0,16},{8,24},{16,0},{24,8},{1,17},{9,25},{17,1},{25,9},{2,18},{10... | collective-permute-start | bytes 2822408 | tf_op jit(solution)/shard_map/ppermute | solution.py:32
  314.5 23.4 %copy-start.27 = (bf16[1024,560]{1,0:T(8,128)(2,1)S(1)}, bf16[1024,560]{1,0:T(8,128)(2,1)}, u32[]{:S(2)}) copy-start(bf16[1024,560]{1,0:T(8,128)(2,1)} %get-tuple-element.34) | copy-start | bytes 3440644
  324.8 139.4 %collective-permute-start.32 = (bf16[16,144,1120]{2,1,0:T(8,128)(2,1)}, bf16[16,144,1120]{2,1,0:T(8,128)(2,1)}, u32[]{:S(2)}, u32[]{:S(2)}) collective-permute-start(bf16[16,144,1120]{2,1,0:T(8,128)(2,1)} %bitcast.252), channel_id=1, source_target_pairs={{0,8},{8,0},{16,24},{24,16},{1,9},{9,1},{17,25},{25,17},{2,10},{10... | collective-permute-start | bytes 15482888 | tf_op jit(solution)/shard_map/ppermute | solution.py:32
  339.4 58.7 %collective-permute-start.13 = (bf16[1,1024,560]{1,2,0:T(8,128)(2,1)}, bf16[1,1024,560]{1,2,0:T(8,128)(2,1)}, u32[]{:S(2)}, u32[]{:S(2)}) collective-permute-start(bf16[1,1024,560]{1,2,0:T(8,128)(2,1)} %copy.95), channel_id=1, source_target_pairs={{0,1},{1,0},{2,3},{3,2},{4,5},{5,4},{6,7},{7,6},{8,9},{9,8},{10,11... | collective-permute-start | bytes 3440648 | tf_op jit(solution)/shard_map/ppermute | solution.py:32
  354.1 41.2 %collective-permute-start.23 = (bf16[8,144,280]{2,1,0:T(8,128)(2,1)}, bf16[8,144,280]{2,1,0:T(8,128)(2,1)}, u32[]{:S(2)}, u32[]{:S(2)}) collective-permute-start(bf16[8,144,280]{2,1,0:T(8,128)(2,1)} %slice.247), channel_id=1, source_target_pairs={{0,1},{1,0},{2,3},{3,2},{4,5},{5,4},{6,7},{7,6},{8,9},{9,8},{10,11... | collective-permute-start | bytes 1935368 | tf_op jit(solution)/shard_map/ppermute | solution.py:32
  355.6 46.9 %all-to-all-start.2 = ((bf16[4,1,256,280]{2,3,1,0:T(8,128)(2,1)}), bf16[4,1,256,280]{2,3,1,0:T(8,128)(2,1)}, u32[]{:S(2)}, u32[]{:S(2)}) async-start(bf16[4,1,256,280]{2,3,1,0:T(8,128)(2,1)} %copy.97), calls=%async_computation.2 | async-start | bytes 1146880 | tf_op jit(solution)/shard_map/all_to_all | solution.py:486
  362.5 34.2 %copy-start.12 = (bf16[2,6,280,140]{2,3,1,0:T(8,128)(2,1)}, bf16[2,6,280,140]{2,3,1,0:T(8,128)(2,1)S(1)}, u32[]{:S(2)}) copy-start(bf16[2,6,280,140]{2,3,1,0:T(8,128)(2,1)S(1)} %fusion.13) | copy-start | bytes 2822404
  363.6 58.7 %collective-permute-start.20 = (bf16[1,6,280,140]{2,3,1,0:T(8,128)(2,1)}, bf16[1,6,280,140]{2,3,1,0:T(8,128)(2,1)}, u32[]{:S(2)}, u32[]{:S(2)}) collective-permute-start(bf16[1,6,280,140]{2,3,1,0:T(8,128)(2,1)} %constant_dynamic-slice_fusion.5), channel_id=1, source_target_pairs={{0,8},{8,0},{16,24},{24,16},{1,9},{9,1},{17,25},{25,17},{2,10},{10... | collective-permute-start | bytes 1411208 | tf_op jit(solution)/shard_map/ppermute | solution.py:32
  397.8 20.1 %collective-permute-start.24 = (bf16[4,144,280]{2,1,0:T(8,128)(2,1)}, bf16[4,144,280]{2,1,0:T(8,128)(2,1)}, u32[]{:S(2)}, u32[]{:S(2)}) collective-permute-start(bf16[4,144,280]{2,1,0:T(8,128)(2,1)} %slice.249), channel_id=1, source_target_pairs={{0,16},{8,24},{16,0},{24,8},{1,17},{9,25},{17,1},{25,9},{2,18},{10... | collective-permute-start | bytes 967688 | tf_op jit(solution)/shard_map/ppermute | solution.py:32
  404.1 42.0 %all-to-all-start.3 = ((bf16[4,1,256,560]{2,3,1,0:T(8,128)(2,1)}), bf16[4,1,256,560]{2,3,1,0:T(8,128)(2,1)S(1)}, u32[]{:S(2)}, u32[]{:S(2)}) async-start(bf16[4,1,256,560]{2,3,1,0:T(8,128)(2,1)} %copy.98), calls=%async_computation.3 | async-start | bytes 2293760 | tf_op jit(solution)/shard_map/all_to_all | solution.py:486
  419.2 26.7 %collective-permute-start.25 = (bf16[2,144,280]{2,1,0:T(8,128)(2,1)S(1)}, bf16[2,144,280]{2,1,0:T(8,128)(2,1)S(1)}, u32[]{:S(2)}, u32[]{:S(2)}) collective-permute-start(bf16[2,144,280]{2,1,0:T(8,128)(2,1)S(1)} %slice.251), channel_id=1, source_target_pairs={{0,4},{2,6},{4,0},{6,2},{1,5},{3,7},{5,1},{7,3},{8,12},{10,14},{12... | collective-permute-start | bytes 483848 | tf_op jit(solution)/shard_map/ppermute | solution.py:32
  424.3 21.8 %copy-start.33 = (f32[1120]{0:T(1024)S(1)}, f32[1120]{0:T(1024)}, u32[]{:S(2)}) copy-start(f32[1120]{0:T(1024)} %param.27) | copy-start | bytes 13444
  424.3 21.9 %copy-start.35 = (f32[256]{0:T(256)S(1)}, f32[256]{0:T(256)}, u32[]{:S(2)}) copy-start(f32[256]{0:T(256)} %copy-done.34) | copy-start | bytes 3076
  424.3 55.6 %collective-permute-start.21 = (bf16[1,6,280,140]{2,3,1,0:T(8,128)(2,1)}, bf16[1,6,280,140]{2,3,1,0:T(8,128)(2,1)}, u32[]{:S(2)}, u32[]{:S(2)}) collective-permute-start(bf16[1,6,280,140]{2,3,1,0:T(8,128)(2,1)} %add_convert_fusion.10), channel_id=1, source_target_pairs={{0,1},{1,0},{2,3},{3,2},{4,5},{5,4},{6,7},{7,6},{8,9},{9,8},{10,11... | collective-permute-start | bytes 1411208 | tf_op jit(solution)/shard_map/ppermute | solution.py:32
  446.0 152.8 %collective-permute-start.26 = (bf16[1,144,280]{2,1,0:T(8,128)(2,1)S(1)}, bf16[1,144,280]{2,1,0:T(8,128)(2,1)S(1)}, u32[]{:S(2)}, u32[]{:S(2)}) collective-permute-start(bf16[1,144,280]{2,1,0:T(8,128)(2,1)S(1)} %get-tuple-element.91), channel_id=1, source_target_pairs={{0,2},{2,0},{4,6},{6,4},{1,3},{3,1},{5,7},{7,5},{8,10},{10,8},{12,... | collective-permute-start | bytes 241928 | tf_op jit(solution)/shard_map/ppermute | solution.py:32
  462.5 124.2 %collective-permute-start.28 = (bf16[8,288,560]{2,1,0:T(8,128)(2,1)}, bf16[8,288,560]{2,1,0:T(8,128)(2,1)}, u32[]{:S(2)}, u32[]{:S(2)}) collective-permute-start(bf16[8,288,560]{2,1,0:T(8,128)(2,1)} %slice.260), channel_id=1, source_target_pairs={{0,16},{8,24},{16,0},{24,8},{1,17},{9,25},{17,1},{25,9},{2,18},{10... | collective-permute-start | bytes 7741448 | tf_op jit(solution)/shard_map/ppermute | solution.py:32
  472.8 120.2 %collective-permute-start.33 = (bf16[8,144,1120]{2,1,0:T(8,128)(2,1)}, bf16[8,144,1120]{2,1,0:T(8,128)(2,1)}, u32[]{:S(2)}, u32[]{:S(2)}) collective-permute-start(bf16[8,144,1120]{2,1,0:T(8,128)(2,1)} %slice.271), channel_id=1, source_target_pairs={{0,16},{8,24},{16,0},{24,8},{1,17},{9,25},{17,1},{25,9},{2,18},{10... | collective-permute-start | bytes 7741448 | tf_op jit(solution)/shard_map/ppermute | solution.py:32
  478.7 107.9 %collective-permute-start.14 = (f32[2,32,280]{2,1,0:T(8,128)S(1)}, f32[2,32,280]{2,1,0:T(8,128)S(1)}, u32[]{:S(2)}, u32[]{:S(2)}) collective-permute-start(f32[2,32,280]{2,1,0:T(8,128)S(1)} %constant_dynamic-slice_fusion.8), channel_id=1, source_target_pairs={{0,16},{8,24},{16,0},{24,8},{1,17},{9,25},{17,1},{25,9},{2,18},{10... | collective-permute-start | bytes 215048 | tf_op jit(solution)/shard_map/ppermute | solution.py:32
  483.7 117.4 %all-to-all-start.4 = ((bf16[4,2,280,140]{2,1,3,0:T(2,128)(2,1)}), bf16[4,2,280,140]{2,1,3,0:T(2,128)(2,1)}, u32[]{:S(2)}, u32[]{:S(2)}) async-start(bf16[4,2,280,140]{2,1,3,0:T(2,128)(2,1)} %copy.103), calls=%async_computation.4 | async-start | bytes 1720320 | tf_op jit(solution)/shard_map/all_to_all | solution.py:574
  586.7 12.9 %collective-permute-start.15 = (f32[1,32,280]{2,1,0:T(8,128)S(1)}, f32[1,32,280]{2,1,0:T(8,128)S(1)}, u32[]{:S(2)}, u32[]{:S(2)}) collective-permute-start(f32[1,32,280]{2,1,0:T(8,128)S(1)} %constant_dynamic-slice_fusion.7), channel_id=1, source_target_pairs={{0,8},{8,0},{16,24},{24,16},{1,9},{9,1},{17,25},{25,17},{2,10},{10... | collective-permute-start | bytes 107528 | tf_op jit(solution)/shard_map/ppermute | solution.py:32
  591.6 74.2 %collective-permute-start.29 = (bf16[4,288,560]{2,1,0:T(8,128)(2,1)}, bf16[4,288,560]{2,1,0:T(8,128)(2,1)}, u32[]{:S(2)}, u32[]{:S(2)}) collective-permute-start(bf16[4,288,560]{2,1,0:T(8,128)(2,1)} %slice.262), channel_id=1, source_target_pairs={{0,1},{1,0},{2,3},{3,2},{4,5},{5,4},{6,7},{7,6},{8,9},{9,8},{10,11... | collective-permute-start | bytes 3870728 | tf_op jit(solution)/shard_map/ppermute | solution.py:32
  598.3 70.1 %collective-permute-start.34 = (bf16[4,144,1120]{2,1,0:T(8,128)(2,1)}, bf16[4,144,1120]{2,1,0:T(8,128)(2,1)}, u32[]{:S(2)}, u32[]{:S(2)}) collective-permute-start(bf16[4,144,1120]{2,1,0:T(8,128)(2,1)} %slice.273), channel_id=1, source_target_pairs={{0,1},{1,0},{2,3},{3,2},{4,5},{5,4},{6,7},{7,6},{8,9},{9,8},{10,11... | collective-permute-start | bytes 3870728 | tf_op jit(solution)/shard_map/ppermute | solution.py:32
  599.5 56.3 %collective-permute-start.16 = (f32[1,32,280]{2,1,0:T(8,128)S(1)}, f32[1,32,280]{2,1,0:T(8,128)S(1)}, u32[]{:S(2)}, u32[]{:S(2)}) collective-permute-start(f32[1,32,280]{2,1,0:T(8,128)S(1)} %dynamic-slice_add_fusion.1), channel_id=1, source_target_pairs={{0,1},{1,0},{2,3},{3,2},{4,5},{5,4},{6,7},{7,6},{8,9},{9,8},{10,11... | collective-permute-start | bytes 107528 | tf_op jit(solution)/shard_map/ppermute | solution.py:32
  655.9 5.4 collective-permute-start.17
  661.2 4.5 collective-permute-start.18
  667.8 47.4 %collective-permute-start.30 = (bf16[2,288,560]{2,1,0:T(8,128)(2,1)S(1)}, bf16[2,288,560]{2,1,0:T(8,128)(2,1)S(1)}, u32[]{:S(2)}, u32[]{:S(2)}) collective-permute-start(bf16[2,288,560]{2,1,0:T(8,128)(2,1)S(1)} %slice.264), channel_id=1, source_target_pairs={{0,4},{2,6},{4,0},{6,2},{1,5},{3,7},{5,1},{7,3},{8,12},{10,14},{12... | collective-permute-start | bytes 1935368 | tf_op jit(solution)/shard_map/ppermute | solution.py:32
  671.1 58.4 %collective-permute-start.35 = (bf16[2,144,1120]{2,1,0:T(8,128)(2,1)S(1)}, bf16[2,144,1120]{2,1,0:T(8,128)(2,1)}, u32[]{:S(2)}, u32[]{:S(2)}) collective-permute-start(bf16[2,144,1120]{2,1,0:T(8,128)(2,1)S(1)} %slice.275), channel_id=1, source_target_pairs={{0,4},{2,6},{4,0},{6,2},{1,5},{3,7},{5,1},{7,3},{8,12},{10,14},{12... | collective-permute-start | bytes 1935368 | tf_op jit(solution)/shard_map/ppermute | solution.py:32
  674.8 54.7 %copy-start.15 = (bf16[4,144,1120]{2,1,0:T(8,128)(2,1)S(1)}, bf16[4,144,1120]{2,1,0:T(8,128)(2,1)}, u32[]{:S(2)}) copy-start(bf16[4,144,1120]{2,1,0:T(8,128)(2,1)} %copy-done.14) | copy-start | bytes 3870724
  716.5 20.8 %collective-permute-start.31 = (bf16[1,288,560]{2,1,0:T(8,128)(2,1)S(1)}, bf16[1,288,560]{2,1,0:T(8,128)(2,1)S(1)}, u32[]{:S(2)}, u32[]{:S(2)}) collective-permute-start(bf16[1,288,560]{2,1,0:T(8,128)(2,1)S(1)} %get-tuple-element.87), channel_id=1, source_target_pairs={{0,2},{2,0},{4,6},{6,4},{1,3},{3,1},{5,7},{7,5},{8,10},{10,8},{12,... | collective-permute-start | bytes 967688 | tf_op jit(solution)/shard_map/ppermute | solution.py:32
  729.5 15.7 %copy-start.1 = (bf16[1120,1120]{1,0:T(8,128)(2,1)S(1)}, bf16[1120,1120]{1,0:T(8,128)(2,1)}, u32[]{:S(2)}) copy-start(bf16[1120,1120]{1,0:T(8,128)(2,1)} %param.32) | copy-start | bytes 7526404
  731.0 13.3 %collective-permute-start.36 = (bf16[1,144,1120]{2,1,0:T(8,128)(2,1)S(1)}, bf16[1,144,1120]{2,1,0:T(8,128)(2,1)S(1)}, u32[]{:S(2)}, u32[]{:S(2)}) collective-permute-start(bf16[1,144,1120]{2,1,0:T(8,128)(2,1)S(1)} %get-tuple-element.89), channel_id=1, source_target_pairs={{0,2},{2,0},{4,6},{6,4},{1,3},{3,1},{5,7},{7,5},{8,10},{10,8},{12,... | collective-permute-start | bytes 967688 | tf_op jit(solution)/shard_map/ppermute | solution.py:32
  (31 other events, 104.1 us)

commit v4 on v2

--- a/solution.py
+++ b/solution.py
@@ -48,54 +48,98 @@
     return lax.dot_general(a, b, (((1,), (1,)), ((), ())), preferred_element_type=jnp.float32)
 
 
-def weight_blocks(left, right, by_cell_left, y_first):
+def relative_order(count, axis_bits):
+    rel = np.zeros((count,), np.int32)
+    for s, bit in enumerate(axis_bits):
+        rel += ((np.arange(count) >> (len(axis_bits) - 1 - s)) & 1).astype(np.int32) * bit
+    return jnp.asarray(rel)
+
+
+def weight_blocks(pairs, by_cell_left):
     cells, groups, halves = lax.axis_size("cell"), lax.axis_size("head"), lax.axis_size("ctx")
     parts, half_cells = groups * halves, cells // 2
-    steps = bits_of("cell")
-    rel = np.zeros((cells,), np.int32)
-    for s, (_, bit) in enumerate(steps):
-        rel += ((np.arange(cells) >> (len(steps) - 1 - s)) & 1).astype(np.int32) * bit
-    cell_ids = jnp.asarray(rel) ^ lax.axis_index("cell")
+    cell_ids = relative_order(cells, [b for _, b in bits_of("cell")]) ^ lax.axis_index("cell")
     places = jnp.arange(parts, dtype=jnp.int32)
     part_ids = ((places % groups) ^ lax.axis_index("head")) * halves + (
         (places // groups) ^ lax.axis_index("ctx")
     )
-    rows, cols = left.shape[1], right.shape[2]
-
-    def kernel(ci, pi, left_ref, right_ref, kept, sent):
-        part = pi[pl.program_id(0)]
-        for n in range(cells):
-            cell = ci[n]
-            out, at = (kept, n) if n < half_cells else (sent, n - half_cells)
+    left_ids, right_ids = (cell_ids, part_ids) if by_cell_left else (part_ids, cell_ids)
+    left_count, right_count = (cells, parts) if by_cell_left else (parts, cells)
+    tokens = pairs[0][0].shape[0]
+    left_rows = pairs[0][0].shape[1] // left_count
+    rows = left_rows + -left_rows % 16
+    widths = [right.shape[1] // right_count for _, right in pairs]
+    cols = sum(widths)
+    count = len(pairs)
+
+    def kernel(left_at, right_at, *refs):
+        sources, (kept, sent), scratch = refs[: 2 * count], refs[2 * count : 2 * count + 2], refs[2 * count + 2 :]
+        step = pl.program_id(0)
+
+        @pl.when(step == 0)
+        def _():
+            turned = scratch[-1]
+            turned[...] = jnp.zeros_like(turned)
+            for p in range(count):
+                left_t = sources[2 * p][...].astype(jnp.float32).T.astype(jnp.bfloat16)
+                for n in range(left_count):
+                    turned[n, :left_rows] = left_t[n * left_rows : (n + 1) * left_rows]
+                for n in range(left_count):
+                    scratch[2 * p][n * rows : (n + 1) * rows, :] = turned[left_at[n]]
+                width = widths[p]
+                for n in range(right_count):
+                    scratch[2 * p + 1][n] = sources[2 * p + 1][:, n * width : (n + 1) * width]
+
+        index = step if by_cell_left else (step + half_cells) % cells
+        offset = 0
+        for p in range(count):
+            block = nn(scratch[2 * p][...], scratch[2 * p + 1][right_at[index]])
+            at = slice(offset, offset + widths[p])
+            offset += widths[p]
             if by_cell_left:
-                block = nn(left_ref[cell], right_ref[part])
+                for n in range(cells):
+                    out, place = (kept, n) if n < half_cells else (sent, n - half_cells)
+                    out[place, 0, :, at] = block[n * rows : (n + 1) * rows].astype(jnp.bfloat16)
             else:
-                block = nn(left_ref[part], right_ref[cell])
-            if y_first:
-                out[0, at, 0] = block.astype(jnp.bfloat16)
-            else:
-                out[at, 0] = block.astype(jnp.bfloat16)
-
-    if y_first:
-        shape = (halves, half_cells, groups, rows, cols)
-        spec = pl.BlockSpec(
-            (1, half_cells, 1, rows, cols), lambda i, ci, pi: (i // groups, 0, i % groups, 0, 0)
-        )
+
+                def fill(out, block=block, at=at):
+                    for n in range(parts):
+                        out[0, n, :, at] = block[n * rows : (n + 1) * rows].astype(jnp.bfloat16)
+
+                pl.when(step < half_cells)(lambda: fill(sent))
+                pl.when(step >= half_cells)(lambda: fill(kept))
+
+    last = half_cells - 1
+    shape = (half_cells, parts, rows, cols)
+    if by_cell_left:
+        specs = [pl.BlockSpec((half_cells, 1, rows, cols), lambda i, a, b: (0, i, 0, 0))] * 2
     else:
-        shape = (half_cells, parts, rows, cols)
-        spec = pl.BlockSpec((half_cells, 1, rows, cols), lambda i, ci, pi: (0, i, 0, 0))
-    whole = [
-        pl.BlockSpec(x.shape, lambda i, ci, pi: (0, 0, 0), pipeline_mode=pl.Buffered(1))
-        for x in (left, right)
-    ]
+        block_shape = (1, parts, rows, cols)
+        specs = [
+            pl.BlockSpec(block_shape, lambda i, a, b: (jnp.maximum(i - last - 1, 0), 0, 0, 0)),
+            pl.BlockSpec(block_shape, lambda i, a, b: (jnp.minimum(i, last), 0, 0, 0)),
+        ]
+    scratch = []
+    for width in widths:
+        scratch.append(pltpu.VMEM((left_count * rows, tokens), jnp.bfloat16))
+        scratch.append(pltpu.VMEM((right_count, tokens, width), jnp.bfloat16))
+    scratch.append(pltpu.VMEM((left_count, rows, tokens), jnp.bfloat16))
+    flat = [x for pair in pairs for x in pair]
     kept, sent = pl.pallas_call(
         kernel,
         out_shape=[jax.ShapeDtypeStruct(shape, jnp.bfloat16)] * 2,
         grid_spec=pltpu.PrefetchScalarGridSpec(
-            num_scalar_prefetch=2, grid=(parts,), in_specs=whole, out_specs=[spec, spec]
+            num_scalar_prefetch=2,
+            grid=(right_count,),
+            in_specs=[
+                pl.BlockSpec(x.shape, lambda i, a, b: (0, 0), pipeline_mode=pl.Buffered(1))
+                for x in flat
+            ],
+            out_specs=specs,
+            scratch_shapes=scratch,
         ),
         name="weight_blocks",
-    )(cell_ids, part_ids, left, right)
+    )(left_ids, right_ids, *flat)
     return kept.reshape(-1, rows, cols), sent.reshape(-1, rows, cols)
 
 
@@ -334,14 +378,6 @@
     )(info, qkv, kv_other, grad, out_t, logs)
 
 
-def column_blocks(values, count):
-    return values.reshape(values.shape[0], count, -1).transpose(1, 0, 2)
-
-
-def row_blocks(values, count):
-    return values.reshape(values.shape[0], count, -1).transpose(1, 2, 0)
-
-
 def head_columns(groups, halves, sections, units):
     local, owned = units // groups, sections * units // (groups * halves)
     send = [[[[] for _ in range(groups)] for _ in range(halves)] for _ in range(groups)]
@@ -394,7 +430,6 @@
     ctx_rows = groups * row_count
     cell_steps, ctx_steps, head_steps = bits_of("cell"), bits_of("ctx"), bits_of("head")[::-1]
     steps_x = cell_steps + ctx_steps + head_steps
-    steps_y = cell_steps[:1] + ctx_steps + cell_steps[1:] + head_steps
     one_hot = (
         dataset_ids[:, None] == jnp.arange(dataset_table.shape[0], dtype=jnp.int32)[None, :]
     ).astype(jnp.bfloat16)
@@ -404,6 +439,7 @@
     mixed_qkv = jnp.dot(normed, qkv_weight, preferred_element_type=jnp.float32)
     bias_row = jnp.concatenate([query_bias, jnp.zeros_like(query_bias), value_bias])
     mixed_qkv = (mixed_qkv + bias_row).astype(jnp.bfloat16)
+    head_index = lax.axis_index("head")
 
     def to_heads(values):
         sections = values.shape[1] // model_width
@@ -437,11 +473,9 @@
     branch = jnp.dot(active, proj_weight, preferred_element_type=jnp.float32) + proj_bias
     block_out = (middle + branch).astype(jnp.bfloat16).reshape(cell_count, row_count, model_width)
     grad_low = cotangent.reshape(token_count, model_width)
-    proj_kept, proj_sent = weight_blocks(
-        row_blocks(grad_low, parts), column_blocks(active, cells), False, False
-    )
-    grad_low, proj_kept, proj_sent = lax.optimization_barrier((grad_low, proj_kept, proj_sent))
-    proj_weight_grad = scatter_sum(proj_kept, proj_sent, steps_x).T
+    proj_kept, proj_sent = weight_blocks([(grad_low, active)], False)
+    part_columns = model_width // parts
+    proj_weight_grad = scatter_sum(proj_kept, proj_sent, steps_x)[:part_columns].T
     grad_top = grad_low.astype(jnp.float32)
     proj_bias_grad = jnp.sum(grad_top, axis=0)
     active_grad = jnp.einsum("nd,fd->nf", grad_low, proj_weight, preferred_element_type=jnp.float32)
@@ -461,17 +495,11 @@
     ).astype(jnp.bfloat16)
     grad_heads = to_heads(attended_grad)
 
-    fc_kept, fc_sent = weight_blocks(
-        row_blocks(mlp_normed, cells), column_blocks(hidden_grad, parts), True, False
-    )
-    out_kept, out_sent = weight_blocks(
-        row_blocks(middle_low, parts), column_blocks(attended_rows, cells), False, True
-    )
-    grad_heads, fc_kept, fc_sent, out_kept, out_sent = lax.optimization_barrier(
-        (grad_heads, fc_kept, fc_sent, out_kept, out_sent)
-    )
-    fc_weight_grad = scatter_sum(fc_kept, fc_sent, steps_x)
-    out_weight_grad = scatter_sum(out_kept, out_sent, steps_y).T
+    fc_kept, fc_sent = weight_blocks([(mlp_normed, hidden_grad), (attended_rows, middle_low)], True)
+    fc_out_grad = scatter_sum(fc_kept, fc_sent, steps_x)[: model_width // cells]
+    fc_columns = fc_weight.shape[1] // parts
+    fc_weight_grad = fc_out_grad[:, :fc_columns]
+    out_weight_grad = fc_out_grad[:, fc_columns:]
 
     backs = [
       attend_back(
@@ -489,6 +517,8 @@
     def over_tokens(a, b):
         return jnp.einsum("nd,ne->de", a, b, preferred_element_type=jnp.float32)
 
+    dkv_got = swap(dkv_far, "ctx", 1)
+    dq_rows = to_rows(dq)
     qkv_part = jnp.concatenate(
         [
             over_tokens(normed_near, tall(dq)),
@@ -508,7 +538,6 @@
         qkv_part = add_up(kept, swap(sent, axis, bit)).astype(jnp.bfloat16)
     qkv_part = add_up(qkv_part, swap(qkv_part, "ctx", 1)).astype(jnp.bfloat16)[0]
     send_table, take_table = head_columns(groups, halves, 3, units)
-    head_index = lax.axis_index("head")
     sent = qkv_part[jnp.asarray(send_table)[head_index, half_index]]
     got = lax.all_to_all(sent, "head", split_axis=0, concat_axis=0, tiled=True)
     taken = jnp.asarray(take_table)[head_index, half_index]
@@ -516,9 +545,10 @@
         [got[taken[n, 0], taken[n, 1]] for n in range(take_table.shape[2])], axis=-1
     ).astype(jnp.float32)
 
-    dkv_got = swap(dkv_far, "ctx", 1)
     dkv = add_up(dkv, dkv_got).astype(jnp.bfloat16)
-    qkv_grad = to_rows(jnp.concatenate([dq, dkv], axis=-1))
+    dkv, dq_rows = lax.optimization_barrier((dkv, dq_rows))
+    dkv_rows = to_rows(dkv)
+    qkv_grad = jnp.concatenate([dq_rows, dkv_rows], axis=-1)
     column_sums = jnp.sum(qkv_grad, axis=0, dtype=jnp.float32)
     query_bias_grad = column_sums[:model_width]
     value_bias_grad = column_sums[2 * model_width :]

time: 678 us -> 691 us (1.019)
  waiting for transfers between devices: 226 us -> 285 us
  local copies, waits for them, and re-layouts: 103 us -> 83.4 us
  matrix products: 63.4 us -> 54.5 us
    ppermute x26 -> x21, waiting for transfers between devices: 218 us -> 258 us  [swap(): lax.ppermute(values, axis, [(i, i ^ bit) for i in range(lax.axis_size(axi...]
    all_gather x1, waiting for transfers between devices: 0.02 us -> 19 us  [body(): normed_near = lax.all_gather(normed_near, 'head', axis=1, tiled=True)]
    reshape x3 -> x1, local copies, waits for them, and re-layouts: 10.6 us -> 2.14 us  [to_rows(): values.transpose(1, 2, 3, 0, 4).reshape(token_count, sections * model_width)]
    ppermute x26 -> x21, starting transfers between devices: 37.3 us -> 29.6 us  [swap(): lax.ppermute(values, axis, [(i, i ^ bit) for i in range(lax.axis_size(axi...]
    optimization_barrier x2 -> x0, local copies, waits for them, and re-layouts: 7.42 us -> none  [the longest x1 5.83 us: body(): lax.optimization_barrier((grad_low, proj_kept, proj_sent))]
    unnamed x106 -> x99, local copies, waits for them, and re-layouts: 13.7 us -> 17.7 us
    pallas_call x3 -> x2, Pallas kernels: 27.2 us -> 24.2 us  [weight_blocks(): pl.pallas_call(kernel, out_shape=[jax.ShapeDtypeStruct(shape, jnp.bfloat1...]
    convert_element_type x12 -> x8, other arithmetic: 27.9 us -> 28.3 us  [scatter_sum(): total = total.astype(jnp.bfloat16)]
  transfers between devices with their start and end apart: 31 -> 27, of which waited for: 11 -> 11; matrix products, arithmetic and copies ran while one was open for 29% -> 23% of each run, Pallas kernels for 9% -> 8%
where the time goes in v4:
time: 691 us; the launch traced here: 683 us
  waiting for transfers between devices  285 us (41%)
  Pallas kernels  85.4 us (12%)
  local copies, waits for them, and re-layouts  83.4 us (12%)
  matrix products  54.5 us (8%)
  starting transfers between devices  52 us (8%)
  other arithmetic  47.9 us (7%)
  blocking collectives  46.3 us (7%)
  between operations  28.4 us (4%)
    ppermute x21, waiting for transfers between devices, swap(): lax.ppermute(values, axis, [(i, i ^ bit) for i in range(lax.axis_size(axi...  258 us
    all_to_all x1, blocking collectives, to_heads(): lax.all_to_all(values, 'head', split_axis=0, concat_axis=0, tiled=True)  46.3 us
    pallas_call x1, Pallas kernels, attend_back(): pl.pallas_call(back_kernel, out_shape=(jax.ShapeDtypeStruct((rows_all, wi...  32.4 us
    ppermute x21, starting transfers between devices, swap(): lax.ppermute(values, axis, [(i, i ^ bit) for i in range(lax.axis_size(axi...  29.6 us
    pallas_call x1, Pallas kernels, attend(): pl.pallas_call(attend_kernel, out_shape=(jax.ShapeDtypeStruct((rows_all,...  28.8 us
    convert_element_type x8, other arithmetic, scatter_sum(): total = total.astype(jnp.bfloat16)  28.3 us
    pallas_call x2, Pallas kernels, weight_blocks(): pl.pallas_call(kernel, out_shape=[jax.ShapeDtypeStruct(shape, jnp.bfloat1...  24.2 us
    all_gather x1, waiting for transfers between devices, body(): normed_near = lax.all_gather(normed_near, 'head', axis=1, tiled=True)  19 us
  transfers between devices with their start and end apart: 27, of which 11 were waited for; matrix products, arithmetic and copies ran while one was open for 23% of the time, Pallas kernels for 8%

profile of v4, /device:TPU:0, one launch (start us, length us, event | category | flops | bytes accessed | tf_op | source)
XLA Modules:
  0.0 682.5 jit_solution(17303151053848385729)
XLA Ops:
  11.6 6.9 %fusion.2 = bf16[256,3360]{0,1:T(8,128)(2,1)S(1)} fusion(bf16[1120,3360]{1,0:T(8,128)(2,1)} %param.28, f32[3360]{0:T(1024)S(1)} %concatenate.16, bf16[1,256,1120]{2,1,0:T(8,128)(2,1)S(1)} %copy.108, f32[1120]{0:T(1024)S(1)} %copy-done.32, f32[1120]{0:T(1024)S(1)} %copy-done.28, f32[256]{0:T(256)S(1)} %fusion.39, f32[256]{0:T(256)S(1)} %broadcast_multiply_fusion.1, ...), kind=kOutput, calls=%fused_computation.11 | convolution fusion | flops 1930485760 | bytes 9849088 | tf_op jit(solution)/shard_map/dot_general | solution.py:439
  18.6 46.3 %all_to_all.30 = bf16[4,1,256,840]{2,3,1,0:T(8,128)(2,1)S(1)} all-to-all(bf16[4,1,256,840]{2,3,1,0:T(8,128)(2,1)S(1)} %bitcast.171), channel_id=1, replica_groups=mesh['cell'=4,'head'=4,'ctx'=2] {'head'}, dimensions={0} | all-to-all | bytes 3440640 | tf_op jit(solution)/shard_map/all_to_all | solution.py:448
  69.9 3.5 copy.111
  73.4 20.3 %collective-permute-done = bf16[1,1024,560]{1,2,0:T(8,128)(2,1)} collective-permute-done((bf16[1,1024,560]{1,2,0:T(8,128)(2,1)}, bf16[1,1024,560]{1,2,0:T(8,128)(2,1)}, u32[]{:S(2)}, u32[]{:S(2)}) %collective-permute-start) | collective-permute-done | bytes 1146912 | tf_op jit(solution)/shard_map/ppermute | solution.py:32
  93.7 2.4 copy.113
  96.1 28.8 %attend.1 = (bf16[1024,280]{1,0:T(8,128)(2,1)}, f32[4,280,256]{2,1,0:T(8,128)}, f32[4,5,1,256]{3,2,1,0:T(1,128)}) custom-call(s32[2]{0:T(128)} %pad_add_fusion.info, bf16[1024,840]{1,0:T(8,128)(2,1)} %bitcast.178, bf16[1024,560]{1,0:T(8,128)(2,1)} %bitcast.181), custom_call_target="tpu_custom_call" | custom-call | flops 21474836480 | bytes 8388608 | tf_op jit(solution)/shard_map/attend/pallas_call | solution.py:255
  124.9 2.2 copy.114
  127.2 4.1 all-to-all-start.1
  132.7 2.1 copy.128
  134.8 2.1 copy.117
  136.9 7.2 %all-to-all-done.1 = bf16[4,1,256,280]{2,3,1,0:T(8,128)(2,1)} async-done(((bf16[4,1,256,280]{2,3,1,0:T(8,128)(2,1)}), bf16[4,1,256,280]{2,3,1,0:T(8,128)(2,1)}, u32[]{:S(2)}, u32[]{:S(2)}) %all-to-all-start.1) | async-done | bytes 573472 | tf_op jit(solution)/shard_map/all_to_all | solution.py:454
  144.2 2.2 fusion.57
  147.8 9.4 %multiply_convert_fusion = (bf16[256,4480]{1,0:T(8,128)(2,1)}, f32[256,4480]{1,0:T(8,128)S(1)}) fusion(f32[4480]{0:T(1024)S(1)} %copy-done.36, bf16[256,1120]{1,0:T(8,128)(2,1)S(1)} %add_convert_fusion.8.refs_0_, bf16[1120,4480]{1,0:T(8,128)(2,1)} %param.35), kind=kOutput, calls=%fused_computation.20 | convolution fusion | flops 2580480000 | bytes 17507840 | tf_op jit(solution)/shard_map/dot_general | solution.py:471
  157.3 6.3 convert_reduce_fusion
  163.6 3.9 fusion.59
  167.5 2.6 copy.118
  170.2 2.2 multiply_reduce_fusion
  175.7 4.5 all-to-all-start.2
  181.3 19.0 %all-gather.2.cloned.1.call-done = bf16[1,4,256,1120]{2,3,0,1:T(8,128)(2,1)} async-done(((bf16[1,1,256,1120]{2,3,0,1:T(8,128)(2,1)}), bf16[1,4,256,1120]{2,3,0,1:T(8,128)(2,1)}) %all-gather.2.cloned.1.call-update) | async-done | bytes 2293776 | tf_op jit(solution)/shard_map/all_gather | solution.py:461
  200.3 3.0 copy.129
  203.3 2.5 copy.130
  205.8 2.1 copy.138.refs_2_
  207.9 10.8 %weight_blocks.3 = (bf16[2,8,144,1120]{3,2,1,0:T(8,128)(2,1)}, bf16[2,8,144,1120]{3,2,1,0:T(8,128)(2,1)}) custom-call(s32[8]{0:T(128)} %fusion.44.right_at.left_at, s32[4]{0:T(128)} %broadcast_xor_fusion.left_at.right_at, bf16[256,1120]{1,0:T(8,128)(2,1)} %bitcast.170, bf16[256,4480]{1,0:T(8,128)(2,1)} %get-tuple-element.142.refs_1_), custom_call_target="tpu_custom_call" | custom-call | tf_op jit(solution)/shard_map/weight_blocks/pallas_call | solution.py:128
  218.7 13.5 %weight_blocks.2 = (bf16[2,8,288,700]{3,2,1,0:T(8,128)(2,1)}, bf16[2,8,288,700]{3,2,1,0:T(8,128)(2,1)}) custom-call(s32[4]{0:T(128)} %broadcast_xor_fusion.left_at.right_at, s32[8]{0:T(128)} %fusion.44.right_at.left_at, bf16[256,1120]{1,0:T(8,128)(2,1)} %copy-done.18, bf16[256,4480]{1,0:T(8,128)(2,1)} %copy-done.21, bf16[256,1120]{1,0:T(8,128)(2,1)} %copy.138.refs_2_, ...), custom_call_target="tpu_custom_call" | custom-call | tf_op jit(solution)/shard_map/weight_blocks/pallas_call | solution.py:128
  232.6 2.2 copy.119
  234.9 32.4 %attend_back.1 = (bf16[1024,280]{1,0:T(8,128)(2,1)}, bf16[1024,560]{1,0:T(8,128)(2,1)}, bf16[1024,560]{1,0:T(8,128)(2,1)}) custom-call(s32[2]{0:T(128)} %pad_add_fusion.info, bf16[1024,840]{1,0:T(8,128)(2,1)} %bitcast.179, bf16[1024,560]{1,0:T(8,128)(2,1)} %bitcast.182, bf16[1024,280]{1,0:T(8,128)(2,1)} %bitcast.185, ...), custom_call_target="tpu_custom_call" | custom-call | flops 64424509440 | bytes 8388608 | tf_op jit(solution)/shard_map/attend_back/pallas_call | solution.py:354
  267.2 2.2 copy.122
  269.5 4.3 all-to-all-start.3
  273.8 2.4 copy.120
  276.2 7.5 %collective-permute-start.1 = (bf16[1,1024,560]{1,2,0:T(8,128)(2,1)}, bf16[1,1024,560]{1,2,0:T(8,128)(2,1)}, u32[]{:S(2)}, u32[]{:S(2)}) collective-permute-start(bf16[1,1024,560]{1,2,0:T(8,128)(2,1)} %copy.120), channel_id=1, source_target_pairs={{0,1},{1,0},{2,3},{3,2},{4,5},{5,4},{6,7},{7,6},{8,9},{9,8},{10,11... | collective-permute-start | bytes 3440648 | tf_op jit(solution)/shard_map/ppermute | solution.py:32
  283.7 2.9 convolution_convert_fusion
  286.6 3.5 fusion.60
  290.2 2.9 fusion.10
  293.1 13.6 %collective-permute-done.1 = bf16[1,1024,560]{1,2,0:T(8,128)(2,1)} collective-permute-done((bf16[1,1024,560]{1,2,0:T(8,128)(2,1)}, bf16[1,1024,560]{1,2,0:T(8,128)(2,1)}, u32[]{:S(2)}, u32[]{:S(2)}) %collective-permute-start.1) | collective-permute-done | bytes 1146912 | tf_op jit(solution)/shard_map/ppermute | solution.py:32
  306.7 2.4 copy.121
  309.1 2.0 fusion.14
  312.6 4.9 all-to-all-start.4
  318.9 5.2 convert_element_type.212
  324.1 4.1 dynamic-slice_bitcast_fusion
  330.0 25.6 %collective-permute-done.8 = bf16[2,6,280,140]{2,0,3,1:T(2,128)(2,1)S(1)} collective-permute-done((bf16[2,6,280,140]{2,0,3,1:T(2,128)(2,1)}, bf16[2,6,280,140]{2,0,3,1:T(2,128)(2,1)S(1)}, u32[]{:S(2)}, u32[]{:S(2)}) %collective-permute-start.8) | collective-permute-done | bytes 940832 | tf_op jit(solution)/shard_map/ppermute | solution.py:32
  356.7 1.9 fusion.13
  361.1 6.6 fusion.58
  372.3 5.5 fusion.1
  377.8 1.9 slice.220
  382.7 10.1 %fusion = bf16[16,288,700]{2,1,0:T(8,128)(2,1)} fusion(bf16[16,288,700]{2,1,0:T(8,128)(2,1)} %collective-permute-done.11, bf16[2,8,288,700]{3,2,1,0:T(8,128)(2,1)} %get-tuple-element.36), kind=kLoop, calls=%fused_computation.2 | loop fusion | flops 12902400 | bytes 19353600 | tf_op jit(solution)/shard_map/convert_element_type | solution.py:154
  392.8 4.2 slice.204
  399.7 1.8 collective-permute-start.2
  402.9 2.3 collective-permute-start.10
  405.2 113.9 %collective-permute-done.2 = f32[2,32,280]{2,1,0:T(8,128)S(1)} collective-permute-done((f32[2,32,280]{2,1,0:T(8,128)S(1)}, f32[2,32,280]{2,1,0:T(8,128)S(1)}, u32[]{:S(2)}, u32[]{:S(2)}) %collective-permute-start.2) | collective-permute-done | bytes 71712 | tf_op jit(solution)/shard_map/ppermute | solution.py:32
  520.5 2.3 collective-permute-start.4
  534.4 2.7 collective-permute-start.5
  539.6 4.2 all-to-all-start.5
  543.9 2.0 collective-permute-start.6
  545.9 3.2 add_convert_fusion.1
  551.0 3.9 add_convert_fusion
  559.1 7.1 %fusion.16 = bf16[1,256,1120]{2,1,0:T(8,128)(2,1)S(1)} fusion(f32[256,1120]{1,0:T(8,128)S(1)} %copy-done.5, bf16[256,4480]{1,0:T(8,128)(2,1)S(1)} %copy-done.20, bf16[4480,1120]{0,1:T(8,128)(2,1)} %param.37, f32[1120]{0:T(1024)S(1)} %copy-done.38), kind=kOutput, calls=%fused_computation.37 | convolution fusion | flops 2569871360 | bytes 14053760 | tf_op jit(solution)/shard_map/dot_general | solution.py:473
  567.2 2.3 copy.140
  573.3 9.4 %collective-permute-done.18 = bf16[4,144,1120]{2,1,0:T(8,128)(2,1)} collective-permute-done((bf16[4,144,1120]{2,1,0:T(8,128)(2,1)}, bf16[4,144,1120]{2,1,0:T(8,128)(2,1)}, u32[]{:S(2)}, u32[]{:S(2)}) %collective-permute-start.18) | collective-permute-done | bytes 1290272 | tf_op jit(solution)/shard_map/ppermute | solution.py:32
  586.4 2.4 collective-permute-start.19
  589.9 28.8 %collective-permute-done.13 = bf16[4,288,700]{2,1,0:T(8,128)(2,1)} collective-permute-done((bf16[4,288,700]{2,1,0:T(8,128)(2,1)}, bf16[4,288,700]{2,1,0:T(8,128)(2,1)}, u32[]{:S(2)}, u32[]{:S(2)}) %collective-permute-start.13) | collective-permute-done | bytes 1612832 | tf_op jit(solution)/shard_map/ppermute | solution.py:32
  618.7 2.4 add_convert_fusion.2
  621.2 2.4 collective-permute-start.14
  625.6 35.3 %collective-permute-done.14 = bf16[2,288,700]{2,1,0:T(8,128)(2,1)S(1)} collective-permute-done((bf16[2,288,700]{2,1,0:T(8,128)(2,1)S(1)}, bf16[2,288,700]{2,1,0:T(8,128)(2,1)S(1)}, u32[]{:S(2)}, u32[]{:S(2)}) %collective-permute-start.14) | collective-permute-done | bytes 806432 | tf_op jit(solution)/shard_map/ppermute | solution.py:32
  662.2 11.1 %collective-permute-done.15 = bf16[1,288,700]{2,1,0:T(8,128)(2,1)S(1)} collective-permute-done((bf16[1,288,700]{2,1,0:T(8,128)(2,1)S(1)}, bf16[1,288,700]{2,1,0:T(8,128)(2,1)S(1)}, u32[]{:S(2)}, u32[]{:S(2)}) %collective-permute-start.15) | collective-permute-done | bytes 403232 | tf_op jit(solution)/shard_map/ppermute | solution.py:32
  (216 shorter events, 60.3 us)
Async XLA Ops:
  7.2 137.0 %copy-start = (bf16[1120,1120]{1,0:T(8,128)(2,1)S(1)}, bf16[1120,1120]{1,0:T(8,128)(2,1)}, u32[]{:S(2)}) copy-start(bf16[1120,1120]{1,0:T(8,128)(2,1)} %param.31) | copy-start | bytes 7526404
  7.2 4.3 copy-start.35
  7.2 4.3 copy-start.34
  7.2 4.3 copy-start.28
  7.2 4.3 copy-start.32
  67.2 26.5 %collective-permute-start = (bf16[1,1024,560]{1,2,0:T(8,128)(2,1)}, bf16[1,1024,560]{1,2,0:T(8,128)(2,1)}, u32[]{:S(2)}, u32[]{:S(2)}) collective-permute-start(bf16[1,1024,560]{1,2,0:T(8,128)(2,1)} %slice.195), channel_id=1, source_target_pairs={{0,1},{1,0},{2,3},{3,2},{4,5},{5,4},{6,7},{7,6},{8,9},{9,8},{10,11... | collective-permute-start | bytes 3440648 | tf_op jit(solution)/shard_map/ppermute | solution.py:32
  127.2 17.0 %all-to-all-start.1 = ((bf16[4,1,256,280]{2,3,1,0:T(8,128)(2,1)}), bf16[4,1,256,280]{2,3,1,0:T(8,128)(2,1)}, u32[]{:S(2)}, u32[]{:S(2)}) async-start(bf16[4,1,256,280]{2,3,1,0:T(8,128)(2,1)} %copy.114), calls=%async_computation.1 | async-start | bytes 1146880 | tf_op jit(solution)/shard_map/all_to_all | solution.py:454
  131.3 69.0 %all-gather.2.cloned.1.call-start = ((), (), s32[]{:S(2)}) async-start(), calls=%async_computation.6 | async-start | bytes 2867200 | tf_op jit(solution)/shard_map/all_gather | solution.py:461
  132.7 11.5 %copy-start.37 = (f32[1120]{0:T(1024)S(1)}, f32[1120]{0:T(1024)}, u32[]{:S(2)}) copy-start(f32[1120]{0:T(1024)} %param.32) | copy-start | bytes 13444
  144.2 3.3 copy-start.29
  144.2 3.3 copy-start.33
  147.4 9.8 %slice-start.3 = ((s8[10035200]{0:T(1024)(128)(4,1)}), s8[4194304]{0:T(1024)(128)(4,1)S(1)}, s32[]{:S(2)}) async-start(s8[10035200]{0:T(1024)(128)(4,1)} %bitcast.191), calls=%async_computation.10 | async-start | bytes 8388608
  147.7 9.5 %copy-start.18 = (bf16[256,1120]{1,0:T(8,128)(2,1)}, bf16[256,1120]{1,0:T(8,128)(2,1)S(1)}, u32[]{:S(2)}) copy-start(bf16[256,1120]{1,0:T(8,128)(2,1)S(1)} %add_convert_fusion.8.refs_0_) | copy-start | bytes 1720324
  147.7 9.5 %copy-start.27 = (bf16[1,256,1120]{1,2,0:T(8,128)(2,1)S(1)}, bf16[1,256,1120]{1,2,0:T(8,128)(2,1)}, u32[]{:S(2)}) copy-start(bf16[1,256,1120]{1,2,0:T(8,128)(2,1)} %param.39) | copy-start | bytes 1720324
  147.8 9.5 %slice-start.4 = ((s8[10035200]{0:T(1024)(128)(4,1)}), s8[4194304]{0:T(1024)(128)(4,1)S(1)}, s32[]{:S(2)}) async-start(s8[10035200]{0:T(1024)(128)(4,1)} %bitcast.191), calls=%async_computation.11 | async-start | bytes 8388608
  147.8 9.5 %slice-start.5 = ((s8[10035200]{0:T(1024)(128)(4,1)}), s8[1646592]{0:T(1024)(128)(4,1)S(1)}, s32[]{:S(2)}) async-start(s8[10035200]{0:T(1024)(128)(4,1)} %bitcast.191), calls=%async_computation.12 | async-start | bytes 3293184
  147.8 15.8 %slice-start = ((s8[10035200]{0:T(1024)(128)(4,1)}), s8[4194304]{0:T(1024)(128)(4,1)S(1)}, s32[]{:S(2)}) async-start(s8[10035200]{0:T(1024)(128)(4,1)} %bitcast.189), calls=%async_computation.7 | async-start | bytes 8388608
  147.8 15.8 %slice-start.1 = ((s8[10035200]{0:T(1024)(128)(4,1)}), s8[4194304]{0:T(1024)(128)(4,1)S(1)}, s32[]{:S(2)}) async-start(s8[10035200]{0:T(1024)(128)(4,1)} %bitcast.189), calls=%async_computation.8 | async-start | bytes 8388608
  157.3 6.3 slice-start.2
  163.6 4.0 copy-start.21
  170.2 2.2 copy-start.4
  170.2 2.3 copy-start.8
  173.0 2.7 copy-start.11
  173.9 6.9 %copy-start.39 = (s32[4]{0:T(128)S(1)}, s32[4]{0:T(128)}, u32[]{:S(2)}) copy-start(s32[4]{0:T(128)} %constant.129.clone) | copy-start | bytes 52
  175.7 56.9 %all-to-all-start.2 = ((bf16[4,1,256,280]{2,3,1,0:T(8,128)(2,1)}), bf16[4,1,256,280]{2,3,1,0:T(8,128)(2,1)}, u32[]{:S(2)}, u32[]{:S(2)}) async-start(bf16[4,1,256,280]{2,3,1,0:T(8,128)(2,1)} %bitcast.187), calls=%async_computation.2 | async-start | bytes 1146880 | tf_op jit(solution)/shard_map/all_to_all | solution.py:448
  205.8 80.9 %collective-permute-start.7 = (bf16[1024,1120]{0,1:T(8,128)(2,1)}, bf16[1024,1120]{0,1:T(8,128)(2,1)}, u32[]{:S(2)}, u32[]{:S(2)}) collective-permute-start(bf16[1024,1120]{0,1:T(8,128)(2,1)} %copy.130), channel_id=1, source_target_pairs={{0,1},{1,0},{2,3},{3,2},{4,5},{5,4},{6,7},{7,6},{8,9},{9,8},{10,11... | collective-permute-start | bytes 6881288 | tf_op jit(solution)/shard_map/ppermute | solution.py:32
  218.7 153.7 %collective-permute-start.16 = (bf16[16,144,1120]{2,1,0:T(8,128)(2,1)}, bf16[16,144,1120]{2,1,0:T(8,128)(2,1)}, u32[]{:S(2)}, u32[]{:S(2)}) collective-permute-start(bf16[16,144,1120]{2,1,0:T(8,128)(2,1)} %bitcast.194), channel_id=1, source_target_pairs={{0,8},{8,0},{16,24},{24,16},{1,9},{9,1},{17,25},{25,17},{2,10},{10... | collective-permute-start | bytes 15482888 | tf_op jit(solution)/shard_map/ppermute | solution.py:32
  232.1 150.6 %collective-permute-start.11 = (bf16[16,288,700]{2,1,0:T(8,128)(2,1)}, bf16[16,288,700]{2,1,0:T(8,128)(2,1)}, u32[]{:S(2)}, u32[]{:S(2)}) collective-permute-start(bf16[16,288,700]{2,1,0:T(8,128)(2,1)} %bitcast.193), channel_id=1, source_target_pairs={{0,8},{8,0},{16,24},{24,16},{1,9},{9,1},{17,25},{25,17},{2,10},{10... | collective-permute-start | bytes 19353608 | tf_op jit(solution)/shard_map/ppermute | solution.py:32
  269.5 41.7 %all-to-all-start.3 = ((bf16[4,1,256,280]{2,3,1,0:T(8,128)(2,1)}), bf16[4,1,256,280]{2,3,1,0:T(8,128)(2,1)}, u32[]{:S(2)}, u32[]{:S(2)}) async-start(bf16[4,1,256,280]{2,3,1,0:T(8,128)(2,1)} %copy.122), calls=%async_computation.3 | async-start | bytes 1146880 | tf_op jit(solution)/shard_map/all_to_all | solution.py:454
  276.2 10.4 %copy-start.22 = (bf16[1024,560]{1,0:T(8,128)(2,1)S(1)}, bf16[1024,560]{1,0:T(8,128)(2,1)}, u32[]{:S(2)}) copy-start(bf16[1024,560]{1,0:T(8,128)(2,1)} %get-tuple-element.32) | copy-start | bytes 3440644
  276.2 30.5 %collective-permute-start.1 = (bf16[1,1024,560]{1,2,0:T(8,128)(2,1)}, bf16[1,1024,560]{1,2,0:T(8,128)(2,1)}, u32[]{:S(2)}, u32[]{:S(2)}) collective-permute-start(bf16[1,1024,560]{1,2,0:T(8,128)(2,1)} %copy.120), channel_id=1, source_target_pairs={{0,1},{1,0},{2,3},{3,2},{4,5},{5,4},{6,7},{7,6},{8,9},{9,8},{10,11... | collective-permute-start | bytes 3440648 | tf_op jit(solution)/shard_map/ppermute | solution.py:32
  286.6 3.6 copy-start.23
  312.6 4.9 copy-start.24
  312.6 4.9 copy-start.26
  312.6 47.1 %all-to-all-start.4 = ((bf16[4,1,256,560]{2,3,1,0:T(8,128)(2,1)}), bf16[4,1,256,560]{2,3,1,0:T(8,128)(2,1)}, u32[]{:S(2)}, u32[]{:S(2)}) async-start(bf16[4,1,256,560]{2,3,1,0:T(8,128)(2,1)} %copy.123), calls=%async_computation.4 | async-start | bytes 2293760 | tf_op jit(solution)/shard_map/all_to_all | solution.py:454
  328.2 27.3 %collective-permute-start.8 = (bf16[2,6,280,140]{2,0,3,1:T(2,128)(2,1)}, bf16[2,6,280,140]{2,0,3,1:T(2,128)(2,1)S(1)}, u32[]{:S(2)}, u32[]{:S(2)}) collective-permute-start(bf16[2,6,280,140]{2,0,3,1:T(2,128)(2,1)} %get-tuple-element.122), channel_id=1, source_target_pairs={{0,16},{8,24},{16,0},{24,8},{1,17},{9,25},{17,1},{25,9},{2,18},{10... | collective-permute-start | bytes 2822408 | tf_op jit(solution)/shard_map/ppermute | solution.py:32
  358.6 2.4 copy-start.15
  359.7 41.8 %collective-permute-start.9 = (bf16[1,6,280,140]{2,3,1,0:T(8,128)(2,1)}, bf16[1,6,280,140]{2,3,1,0:T(8,128)(2,1)}, u32[]{:S(2)}, u32[]{:S(2)}) collective-permute-start(bf16[1,6,280,140]{2,3,1,0:T(8,128)(2,1)} %constant_dynamic-slice_fusion.5), channel_id=1, source_target_pairs={{0,8},{8,0},{16,24},{24,16},{1,9},{9,1},{17,25},{25,17},{2,10},{10... | collective-permute-start | bytes 1411208 | tf_op jit(solution)/shard_map/ppermute | solution.py:32
  377.8 3.2 copy-start.2
  381.0 164.9 %collective-permute-start.17 = (bf16[8,144,1120]{2,1,0:T(8,128)(2,1)}, bf16[8,144,1120]{2,1,0:T(8,128)(2,1)}, u32[]{:S(2)}, u32[]{:S(2)}) collective-permute-start(bf16[8,144,1120]{2,1,0:T(8,128)(2,1)} %slice.220), channel_id=1, source_target_pairs={{0,16},{8,24},{16,0},{24,8},{1,17},{9,25},{17,1},{25,9},{2,18},{10... | collective-permute-start | bytes 7741448 | tf_op jit(solution)/shard_map/ppermute | solution.py:32
  392.8 4.5 copy-start.12
  392.8 4.5 copy-start.14
  397.0 153.4 %collective-permute-start.12 = (bf16[8,288,700]{2,1,0:T(8,128)(2,1)}, bf16[8,288,700]{2,1,0:T(8,128)(2,1)}, u32[]{:S(2)}, u32[]{:S(2)}) collective-permute-start(bf16[8,288,700]{2,1,0:T(8,128)(2,1)} %slice.204), channel_id=1, source_target_pairs={{0,16},{8,24},{16,0},{24,8},{1,17},{9,25},{17,1},{25,9},{2,18},{10... | collective-permute-start | bytes 9676808 | tf_op jit(solution)/shard_map/ppermute | solution.py:32
  399.7 119.4 %collective-permute-start.2 = (f32[2,32,280]{2,1,0:T(8,128)S(1)}, f32[2,32,280]{2,1,0:T(8,128)S(1)}, u32[]{:S(2)}, u32[]{:S(2)}) collective-permute-start(f32[2,32,280]{2,1,0:T(8,128)S(1)} %constant_dynamic-slice_fusion.8), channel_id=1, source_target_pairs={{0,16},{8,24},{16,0},{24,8},{1,17},{9,25},{17,1},{25,9},{2,18},{10... | collective-permute-start | bytes 215048 | tf_op jit(solution)/shard_map/ppermute | solution.py:32
  402.9 134.2 %collective-permute-start.10 = (bf16[1,6,280,140]{2,3,1,0:T(8,128)(2,1)S(1)}, bf16[1,6,280,140]{2,3,1,0:T(8,128)(2,1)S(1)}, u32[]{:S(2)}, u32[]{:S(2)}) collective-permute-start(bf16[1,6,280,140]{2,3,1,0:T(8,128)(2,1)S(1)} %add_convert_fusion.7), channel_id=1, source_target_pairs={{0,1},{1,0},{2,3},{3,2},{4,5},{5,4},{6,7},{7,6},{8,9},{9,8},{10,11... | collective-permute-start | bytes 1411208 | tf_op jit(solution)/shard_map/ppermute | solution.py:32
  519.2 1.3 collective-permute-start.3
  520.5 13.9 %collective-permute-start.4 = (f32[1,32,280]{2,1,0:T(8,128)S(1)}, f32[1,32,280]{2,1,0:T(8,128)S(1)}, u32[]{:S(2)}, u32[]{:S(2)}) collective-permute-start(f32[1,32,280]{2,1,0:T(8,128)S(1)} %dynamic-slice_add_fusion.1), channel_id=1, source_target_pairs={{0,1},{1,0},{2,3},{3,2},{4,5},{5,4},{6,7},{7,6},{8,9},{9,8},{10,11... | collective-permute-start | bytes 107528 | tf_op jit(solution)/shard_map/ppermute | solution.py:32
  534.4 9.5 %collective-permute-start.5 = (f32[1,32,280]{2,1,0:T(8,128)S(1)}, f32[1,32,280]{2,1,0:T(8,128)S(1)}, u32[]{:S(2)}, u32[]{:S(2)}) collective-permute-start(f32[1,32,280]{2,1,0:T(8,128)S(1)} %add.278), channel_id=1, source_target_pairs={{0,4},{2,6},{4,0},{6,2},{1,5},{3,7},{5,1},{7,3},{8,12},{10,14},{12... | collective-permute-start | bytes 107528 | tf_op jit(solution)/shard_map/ppermute | solution.py:32
  539.6 31.8 %all-to-all-start.5 = ((bf16[4,2,280,140]{2,1,3,0:T(2,128)(2,1)}), bf16[4,2,280,140]{2,1,3,0:T(2,128)(2,1)}, u32[]{:S(2)}, u32[]{:S(2)}) async-start(bf16[4,2,280,140]{2,1,3,0:T(2,128)(2,1)} %copy.134), calls=%async_computation.5 | async-start | bytes 1720320 | tf_op jit(solution)/shard_map/all_to_all | solution.py:542
  543.9 25.6 %collective-permute-start.6 = (f32[1,32,280]{2,1,0:T(8,128)S(1)}, f32[1,32,280]{2,1,0:T(8,128)S(1)}, u32[]{:S(2)}, u32[]{:S(2)}) collective-permute-start(f32[1,32,280]{2,1,0:T(8,128)S(1)} %add.279), channel_id=1, source_target_pairs={{0,2},{2,0},{4,6},{6,4},{1,3},{3,1},{5,7},{7,5},{8,10},{10,8},{12,... | collective-permute-start | bytes 107528 | tf_op jit(solution)/shard_map/ppermute | solution.py:32
  549.1 1.9 copy-start.9
  550.4 32.3 %collective-permute-start.18 = (bf16[4,144,1120]{2,1,0:T(8,128)(2,1)}, bf16[4,144,1120]{2,1,0:T(8,128)(2,1)}, u32[]{:S(2)}, u32[]{:S(2)}) collective-permute-start(bf16[4,144,1120]{2,1,0:T(8,128)(2,1)} %slice.222), channel_id=1, source_target_pairs={{0,1},{1,0},{2,3},{3,2},{4,5},{5,4},{6,7},{7,6},{8,9},{9,8},{10,11... | collective-permute-start | bytes 3870728 | tf_op jit(solution)/shard_map/ppermute | solution.py:32
  554.9 2.7 copy-start.7
  555.0 4.1 copy-start.5
  555.0 4.1 copy-start.20
  555.0 4.1 copy-start.38
  557.6 61.1 %collective-permute-start.13 = (bf16[4,288,700]{2,1,0:T(8,128)(2,1)}, bf16[4,288,700]{2,1,0:T(8,128)(2,1)}, u32[]{:S(2)}, u32[]{:S(2)}) collective-permute-start(bf16[4,288,700]{2,1,0:T(8,128)(2,1)} %slice.206), channel_id=1, source_target_pairs={{0,1},{1,0},{2,3},{3,2},{4,5},{5,4},{6,7},{7,6},{8,9},{9,8},{10,11... | collective-permute-start | bytes 4838408 | tf_op jit(solution)/shard_map/ppermute | solution.py:32
  567.2 15.5 %copy-start.10 = (bf16[8,144,1120]{2,1,0:T(8,128)(2,1)S(1)}, bf16[8,144,1120]{2,1,0:T(8,128)(2,1)}, u32[]{:S(2)}) copy-start(bf16[8,144,1120]{2,1,0:T(8,128)(2,1)} %copy-done.9) | copy-start | bytes 7741444
  586.4 37.2 %collective-permute-start.19 = (bf16[2,144,1120]{2,1,0:T(8,128)(2,1)}, bf16[2,144,1120]{2,1,0:T(8,128)(2,1)}, u32[]{:S(2)}, u32[]{:S(2)}) collective-permute-start(bf16[2,144,1120]{2,1,0:T(8,128)(2,1)} %slice.224), channel_id=1, source_target_pairs={{0,4},{2,6},{4,0},{6,2},{1,5},{3,7},{5,1},{7,3},{8,12},{10,14},{12... | collective-permute-start | bytes 1935368 | tf_op jit(solution)/shard_map/ppermute | solution.py:32
  621.1 2.5 copy-start.17
  621.2 39.6 %collective-permute-start.14 = (bf16[2,288,700]{2,1,0:T(8,128)(2,1)S(1)}, bf16[2,288,700]{2,1,0:T(8,128)(2,1)S(1)}, u32[]{:S(2)}, u32[]{:S(2)}) collective-permute-start(bf16[2,288,700]{2,1,0:T(8,128)(2,1)S(1)} %slice.208), channel_id=1, source_target_pairs={{0,4},{2,6},{4,0},{6,2},{1,5},{3,7},{5,1},{7,3},{8,12},{10,14},{12... | collective-permute-start | bytes 2419208 | tf_op jit(solution)/shard_map/ppermute | solution.py:32
  625.0 36.3 %collective-permute-start.20 = (bf16[1,144,1120]{2,1,0:T(8,128)(2,1)S(1)}, bf16[1,144,1120]{2,1,0:T(8,128)(2,1)S(1)}, u32[]{:S(2)}, u32[]{:S(2)}) collective-permute-start(bf16[1,144,1120]{2,1,0:T(8,128)(2,1)S(1)} %get-tuple-element.130), channel_id=1, source_target_pairs={{0,2},{2,0},{4,6},{6,4},{1,3},{3,1},{5,7},{7,5},{8,10},{10,8},{12,... | collective-permute-start | bytes 967688 | tf_op jit(solution)/shard_map/ppermute | solution.py:32
  661.2 12.1 %collective-permute-start.15 = (bf16[1,288,700]{2,1,0:T(8,128)(2,1)S(1)}, bf16[1,288,700]{2,1,0:T(8,128)(2,1)S(1)}, u32[]{:S(2)}, u32[]{:S(2)}) collective-permute-start(bf16[1,288,700]{2,1,0:T(8,128)(2,1)S(1)} %get-tuple-element.125), channel_id=1, source_target_pairs={{0,2},{2,0},{4,6},{6,4},{1,3},{3,1},{5,7},{7,5},{8,10},{10,8},{12,... | collective-permute-start | bytes 1209608 | tf_op jit(solution)/shard_map/ppermute | solution.py:32
  673.3 2.0 copy-start.1
  (9 other events, 10.0 us)
Sparse Core Ops, SparseCore 0:
  135.0 65.2 all-gather.1

commit v5 on v4

--- a/solution.py
+++ b/solution.py
@@ -143,20 +143,70 @@
     return kept.reshape(-1, rows, cols), sent.reshape(-1, rows, cols)
 
 
-def add_up(kept, got):
-    return kept.astype(jnp.float32) + got.astype(jnp.float32)
-
-
-def scatter_sum(kept, sent, steps):
-    total = None
+def qkv_blocks(near, far, dq, dkv, dkv_far):
+    cells = lax.axis_size("cell")
+    steps = [b for _, b in bits_of("cell")]
+    rel = np.zeros((cells,), np.int32)
+    for s, bit in enumerate(steps):
+        rel += ((np.arange(cells) >> (len(steps) - 1 - s)) & 1).astype(np.int32) * bit
+    place_at = jnp.asarray(np.argsort(rel).astype(np.int32))[
+        jnp.arange(cells, dtype=jnp.int32) ^ lax.axis_index("cell")
+    ]
+    pieces, wide, tokens = near.shape
+    rows = wide // cells
+    width = dq.shape[1]
+    row_at = (jnp.arange(pieces, dtype=jnp.int32) ^ lax.axis_index("head")) * tokens
+
+    def kernel(place, row, near_ref, far_ref, dq_ref, dkv_ref, far_grad, out, tall, q, kv):
+        for p in range(pieces):
+            at = pl.ds(pl.multiple_of(row[p], tokens), tokens)
+            here, there = slice(p * tokens, (p + 1) * tokens), slice(
+                (pieces + p) * tokens, (pieces + p + 1) * tokens
+            )
+            tall[:, here] = near_ref[p]
+            tall[:, there] = far_ref[p]
+            q[here, :] = dq_ref[at, :]
+            kv[here, :] = dkv_ref[at, :]
+            kv[there, :] = far_grad[at, :]
+        for a in range(cells):
+            left = tall[a * rows : (a + 1) * rows, :]
+            out[place[a], :, :width] = nn(left[:, : pieces * tokens], q[...]).astype(jnp.bfloat16)
+            out[place[a], :, width:] = nn(left, kv[...]).astype(jnp.bfloat16)
+
+    smem = pl.BlockSpec(memory_space=pltpu.SMEM)
+    return pl.pallas_call(
+        kernel,
+        out_shape=jax.ShapeDtypeStruct((cells, rows, 3 * width), jnp.bfloat16),
+        in_specs=[smem, smem] + vmem_specs(5),
+        out_specs=vmem_specs(1)[0],
+        scratch_shapes=[
+            pltpu.VMEM((wide, 2 * pieces * tokens), jnp.bfloat16),
+            pltpu.VMEM((pieces * tokens, width), jnp.bfloat16),
+            pltpu.VMEM((2 * pieces * tokens, 2 * width), jnp.bfloat16),
+        ],
+        name="qkv_blocks",
+    )(place_at, row_at, near, far, dq, dkv, dkv_far)
+
+
+def add_up(*terms):
+    total = terms[0].astype(jnp.float32)
+    for term in terms[1:]:
+        total = total + term.astype(jnp.float32)
+    return total
+
+
+def scatter_sum(kept, sent, steps, ties=None):
+    ties = ties or {}
+    terms = [kept]
     for s, (axis, bit) in enumerate(steps):
         if s:
-            total = total.astype(jnp.bfloat16)
-            half = total.shape[0] // 2
-            kept, sent = total[:half], total[half:]
-        got = swap(sent, axis, bit)
-        total = add_up(kept, got)
-    return total[0]
+            half = terms[0].shape[0] // 2
+            sent = add_up(*[t[half:] for t in terms]).astype(jnp.bfloat16)
+            terms = [t[:half] for t in terms]
+        if s in ties:
+            sent, ties[s][0] = lax.optimization_barrier((sent, ties[s][0]))
+        terms.append(swap(sent, axis, bit))
+    return add_up(*terms)[0]
 
 
 def head_dims(qkv_ref):
@@ -457,9 +507,13 @@
 
     qkv_heads = to_heads(mixed_qkv)
     kv_other = swap(qkv_heads[:, :, head_width:], "ctx", 1)
-    normed_near = normed.reshape(cell_count, 1, row_count, model_width)
-    normed_near = lax.all_gather(normed_near, "head", axis=1, tiled=True)
-    normed_near = normed_near.reshape(cell_count * ctx_rows, model_width)
+    normed_t = normed.T.reshape(cells, model_width // cells, token_count)
+    normed_t = jnp.pad(normed_t, ((0, 0), (0, -normed_t.shape[1] % 16), (0, 0)))
+    normed_t, kv_other = lax.optimization_barrier((normed_t.reshape(-1, token_count), kv_other))
+    pieces = [normed_t]
+    for p in range(1, groups):
+        pieces.append(swap(normed_t, "head", p))
+    normed_near = jnp.stack(pieces)
     normed_far = swap(normed_near, "ctx", 1)
     infos = [jnp.stack([lengths[n], half_index.astype(jnp.int32)]) for n in range(cell_count)]
     runs = [attend(infos[n], qkv_heads[n], kv_other[n], groups) for n in range(cell_count)]
@@ -475,13 +529,16 @@
     grad_low = cotangent.reshape(token_count, model_width)
     proj_kept, proj_sent = weight_blocks([(grad_low, active)], False)
     part_columns = model_width // parts
-    proj_weight_grad = scatter_sum(proj_kept, proj_sent, steps_x)[:part_columns].T
     grad_top = grad_low.astype(jnp.float32)
     proj_bias_grad = jnp.sum(grad_top, axis=0)
     active_grad = jnp.einsum("nd,fd->nf", grad_low, proj_weight, preferred_element_type=jnp.float32)
     gelu_pull = jax.vjp(gelu_tanh, hidden)[1]
     hidden_grad = gelu_pull(active_grad)[0].astype(jnp.bfloat16)
     fc_bias_grad = jnp.sum(hidden_grad, axis=0, dtype=jnp.float32)
+    hidden_tie = [hidden_grad]
+    proj_total = scatter_sum(proj_kept, proj_sent, steps_x, {1: hidden_tie})
+    proj_weight_grad = proj_total[:part_columns].T
+    hidden_grad = hidden_tie[0]
     normed_grad = jnp.einsum(
         "nf,df->nd", hidden_grad, fc_weight, preferred_element_type=jnp.float32
     )
@@ -496,7 +553,10 @@
     grad_heads = to_heads(attended_grad)
 
     fc_kept, fc_sent = weight_blocks([(mlp_normed, hidden_grad), (attended_rows, middle_low)], True)
-    fc_out_grad = scatter_sum(fc_kept, fc_sent, steps_x)[: model_width // cells]
+    back_tie = [grad_heads]
+    fc_out_grad = scatter_sum(fc_kept, fc_sent, steps_x, {1: back_tie})
+    grad_heads = back_tie[0]
+    fc_out_grad = fc_out_grad[: model_width // cells]
     fc_columns = fc_weight.shape[1] // parts
     fc_weight_grad = fc_out_grad[:, :fc_columns]
     out_weight_grad = fc_out_grad[:, fc_columns:]
@@ -511,32 +571,15 @@
     dkv = jnp.stack([b[1] for b in backs])
     dkv_far = jnp.stack([b[2] for b in backs])
 
-    def tall(values):
-        return values.reshape(cell_count * ctx_rows, -1)
-
-    def over_tokens(a, b):
-        return jnp.einsum("nd,ne->de", a, b, preferred_element_type=jnp.float32)
-
     dkv_got = swap(dkv_far, "ctx", 1)
     dq_rows = to_rows(dq)
-    qkv_part = jnp.concatenate(
-        [
-            over_tokens(normed_near, tall(dq)),
-            over_tokens(normed_near, tall(dkv)) + over_tokens(normed_far, tall(dkv_far)),
-        ],
-        axis=1,
-    ).astype(jnp.bfloat16)
+    qkv_part = qkv_blocks(normed_near, normed_far, dq[0], dkv[0], dkv_far[0])
+    half_cells = cells // 2
+    qkv_part = scatter_sum(qkv_part[:half_cells], qkv_part[half_cells:], cell_steps)
+    qkv_part = qkv_part[: model_width // cells].astype(jnp.bfloat16)
+    qkv_part = add_up(qkv_part, swap(qkv_part, "ctx", 1)).astype(jnp.bfloat16)
     units = 2 * groups
-    local_units = 3 * units // groups
-    qkv_part = qkv_part.reshape(cells, model_width // cells, local_units, -1).transpose(0, 2, 1, 3)
-    cell_index = lax.axis_index("cell")
-    for axis, bit in cell_steps[::-1]:
-        on = (cell_index // bit) % 2
-        half = qkv_part.shape[0] // 2
-        kept = lax.dynamic_slice_in_dim(qkv_part, on * half, half, 0)
-        sent = lax.dynamic_slice_in_dim(qkv_part, (1 - on) * half, half, 0)
-        qkv_part = add_up(kept, swap(sent, axis, bit)).astype(jnp.bfloat16)
-    qkv_part = add_up(qkv_part, swap(qkv_part, "ctx", 1)).astype(jnp.bfloat16)[0]
+    qkv_part = qkv_part.reshape(qkv_part.shape[0], 3 * units // groups, -1).transpose(1, 0, 2)
     send_table, take_table = head_columns(groups, halves, 3, units)
     sent = qkv_part[jnp.asarray(send_table)[head_index, half_index]]
     got = lax.all_to_all(sent, "head", split_axis=0, concat_axis=0, tiled=True)
@@ -580,6 +623,7 @@
         + [fc_bias_grad.reshape(cells, fc_rows, width)],
         axis=1,
     )
+    cell_index = lax.axis_index("cell")
     for axis, bit in cell_steps[::-1]:
         on = (cell_index // bit) % 2
         half = packed.shape[0] // 2

time: 691 us -> 584 us (0.85)
  waiting for transfers between devices: 285 us -> 143 us
  starting transfers between devices: 52 us -> 82 us
  Pallas kernels: 85.4 us -> 105 us
  between operations: 28.4 us -> 14.8 us
  local copies, waits for them, and re-layouts: 83.4 us -> 70.8 us
    ppermute x21 -> x24, waiting for transfers between devices: 258 us -> 123 us  [swap(): lax.ppermute(values, axis, [(i, i ^ bit) for i in range(lax.axis_size(axi...]
    ppermute x21 -> x24, starting transfers between devices: 29.6 us -> 58.1 us  [swap(): lax.ppermute(values, axis, [(i, i ^ bit) for i in range(lax.axis_size(axi...]
    all_gather x1 -> x0, waiting for transfers between devices: 19 us -> none  [body(): normed_near = lax.all_gather(normed_near, 'head', axis=1, tiled=True)]
    all_to_all x1, waiting for transfers between devices: 0.01 us -> 10.3 us  [to_heads(): lax.all_to_all(values, 'head', split_axis=0, concat_axis=0, tiled=True)]
    pallas_call x0 -> x1, Pallas kernels: none -> 9.86 us  [qkv_blocks(): pl.pallas_call(kernel, out_shape=jax.ShapeDtypeStruct((cells, rows, 3 * w...]
    pallas_call x2, Pallas kernels: 24.2 us -> 33.9 us  [weight_blocks(): pl.pallas_call(kernel, out_shape=[jax.ShapeDtypeStruct(shape, jnp.bfloat1...]
    dot_general x3 -> x0, matrix products: 9.4 us -> none  [over_tokens(): return jnp.einsum('nd,ne->de', a, b, preferred_element_type=jnp.float32)]
    convert_element_type x2 -> x1, local copies, waits for them, and re-layouts: 7.31 us -> 0.34 us  [body(): qkv_part = add_up(qkv_part, swap(qkv_part, 'ctx', 1)).astype(jnp.bfloat16)]
  transfers between devices with their start and end apart: 27 -> 29, of which waited for: 11 -> 10; matrix products, arithmetic and copies ran while one was open for 23% -> 22% of each run, Pallas kernels for 8% -> 7%
where the time goes in v5:
time: 584 us; the launch traced here: 574 us
  waiting for transfers between devices  143 us (24%)
  Pallas kernels  105 us (18%)
  starting transfers between devices  82 us (14%)
  local copies, waits for them, and re-layouts  70.8 us (12%)
  matrix products  57.9 us (10%)
  other arithmetic  53.5 us (9%)
  blocking collectives  46.3 us (8%)
  between operations  14.8 us (3%)
    ppermute x24, waiting for transfers between devices, swap(): lax.ppermute(values, axis, [(i, i ^ bit) for i in range(lax.axis_size(axi...  123 us
    ppermute x24, starting transfers between devices, swap(): lax.ppermute(values, axis, [(i, i ^ bit) for i in range(lax.axis_size(axi...  58.1 us
    all_to_all x1, blocking collectives, to_heads(): lax.all_to_all(values, 'head', split_axis=0, concat_axis=0, tiled=True)  46.3 us
    pallas_call x2, Pallas kernels, weight_blocks(): pl.pallas_call(kernel, out_shape=[jax.ShapeDtypeStruct(shape, jnp.bfloat1...  33.9 us
    pallas_call x1, Pallas kernels, attend_back(): pl.pallas_call(back_kernel, out_shape=(jax.ShapeDtypeStruct((rows_all, wi...  32.4 us
    convert_element_type x9, other arithmetic, scatter_sum(): sent = add_up(*[t[half:] for t in terms]).astype(jnp.bfloat16)  30.2 us
    pallas_call x1, Pallas kernels, attend(): pl.pallas_call(attend_kernel, out_shape=(jax.ShapeDtypeStruct((rows_all,...  28.8 us
    all_to_all x3, starting transfers between devices, to_rows(): lax.all_to_all(values, 'head', split_axis=0, concat_axis=0, tiled=True)  16.4 us
  transfers between devices with their start and end apart: 29, of which 10 were waited for; matrix products, arithmetic and copies ran while one was open for 22% of the time, Pallas kernels for 7%

profile of v5, /device:TPU:0, one launch (start us, length us, event | category | flops | bytes accessed | tf_op | source)
XLA Modules:
  0.0 573.5 jit_solution(13049616322098151444)
XLA Ops:
  5.1 6.9 %fusion.2 = bf16[256,3360]{0,1:T(8,128)(2,1)S(1)} fusion(bf16[1120,3360]{1,0:T(8,128)(2,1)} %param.29, f32[3360]{0:T(1024)S(1)} %concatenate.12, bf16[1,256,1120]{2,1,0:T(8,128)(2,1)S(1)} %copy.134, f32[1120]{0:T(1024)S(1)} %copy-done.42, f32[1120]{0:T(1024)S(1)} %copy-done.27, f32[256]{0:T(256)S(1)} %fusion.56, f32[256]{0:T(256)S(1)} %broadcast_multiply_fusion.1, ...), kind=kOutput, calls=%fused_computation.10 | convolution fusion | flops 1930485760 | bytes 9849088 | tf_op jit(solution)/shard_map/dot_general | solution.py:489
  12.1 46.3 %all_to_all.30 = bf16[4,1,256,840]{2,3,1,0:T(8,128)(2,1)S(1)} all-to-all(bf16[4,1,256,840]{2,3,1,0:T(8,128)(2,1)S(1)} %bitcast.183), channel_id=1, replica_groups=mesh['cell'=4,'head'=4,'ctx'=2] {'head'}, dimensions={0} | all-to-all | bytes 3440640 | tf_op jit(solution)/shard_map/all_to_all | solution.py:498
  63.3 2.1 copy.138
  66.0 1.9 pad.4
  68.5 3.5 copy.137
  72.0 15.1 %collective-permute-done = bf16[1,1024,560]{1,2,0:T(8,128)(2,1)} collective-permute-done((bf16[1,1024,560]{1,2,0:T(8,128)(2,1)}, bf16[1,1024,560]{1,2,0:T(8,128)(2,1)}, u32[]{:S(2)}, u32[]{:S(2)}) %collective-permute-start) | collective-permute-done | bytes 1146912 | tf_op jit(solution)/shard_map/ppermute | solution.py:32
  87.2 2.4 copy.140
  89.6 28.8 %attend.1 = (bf16[1024,280]{1,0:T(8,128)(2,1)}, f32[4,280,256]{2,1,0:T(8,128)}, f32[4,5,1,256]{3,2,1,0:T(1,128)}) custom-call(s32[2]{0:T(128)} %pad_add_fusion.info, bf16[1024,840]{1,0:T(8,128)(2,1)} %bitcast.202, bf16[1024,560]{1,0:T(8,128)(2,1)} %bitcast.205), custom_call_target="tpu_custom_call" | custom-call | flops 21474836480 | bytes 8388608 | tf_op jit(solution)/shard_map/attend/pallas_call | solution.py:305
  118.4 2.2 copy.141
  120.6 4.4 all-to-all-start.1
  125.0 2.1 copy.144
  128.1 9.7 %all-to-all-done.1 = bf16[4,1,256,280]{2,3,1,0:T(8,128)(2,1)} async-done(((bf16[4,1,256,280]{2,3,1,0:T(8,128)(2,1)}), bf16[4,1,256,280]{2,3,1,0:T(8,128)(2,1)}, u32[]{:S(2)}, u32[]{:S(2)}) %all-to-all-start.1) | async-done | bytes 573472 | tf_op jit(solution)/shard_map/all_to_all | solution.py:504
  137.9 2.2 fusion.74
  141.5 9.8 %multiply_convert_fusion = (bf16[256,4480]{1,0:T(8,128)(2,1)}, f32[256,4480]{1,0:T(8,128)}) fusion(f32[4480]{0:T(1024)S(1)} %copy-done.48, bf16[256,1120]{1,0:T(8,128)(2,1)S(1)} %add_convert_fusion.refs_0_, bf16[1120,4480]{1,0:T(8,128)(2,1)} %param.36), kind=kOutput, calls=%fused_computation.19 | convolution fusion | flops 2580480000 | bytes 17507840 | tf_op jit(solution)/shard_map/dot_general | solution.py:525
  151.3 10.9 %weight_blocks.2 = (bf16[2,8,144,1120]{3,2,1,0:T(8,128)(2,1)}, bf16[2,8,144,1120]{3,2,1,0:T(8,128)(2,1)}) custom-call(s32[8]{0:T(128)} %fusion.60.left_at.right_at, s32[4]{0:T(128)} %broadcast_xor_fusion.right_at.left_at, bf16[256,1120]{1,0:T(8,128)(2,1)} %bitcast.182, bf16[256,4480]{1,0:T(8,128)(2,1)} %get-tuple-element.164.refs_1_), custom_call_target="tpu_custom_call" | custom-call | tf_op jit(solution)/shard_map/weight_blocks/pallas_call | solution.py:128
  162.2 2.1 copy.146.refs_2_
  164.3 12.2 %convert_reduce_fusion = (f32[4480]{0:T(1024)}, bf16[256,4480]{1,0:T(8,128)(2,1)S(1)}) fusion(f32[256,4480]{1,0:T(8,128)} %get-tuple-element.165, bf16[4480,1120]{0,1:T(8,128)(2,1)} %param.38, bf16[1,256,1120]{1,2,0:T(8,128)(2,1)} %param.40), kind=kOutput, calls=%fused_computation.18 | convolution fusion | flops 2594237952 | bytes 17507840 | tf_op jit(solution)/shard_map/nd,fd->nf/dot_general | solution.py:534
  176.5 4.7 fusion.1
  181.3 8.3 %fusion.76 = (f32[1120]{0:T(1024)}, f32[256,1120]{0,1:T(8,128)}) fusion(bf16[256,4480]{1,0:T(8,128)(2,1)S(1)} %get-tuple-element.38.refs_1_, bf16[1120,4480]{1,0:T(8,128)(2,1)} %param.36), kind=kOutput, calls=%fused_computation.164 | convolution fusion | flops 2569296896 | bytes 13480320 | tf_op jit(solution)/shard_map/nf,df->nd/dot_general | solution.py:542
  189.6 2.6 copy.145
  192.2 2.1 multiply_reduce_fusion
  197.7 23.0 %weight_blocks.3 = (bf16[2,8,288,700]{3,2,1,0:T(8,128)(2,1)}, bf16[2,8,288,700]{3,2,1,0:T(8,128)(2,1)}) custom-call(s32[4]{0:T(128)} %broadcast_xor_fusion.right_at.left_at, s32[8]{0:T(128)} %fusion.60.left_at.right_at, bf16[256,1120]{1,0:T(8,128)(2,1)} %copy-done.17, bf16[256,4480]{1,0:T(8,128)(2,1)} %copy-done.18, bf16[256,1120]{1,0:T(8,128)(2,1)} %copy.146.refs_2_, ...), custom_call_target="tpu_custom_call" | custom-call | tf_op jit(solution)/shard_map/weight_blocks/pallas_call | solution.py:128
  221.3 2.9 collective-permute-start.20
  225.5 2.0 collective-permute-start.10
  227.5 2.4 collective-permute-start.11
  229.9 2.8 convolution_convert_fusion
  232.7 3.6 all-to-all-start.2
  250.8 3.4 collective-permute-done.9
  254.2 17.2 %collective-permute-done.10 = bf16[1152,256]{1,0:T(8,128)(2,1)} collective-permute-done((bf16[1152,256]{1,0:T(8,128)(2,1)}, bf16[1152,256]{1,0:T(8,128)(2,1)}, u32[]{:S(2)}, u32[]{:S(2)}) %collective-permute-start.10) | collective-permute-done | bytes 589856 | tf_op jit(solution)/shard_map/ppermute | solution.py:32
  271.5 3.1 pad_maximum_fusion.near_ref
  274.6 7.0 %collective-permute-start.12 = (bf16[4,1152,256]{2,1,0:T(8,128)(2,1)}, bf16[4,1152,256]{2,1,0:T(8,128)(2,1)}, u32[]{:S(2)}, u32[]{:S(2)}) collective-permute-start(bf16[4,1152,256]{2,1,0:T(8,128)(2,1)} %pad_maximum_fusion.near_ref), channel_id=1, source_target_pairs={{0,1},{1,0},{2,3},{3,2},{4,5},{5,4},{6,7},{7,6},{8,9},{9,8},{10,11... | collective-permute-start | bytes 7077896 | tf_op jit(solution)/shard_map/ppermute | solution.py:32
  281.7 10.3 %all-to-all-done.2 = bf16[4,1,256,280]{2,3,1,0:T(8,128)(2,1)S(1)} async-done(((bf16[4,1,256,280]{2,3,1,0:T(8,128)(2,1)}), bf16[4,1,256,280]{2,3,1,0:T(8,128)(2,1)S(1)}, u32[]{:S(2)}, u32[]{:S(2)}) %all-to-all-start.2) | async-done | bytes 573472 | tf_op jit(solution)/shard_map/all_to_all | solution.py:498
  293.1 3.7 fusion.15
  296.9 7.1 %collective-permute-start.21 = (bf16[4,144,1120]{2,1,0:T(8,128)(2,1)}, bf16[4,144,1120]{2,1,0:T(8,128)(2,1)}, u32[]{:S(2)}, u32[]{:S(2)}) collective-permute-start(bf16[4,144,1120]{2,1,0:T(8,128)(2,1)} %fusion.15), channel_id=1, source_target_pairs={{0,1},{1,0},{2,3},{3,2},{4,5},{5,4},{6,7},{7,6},{8,9},{9,8},{10,11... | collective-permute-start | bytes 3870728 | tf_op jit(solution)/shard_map/ppermute | solution.py:32
  303.9 5.7 fusion
  309.6 32.4 %attend_back.1 = (bf16[1024,280]{1,0:T(8,128)(2,1)}, bf16[1024,560]{1,0:T(8,128)(2,1)}, bf16[1024,560]{1,0:T(8,128)(2,1)}) custom-call(s32[2]{0:T(128)} %pad_add_fusion.info, bf16[1024,840]{1,0:T(8,128)(2,1)} %bitcast.203, bf16[1024,560]{1,0:T(8,128)(2,1)} %bitcast.206, bf16[1024,280]{1,0:T(8,128)(2,1)} %bitcast.207, ...), custom_call_target="tpu_custom_call" | custom-call | flops 64424509440 | bytes 8388608 | tf_op jit(solution)/shard_map/attend_back/pallas_call | solution.py:404
  342.0 2.5 copy.148
  344.5 5.5 collective-permute-start.3
  350.0 7.8 %fusion.18 = bf16[1,256,1120]{2,1,0:T(8,128)(2,1)S(1)} fusion(f32[256,1120]{1,0:T(8,128)S(1)} %copy-done.5, bf16[256,4480]{1,0:T(8,128)(2,1)} %get-tuple-element.164.refs_1_, bf16[4480,1120]{0,1:T(8,128)(2,1)} %param.38, f32[1120]{0:T(1024)S(1)} %copy-done.50), kind=kOutput, calls=%fused_computation.35 | convolution fusion | flops 2569871360 | bytes 14053760 | tf_op jit(solution)/shard_map/dot_general | solution.py:527
  358.9 3.7 all-to-all-start.3
  362.6 2.9 fusion.24
  365.5 16.1 %collective-permute-start.22 = (bf16[2,144,1120]{2,1,0:T(8,128)(2,1)}, bf16[2,144,1120]{2,1,0:T(8,128)(2,1)}, u32[]{:S(2)}, u32[]{:S(2)}) collective-permute-start(bf16[2,144,1120]{2,1,0:T(8,128)(2,1)} %fusion.24), channel_id=1, source_target_pairs={{0,4},{2,6},{4,0},{6,2},{1,5},{3,7},{5,1},{7,3},{8,12},{10,14},{12... | collective-permute-start | bytes 1935368 | tf_op jit(solution)/shard_map/ppermute | solution.py:32
  381.6 9.9 %qkv_blocks.1 = bf16[4,288,840]{2,1,0:T(8,128)(2,1)} custom-call(s32[4]{0:T(128)} %gather_fusion, s32[4]{0:T(128)} %xor_multiply_fusion.row, bf16[4,1152,256]{2,1,0:T(8,128)(2,1)} %pad_maximum_fusion.near_ref, bf16[4,1152,256]{2,1,0:T(8,128)(2,1)} %collective-permute-done.12.far_ref, bf16[1024,280]{1,0:T(8,128)(2,1)} %get-tuple-element.46.dq_ref, ...), custom_call_target="tpu_custom_call" | custom-call | tf_op jit(solution)/shard_map/qkv_blocks/pallas_call | solution.py:177
  391.4 2.3 slice.393
  393.8 2.4 copy.149
  396.1 2.0 fusion.16
  399.7 8.3 %all-to-all-start.4 = ((bf16[4,1,256,560]{2,3,1,0:T(8,128)(2,1)}), bf16[4,1,256,560]{2,3,1,0:T(8,128)(2,1)}, u32[]{:S(2)}, u32[]{:S(2)}) async-start(bf16[4,1,256,560]{2,3,1,0:T(8,128)(2,1)} %copy.151), calls=%async_computation.4 | async-start | bytes 2293760 | tf_op jit(solution)/shard_map/all_to_all | solution.py:504
  413.4 1.8 slice_bitcast_fusion
  420.5 2.3 fusion.41
  422.9 3.0 collective-permute-start.23
  428.6 36.7 %collective-permute-done.14 = bf16[1,288,840]{2,1,0:T(8,128)(2,1)S(1)} collective-permute-done((bf16[1,288,840]{2,1,0:T(8,128)(2,1)S(1)}, bf16[1,288,840]{2,1,0:T(8,128)(2,1)S(1)}, u32[]{:S(2)}, u32[]{:S(2)}) %collective-permute-start.14) | collective-permute-done | bytes 483872 | tf_op jit(solution)/shard_map/ppermute | solution.py:32
  469.2 6.9 %fusion.75 = (f32[1120]{0:T(1024)S(1)}, f32[256,1120]{0,1:T(8,128)}) fusion(bf16[1120,3360]{1,0:T(8,128)(2,1)} %param.29, bf16[256,2240]{0,1:T(8,128)(2,1)S(1)} %bitcast.191, bf16[256,1120]{0,1:T(8,128)(2,1)S(1)} %bitcast.199), kind=kOutput, calls=%fused_computation.163 | convolution fusion | flops 1930484608 | bytes 10398080 | tf_op jit(solution)/shard_map/ne,de->nd/dot_general | solution.py:598
  478.8 4.6 fusion.11
  491.4 3.9 all-to-all-start.5
  495.5 21.3 %collective-permute-done.17 = bf16[4,288,700]{2,1,0:T(8,128)(2,1)} collective-permute-done((bf16[4,288,700]{2,1,0:T(8,128)(2,1)}, bf16[4,288,700]{2,1,0:T(8,128)(2,1)}, u32[]{:S(2)}, u32[]{:S(2)}) %collective-permute-start.17) | collective-permute-done | bytes 1612832 | tf_op jit(solution)/shard_map/ppermute | solution.py:32
  516.8 3.3 fusion.21
  520.7 2.1 fusion.46
  522.8 1.8 slice.402
  526.5 2.3 collective-permute-done.6
  528.8 2.4 collective-permute-start.7
  531.3 24.3 %collective-permute-done.7 = f32[1,32,280]{2,1,0:T(8,128)S(1)} collective-permute-done((f32[1,32,280]{2,1,0:T(8,128)S(1)}, f32[1,32,280]{2,1,0:T(8,128)S(1)}, u32[]{:S(2)}, u32[]{:S(2)}) %collective-permute-start.7) | collective-permute-done | bytes 35872 | tf_op jit(solution)/shard_map/ppermute | solution.py:32
  555.7 1.8 fusion.31
  557.5 2.1 collective-permute-start.19
  566.8 2.7 collective-permute-done.19
  (238 shorter events, 64.8 us)
Async XLA Ops:
  0.6 137.2 %copy-start = (bf16[1120,1120]{1,0:T(8,128)(2,1)S(1)}, bf16[1120,1120]{1,0:T(8,128)(2,1)}, u32[]{:S(2)}) copy-start(bf16[1120,1120]{1,0:T(8,128)(2,1)} %param.32) | copy-start | bytes 7526404
  0.7 4.3 copy-start.44
  0.7 4.3 copy-start.45
  0.7 4.4 copy-start.27
  0.7 4.4 copy-start.42
  4.1 58.1 %copy-start.30 = (f32[256]{0:T(256)}, f32[256]{0:T(256)S(1)}, u32[]{:S(2)}) copy-start(f32[256]{0:T(256)S(1)} %broadcast_multiply_fusion.1) | copy-start | bytes 3076
  4.9 57.2 %copy-start.36 = (f32[256]{0:T(256)}, f32[256]{0:T(256)S(1)}, u32[]{:S(2)}) copy-start(f32[256]{0:T(256)S(1)} %fusion.56) | copy-start | bytes 3076
  60.6 26.5 %collective-permute-start = (bf16[1,1024,560]{1,2,0:T(8,128)(2,1)}, bf16[1,1024,560]{1,2,0:T(8,128)(2,1)}, u32[]{:S(2)}, u32[]{:S(2)}) collective-permute-start(bf16[1,1024,560]{1,2,0:T(8,128)(2,1)} %slice.384), channel_id=1, source_target_pairs={{0,1},{1,0},{2,3},{3,2},{4,5},{5,4},{6,7},{7,6},{8,9},{9,8},{10,11... | collective-permute-start | bytes 3440648 | tf_op jit(solution)/shard_map/ppermute | solution.py:32
  118.3 9.3 %copy-start.2 = (s32[4]{0:T(128)S(1)}, s32[4]{0:T(128)}, u32[]{:S(2)}) copy-start(s32[4]{0:T(128)} %constant.127.clone) | copy-start | bytes 52
  118.3 19.5 %copy-start.49 = (f32[1120]{0:T(1024)S(1)}, f32[1120]{0:T(1024)}, u32[]{:S(2)}) copy-start(f32[1120]{0:T(1024)} %param.33) | copy-start | bytes 13444
  120.6 17.3 %all-to-all-start.1 = ((bf16[4,1,256,280]{2,3,1,0:T(8,128)(2,1)}), bf16[4,1,256,280]{2,3,1,0:T(8,128)(2,1)}, u32[]{:S(2)}, u32[]{:S(2)}) async-start(bf16[4,1,256,280]{2,3,1,0:T(8,128)(2,1)} %copy.141), calls=%async_computation.1 | async-start | bytes 1146880 | tf_op jit(solution)/shard_map/all_to_all | solution.py:504
  137.9 3.3 copy-start.43
  141.5 9.8 %copy-start.17 = (bf16[256,1120]{1,0:T(8,128)(2,1)}, bf16[256,1120]{1,0:T(8,128)(2,1)S(1)}, u32[]{:S(2)}) copy-start(bf16[256,1120]{1,0:T(8,128)(2,1)S(1)} %add_convert_fusion.refs_0_) | copy-start | bytes 1720324
  162.2 14.4 %collective-permute-start.1 = (bf16[16,144,1120]{2,1,0:T(8,128)(2,1)}, bf16[16,144,1120]{2,1,0:T(8,128)(2,1)}, u32[]{:S(2)}, u32[]{:S(2)}) collective-permute-start(bf16[16,144,1120]{2,1,0:T(8,128)(2,1)} %bitcast.212), channel_id=1, source_target_pairs={{0,8},{8,0},{16,24},{24,16},{1,9},{9,1},{17,25},{25,17},{2,10},{10... | collective-permute-start | bytes 15482888 | tf_op jit(solution)/shard_map/ppermute | solution.py:32
  164.3 12.2 %slice-start.1 = ((s8[5308416]{0:T(1024)(128)(4,1)}), s8[4194304]{0:T(1024)(128)(4,1)S(1)}, s32[]{:S(2)}) async-start(s8[5308416]{0:T(1024)(128)(4,1)} %bitcast.184), calls=%async_computation.7 | async-start | bytes 8388608
  164.3 12.2 %slice-start.2 = ((s8[5308416]{0:T(1024)(128)(4,1)}), s8[1114112]{0:T(1024)(128)(4,1)S(1)}, s32[]{:S(2)}) async-start(s8[5308416]{0:T(1024)(128)(4,1)} %bitcast.184), calls=%async_computation.8 | async-start | bytes 2228224
  176.5 4.7 copy-start.18
  195.0 25.8 %copy-start.40 = (f32[256]{0:T(256)}, f32[256]{0:T(256)S(1)}, u32[]{:S(2)}) copy-start(f32[256]{0:T(256)S(1)} %negate_multiply_fusion.1) | copy-start | bytes 3076
  220.8 83.1 %collective-permute-start.2 = (bf16[16,288,700]{2,1,0:T(8,128)(2,1)}, bf16[16,288,700]{2,1,0:T(8,128)(2,1)}, u32[]{:S(2)}, u32[]{:S(2)}) collective-permute-start(bf16[16,288,700]{2,1,0:T(8,128)(2,1)} %bitcast.211), channel_id=1, source_target_pairs={{0,8},{8,0},{16,24},{24,16},{1,9},{9,1},{17,25},{25,17},{2,10},{10... | collective-permute-start | bytes 19353608 | tf_op jit(solution)/shard_map/ppermute | solution.py:32
  221.3 71.8 %collective-permute-start.20 = (bf16[8,144,1120]{2,1,0:T(8,128)(2,1)}, bf16[8,144,1120]{2,1,0:T(8,128)(2,1)}, u32[]{:S(2)}, u32[]{:S(2)}) collective-permute-start(bf16[8,144,1120]{2,1,0:T(8,128)(2,1)} %fusion.1), channel_id=1, source_target_pairs={{0,16},{8,24},{16,0},{24,8},{1,17},{9,25},{17,1},{25,9},{2,18},{10... | collective-permute-start | bytes 7741448 | tf_op jit(solution)/shard_map/ppermute | solution.py:32
  225.5 28.7 %collective-permute-start.9 = (bf16[1152,256]{1,0:T(8,128)(2,1)}, bf16[1152,256]{1,0:T(8,128)(2,1)}, u32[]{:S(2)}, u32[]{:S(2)}) collective-permute-start(bf16[1152,256]{1,0:T(8,128)(2,1)} %bitcast.194), channel_id=1, source_target_pairs={{0,2},{2,0},{4,6},{6,4},{1,3},{3,1},{5,7},{7,5},{8,10},{10,8},{12,... | collective-permute-start | bytes 1769480 | tf_op jit(solution)/shard_map/ppermute | solution.py:32
  225.5 46.0 %collective-permute-start.10 = (bf16[1152,256]{1,0:T(8,128)(2,1)}, bf16[1152,256]{1,0:T(8,128)(2,1)}, u32[]{:S(2)}, u32[]{:S(2)}) collective-permute-start(bf16[1152,256]{1,0:T(8,128)(2,1)} %bitcast.195), channel_id=1, source_target_pairs={{0,4},{2,6},{4,0},{6,2},{1,5},{3,7},{5,1},{7,3},{8,12},{10,14},{12... | collective-permute-start | bytes 1769480 | tf_op jit(solution)/shard_map/ppermute | solution.py:32
  227.5 44.0 %collective-permute-start.11 = (bf16[1152,256]{1,0:T(8,128)(2,1)}, bf16[1152,256]{1,0:T(8,128)(2,1)}, u32[]{:S(2)}, u32[]{:S(2)}) collective-permute-start(bf16[1152,256]{1,0:T(8,128)(2,1)} %bitcast.196), channel_id=1, source_target_pairs={{0,6},{2,4},{4,2},{6,0},{1,7},{3,5},{5,3},{7,1},{8,14},{10,12},{12... | collective-permute-start | bytes 1769480 | tf_op jit(solution)/shard_map/ppermute | solution.py:32
  232.7 38.8 %copy-start.16 = (bf16[4,288,256]{2,1,0:T(8,128)(2,1)S(1)}, bf16[4,288,256]{2,1,0:T(8,128)(2,1)}, u32[]{:S(2)}) copy-start(bf16[4,288,256]{2,1,0:T(8,128)(2,1)} %pad.4) | copy-start | bytes 1769476
  232.7 59.2 %all-to-all-start.2 = ((bf16[4,1,256,280]{2,3,1,0:T(8,128)(2,1)}), bf16[4,1,256,280]{2,3,1,0:T(8,128)(2,1)S(1)}, u32[]{:S(2)}, u32[]{:S(2)}) async-start(bf16[4,1,256,280]{2,3,1,0:T(8,128)(2,1)} %bitcast.209), calls=%async_computation.2 | async-start | bytes 1146880 | tf_op jit(solution)/shard_map/all_to_all | solution.py:498
  274.6 107.0 %collective-permute-start.12 = (bf16[4,1152,256]{2,1,0:T(8,128)(2,1)}, bf16[4,1152,256]{2,1,0:T(8,128)(2,1)}, u32[]{:S(2)}, u32[]{:S(2)}) collective-permute-start(bf16[4,1152,256]{2,1,0:T(8,128)(2,1)} %pad_maximum_fusion.near_ref), channel_id=1, source_target_pairs={{0,1},{1,0},{2,3},{3,2},{4,5},{5,4},{6,7},{7,6},{8,9},{9,8},{10,11... | collective-permute-start | bytes 7077896 | tf_op jit(solution)/shard_map/ppermute | solution.py:32
  296.9 65.7 %collective-permute-start.21 = (bf16[4,144,1120]{2,1,0:T(8,128)(2,1)}, bf16[4,144,1120]{2,1,0:T(8,128)(2,1)}, u32[]{:S(2)}, u32[]{:S(2)}) collective-permute-start(bf16[4,144,1120]{2,1,0:T(8,128)(2,1)} %fusion.15), channel_id=1, source_target_pairs={{0,1},{1,0},{2,3},{3,2},{4,5},{5,4},{6,7},{7,6},{8,9},{9,8},{10,11... | collective-permute-start | bytes 3870728 | tf_op jit(solution)/shard_map/ppermute | solution.py:32
  342.0 8.0 %copy-start.5 = (f32[256,1120]{1,0:T(8,128)S(1)}, f32[256,1120]{1,0:T(8,128)}, u32[]{:S(2)}) copy-start(f32[256,1120]{1,0:T(8,128)} %copy-done.3) | copy-start | bytes 3440644
  342.0 8.0 %copy-start.50 = (f32[1120]{0:T(1024)S(1)}, f32[1120]{0:T(1024)}, u32[]{:S(2)}) copy-start(f32[1120]{0:T(1024)} %param.39) | copy-start | bytes 13444
  344.5 13.3 %copy-start.15 = (bf16[1024,280]{1,0:T(8,128)(2,1)S(1)}, bf16[1024,280]{1,0:T(8,128)(2,1)}, u32[]{:S(2)}) copy-start(bf16[1024,280]{1,0:T(8,128)(2,1)} %get-tuple-element.46.dq_ref) | copy-start | bytes 1720324
  344.5 49.2 %collective-permute-start.3 = (bf16[1,1024,560]{1,2,0:T(8,128)(2,1)}, bf16[1,1024,560]{1,2,0:T(8,128)(2,1)}, u32[]{:S(2)}, u32[]{:S(2)}) collective-permute-start(bf16[1,1024,560]{1,2,0:T(8,128)(2,1)} %copy.148), channel_id=1, source_target_pairs={{0,1},{1,0},{2,3},{3,2},{4,5},{5,4},{6,7},{7,6},{8,9},{9,8},{10,11... | collective-permute-start | bytes 3440648 | tf_op jit(solution)/shard_map/ppermute | solution.py:32
  358.9 39.3 %all-to-all-start.3 = ((bf16[4,1,256,280]{2,3,1,0:T(8,128)(2,1)}), bf16[4,1,256,280]{2,3,1,0:T(8,128)(2,1)S(1)}, u32[]{:S(2)}, u32[]{:S(2)}) async-start(bf16[4,1,256,280]{2,3,1,0:T(8,128)(2,1)} %copy.150), calls=%async_computation.3 | async-start | bytes 1146880 | tf_op jit(solution)/shard_map/all_to_all | solution.py:504
  365.5 55.1 %collective-permute-start.22 = (bf16[2,144,1120]{2,1,0:T(8,128)(2,1)}, bf16[2,144,1120]{2,1,0:T(8,128)(2,1)}, u32[]{:S(2)}, u32[]{:S(2)}) collective-permute-start(bf16[2,144,1120]{2,1,0:T(8,128)(2,1)} %fusion.24), channel_id=1, source_target_pairs={{0,4},{2,6},{4,0},{6,2},{1,5},{3,7},{5,1},{7,3},{8,12},{10,14},{12... | collective-permute-start | bytes 1935368 | tf_op jit(solution)/shard_map/ppermute | solution.py:32
  381.5 97.3 %collective-permute-start.16 = (bf16[8,288,700]{2,1,0:T(8,128)(2,1)}, bf16[8,288,700]{2,1,0:T(8,128)(2,1)}, u32[]{:S(2)}, u32[]{:S(2)}) collective-permute-start(bf16[8,288,700]{2,1,0:T(8,128)(2,1)} %fusion), channel_id=1, source_target_pairs={{0,16},{8,24},{16,0},{24,8},{1,17},{9,25},{17,1},{25,9},{2,18},{10... | collective-permute-start | bytes 9676808 | tf_op jit(solution)/shard_map/ppermute | solution.py:32
  393.7 25.0 %collective-permute-start.13 = (bf16[2,288,840]{2,1,0:T(8,128)(2,1)}, bf16[2,288,840]{2,1,0:T(8,128)(2,1)}, u32[]{:S(2)}, u32[]{:S(2)}) collective-permute-start(bf16[2,288,840]{2,1,0:T(8,128)(2,1)} %slice.393), channel_id=1, source_target_pairs={{0,8},{8,0},{16,24},{24,16},{1,9},{9,1},{17,25},{25,17},{2,10},{10... | collective-permute-start | bytes 2903048 | tf_op jit(solution)/shard_map/ppermute | solution.py:32
  399.7 9.3 %copy-start.35 = (f32[4480]{0:T(1024)S(1)}, f32[4480]{0:T(1024)}, u32[]{:S(2)}) copy-start(f32[4480]{0:T(1024)} %get-tuple-element.170) | copy-start | bytes 53764
  399.7 10.5 %copy-start.32 = (f32[1120]{0:T(1024)S(1)}, f32[1120]{0:T(1024)}, u32[]{:S(2)}) copy-start(f32[1120]{0:T(1024)} %get-tuple-element.144) | copy-start | bytes 13444
  399.7 12.0 %copy-start.46 = (f32[1120]{0:T(1024)S(1)}, f32[1120]{0:T(1024)}, u32[]{:S(2)}) copy-start(f32[1120]{0:T(1024)} %get-tuple-element.168) | copy-start | bytes 13444
  399.7 68.1 %all-to-all-start.4 = ((bf16[4,1,256,560]{2,3,1,0:T(8,128)(2,1)}), bf16[4,1,256,560]{2,3,1,0:T(8,128)(2,1)}, u32[]{:S(2)}, u32[]{:S(2)}) async-start(bf16[4,1,256,560]{2,3,1,0:T(8,128)(2,1)} %copy.151), calls=%async_computation.4 | async-start | bytes 2293760 | tf_op jit(solution)/shard_map/all_to_all | solution.py:504
  410.2 8.6 %copy-start.12 = (bf16[4,288,840]{2,1,0:T(8,128)(2,1)S(1)}, bf16[4,288,840]{2,1,0:T(8,128)(2,1)}, u32[]{:S(2)}) copy-start(bf16[4,288,840]{2,1,0:T(8,128)(2,1)} %qkv_blocks.1) | copy-start | bytes 5806084
  419.9 45.5 %collective-permute-start.14 = (bf16[1,288,840]{2,1,0:T(8,128)(2,1)S(1)}, bf16[1,288,840]{2,1,0:T(8,128)(2,1)S(1)}, u32[]{:S(2)}, u32[]{:S(2)}) collective-permute-start(bf16[1,288,840]{2,1,0:T(8,128)(2,1)S(1)} %add_convert_fusion.2), channel_id=1, source_target_pairs={{0,16},{8,24},{16,0},{24,8},{1,17},{9,25},{17,1},{25,9},{2,18},{10... | collective-permute-start | bytes 1451528 | tf_op jit(solution)/shard_map/ppermute | solution.py:32
  422.9 42.5 %slice-start = ((bf16[4,288,840]{2,1,0:T(8,128)(2,1)}), bf16[1,288,840]{2,1,0:T(8,128)(2,1)S(1)}, s32[]{:S(2)}) async-start(bf16[4,288,840]{2,1,0:T(8,128)(2,1)} %qkv_blocks.1), calls=%async_computation.6 | async-start | bytes 1032192 | tf_op jit(solution)/shard_map/slice | solution.py:205
  422.9 97.9 %collective-permute-start.23 = (bf16[1,144,1120]{2,1,0:T(8,128)(2,1)}, bf16[1,144,1120]{2,1,0:T(8,128)(2,1)}, u32[]{:S(2)}, u32[]{:S(2)}) collective-permute-start(bf16[1,144,1120]{2,1,0:T(8,128)(2,1)} %fusion.41), channel_id=1, source_target_pairs={{0,2},{2,0},{4,6},{6,4},{1,3},{3,1},{5,7},{7,5},{8,10},{10,8},{12,... | collective-permute-start | bytes 967688 | tf_op jit(solution)/shard_map/ppermute | solution.py:32
  428.6 40.5 %copy-start.20 = (bf16[4,1,256,280]{2,3,1,0:T(8,128)(2,1)S(1)}, bf16[4,1,256,280]{2,3,1,0:T(8,128)(2,1)}, u32[]{:S(2)}) copy-start(bf16[4,1,256,280]{2,3,1,0:T(8,128)(2,1)} %copy-done.19) | copy-start | bytes 1720324
  466.3 20.9 %collective-permute-start.15 = (bf16[280,840]{1,0:T(8,128)(2,1)}, bf16[280,840]{1,0:T(8,128)(2,1)}, u32[]{:S(2)}, u32[]{:S(2)}) collective-permute-start(bf16[280,840]{1,0:T(8,128)(2,1)} %fusion.51), channel_id=1, source_target_pairs={{0,1},{1,0},{2,3},{3,2},{4,5},{5,4},{6,7},{7,6},{8,9},{9,8},{10,11... | collective-permute-start | bytes 1411208 | tf_op jit(solution)/shard_map/ppermute | solution.py:32
  469.1 6.9 %copy-start.13 = (bf16[1,256,2,4,280]{1,4,3,2,0:T(8,128)(2,1)}, bf16[1,256,2,4,280]{1,4,3,2,0:T(8,128)(2,1)S(1)}, u32[]{:S(2)}) copy-start(bf16[1,256,2,4,280]{1,4,3,2,0:T(8,128)(2,1)S(1)} %copy.152) | copy-start | bytes 3440644
  478.8 5.2 copy-start.14
  478.8 5.2 copy-start.21
  478.8 5.7 %copy-start.11 = (bf16[1,256,1120]{2,1,0:T(8,128)(2,1)S(1)}, bf16[1,256,1120]{2,1,0:T(8,128)(2,1)}, u32[]{:S(2)}) copy-start(bf16[1,256,1120]{2,1,0:T(8,128)(2,1)} %copy.144) | copy-start | bytes 1720324
  483.4 33.4 %collective-permute-start.17 = (bf16[4,288,700]{2,1,0:T(8,128)(2,1)}, bf16[4,288,700]{2,1,0:T(8,128)(2,1)}, u32[]{:S(2)}, u32[]{:S(2)}) collective-permute-start(bf16[4,288,700]{2,1,0:T(8,128)(2,1)} %fusion.11), channel_id=1, source_target_pairs={{0,1},{1,0},{2,3},{3,2},{4,5},{5,4},{6,7},{7,6},{8,9},{9,8},{10,11... | collective-permute-start | bytes 4838408 | tf_op jit(solution)/shard_map/ppermute | solution.py:32
  486.1 9.2 %collective-permute-start.4 = (f32[2,32,280]{2,1,0:T(8,128)S(1)}, f32[2,32,280]{2,1,0:T(8,128)S(1)}, u32[]{:S(2)}, u32[]{:S(2)}) collective-permute-start(f32[2,32,280]{2,1,0:T(8,128)S(1)} %constant_dynamic-slice_fusion.6), channel_id=1, source_target_pairs={{0,16},{8,24},{16,0},{24,8},{1,17},{9,25},{17,1},{25,9},{2,18},{10... | collective-permute-start | bytes 215048 | tf_op jit(solution)/shard_map/ppermute | solution.py:32
  491.4 34.4 %all-to-all-start.5 = ((bf16[4,2,280,140]{2,1,3,0:T(2,128)(2,1)}), bf16[4,2,280,140]{2,1,3,0:T(2,128)(2,1)S(1)}, u32[]{:S(2)}, u32[]{:S(2)}) async-start(bf16[4,2,280,140]{2,1,3,0:T(2,128)(2,1)} %copy.158), calls=%async_computation.5 | async-start | bytes 1720320 | tf_op jit(solution)/shard_map/all_to_all | solution.py:585
  495.4 25.4 %copy-start.23 = (bf16[1,144,1120]{2,1,0:T(8,128)(2,1)S(1)}, bf16[1,144,1120]{2,1,0:T(8,128)(2,1)}, u32[]{:S(2)}) copy-start(bf16[1,144,1120]{2,1,0:T(8,128)(2,1)} %slice.427) | copy-start | bytes 967684
  495.4 25.4 %copy-start.24 = (bf16[1,144,1120]{2,1,0:T(8,128)(2,1)S(1)}, bf16[1,144,1120]{2,1,0:T(8,128)(2,1)}, u32[]{:S(2)}) copy-start(bf16[1,144,1120]{2,1,0:T(8,128)(2,1)} %slice.428) | copy-start | bytes 967684
  495.4 25.3 %copy-start.25 = (bf16[1,144,1120]{2,1,0:T(8,128)(2,1)S(1)}, bf16[1,144,1120]{2,1,0:T(8,128)(2,1)}, u32[]{:S(2)}) copy-start(bf16[1,144,1120]{2,1,0:T(8,128)(2,1)} %slice.431) | copy-start | bytes 967684
  495.4 25.3 %copy-start.26 = (bf16[1,144,1120]{2,1,0:T(8,128)(2,1)S(1)}, bf16[1,144,1120]{2,1,0:T(8,128)(2,1)}, u32[]{:S(2)}) copy-start(bf16[1,144,1120]{2,1,0:T(8,128)(2,1)} %slice.435) | copy-start | bytes 967684
  495.4 29.2 %collective-permute-start.5 = (f32[1,32,280]{2,1,0:T(8,128)S(1)}, f32[1,32,280]{2,1,0:T(8,128)S(1)}, u32[]{:S(2)}, u32[]{:S(2)}) collective-permute-start(f32[1,32,280]{2,1,0:T(8,128)S(1)} %constant_dynamic-slice_fusion.5), channel_id=1, source_target_pairs={{0,8},{8,0},{16,24},{24,16},{1,9},{9,1},{17,25},{25,17},{2,10},{10... | collective-permute-start | bytes 107528 | tf_op jit(solution)/shard_map/ppermute | solution.py:32
  520.2 35.5 %collective-permute-start.18 = (bf16[2,288,700]{2,1,0:T(8,128)(2,1)}, bf16[2,288,700]{2,1,0:T(8,128)(2,1)}, u32[]{:S(2)}, u32[]{:S(2)}) collective-permute-start(bf16[2,288,700]{2,1,0:T(8,128)(2,1)} %fusion.21), channel_id=1, source_target_pairs={{0,4},{2,6},{4,0},{6,2},{1,5},{3,7},{5,1},{7,3},{8,12},{10,14},{12... | collective-permute-start | bytes 2419208 | tf_op jit(solution)/shard_map/ppermute | solution.py:32
  524.6 4.2 collective-permute-start.6
  528.8 26.8 %collective-permute-start.7 = (f32[1,32,280]{2,1,0:T(8,128)S(1)}, f32[1,32,280]{2,1,0:T(8,128)S(1)}, u32[]{:S(2)}, u32[]{:S(2)}) collective-permute-start(f32[1,32,280]{2,1,0:T(8,128)S(1)} %add.337), channel_id=1, source_target_pairs={{0,4},{2,6},{4,0},{6,2},{1,5},{3,7},{5,1},{7,3},{8,12},{10,14},{12... | collective-permute-start | bytes 107528 | tf_op jit(solution)/shard_map/ppermute | solution.py:32
  555.6 6.1 %collective-permute-start.8 = (f32[1,32,280]{2,1,0:T(8,128)S(1)}, f32[1,32,280]{2,1,0:T(8,128)S(1)}, u32[]{:S(2)}, u32[]{:S(2)}) collective-permute-start(f32[1,32,280]{2,1,0:T(8,128)S(1)} %add.338), channel_id=1, source_target_pairs={{0,2},{2,0},{4,6},{6,4},{1,3},{3,1},{5,7},{7,5},{8,10},{10,8},{12,... | collective-permute-start | bytes 107528 | tf_op jit(solution)/shard_map/ppermute | solution.py:32
  557.5 12.0 %collective-permute-start.19 = (bf16[1,288,700]{2,1,0:T(8,128)(2,1)S(1)}, bf16[1,288,700]{2,1,0:T(8,128)(2,1)}, u32[]{:S(2)}, u32[]{:S(2)}) collective-permute-start(bf16[1,288,700]{2,1,0:T(8,128)(2,1)S(1)} %fusion.31), channel_id=1, source_target_pairs={{0,2},{2,0},{4,6},{6,4},{1,3},{3,1},{5,7},{7,5},{8,10},{10,8},{12,... | collective-permute-start | bytes 1209608 | tf_op jit(solution)/shard_map/ppermute | solution.py:32
  561.7 7.8 %copy-start.22 = (bf16[1,288,700]{2,1,0:T(8,128)(2,1)S(1)}, bf16[1,288,700]{2,1,0:T(8,128)(2,1)}, u32[]{:S(2)}) copy-start(bf16[1,288,700]{2,1,0:T(8,128)(2,1)} %slice_bitcast_fusion) | copy-start | bytes 1209604
  569.5 3.5 copy-start.1
  (19 other events, 29.7 us)

commit v6 on v5

--- a/solution.py
+++ b/solution.py
@@ -18,6 +18,9 @@
 LOG2E = math.log2(math.e)
 
 
+CELL, HEAD, CTX = "cell", "head", "ctx"
+
+
 def layer_norm(values, gain_row, shift_row):
     center = values - jnp.mean(values, axis=-1, keepdims=True)
     spread = jnp.mean(center * center, axis=-1, keepdims=True)
@@ -56,12 +59,12 @@
 
 
 def weight_blocks(pairs, by_cell_left):
-    cells, groups, halves = lax.axis_size("cell"), lax.axis_size("head"), lax.axis_size("ctx")
+    cells, groups, halves = lax.axis_size(CELL), lax.axis_size(HEAD), lax.axis_size(CTX)
     parts, half_cells = groups * halves, cells // 2
-    cell_ids = relative_order(cells, [b for _, b in bits_of("cell")]) ^ lax.axis_index("cell")
+    cell_ids = relative_order(cells, [b for _, b in bits_of(CELL)]) ^ lax.axis_index(CELL)
     places = jnp.arange(parts, dtype=jnp.int32)
-    part_ids = ((places % groups) ^ lax.axis_index("head")) * halves + (
-        (places // groups) ^ lax.axis_index("ctx")
+    part_ids = ((places % groups) ^ lax.axis_index(HEAD)) * halves + (
+        (places // groups) ^ lax.axis_index(CTX)
     )
     left_ids, right_ids = (cell_ids, part_ids) if by_cell_left else (part_ids, cell_ids)
     left_count, right_count = (cells, parts) if by_cell_left else (parts, cells)
@@ -138,24 +141,24 @@
             out_specs=specs,
             scratch_shapes=scratch,
         ),
-        name="weight_blocks",
+        name="wb",
     )(left_ids, right_ids, *flat)
     return kept.reshape(-1, rows, cols), sent.reshape(-1, rows, cols)
 
 
 def qkv_blocks(near, far, dq, dkv, dkv_far):
-    cells = lax.axis_size("cell")
-    steps = [b for _, b in bits_of("cell")]
+    cells = lax.axis_size(CELL)
+    steps = [b for _, b in bits_of(CELL)]
     rel = np.zeros((cells,), np.int32)
     for s, bit in enumerate(steps):
         rel += ((np.arange(cells) >> (len(steps) - 1 - s)) & 1).astype(np.int32) * bit
     place_at = jnp.asarray(np.argsort(rel).astype(np.int32))[
-        jnp.arange(cells, dtype=jnp.int32) ^ lax.axis_index("cell")
+        jnp.arange(cells, dtype=jnp.int32) ^ lax.axis_index(CELL)
     ]
     pieces, wide, tokens = near.shape
     rows = wide // cells
     width = dq.shape[1]
-    row_at = (jnp.arange(pieces, dtype=jnp.int32) ^ lax.axis_index("head")) * tokens
+    row_at = (jnp.arange(pieces, dtype=jnp.int32) ^ lax.axis_index(HEAD)) * tokens
 
     def kernel(place, row, near_ref, far_ref, dq_ref, dkv_ref, far_grad, out, tall, q, kv):
         for p in range(pieces):
@@ -184,7 +187,7 @@
             pltpu.VMEM((pieces * tokens, width), jnp.bfloat16),
             pltpu.VMEM((2 * pieces * tokens, 2 * width), jnp.bfloat16),
         ],
-        name="qkv_blocks",
+        name="qb",
     )(place_at, row_at, near, far, dq, dkv, dkv_far)
 
 
@@ -209,8 +212,8 @@
     return add_up(*terms)[0]
 
 
-def head_dims(qkv_ref):
-    width = qkv_ref.shape[-1] // 3
+def head_dims(query):
+    width = query.shape[-1]
     return width, width // HD
 
 
@@ -239,23 +242,24 @@
     visit(i, (2 * i + half) * rows, True)
 
 
-def attend_kernel(info, qkv, kv_other, out, out_t, logs, q_t, k_n, v_t, acc, m_ref, l_ref):
-    width, heads = head_dims(qkv)
+def attend_kernel(info, query, kv_near, kv_other, out, out_t, logs, q_t, k_n, v_t, acc, m_ref, l_ref):
+    width, heads = head_dims(query)
     blocks, rows = q_t.shape[0], q_t.shape[-1]
     seq_len, half = info[0], info[1]
     factor = LOG2E / math.sqrt(HD)
 
     def prepare(b, carry):
         at = pl.ds(pl.multiple_of(b * rows, rows), rows)
-        mine = qkv[at, :]
-        mine_t = mine.astype(jnp.float32).T
+        query_t = query[at, :].astype(jnp.float32).T
+        mine = kv_near[at, :]
+        mine_t = mine[:, width:].astype(jnp.float32).T
         theirs = kv_other[at, :]
         theirs_t = theirs[:, width:].astype(jnp.float32).T
         for h in range(heads):
             lo, hi = h * HD, (h + 1) * HD
-            q_t[b, h] = mine_t[lo:hi].astype(jnp.bfloat16)
-            v_t[b, h] = mine_t[2 * width + lo : 2 * width + hi].astype(jnp.bfloat16)
-            k_n[b, h] = mine[:, width + lo : width + hi]
+            q_t[b, h] = query_t[lo:hi].astype(jnp.bfloat16)
+            v_t[b, h] = mine_t[lo:hi].astype(jnp.bfloat16)
+            k_n[b, h] = mine[:, lo:hi]
             v_t[blocks + b, h] = theirs_t[lo:hi].astype(jnp.bfloat16)
             k_n[blocks + b, h] = theirs[:, lo:hi]
         return carry
@@ -296,9 +300,8 @@
     return [pl.BlockSpec(memory_space=pltpu.VMEM)] * count
 
 
-def attend(info, qkv, kv_other, blocks):
-    rows_all, wide = qkv.shape
-    width = wide // 3
+def attend(info, query, kv_near, kv_other, blocks):
+    rows_all, width = query.shape
     heads, rows = width // HD, rows_all // blocks
     bf, f32 = jnp.bfloat16, jnp.float32
     pairs = blocks * rows * rows * (blocks + 1)
@@ -309,7 +312,7 @@
             jax.ShapeDtypeStruct((blocks, width, rows), f32),
             jax.ShapeDtypeStruct((blocks, heads, 1, rows), f32),
         ),
-        in_specs=[pl.BlockSpec(memory_space=pltpu.SMEM)] + vmem_specs(2),
+        in_specs=[pl.BlockSpec(memory_space=pltpu.SMEM)] + vmem_specs(3),
         out_specs=tuple(vmem_specs(3)),
         scratch_shapes=[
             pltpu.VMEM((blocks, heads, HD, rows), bf),
@@ -323,15 +326,15 @@
             flops=20 * 1024 * 1024 * 1024, transcendentals=pairs * heads, bytes_accessed=8 * 1024 * 1024
         ),
         name="attend",
-    )(info, qkv, kv_other)
+    )(info, query, kv_near, kv_other)
 
 
 def back_kernel(
-    info, qkv, kv_other, grad, out_t, logs,
+    info, query, kv_near, kv_other, grad, out_t, logs,
     dq, dkv, dkv_other,
     q_t, g_t, k_n, k_t, v_n, dq_t, dk_t, dv_t, delta,
 ):
-    width, heads = head_dims(qkv)
+    width, heads = head_dims(query)
     blocks, rows = q_t.shape[0], q_t.shape[-1]
     seq_len, half = info[0], info[1]
     scale = 1.0 / math.sqrt(HD)
@@ -339,19 +342,20 @@
 
     def prepare(b, carry):
         at = pl.ds(pl.multiple_of(b * rows, rows), rows)
-        mine = qkv[at, :]
-        mine_t = mine[:, : 2 * width].astype(jnp.float32).T
+        query_t = query[at, :].astype(jnp.float32).T
+        mine = kv_near[at, :]
+        mine_t = mine[:, :width].astype(jnp.float32).T
         grad_t = grad[at, :].astype(jnp.float32).T
         theirs = kv_other[at, :]
         theirs_t = theirs[:, :width].astype(jnp.float32).T
         for h in range(heads):
             lo, hi = h * HD, (h + 1) * HD
-            q_t[b, h] = mine_t[lo:hi].astype(jnp.bfloat16)
+            q_t[b, h] = query_t[lo:hi].astype(jnp.bfloat16)
             g_t[b, h] = grad_t[lo:hi].astype(jnp.bfloat16)
             delta[b, h] = jnp.sum(grad_t[lo:hi] * out_t[b, lo:hi], axis=0, keepdims=True)
-            k_t[b, h] = mine_t[width + lo : width + hi].astype(jnp.bfloat16)
-            k_n[b, h] = mine[:, width + lo : width + hi]
-            v_n[b, h] = mine[:, 2 * width + lo : 2 * width + hi]
+            k_t[b, h] = mine_t[lo:hi].astype(jnp.bfloat16)
+            k_n[b, h] = mine[:, lo:hi]
+            v_n[b, h] = mine[:, width + lo : width + hi]
             k_t[blocks + b, h] = theirs_t[lo:hi].astype(jnp.bfloat16)
             k_n[blocks + b, h] = theirs[:, lo:hi]
             v_n[blocks + b, h] = theirs[:, width + lo : width + hi]
@@ -395,9 +399,8 @@
     lax.fori_loop(0, blocks, finish, 0)
 
 
-def attend_back(info, qkv, kv_other, grad, out_t, logs, blocks):
-    rows_all, wide = qkv.shape
-    width = wide // 3
+def attend_back(info, query, kv_near, kv_other, grad, out_t, logs, blocks):
+    rows_all, width = query.shape
     heads, rows = width // HD, rows_all // blocks
     bf, f32 = jnp.bfloat16, jnp.float32
     pairs = blocks * rows * rows * (blocks + 1)
@@ -408,7 +411,7 @@
             jax.ShapeDtypeStruct((rows_all, 2 * width), bf),
             jax.ShapeDtypeStruct((rows_all, 2 * width), bf),
         ),
-        in_specs=[pl.BlockSpec(memory_space=pltpu.SMEM)] + vmem_specs(5),
+        in_specs=[pl.BlockSpec(memory_space=pltpu.SMEM)] + vmem_specs(6),
         out_specs=tuple(vmem_specs(3)),
         scratch_shapes=[
             pltpu.VMEM((blocks, heads, HD, rows), bf),
@@ -425,7 +428,7 @@
             flops=60 * 1024 * 1024 * 1024, transcendentals=pairs * heads, bytes_accessed=8 * 1024 * 1024
         ),
         name="attend_back",
-    )(info, qkv, kv_other, grad, out_t, logs)
+    )(info, query, kv_near, kv_other, grad, out_t, logs)
 
 
 def head_columns(groups, halves, sections, units):
@@ -470,15 +473,15 @@
     cotangent,
 ):
     cell_count, row_count, model_width = inputs.shape
-    cells = lax.axis_size("cell")
-    groups = lax.axis_size("head")
-    halves = lax.axis_size("ctx")
+    cells = lax.axis_size(CELL)
+    groups = lax.axis_size(HEAD)
+    halves = lax.axis_size(CTX)
     parts = groups * halves
-    half_index = lax.axis_index("ctx")
+    half_index = lax.axis_index(CTX)
     head_width = HEADS // groups * HD
     token_count = cell_count * row_count
     ctx_rows = groups * row_count
-    cell_steps, ctx_steps, head_steps = bits_of("cell"), bits_of("ctx"), bits_of("head")[::-1]
+    cell_steps, ctx_steps, head_steps = bits_of(CELL), bits_of(CTX), bits_of(HEAD)[::-1]
     steps_x = cell_steps + ctx_steps + head_steps
     one_hot = (
         dataset_ids[:, None] == jnp.arange(dataset_table.shape[0], dtype=jnp.int32)[None, :]
@@ -489,34 +492,38 @@
     mixed_qkv = jnp.dot(normed, qkv_weight, preferred_element_type=jnp.float32)
     bias_row = jnp.concatenate([query_bias, jnp.zeros_like(query_bias), value_bias])
     mixed_qkv = (mixed_qkv + bias_row).astype(jnp.bfloat16)
-    head_index = lax.axis_index("head")
+    head_index = lax.axis_index(HEAD)
 
     def to_heads(values):
         sections = values.shape[1] // model_width
         values = values.reshape(cell_count, row_count, sections, groups, head_width)
         values = values.transpose(3, 0, 1, 2, 4).reshape(groups, cell_count, row_count, -1)
-        values = lax.all_to_all(values, "head", split_axis=0, concat_axis=0, tiled=True)
+        values = lax.all_to_all(values, HEAD, split_axis=0, concat_axis=0, tiled=True)
         return values.transpose(1, 0, 2, 3).reshape(cell_count, ctx_rows, -1)
 
     def to_rows(values):
         sections = values.shape[-1] // head_width
         values = values.reshape(cell_count, groups, row_count, -1).transpose(1, 0, 2, 3)
-        values = lax.all_to_all(values, "head", split_axis=0, concat_axis=0, tiled=True)
+        values = lax.all_to_all(values, HEAD, split_axis=0, concat_axis=0, tiled=True)
         values = values.reshape(groups, cell_count, row_count, sections, head_width)
         return values.transpose(1, 2, 3, 0, 4).reshape(token_count, sections * model_width)
 
-    qkv_heads = to_heads(mixed_qkv)
-    kv_other = swap(qkv_heads[:, :, head_width:], "ctx", 1)
+    kv_near = to_heads(mixed_qkv[:, model_width:])
+    mixed_query, kv_near = lax.optimization_barrier((mixed_qkv[:, :model_width], kv_near))
+    kv_other = swap(kv_near, CTX, 1)
+    query_heads = to_heads(mixed_query)
     normed_t = normed.T.reshape(cells, model_width // cells, token_count)
     normed_t = jnp.pad(normed_t, ((0, 0), (0, -normed_t.shape[1] % 16), (0, 0)))
-    normed_t, kv_other = lax.optimization_barrier((normed_t.reshape(-1, token_count), kv_other))
+    normed_t, query_heads = lax.optimization_barrier(
+        (normed_t.reshape(-1, token_count), query_heads)
+    )
     pieces = [normed_t]
     for p in range(1, groups):
-        pieces.append(swap(normed_t, "head", p))
+        pieces.append(swap(normed_t, HEAD, p))
     normed_near = jnp.stack(pieces)
-    normed_far = swap(normed_near, "ctx", 1)
+    normed_far = swap(normed_near, CTX, 1)
     infos = [jnp.stack([lengths[n], half_index.astype(jnp.int32)]) for n in range(cell_count)]
-    runs = [attend(infos[n], qkv_heads[n], kv_other[n], groups) for n in range(cell_count)]
+    runs = [attend(infos[n], query_heads[n], kv_near[n], kv_other[n], groups) for n in range(cell_count)]
     attended = jnp.stack([r[0] for r in runs])
     attended_rows = to_rows(attended)
     attn_out = jnp.dot(attended_rows, out_weight, preferred_element_type=jnp.float32) + out_bias
@@ -531,14 +538,14 @@
     part_columns = model_width // parts
     grad_top = grad_low.astype(jnp.float32)
     proj_bias_grad = jnp.sum(grad_top, axis=0)
+    low_tie = [grad_low]
+    proj_total = scatter_sum(proj_kept, proj_sent, steps_x, {1: low_tie})
+    proj_weight_grad = proj_total[:part_columns].T
+    grad_low = low_tie[0]
     active_grad = jnp.einsum("nd,fd->nf", grad_low, proj_weight, preferred_element_type=jnp.float32)
     gelu_pull = jax.vjp(gelu_tanh, hidden)[1]
     hidden_grad = gelu_pull(active_grad)[0].astype(jnp.bfloat16)
     fc_bias_grad = jnp.sum(hidden_grad, axis=0, dtype=jnp.float32)
-    hidden_tie = [hidden_grad]
-    proj_total = scatter_sum(proj_kept, proj_sent, steps_x, {1: hidden_tie})
-    proj_weight_grad = proj_total[:part_columns].T
-    hidden_grad = hidden_tie[0]
     normed_grad = jnp.einsum(
         "nf,df->nd", hidden_grad, fc_weight, preferred_element_type=jnp.float32
     )
@@ -563,7 +570,7 @@
 
     backs = [
       attend_back(
-        infos[n], qkv_heads[n], kv_other[n], grad_heads[n], runs[n][1], runs[n][2], groups
+        infos[n], query_heads[n], kv_near[n], kv_other[n], grad_heads[n], runs[n][1], runs[n][2], groups
       )
       for n in range(cell_count)
     ]
@@ -571,18 +578,18 @@
     dkv = jnp.stack([b[1] for b in backs])
     dkv_far = jnp.stack([b[2] for b in backs])
 
-    dkv_got = swap(dkv_far, "ctx", 1)
+    dkv_got = swap(dkv_far, CTX, 1)
     dq_rows = to_rows(dq)
     qkv_part = qkv_blocks(normed_near, normed_far, dq[0], dkv[0], dkv_far[0])
     half_cells = cells // 2
     qkv_part = scatter_sum(qkv_part[:half_cells], qkv_part[half_cells:], cell_steps)
     qkv_part = qkv_part[: model_width // cells].astype(jnp.bfloat16)
-    qkv_part = add_up(qkv_part, swap(qkv_part, "ctx", 1)).astype(jnp.bfloat16)
+    qkv_part = add_up(qkv_part, swap(qkv_part, CTX, 1)).astype(jnp.bfloat16)
     units = 2 * groups
     qkv_part = qkv_part.reshape(qkv_part.shape[0], 3 * units // groups, -1).transpose(1, 0, 2)
     send_table, take_table = head_columns(groups, halves, 3, units)
     sent = qkv_part[jnp.asarray(send_table)[head_index, half_index]]
-    got = lax.all_to_all(sent, "head", split_axis=0, concat_axis=0, tiled=True)
+    got = lax.all_to_all(sent, HEAD, split_axis=0, concat_axis=0, tiled=True)
     taken = jnp.asarray(take_table)[head_index, half_index]
     qkv_weight_grad = jnp.concatenate(
         [got[taken[n, 0], taken[n, 1]] for n in range(take_table.shape[2])], axis=-1
@@ -595,7 +602,9 @@
     column_sums = jnp.sum(qkv_grad, axis=0, dtype=jnp.float32)
     query_bias_grad = column_sums[:model_width]
     value_bias_grad = column_sums[2 * model_width :]
-    normed_back = jnp.einsum("ne,de->nd", qkv_grad, qkv_weight, preferred_element_type=jnp.float32)
+    normed_back = jnp.einsum(
+        "ne,de->nd", qkv_grad, qkv_weight, preferred_element_type=jnp.float32
+    )
     attn_pull = jax.vjp(layer_norm, residual, attn_gain, attn_shift)[1]
     residual_part, attn_gain_grad, attn_shift_grad = attn_pull(normed_back)
     residual_grad = middle_grad + residual_part
@@ -623,7 +632,7 @@
         + [fc_bias_grad.reshape(cells, fc_rows, width)],
         axis=1,
     )
-    cell_index = lax.axis_index("cell")
+    cell_index = lax.axis_index(CELL)
     for axis, bit in cell_steps[::-1]:
         on = (cell_index // bit) % 2
         half = packed.shape[0] // 2
@@ -668,41 +677,41 @@
 
 def solution(mesh):
     in_specs = (
-        P("cell", ("head", "ctx"), None),
-        P("cell"),
-        P("cell"),
-        P(),
-        P(),
-        P(),
-        P(),
-        P(),
-        P(),
-        P(),
-        P(),
-        P(),
-        P(),
-        P(),
-        P(),
-        P(),
-        P(),
-        P("cell", ("head", "ctx"), None),
+        P(CELL, (HEAD, CTX), None),
+        P(CELL),
+        P(CELL),
+        P(),
+        P(),
+        P(),
+        P(),
+        P(),
+        P(),
+        P(),
+        P(),
+        P(),
+        P(),
+        P(),
+        P(),
+        P(),
+        P(),
+        P(CELL, (HEAD, CTX), None),
     )
     out_specs = (
-        P("cell", ("head", "ctx"), None),
-        P("cell", ("head", "ctx"), None),
-        P(None, "cell"),
-        P("cell"),
-        P("cell"),
-        P("cell", ("head", "ctx")),
-        P("cell"),
-        P("cell"),
-        P("cell", ("head", "ctx")),
-        P("cell"),
-        P("cell"),
-        P("cell"),
-        P("cell", ("head", "ctx")),
-        P("cell"),
-        P("cell", ("head", "ctx")),
-        P("cell"),
+        P(CELL, (HEAD, CTX), None),
+        P(CELL, (HEAD, CTX), None),
+        P(None, CELL),
+        P(CELL),
+        P(CELL),
+        P(CELL, (HEAD, CTX)),
+        P(CELL),
+        P(CELL),
+        P(CELL, (HEAD, CTX)),
+        P(CELL),
+        P(CELL),
+        P(CELL),
+        P(CELL, (HEAD, CTX)),
+        P(CELL),
+        P(CELL, (HEAD, CTX)),
+        P(CELL),
     )
     return jax.shard_map(body, mesh=mesh, in_specs=in_specs, out_specs=out_specs, check_vma=False)

time: 584 us -> 570 us (0.976)
  blocking collectives: 46.3 us -> 0 us
  waiting for transfers between devices: 143 us -> 176 us
  starting transfers between devices: 82 us -> 92.1 us
  Pallas kernels: 105 us -> 95.9 us
    all_to_all x1 -> x0, blocking collectives: 46.3 us -> none  [to_heads(): lax.all_to_all(values, 'head', split_axis=0, concat_axis=0, tiled=True)]
    all_to_all x5 -> x7, waiting for transfers between devices: 20 us -> 54.9 us  [the longest x3 45.2 us: to_heads(): lax.all_to_all(values, HEAD, split_axis=0, concat_axis=0, tiled=True)]
    all_to_all x5 -> x7, starting transfers between devices: 23.9 us -> 35 us  [the longest x3 17.1 us: to_rows(): lax.all_to_all(values, HEAD, split_axis=0, concat_axis=0, tiled=True)]
    pallas_call x2, Pallas kernels: 33.9 us -> 24.5 us  [weight_blocks(): pl.pallas_call(kernel, out_shape=[jax.ShapeDtypeStruct(shape, jnp.bfloat1...]
  transfers between devices with their start and end apart: 29 -> 31, of which waited for: 10 -> 13; matrix products, arithmetic and copies ran while one was open for 22% -> 21% of each run, Pallas kernels for 7% -> 8%
where the time goes in v6:
time: 570 us; the launch traced here: 560 us
  waiting for transfers between devices  176 us (31%)
  Pallas kernels  95.9 us (17%)
  starting transfers between devices  92.1 us (16%)
  local copies, waits for them, and re-layouts  76.2 us (13%)
  other arithmetic  53 us (9%)
  matrix products  52.2 us (9%)
  between operations  14.8 us (3%)
    ppermute x24, waiting for transfers between devices, swap(): lax.ppermute(values, axis, [(i, i ^ bit) for i in range(lax.axis_size(axi...  121 us
    ppermute x24, starting transfers between devices, swap(): lax.ppermute(values, axis, [(i, i ^ bit) for i in range(lax.axis_size(axi...  57.1 us
    all_to_all x3, waiting for transfers between devices, to_heads(): lax.all_to_all(values, HEAD, split_axis=0, concat_axis=0, tiled=True)  45.2 us
    pallas_call x1, Pallas kernels, attend_back(): pl.pallas_call(back_kernel, out_shape=(jax.ShapeDtypeStruct((rows_all, wi...  32.5 us
    convert_element_type x9, other arithmetic, scatter_sum(): sent = add_up(*[t[half:] for t in terms]).astype(jnp.bfloat16)  30.2 us
    pallas_call x1, Pallas kernels, attend(): pl.pallas_call(attend_kernel, out_shape=(jax.ShapeDtypeStruct((rows_all,...  29 us
    pallas_call x2, Pallas kernels, weight_blocks(): pl.pallas_call(kernel, out_shape=[jax.ShapeDtypeStruct(shape, jnp.bfloat1...  24.5 us
    all_to_all x3, starting transfers between devices, to_rows(): lax.all_to_all(values, HEAD, split_axis=0, concat_axis=0, tiled=True)  17.1 us
  transfers between devices with their start and end apart: 31, of which 13 were waited for; matrix products, arithmetic and copies ran while one was open for 21% of the time, Pallas kernels for 8%

profile of v6, /device:TPU:0, one launch (start us, length us, event | category | flops | bytes accessed | tf_op | source)
XLA Modules:
  0.0 560.0 jit_solution(11023009192504841189)
XLA Ops:
  5.1 6.9 %fusion.2 = bf16[256,3360]{0,1:T(8,128)(2,1)S(1)} fusion(bf16[1120,3360]{1,0:T(8,128)(2,1)} %param.29, f32[3360]{0:T(1024)S(1)} %concatenate.12, bf16[1,256,1120]{2,1,0:T(8,128)(2,1)S(1)} %copy.104, f32[1120]{0:T(1024)S(1)} %copy-done.42, f32[1120]{0:T(1024)S(1)} %copy-done.28, f32[256]{0:T(256)S(1)} %fusion.52, f32[256]{0:T(256)S(1)} %broadcast_multiply_fusion.1, ...), kind=kOutput, calls=%fused_computation.10 | convolution fusion | flops 1930485760 | bytes 9849088 | tf_op jit(solution)/shard_map/dot_general | solution.py:492
  13.5 6.3 %all-to-all-start = ((bf16[4,1,256,560]{2,3,1,0:T(8,128)(2,1)}), bf16[4,1,256,560]{2,3,1,0:T(8,128)(2,1)}, u32[]{:S(2)}, u32[]{:S(2)}) async-start(bf16[4,1,256,560]{2,3,1,0:T(8,128)(2,1)} %bitcast.192), calls=%async_computation | async-start | bytes 2293760 | tf_op jit(solution)/shard_map/all_to_all | solution.py:501
  21.8 26.0 %all-to-all-done = bf16[4,1,256,560]{2,3,1,0:T(8,128)(2,1)} async-done(((bf16[4,1,256,560]{2,3,1,0:T(8,128)(2,1)}), bf16[4,1,256,560]{2,3,1,0:T(8,128)(2,1)}, u32[]{:S(2)}, u32[]{:S(2)}) %all-to-all-start) | async-done | bytes 1146912 | tf_op jit(solution)/shard_map/all_to_all | solution.py:501
  47.8 2.4 copy.108
  50.2 2.4 copy.110
  54.1 4.1 all-to-all-start.1
  59.4 2.1 copy.105
  64.7 8.5 %all-to-all-done.1 = bf16[4,1,256,280]{2,3,1,0:T(8,128)(2,1)} async-done(((bf16[4,1,256,280]{2,3,1,0:T(8,128)(2,1)}), bf16[4,1,256,280]{2,3,1,0:T(8,128)(2,1)}, u32[]{:S(2)}, u32[]{:S(2)}) %all-to-all-start.1) | async-done | bytes 573472 | tf_op jit(solution)/shard_map/all_to_all | solution.py:501
  73.2 2.2 copy.109
  75.4 3.8 collective-permute-done
  79.2 2.4 copy.111
  81.6 29.0 %attend.1 = (bf16[1024,280]{1,0:T(8,128)(2,1)}, f32[4,280,256]{2,1,0:T(8,128)}, f32[4,5,1,256]{3,2,1,0:T(1,128)}) custom-call(s32[2]{0:T(128)} %pad_add_fusion.info, bf16[1024,280]{1,0:T(8,128)(2,1)} %bitcast.206, bf16[1024,560]{1,0:T(8,128)(2,1)} %bitcast.184, bf16[1024,560]{1,0:T(8,128)(2,1)} %bitcast.204), custom_call_target="tpu_custom_call" | custom-call | flops 21474836480 | bytes 8388608 | tf_op jit(solution)/shard_map/attend/pallas_call | solution.py:308
  110.6 2.2 copy.112
  112.8 4.3 all-to-all-start.2
  117.2 2.1 copy.115
  120.3 9.8 %all-to-all-done.2 = bf16[4,1,256,280]{2,3,1,0:T(8,128)(2,1)} async-done(((bf16[4,1,256,280]{2,3,1,0:T(8,128)(2,1)}), bf16[4,1,256,280]{2,3,1,0:T(8,128)(2,1)}, u32[]{:S(2)}, u32[]{:S(2)}) %all-to-all-start.2) | async-done | bytes 573472 | tf_op jit(solution)/shard_map/all_to_all | solution.py:507
  130.1 2.2 fusion.71
  133.7 9.9 %multiply_convert_fusion = (bf16[256,4480]{1,0:T(8,128)(2,1)}, f32[256,4480]{1,0:T(8,128)}) fusion(f32[4480]{0:T(1024)S(1)} %copy-done.47, bf16[256,1120]{1,0:T(8,128)(2,1)S(1)} %add_convert_fusion.refs_0_, bf16[1120,4480]{1,0:T(8,128)(2,1)} %param.36), kind=kOutput, calls=%fused_computation.19 | convolution fusion | flops 2580480000 | bytes 17507840 | tf_op jit(solution)/shard_map/dot_general | solution.py:532
  143.6 10.9 %wb.2 = (bf16[2,8,144,1120]{3,2,1,0:T(8,128)(2,1)}, bf16[2,8,144,1120]{3,2,1,0:T(8,128)(2,1)}) custom-call(s32[8]{0:T(128)} %fusion.56.left_at.right_at, s32[4]{0:T(128)} %broadcast_xor_fusion.right_at.left_at, bf16[256,1120]{1,0:T(8,128)(2,1)} %bitcast.181, bf16[256,4480]{1,0:T(8,128)(2,1)} %get-tuple-element.154.refs_1_), custom_call_target="tpu_custom_call" | custom-call | tf_op jit(solution)/shard_map/wb/pallas_call | solution.py:131
  154.5 2.1 copy.117.refs_2_
  156.6 7.0 %collective-permute-done.1 = bf16[16,144,1120]{2,1,0:T(8,128)(2,1)} collective-permute-done((bf16[16,144,1120]{2,1,0:T(8,128)(2,1)}, bf16[16,144,1120]{2,1,0:T(8,128)(2,1)}, u32[]{:S(2)}, u32[]{:S(2)}) %collective-permute-start.1) | collective-permute-done | bytes 5160992 | tf_op jit(solution)/shard_map/ppermute | solution.py:35
  163.6 4.8 fusion.1
  168.4 10.3 %convert_reduce_fusion = (f32[4480]{0:T(1024)}, bf16[256,4480]{1,0:T(8,128)(2,1)S(1)}) fusion(f32[256,4480]{1,0:T(8,128)} %get-tuple-element.155, bf16[256,1120]{1,0:T(8,128)(2,1)S(1)} %bitcast.182, bf16[4480,1120]{0,1:T(8,128)(2,1)} %param.38), kind=kOutput, calls=%fused_computation.18 | convolution fusion | flops 2594237952 | bytes 17507840 | tf_op jit(solution)/shard_map/nd,fd->nf/dot_general | solution.py:545
  178.7 4.5 fusion.73
  183.2 2.7 copy.116
  185.9 2.1 multiply_reduce_fusion
  190.8 13.7 %wb.3 = (bf16[2,8,288,700]{3,2,1,0:T(8,128)(2,1)}, bf16[2,8,288,700]{3,2,1,0:T(8,128)(2,1)}) custom-call(s32[4]{0:T(128)} %broadcast_xor_fusion.right_at.left_at, s32[8]{0:T(128)} %fusion.56.left_at.right_at, bf16[256,1120]{1,0:T(8,128)(2,1)} %copy-done.17, bf16[256,4480]{1,0:T(8,128)(2,1)} %copy-done.18, bf16[256,1120]{1,0:T(8,128)(2,1)} %copy.117.refs_2_, ...), custom_call_target="tpu_custom_call" | custom-call | tf_op jit(solution)/shard_map/wb/pallas_call | solution.py:131
  204.6 2.9 collective-permute-start.20
  210.8 2.4 collective-permute-start.11
  213.2 2.8 convolution_convert_fusion
  216.0 3.6 all-to-all-start.3
  234.4 3.0 collective-permute-done.9
  237.4 17.3 %collective-permute-done.10 = bf16[1152,256]{1,0:T(8,128)(2,1)} collective-permute-done((bf16[1152,256]{1,0:T(8,128)(2,1)}, bf16[1152,256]{1,0:T(8,128)(2,1)}, u32[]{:S(2)}, u32[]{:S(2)}) %collective-permute-start.10) | collective-permute-done | bytes 589856 | tf_op jit(solution)/shard_map/ppermute | solution.py:35
  254.7 3.2 pad_maximum_fusion.near_ref
  257.8 7.0 %collective-permute-start.12 = (bf16[4,1152,256]{2,1,0:T(8,128)(2,1)}, bf16[4,1152,256]{2,1,0:T(8,128)(2,1)}, u32[]{:S(2)}, u32[]{:S(2)}) collective-permute-start(bf16[4,1152,256]{2,1,0:T(8,128)(2,1)} %pad_maximum_fusion.near_ref), channel_id=1, source_target_pairs={{0,1},{1,0},{2,3},{3,2},{4,5},{5,4},{6,7},{7,6},{8,9},{9,8},{10,11... | collective-permute-start | bytes 7077896 | tf_op jit(solution)/shard_map/ppermute | solution.py:35
  264.9 10.7 %all-to-all-done.3 = bf16[4,1,256,280]{2,3,1,0:T(8,128)(2,1)S(1)} async-done(((bf16[4,1,256,280]{2,3,1,0:T(8,128)(2,1)}), bf16[4,1,256,280]{2,3,1,0:T(8,128)(2,1)S(1)}, u32[]{:S(2)}, u32[]{:S(2)}) %all-to-all-start.3) | async-done | bytes 573472 | tf_op jit(solution)/shard_map/all_to_all | solution.py:501
  276.8 3.7 fusion.15
  280.4 7.1 %collective-permute-start.21 = (bf16[4,144,1120]{2,1,0:T(8,128)(2,1)}, bf16[4,144,1120]{2,1,0:T(8,128)(2,1)}, u32[]{:S(2)}, u32[]{:S(2)}) collective-permute-start(bf16[4,144,1120]{2,1,0:T(8,128)(2,1)} %fusion.15), channel_id=1, source_target_pairs={{0,1},{1,0},{2,3},{3,2},{4,5},{5,4},{6,7},{7,6},{8,9},{9,8},{10,11... | collective-permute-start | bytes 3870728 | tf_op jit(solution)/shard_map/ppermute | solution.py:35
  287.5 5.7 %fusion = bf16[8,288,700]{2,1,0:T(8,128)(2,1)} fusion(bf16[16,288,700]{2,1,0:T(8,128)(2,1)} %collective-permute-done.2, bf16[2,8,288,700]{3,2,1,0:T(8,128)(2,1)} %get-tuple-element.43), kind=kLoop, calls=%fused_computation.3 | loop fusion | flops 6451200 | bytes 9676800 | tf_op jit(solution)/shard_map/convert_element_type | solution.py:207
  293.2 32.5 %attend_back.1 = (bf16[1024,280]{1,0:T(8,128)(2,1)}, bf16[1024,560]{1,0:T(8,128)(2,1)}, bf16[1024,560]{1,0:T(8,128)(2,1)}) custom-call(s32[2]{0:T(128)} %pad_add_fusion.info, bf16[1024,280]{1,0:T(8,128)(2,1)} %bitcast.207, bf16[1024,560]{1,0:T(8,128)(2,1)} %bitcast.185, bf16[1024,560]{1,0:T(8,128)(2,1)} %bitcast.205, bf16[1024,280]{1,0:T(8,128)(2,1)} %bitcast.208, ...), custom_call_target="tpu_custom_call" | custom-call | flops 64424509440 | bytes 8388608 | tf_op jit(solution)/shard_map/attend_back/pallas_call | solution.py:407
  325.7 2.5 copy.119
  328.2 5.5 collective-permute-start.3
  333.7 7.8 %fusion.18 = bf16[1,256,1120]{2,1,0:T(8,128)(2,1)S(1)} fusion(f32[256,1120]{1,0:T(8,128)S(1)} %copy-done.5, bf16[256,4480]{1,0:T(8,128)(2,1)} %get-tuple-element.154.refs_1_, bf16[4480,1120]{0,1:T(8,128)(2,1)} %param.38, f32[1120]{0:T(1024)S(1)} %copy-done.49), kind=kOutput, calls=%fused_computation.35 | convolution fusion | flops 2569871360 | bytes 14053760 | tf_op jit(solution)/shard_map/dot_general | solution.py:534
  342.6 3.9 all-to-all-start.4
  346.5 2.9 fusion.24
  349.4 15.5 %collective-permute-start.22 = (bf16[2,144,1120]{2,1,0:T(8,128)(2,1)}, bf16[2,144,1120]{2,1,0:T(8,128)(2,1)}, u32[]{:S(2)}, u32[]{:S(2)}) collective-permute-start(bf16[2,144,1120]{2,1,0:T(8,128)(2,1)} %fusion.24), channel_id=1, source_target_pairs={{0,4},{2,6},{4,0},{6,2},{1,5},{3,7},{5,1},{7,3},{8,12},{10,14},{12... | collective-permute-start | bytes 1935368 | tf_op jit(solution)/shard_map/ppermute | solution.py:35
  364.9 9.9 %qb.1 = bf16[4,288,840]{2,1,0:T(8,128)(2,1)} custom-call(s32[4]{0:T(128)} %gather_fusion, s32[4]{0:T(128)} %xor_multiply_fusion.row, bf16[4,1152,256]{2,1,0:T(8,128)(2,1)} %pad_maximum_fusion.near_ref, bf16[4,1152,256]{2,1,0:T(8,128)(2,1)} %collective-permute-done.12.far_ref, bf16[1024,280]{1,0:T(8,128)(2,1)} %get-tuple-element.50.dq_ref, ...), custom_call_target="tpu_custom_call" | custom-call | tf_op jit(solution)/shard_map/qb/pallas_call | solution.py:180
  374.8 2.3 slice.398
  377.1 2.4 copy.120
  383.0 8.9 %all-to-all-start.5 = ((bf16[4,1,256,560]{2,3,1,0:T(8,128)(2,1)}), bf16[4,1,256,560]{2,3,1,0:T(8,128)(2,1)}, u32[]{:S(2)}, u32[]{:S(2)}) async-start(bf16[4,1,256,560]{2,3,1,0:T(8,128)(2,1)} %copy.122), calls=%async_computation.5 | async-start | bytes 2293760 | tf_op jit(solution)/shard_map/all_to_all | solution.py:507
  405.0 2.3 fusion.41
  407.3 3.0 collective-permute-start.23
  413.1 36.7 %collective-permute-done.14 = bf16[1,288,840]{2,1,0:T(8,128)(2,1)S(1)} collective-permute-done((bf16[1,288,840]{2,1,0:T(8,128)(2,1)S(1)}, bf16[1,288,840]{2,1,0:T(8,128)(2,1)S(1)}, u32[]{:S(2)}, u32[]{:S(2)}) %collective-permute-start.14) | collective-permute-done | bytes 483872 | tf_op jit(solution)/shard_map/ppermute | solution.py:35
  453.7 6.9 %fusion.72 = (f32[1120]{0:T(1024)S(1)}, f32[256,1120]{0,1:T(8,128)}) fusion(bf16[1120,3360]{1,0:T(8,128)(2,1)} %param.29, bf16[256,2240]{0,1:T(8,128)(2,1)S(1)} %bitcast.190, bf16[256,1120]{0,1:T(8,128)(2,1)S(1)} %bitcast.200), kind=kOutput, calls=%fused_computation.161 | convolution fusion | flops 1930484608 | bytes 10398080 | tf_op jit(solution)/shard_map/ne,de->nd/dot_general | solution.py:605
  463.3 4.6 fusion.11
  475.9 3.8 all-to-all-start.6
  479.9 22.5 %collective-permute-done.17 = bf16[4,288,700]{2,1,0:T(8,128)(2,1)} collective-permute-done((bf16[4,288,700]{2,1,0:T(8,128)(2,1)}, bf16[4,288,700]{2,1,0:T(8,128)(2,1)}, u32[]{:S(2)}, u32[]{:S(2)}) %collective-permute-start.17) | collective-permute-done | bytes 1612832 | tf_op jit(solution)/shard_map/ppermute | solution.py:35
  502.4 3.3 fusion.21
  506.3 2.1 fusion.46
  512.0 2.4 collective-permute-done.6
  514.4 2.4 collective-permute-start.7
  516.9 25.4 %collective-permute-done.7 = f32[1,32,280]{2,1,0:T(8,128)S(1)} collective-permute-done((f32[1,32,280]{2,1,0:T(8,128)S(1)}, f32[1,32,280]{2,1,0:T(8,128)S(1)}, u32[]{:S(2)}, u32[]{:S(2)}) %collective-permute-start.7) | collective-permute-done | bytes 35872 | tf_op jit(solution)/shard_map/ppermute | solution.py:35
  544.2 2.1 collective-permute-start.19
  553.5 2.7 collective-permute-done.19
  (243 shorter events, 76.9 us)
Async XLA Ops:
  0.6 129.4 %copy-start = (bf16[1120,1120]{1,0:T(8,128)(2,1)S(1)}, bf16[1120,1120]{1,0:T(8,128)(2,1)}, u32[]{:S(2)}) copy-start(bf16[1120,1120]{1,0:T(8,128)(2,1)} %param.32) | copy-start | bytes 7526404
  0.7 4.3 copy-start.44
  0.7 4.3 copy-start.45
  0.7 4.4 copy-start.28
  0.7 4.4 copy-start.42
  4.1 54.2 %copy-start.31 = (f32[256]{0:T(256)}, f32[256]{0:T(256)S(1)}, u32[]{:S(2)}) copy-start(f32[256]{0:T(256)S(1)} %broadcast_multiply_fusion.1) | copy-start | bytes 3076
  4.9 53.4 %copy-start.36 = (f32[256]{0:T(256)}, f32[256]{0:T(256)S(1)}, u32[]{:S(2)}) copy-start(f32[256]{0:T(256)S(1)} %fusion.52) | copy-start | bytes 3076
  13.5 34.3 %all-to-all-start = ((bf16[4,1,256,560]{2,3,1,0:T(8,128)(2,1)}), bf16[4,1,256,560]{2,3,1,0:T(8,128)(2,1)}, u32[]{:S(2)}, u32[]{:S(2)}) async-start(bf16[4,1,256,560]{2,3,1,0:T(8,128)(2,1)} %bitcast.192), calls=%async_computation | async-start | bytes 2293760 | tf_op jit(solution)/shard_map/all_to_all | solution.py:501
  52.6 26.6 %collective-permute-start = (bf16[1,1024,560]{1,2,0:T(8,128)(2,1)}, bf16[1,1024,560]{1,2,0:T(8,128)(2,1)}, u32[]{:S(2)}, u32[]{:S(2)}) collective-permute-start(bf16[1,1024,560]{1,2,0:T(8,128)(2,1)} %copy.110), channel_id=1, source_target_pairs={{0,1},{1,0},{2,3},{3,2},{4,5},{5,4},{6,7},{7,6},{8,9},{9,8},{10,11... | collective-permute-start | bytes 3440648 | tf_op jit(solution)/shard_map/ppermute | solution.py:35
  54.1 19.0 %all-to-all-start.1 = ((bf16[4,1,256,280]{2,3,1,0:T(8,128)(2,1)}), bf16[4,1,256,280]{2,3,1,0:T(8,128)(2,1)}, u32[]{:S(2)}, u32[]{:S(2)}) async-start(bf16[4,1,256,280]{2,3,1,0:T(8,128)(2,1)} %bitcast.202), calls=%async_computation.1 | async-start | bytes 1146880 | tf_op jit(solution)/shard_map/all_to_all | solution.py:501
  110.6 9.2 %copy-start.2 = (s32[4]{0:T(128)S(1)}, s32[4]{0:T(128)}, u32[]{:S(2)}) copy-start(s32[4]{0:T(128)} %constant.127.clone) | copy-start | bytes 52
  110.6 19.5 %copy-start.48 = (f32[1120]{0:T(1024)S(1)}, f32[1120]{0:T(1024)}, u32[]{:S(2)}) copy-start(f32[1120]{0:T(1024)} %param.33) | copy-start | bytes 13444
  112.8 17.3 %all-to-all-start.2 = ((bf16[4,1,256,280]{2,3,1,0:T(8,128)(2,1)}), bf16[4,1,256,280]{2,3,1,0:T(8,128)(2,1)}, u32[]{:S(2)}, u32[]{:S(2)}) async-start(bf16[4,1,256,280]{2,3,1,0:T(8,128)(2,1)} %copy.112), calls=%async_computation.2 | async-start | bytes 1146880 | tf_op jit(solution)/shard_map/all_to_all | solution.py:507
  133.7 9.9 %copy-start.17 = (bf16[256,1120]{1,0:T(8,128)(2,1)}, bf16[256,1120]{1,0:T(8,128)(2,1)S(1)}, u32[]{:S(2)}) copy-start(bf16[256,1120]{1,0:T(8,128)(2,1)S(1)} %add_convert_fusion.refs_0_) | copy-start | bytes 1720324
  154.5 9.1 %collective-permute-start.1 = (bf16[16,144,1120]{2,1,0:T(8,128)(2,1)}, bf16[16,144,1120]{2,1,0:T(8,128)(2,1)}, u32[]{:S(2)}, u32[]{:S(2)}) collective-permute-start(bf16[16,144,1120]{2,1,0:T(8,128)(2,1)} %bitcast.215), channel_id=1, source_target_pairs={{0,8},{8,0},{16,24},{24,16},{1,9},{9,1},{17,25},{25,17},{2,10},{10... | collective-permute-start | bytes 15482888 | tf_op jit(solution)/shard_map/ppermute | solution.py:35
  163.6 4.8 copy-start.9
  163.6 15.1 %slice-start.1 = ((s8[10035200]{0:T(1024)(128)(4,1)}), s8[4194304]{0:T(1024)(128)(4,1)S(1)}, s32[]{:S(2)}) async-start(s8[10035200]{0:T(1024)(128)(4,1)} %bitcast.212), calls=%async_computation.8 | async-start | bytes 8388608
  168.4 10.3 %slice-start.2 = ((s8[10035200]{0:T(1024)(128)(4,1)}), s8[4194304]{0:T(1024)(128)(4,1)S(1)}, s32[]{:S(2)}) async-start(s8[10035200]{0:T(1024)(128)(4,1)} %bitcast.212), calls=%async_computation.9 | async-start | bytes 8388608
  168.4 10.3 %slice-start.3 = ((s8[10035200]{0:T(1024)(128)(4,1)}), s8[1646592]{0:T(1024)(128)(4,1)S(1)}, s32[]{:S(2)}) async-start(s8[10035200]{0:T(1024)(128)(4,1)} %bitcast.212), calls=%async_computation.10 | async-start | bytes 3293184
  178.7 4.5 copy-start.18
  188.7 15.8 %copy-start.40 = (f32[256]{0:T(256)}, f32[256]{0:T(256)S(1)}, u32[]{:S(2)}) copy-start(f32[256]{0:T(256)S(1)} %negate_multiply_fusion.1) | copy-start | bytes 3076
  204.5 83.1 %collective-permute-start.2 = (bf16[16,288,700]{2,1,0:T(8,128)(2,1)}, bf16[16,288,700]{2,1,0:T(8,128)(2,1)}, u32[]{:S(2)}, u32[]{:S(2)}) collective-permute-start(bf16[16,288,700]{2,1,0:T(8,128)(2,1)} %bitcast.214), channel_id=1, source_target_pairs={{0,8},{8,0},{16,24},{24,16},{1,9},{9,1},{17,25},{25,17},{2,10},{10... | collective-permute-start | bytes 19353608 | tf_op jit(solution)/shard_map/ppermute | solution.py:35
  204.6 72.2 %collective-permute-start.20 = (bf16[8,144,1120]{2,1,0:T(8,128)(2,1)}, bf16[8,144,1120]{2,1,0:T(8,128)(2,1)}, u32[]{:S(2)}, u32[]{:S(2)}) collective-permute-start(bf16[8,144,1120]{2,1,0:T(8,128)(2,1)} %fusion.1), channel_id=1, source_target_pairs={{0,16},{8,24},{16,0},{24,8},{1,17},{9,25},{17,1},{25,9},{2,18},{10... | collective-permute-start | bytes 7741448 | tf_op jit(solution)/shard_map/ppermute | solution.py:35
  208.8 28.6 %collective-permute-start.9 = (bf16[1152,256]{1,0:T(8,128)(2,1)}, bf16[1152,256]{1,0:T(8,128)(2,1)}, u32[]{:S(2)}, u32[]{:S(2)}) collective-permute-start(bf16[1152,256]{1,0:T(8,128)(2,1)} %bitcast.195), channel_id=1, source_target_pairs={{0,2},{2,0},{4,6},{6,4},{1,3},{3,1},{5,7},{7,5},{8,10},{10,8},{12,... | collective-permute-start | bytes 1769480 | tf_op jit(solution)/shard_map/ppermute | solution.py:35
  208.8 45.9 %collective-permute-start.10 = (bf16[1152,256]{1,0:T(8,128)(2,1)}, bf16[1152,256]{1,0:T(8,128)(2,1)}, u32[]{:S(2)}, u32[]{:S(2)}) collective-permute-start(bf16[1152,256]{1,0:T(8,128)(2,1)} %bitcast.196), channel_id=1, source_target_pairs={{0,4},{2,6},{4,0},{6,2},{1,5},{3,7},{5,1},{7,3},{8,12},{10,14},{12... | collective-permute-start | bytes 1769480 | tf_op jit(solution)/shard_map/ppermute | solution.py:35
  210.8 43.9 %collective-permute-start.11 = (bf16[1152,256]{1,0:T(8,128)(2,1)}, bf16[1152,256]{1,0:T(8,128)(2,1)}, u32[]{:S(2)}, u32[]{:S(2)}) collective-permute-start(bf16[1152,256]{1,0:T(8,128)(2,1)} %bitcast.197), channel_id=1, source_target_pairs={{0,6},{2,4},{4,2},{6,0},{1,7},{3,5},{5,3},{7,1},{8,14},{10,12},{12... | collective-permute-start | bytes 1769480 | tf_op jit(solution)/shard_map/ppermute | solution.py:35
  216.0 38.7 %copy-start.16 = (bf16[4,288,256]{2,1,0:T(8,128)(2,1)S(1)}, bf16[4,288,256]{2,1,0:T(8,128)(2,1)}, u32[]{:S(2)}) copy-start(bf16[4,288,256]{2,1,0:T(8,128)(2,1)} %pad.4) | copy-start | bytes 1769476
  216.0 59.5 %all-to-all-start.3 = ((bf16[4,1,256,280]{2,3,1,0:T(8,128)(2,1)}), bf16[4,1,256,280]{2,3,1,0:T(8,128)(2,1)S(1)}, u32[]{:S(2)}, u32[]{:S(2)}) async-start(bf16[4,1,256,280]{2,3,1,0:T(8,128)(2,1)} %bitcast.210), calls=%async_computation.3 | async-start | bytes 1146880 | tf_op jit(solution)/shard_map/all_to_all | solution.py:501
  257.8 107.1 %collective-permute-start.12 = (bf16[4,1152,256]{2,1,0:T(8,128)(2,1)}, bf16[4,1152,256]{2,1,0:T(8,128)(2,1)}, u32[]{:S(2)}, u32[]{:S(2)}) collective-permute-start(bf16[4,1152,256]{2,1,0:T(8,128)(2,1)} %pad_maximum_fusion.near_ref), channel_id=1, source_target_pairs={{0,1},{1,0},{2,3},{3,2},{4,5},{5,4},{6,7},{7,6},{8,9},{9,8},{10,11... | collective-permute-start | bytes 7077896 | tf_op jit(solution)/shard_map/ppermute | solution.py:35
  280.4 66.1 %collective-permute-start.21 = (bf16[4,144,1120]{2,1,0:T(8,128)(2,1)}, bf16[4,144,1120]{2,1,0:T(8,128)(2,1)}, u32[]{:S(2)}, u32[]{:S(2)}) collective-permute-start(bf16[4,144,1120]{2,1,0:T(8,128)(2,1)} %fusion.15), channel_id=1, source_target_pairs={{0,1},{1,0},{2,3},{3,2},{4,5},{5,4},{6,7},{7,6},{8,9},{9,8},{10,11... | collective-permute-start | bytes 3870728 | tf_op jit(solution)/shard_map/ppermute | solution.py:35
  325.7 8.0 %copy-start.5 = (f32[256,1120]{1,0:T(8,128)S(1)}, f32[256,1120]{1,0:T(8,128)}, u32[]{:S(2)}) copy-start(f32[256,1120]{1,0:T(8,128)} %copy-done.3) | copy-start | bytes 3440644
  325.7 8.0 %copy-start.49 = (f32[1120]{0:T(1024)S(1)}, f32[1120]{0:T(1024)}, u32[]{:S(2)}) copy-start(f32[1120]{0:T(1024)} %param.39) | copy-start | bytes 13444
  328.2 13.3 %copy-start.15 = (bf16[1024,280]{1,0:T(8,128)(2,1)S(1)}, bf16[1024,280]{1,0:T(8,128)(2,1)}, u32[]{:S(2)}) copy-start(bf16[1024,280]{1,0:T(8,128)(2,1)} %get-tuple-element.50.dq_ref) | copy-start | bytes 1720324
  328.2 48.8 %collective-permute-start.3 = (bf16[1,1024,560]{1,2,0:T(8,128)(2,1)}, bf16[1,1024,560]{1,2,0:T(8,128)(2,1)}, u32[]{:S(2)}, u32[]{:S(2)}) collective-permute-start(bf16[1,1024,560]{1,2,0:T(8,128)(2,1)} %copy.119), channel_id=1, source_target_pairs={{0,1},{1,0},{2,3},{3,2},{4,5},{5,4},{6,7},{7,6},{8,9},{9,8},{10,11... | collective-permute-start | bytes 3440648 | tf_op jit(solution)/shard_map/ppermute | solution.py:35
  342.6 38.9 %all-to-all-start.4 = ((bf16[4,1,256,280]{2,3,1,0:T(8,128)(2,1)}), bf16[4,1,256,280]{2,3,1,0:T(8,128)(2,1)S(1)}, u32[]{:S(2)}, u32[]{:S(2)}) async-start(bf16[4,1,256,280]{2,3,1,0:T(8,128)(2,1)} %copy.121), calls=%async_computation.4 | async-start | bytes 1146880 | tf_op jit(solution)/shard_map/all_to_all | solution.py:507
  349.4 55.7 %collective-permute-start.22 = (bf16[2,144,1120]{2,1,0:T(8,128)(2,1)}, bf16[2,144,1120]{2,1,0:T(8,128)(2,1)}, u32[]{:S(2)}, u32[]{:S(2)}) collective-permute-start(bf16[2,144,1120]{2,1,0:T(8,128)(2,1)} %fusion.24), channel_id=1, source_target_pairs={{0,4},{2,6},{4,0},{6,2},{1,5},{3,7},{5,1},{7,3},{8,12},{10,14},{12... | collective-permute-start | bytes 1935368 | tf_op jit(solution)/shard_map/ppermute | solution.py:35
  364.9 98.4 %collective-permute-start.16 = (bf16[8,288,700]{2,1,0:T(8,128)(2,1)}, bf16[8,288,700]{2,1,0:T(8,128)(2,1)}, u32[]{:S(2)}, u32[]{:S(2)}) collective-permute-start(bf16[8,288,700]{2,1,0:T(8,128)(2,1)} %fusion), channel_id=1, source_target_pairs={{0,16},{8,24},{16,0},{24,8},{1,17},{9,25},{17,1},{25,9},{2,18},{10... | collective-permute-start | bytes 9676808 | tf_op jit(solution)/shard_map/ppermute | solution.py:35
  377.1 26.2 %collective-permute-start.13 = (bf16[2,288,840]{2,1,0:T(8,128)(2,1)}, bf16[2,288,840]{2,1,0:T(8,128)(2,1)}, u32[]{:S(2)}, u32[]{:S(2)}) collective-permute-start(bf16[2,288,840]{2,1,0:T(8,128)(2,1)} %slice.398), channel_id=1, source_target_pairs={{0,8},{8,0},{16,24},{24,16},{1,9},{9,1},{17,25},{25,17},{2,10},{10... | collective-permute-start | bytes 2903048 | tf_op jit(solution)/shard_map/ppermute | solution.py:35
  383.0 13.1 %copy-start.35 = (f32[4480]{0:T(1024)S(1)}, f32[4480]{0:T(1024)}, u32[]{:S(2)}) copy-start(f32[4480]{0:T(1024)} %get-tuple-element.132) | copy-start | bytes 53764
  383.0 69.3 %all-to-all-start.5 = ((bf16[4,1,256,560]{2,3,1,0:T(8,128)(2,1)}), bf16[4,1,256,560]{2,3,1,0:T(8,128)(2,1)}, u32[]{:S(2)}, u32[]{:S(2)}) async-start(bf16[4,1,256,560]{2,3,1,0:T(8,128)(2,1)} %copy.122), calls=%async_computation.5 | async-start | bytes 2293760 | tf_op jit(solution)/shard_map/all_to_all | solution.py:507
  393.9 9.3 %copy-start.12 = (bf16[4,288,840]{2,1,0:T(8,128)(2,1)S(1)}, bf16[4,288,840]{2,1,0:T(8,128)(2,1)}, u32[]{:S(2)}) copy-start(bf16[4,288,840]{2,1,0:T(8,128)(2,1)} %qb.1) | copy-start | bytes 5806084
  404.4 45.5 %collective-permute-start.14 = (bf16[1,288,840]{2,1,0:T(8,128)(2,1)S(1)}, bf16[1,288,840]{2,1,0:T(8,128)(2,1)S(1)}, u32[]{:S(2)}, u32[]{:S(2)}) collective-permute-start(bf16[1,288,840]{2,1,0:T(8,128)(2,1)S(1)} %add_convert_fusion.2), channel_id=1, source_target_pairs={{0,16},{8,24},{16,0},{24,8},{1,17},{9,25},{17,1},{25,9},{2,18},{10... | collective-permute-start | bytes 1451528 | tf_op jit(solution)/shard_map/ppermute | solution.py:35
  407.3 42.5 %slice-start = ((bf16[4,288,840]{2,1,0:T(8,128)(2,1)}), bf16[1,288,840]{2,1,0:T(8,128)(2,1)S(1)}, s32[]{:S(2)}) async-start(bf16[4,288,840]{2,1,0:T(8,128)(2,1)} %qb.1), calls=%async_computation.7 | async-start | bytes 1032192 | tf_op jit(solution)/shard_map/slice | solution.py:208
  407.3 99.0 %collective-permute-start.23 = (bf16[1,144,1120]{2,1,0:T(8,128)(2,1)}, bf16[1,144,1120]{2,1,0:T(8,128)(2,1)}, u32[]{:S(2)}, u32[]{:S(2)}) collective-permute-start(bf16[1,144,1120]{2,1,0:T(8,128)(2,1)} %fusion.41), channel_id=1, source_target_pairs={{0,2},{2,0},{4,6},{6,4},{1,3},{3,1},{5,7},{7,5},{8,10},{10,8},{12,... | collective-permute-start | bytes 967688 | tf_op jit(solution)/shard_map/ppermute | solution.py:35
  413.1 40.5 %copy-start.20 = (bf16[4,1,256,280]{2,3,1,0:T(8,128)(2,1)S(1)}, bf16[4,1,256,280]{2,3,1,0:T(8,128)(2,1)}, u32[]{:S(2)}) copy-start(bf16[4,1,256,280]{2,3,1,0:T(8,128)(2,1)} %copy-done.19) | copy-start | bytes 1720324
  450.8 20.9 %collective-permute-start.15 = (bf16[280,840]{1,0:T(8,128)(2,1)}, bf16[280,840]{1,0:T(8,128)(2,1)}, u32[]{:S(2)}, u32[]{:S(2)}) collective-permute-start(bf16[280,840]{1,0:T(8,128)(2,1)} %fusion.47), channel_id=1, source_target_pairs={{0,1},{1,0},{2,3},{3,2},{4,5},{5,4},{6,7},{7,6},{8,9},{9,8},{10,11... | collective-permute-start | bytes 1411208 | tf_op jit(solution)/shard_map/ppermute | solution.py:35
  453.6 6.9 %copy-start.13 = (bf16[1,256,2,4,280]{1,4,3,2,0:T(8,128)(2,1)}, bf16[1,256,2,4,280]{1,4,3,2,0:T(8,128)(2,1)S(1)}, u32[]{:S(2)}) copy-start(bf16[1,256,2,4,280]{1,4,3,2,0:T(8,128)(2,1)S(1)} %copy.123) | copy-start | bytes 3440644
  463.3 5.2 copy-start.14
  463.3 5.2 copy-start.21
  463.3 5.7 %copy-start.11 = (bf16[1,256,1120]{2,1,0:T(8,128)(2,1)S(1)}, bf16[1,256,1120]{2,1,0:T(8,128)(2,1)}, u32[]{:S(2)}) copy-start(bf16[1,256,1120]{2,1,0:T(8,128)(2,1)} %copy.115) | copy-start | bytes 1720324
  467.9 34.5 %collective-permute-start.17 = (bf16[4,288,700]{2,1,0:T(8,128)(2,1)}, bf16[4,288,700]{2,1,0:T(8,128)(2,1)}, u32[]{:S(2)}, u32[]{:S(2)}) collective-permute-start(bf16[4,288,700]{2,1,0:T(8,128)(2,1)} %fusion.11), channel_id=1, source_target_pairs={{0,1},{1,0},{2,3},{3,2},{4,5},{5,4},{6,7},{7,6},{8,9},{9,8},{10,11... | collective-permute-start | bytes 4838408 | tf_op jit(solution)/shard_map/ppermute | solution.py:35
  470.6 9.2 %collective-permute-start.4 = (f32[2,32,280]{2,1,0:T(8,128)S(1)}, f32[2,32,280]{2,1,0:T(8,128)S(1)}, u32[]{:S(2)}, u32[]{:S(2)}) collective-permute-start(f32[2,32,280]{2,1,0:T(8,128)S(1)} %constant_dynamic-slice_fusion.6), channel_id=1, source_target_pairs={{0,16},{8,24},{16,0},{24,8},{1,17},{9,25},{17,1},{25,9},{2,18},{10... | collective-permute-start | bytes 215048 | tf_op jit(solution)/shard_map/ppermute | solution.py:35
  475.9 35.4 %all-to-all-start.6 = ((bf16[4,2,280,140]{2,1,3,0:T(2,128)(2,1)}), bf16[4,2,280,140]{2,1,3,0:T(2,128)(2,1)S(1)}, u32[]{:S(2)}, u32[]{:S(2)}) async-start(bf16[4,2,280,140]{2,1,3,0:T(2,128)(2,1)} %copy.129), calls=%async_computation.6 | async-start | bytes 1720320 | tf_op jit(solution)/shard_map/all_to_all | solution.py:592
  479.8 26.5 %copy-start.24 = (bf16[1,144,1120]{2,1,0:T(8,128)(2,1)S(1)}, bf16[1,144,1120]{2,1,0:T(8,128)(2,1)}, u32[]{:S(2)}) copy-start(bf16[1,144,1120]{2,1,0:T(8,128)(2,1)} %slice.432) | copy-start | bytes 967684
  479.8 26.5 %copy-start.25 = (bf16[1,144,1120]{2,1,0:T(8,128)(2,1)S(1)}, bf16[1,144,1120]{2,1,0:T(8,128)(2,1)}, u32[]{:S(2)}) copy-start(bf16[1,144,1120]{2,1,0:T(8,128)(2,1)} %slice.433) | copy-start | bytes 967684
  479.8 26.5 %copy-start.26 = (bf16[1,144,1120]{2,1,0:T(8,128)(2,1)S(1)}, bf16[1,144,1120]{2,1,0:T(8,128)(2,1)}, u32[]{:S(2)}) copy-start(bf16[1,144,1120]{2,1,0:T(8,128)(2,1)} %slice.436) | copy-start | bytes 967684
  479.8 26.5 %copy-start.27 = (bf16[1,144,1120]{2,1,0:T(8,128)(2,1)S(1)}, bf16[1,144,1120]{2,1,0:T(8,128)(2,1)}, u32[]{:S(2)}) copy-start(bf16[1,144,1120]{2,1,0:T(8,128)(2,1)} %slice.440) | copy-start | bytes 967684
  479.8 30.4 %collective-permute-start.5 = (f32[1,32,280]{2,1,0:T(8,128)S(1)}, f32[1,32,280]{2,1,0:T(8,128)S(1)}, u32[]{:S(2)}, u32[]{:S(2)}) collective-permute-start(f32[1,32,280]{2,1,0:T(8,128)S(1)} %constant_dynamic-slice_fusion.5), channel_id=1, source_target_pairs={{0,8},{8,0},{16,24},{24,16},{1,9},{9,1},{17,25},{25,17},{2,10},{10... | collective-permute-start | bytes 107528 | tf_op jit(solution)/shard_map/ppermute | solution.py:35
  505.7 36.6 %collective-permute-start.18 = (bf16[2,288,700]{2,1,0:T(8,128)(2,1)}, bf16[2,288,700]{2,1,0:T(8,128)(2,1)}, u32[]{:S(2)}, u32[]{:S(2)}) collective-permute-start(bf16[2,288,700]{2,1,0:T(8,128)(2,1)} %fusion.21), channel_id=1, source_target_pairs={{0,4},{2,6},{4,0},{6,2},{1,5},{3,7},{5,1},{7,3},{8,12},{10,14},{12... | collective-permute-start | bytes 2419208 | tf_op jit(solution)/shard_map/ppermute | solution.py:35
  510.2 4.2 collective-permute-start.6
  514.4 27.9 %collective-permute-start.7 = (f32[1,32,280]{2,1,0:T(8,128)S(1)}, f32[1,32,280]{2,1,0:T(8,128)S(1)}, u32[]{:S(2)}, u32[]{:S(2)}) collective-permute-start(f32[1,32,280]{2,1,0:T(8,128)S(1)} %add.337), channel_id=1, source_target_pairs={{0,4},{2,6},{4,0},{6,2},{1,5},{3,7},{5,1},{7,3},{8,12},{10,14},{12... | collective-permute-start | bytes 107528 | tf_op jit(solution)/shard_map/ppermute | solution.py:35
  542.3 6.1 %collective-permute-start.8 = (f32[1,32,280]{2,1,0:T(8,128)S(1)}, f32[1,32,280]{2,1,0:T(8,128)S(1)}, u32[]{:S(2)}, u32[]{:S(2)}) collective-permute-start(f32[1,32,280]{2,1,0:T(8,128)S(1)} %add.338), channel_id=1, source_target_pairs={{0,2},{2,0},{4,6},{6,4},{1,3},{3,1},{5,7},{7,5},{8,10},{10,8},{12,... | collective-permute-start | bytes 107528 | tf_op jit(solution)/shard_map/ppermute | solution.py:35
  544.2 12.0 %collective-permute-start.19 = (bf16[1,288,700]{2,1,0:T(8,128)(2,1)S(1)}, bf16[1,288,700]{2,1,0:T(8,128)(2,1)}, u32[]{:S(2)}, u32[]{:S(2)}) collective-permute-start(bf16[1,288,700]{2,1,0:T(8,128)(2,1)S(1)} %fusion.31), channel_id=1, source_target_pairs={{0,2},{2,0},{4,6},{6,4},{1,3},{3,1},{5,7},{7,5},{8,10},{10,8},{12,... | collective-permute-start | bytes 1209608 | tf_op jit(solution)/shard_map/ppermute | solution.py:35
  548.4 7.8 %copy-start.22 = (bf16[1,288,700]{2,1,0:T(8,128)(2,1)S(1)}, bf16[1,288,700]{2,1,0:T(8,128)(2,1)}, u32[]{:S(2)}) copy-start(bf16[1,288,700]{2,1,0:T(8,128)(2,1)} %slice_bitcast_fusion) | copy-start | bytes 1209604
  (21 other events, 36.7 us)

commit v7 on v6

--- a/solution.py
+++ b/solution.py
@@ -226,20 +226,27 @@
 
 
 def sweep(i, half, seq_len, rows, visit, blocks):
-    def own(j, carry):
-        visit(j, (2 * j + half) * rows, False)
-        return carry
-
-    def other(j, carry):
-        visit(blocks + j, (2 * j + 1 - half) * rows, False)
-        return carry
+    def own(j):
+        return j, (2 * j + half) * rows
+
+    def other(j):
+        return blocks + j, (2 * j + 1 - half) * rows
+
+    def run(low, high, *kinds):
+        def step(j, carry):
+            visit([kind(j) for kind in kinds], False)
+            return carry
+
+        lax.fori_loop(low, high, step, 0)
 
     span = 2 * rows
     own_count = jnp.minimum(i, (seq_len - half * rows + span - 1) // span)
     other_count = jnp.minimum(i + half, (seq_len - (1 - half) * rows + span - 1) // span)
-    lax.fori_loop(0, other_count, other, 0)
-    lax.fori_loop(0, own_count, own, 0)
-    visit(i, (2 * i + half) * rows, True)
+    both = jnp.minimum(own_count, other_count)
+    run(0, both, own, other)
+    run(both, other_count, other)
+    run(both, own_count, own)
+    visit([own(i)], True)
 
 
 def attend_kernel(info, query, kv_near, kv_other, out, out_t, logs, q_t, k_n, v_t, acc, m_ref, l_ref):
@@ -271,18 +278,25 @@
         m_ref[...] = jnp.full_like(m_ref, MASKED)
         l_ref[...] = jnp.zeros_like(l_ref)
 
-        def visit(j, start, diagonal):
+        def visit(chunks, diagonal):
             query_start = (2 * i + half) * rows if diagonal else None
-            allowed = chunk_mask(start, seq_len, query_start, rows, rows)
+            allowed = [chunk_mask(at, seq_len, query_start, rows, rows) for _, at in chunks]
             for h in range(heads):
-                s = nn(k_n[j, h], q_t[i, h]) * factor
-                s = jnp.where(allowed, s, MASKED)
                 old = m_ref[h]
-                new = jnp.maximum(old, jnp.max(s, axis=0, keepdims=True))
+                new, scores = old, []
+                for (j, _), mask in zip(chunks, allowed):
+                    s = nn(k_n[j, h], q_t[i, h]) * factor
+                    s = jnp.where(mask, s, MASKED)
+                    scores.append(s)
+                    new = jnp.maximum(new, jnp.max(s, axis=0, keepdims=True))
                 shrink = jnp.exp2(old - new)
-                p = jnp.exp2(s - new)
-                l_ref[h] = l_ref[h] * shrink + jnp.sum(p, axis=0, keepdims=True)
-                acc[h] = acc[h] * shrink + nn(v_t[j, h], p.astype(jnp.bfloat16))
+                total, result = l_ref[h] * shrink, acc[h] * shrink
+                for (j, _), s in zip(chunks, scores):
+                    p = jnp.exp2(s - new)
+                    total = total + jnp.sum(p, axis=0, keepdims=True)
+                    result = result + nn(v_t[j, h], p.astype(jnp.bfloat16))
+                l_ref[h] = total
+                acc[h] = result
                 m_ref[h] = new
 
         sweep(i, half, seq_len, rows, visit, blocks)
@@ -368,18 +382,19 @@
     def block(i, carry):
         dq_t[...] = jnp.zeros_like(dq_t)
 
-        def visit(j, start, diagonal):
+        def visit(chunks, diagonal):
             query_start = (2 * i + half) * rows if diagonal else None
-            allowed = chunk_mask(start, seq_len, query_start, rows, rows)
+            allowed = [chunk_mask(at, seq_len, query_start, rows, rows) for _, at in chunks]
             for h in range(heads):
                 at = slice(h * HD, (h + 1) * HD)
-                s = nn(k_n[j, h], q_t[i, h]) * factor - logs[i, h]
-                p = jnp.exp2(jnp.where(allowed, s, MASKED))
-                dv_t[j, at] += nt(g_t[i, h], p.astype(jnp.bfloat16))
-                dp = nn(v_n[j, h], g_t[i, h])
-                ds = (p * (dp - delta[i, h])).astype(jnp.bfloat16)
-                dq_t[at] += nn(k_t[j, h], ds)
-                dk_t[j, at] += nt(q_t[i, h], ds)
+                for (j, _), mask in zip(chunks, allowed):
+                    s = nn(k_n[j, h], q_t[i, h]) * factor - logs[i, h]
+                    p = jnp.exp2(jnp.where(mask, s, MASKED))
+                    dv_t[j, at] += nt(g_t[i, h], p.astype(jnp.bfloat16))
+                    dp = nn(v_n[j, h], g_t[i, h])
+                    ds = (p * (dp - delta[i, h])).astype(jnp.bfloat16)
+                    dq_t[at] += nn(k_t[j, h], ds)
+                    dk_t[j, at] += nt(q_t[i, h], ds)
 
         sweep(i, half, seq_len, rows, visit, blocks)
         at = pl.ds(pl.multiple_of(i * rows, rows), rows)
@@ -520,8 +535,6 @@
     pieces = [normed_t]
     for p in range(1, groups):
         pieces.append(swap(normed_t, HEAD, p))
-    normed_near = jnp.stack(pieces)
-    normed_far = swap(normed_near, CTX, 1)
     infos = [jnp.stack([lengths[n], half_index.astype(jnp.int32)]) for n in range(cell_count)]
     runs = [attend(infos[n], query_heads[n], kv_near[n], kv_other[n], groups) for n in range(cell_count)]
     attended = jnp.stack([r[0] for r in runs])
@@ -557,6 +570,10 @@
     attended_grad = jnp.einsum(
         "ne,de->nd", middle_low, out_weight, preferred_element_type=jnp.float32
     ).astype(jnp.bfloat16)
+    held = lax.optimization_barrier((attended_grad, *pieces))
+    attended_grad, pieces = held[0], held[1:]
+    normed_near = jnp.stack(pieces)
+    normed_far = swap(normed_near, CTX, 1)
     grad_heads = to_heads(attended_grad)
 
     fc_kept, fc_sent = weight_blocks([(mlp_normed, hidden_grad), (attended_rows, middle_low)], True)

time: 570 us -> 587 us (1.030)
  waiting for transfers between devices: 176 us -> 199 us
  starting transfers between devices: 92.1 us -> 80.3 us
    ppermute x24, waiting for transfers between devices: 121 us -> 154 us  [swap(): lax.ppermute(values, axis, [(i, i ^ bit) for i in range(lax.axis_size(axi...]
    ppermute x24, starting transfers between devices: 57.1 us -> 37.5 us  [swap(): lax.ppermute(values, axis, [(i, i ^ bit) for i in range(lax.axis_size(axi...]
    all_to_all x3, waiting for transfers between devices: 45.2 us -> 34.5 us  [to_heads(): lax.all_to_all(values, HEAD, split_axis=0, concat_axis=0, tiled=True)]
    pallas_call x2, Pallas kernels: 24.5 us -> 35.2 us  [weight_blocks(): pl.pallas_call(kernel, out_shape=[jax.ShapeDtypeStruct(shape, jnp.bfloat1...]
    all_to_all x3, starting transfers between devices: 14.1 us -> 24.1 us  [to_heads(): lax.all_to_all(values, HEAD, split_axis=0, concat_axis=0, tiled=True)]
    pallas_call x1, Pallas kernels: 29 us -> 22.5 us  [attend(): pl.pallas_call(attend_kernel, out_shape=(jax.ShapeDtypeStruct((rows_all,...]
  transfers between devices with their start and end apart: 31 -> 31, of which waited for: 13 -> 14; matrix products, arithmetic and copies ran while one was open for 21% -> 20% of each run, Pallas kernels for 8% -> 7%
where the time goes in v7:
time: 587 us; the launch traced here: 577 us
  waiting for transfers between devices  199 us (34%)
  Pallas kernels  101 us (17%)
  starting transfers between devices  80.3 us (14%)
  local copies, waits for them, and re-layouts  76.2 us (13%)
  other arithmetic  53 us (9%)
  matrix products  52.2 us (9%)
  between operations  15 us (3%)
    ppermute x24, waiting for transfers between devices, swap(): lax.ppermute(values, axis, [(i, i ^ bit) for i in range(lax.axis_size(axi...  154 us
    ppermute x24, starting transfers between devices, swap(): lax.ppermute(values, axis, [(i, i ^ bit) for i in range(lax.axis_size(axi...  37.5 us
    pallas_call x2, Pallas kernels, weight_blocks(): pl.pallas_call(kernel, out_shape=[jax.ShapeDtypeStruct(shape, jnp.bfloat1...  35.2 us
    all_to_all x3, waiting for transfers between devices, to_heads(): lax.all_to_all(values, HEAD, split_axis=0, concat_axis=0, tiled=True)  34.5 us
    pallas_call x1, Pallas kernels, attend_back(): pl.pallas_call(back_kernel, out_shape=(jax.ShapeDtypeStruct((rows_all, wi...  33.3 us
    convert_element_type x9, other arithmetic, scatter_sum(): sent = add_up(*[t[half:] for t in terms]).astype(jnp.bfloat16)  30.2 us
    all_to_all x3, starting transfers between devices, to_heads(): lax.all_to_all(values, HEAD, split_axis=0, concat_axis=0, tiled=True)  24.1 us
    pallas_call x1, Pallas kernels, attend(): pl.pallas_call(attend_kernel, out_shape=(jax.ShapeDtypeStruct((rows_all,...  22.5 us
  transfers between devices with their start and end apart: 31, of which 14 were waited for; matrix products, arithmetic and copies ran while one was open for 20% of the time, Pallas kernels for 7%

profile of v7, /device:TPU:0, one launch (start us, length us, event | category | flops | bytes accessed | tf_op | source)
XLA Modules:
  0.0 576.6 jit_solution(2531146538931354606)
XLA Ops:
  5.1 6.9 %fusion.2 = bf16[256,3360]{0,1:T(8,128)(2,1)S(1)} fusion(bf16[1120,3360]{1,0:T(8,128)(2,1)} %param.29, f32[3360]{0:T(1024)S(1)} %concatenate.12, bf16[1,256,1120]{2,1,0:T(8,128)(2,1)S(1)} %copy.104, f32[1120]{0:T(1024)S(1)} %copy-done.42, f32[1120]{0:T(1024)S(1)} %copy-done.28, f32[256]{0:T(256)S(1)} %fusion.52, f32[256]{0:T(256)S(1)} %broadcast_multiply_fusion.1, ...), kind=kOutput, calls=%fused_computation.10 | convolution fusion | flops 1930485760 | bytes 9849088 | tf_op jit(solution)/shard_map/dot_general | solution.py:507
  13.5 6.3 %all-to-all-start = ((bf16[4,1,256,560]{2,3,1,0:T(8,128)(2,1)}), bf16[4,1,256,560]{2,3,1,0:T(8,128)(2,1)}, u32[]{:S(2)}, u32[]{:S(2)}) async-start(bf16[4,1,256,560]{2,3,1,0:T(8,128)(2,1)} %bitcast.192), calls=%async_computation | async-start | bytes 2293760 | tf_op jit(solution)/shard_map/all_to_all | solution.py:516
  21.8 26.0 %all-to-all-done = bf16[4,1,256,560]{2,3,1,0:T(8,128)(2,1)} async-done(((bf16[4,1,256,560]{2,3,1,0:T(8,128)(2,1)}), bf16[4,1,256,560]{2,3,1,0:T(8,128)(2,1)}, u32[]{:S(2)}, u32[]{:S(2)}) %all-to-all-start) | async-done | bytes 1146912 | tf_op jit(solution)/shard_map/all_to_all | solution.py:516
  47.8 2.4 copy.108
  50.2 2.4 copy.110
  54.1 4.1 all-to-all-start.1
  59.4 2.1 copy.105
  64.7 8.5 %all-to-all-done.1 = bf16[4,1,256,280]{2,3,1,0:T(8,128)(2,1)} async-done(((bf16[4,1,256,280]{2,3,1,0:T(8,128)(2,1)}), bf16[4,1,256,280]{2,3,1,0:T(8,128)(2,1)}, u32[]{:S(2)}, u32[]{:S(2)}) %all-to-all-start.1) | async-done | bytes 573472 | tf_op jit(solution)/shard_map/all_to_all | solution.py:516
  73.2 2.2 copy.109
  75.4 3.8 collective-permute-done
  79.2 2.4 copy.111
  81.6 22.5 %attend.1 = (bf16[1024,280]{1,0:T(8,128)(2,1)}, f32[4,280,256]{2,1,0:T(8,128)}, f32[4,5,1,256]{3,2,1,0:T(1,128)}) custom-call(s32[2]{0:T(128)} %pad_add_fusion.info, bf16[1024,280]{1,0:T(8,128)(2,1)} %bitcast.206, bf16[1024,560]{1,0:T(8,128)(2,1)} %bitcast.184, bf16[1024,560]{1,0:T(8,128)(2,1)} %bitcast.204), custom_call_target="tpu_custom_call" | custom-call | flops 21474836480 | bytes 8388608 | tf_op jit(solution)/shard_map/attend/pallas_call | solution.py:322
  104.2 2.2 copy.112
  106.4 4.4 all-to-all-start.2
  110.8 2.1 copy.115
  114.0 10.8 %all-to-all-done.2 = bf16[4,1,256,280]{2,3,1,0:T(8,128)(2,1)} async-done(((bf16[4,1,256,280]{2,3,1,0:T(8,128)(2,1)}), bf16[4,1,256,280]{2,3,1,0:T(8,128)(2,1)}, u32[]{:S(2)}, u32[]{:S(2)}) %all-to-all-start.2) | async-done | bytes 573472 | tf_op jit(solution)/shard_map/all_to_all | solution.py:522
  124.8 2.2 fusion.71
  128.4 9.9 %multiply_convert_fusion = (bf16[256,4480]{1,0:T(8,128)(2,1)}, f32[256,4480]{1,0:T(8,128)}) fusion(f32[4480]{0:T(1024)S(1)} %copy-done.47, bf16[256,1120]{1,0:T(8,128)(2,1)S(1)} %add_convert_fusion.refs_0_, bf16[1120,4480]{1,0:T(8,128)(2,1)} %param.36), kind=kOutput, calls=%fused_computation.19 | convolution fusion | flops 2580480000 | bytes 17507840 | tf_op jit(solution)/shard_map/dot_general | solution.py:545
  138.3 10.9 %wb.2 = (bf16[2,8,144,1120]{3,2,1,0:T(8,128)(2,1)}, bf16[2,8,144,1120]{3,2,1,0:T(8,128)(2,1)}) custom-call(s32[8]{0:T(128)} %fusion.56.left_at.right_at, s32[4]{0:T(128)} %broadcast_xor_fusion.right_at.left_at, bf16[256,1120]{1,0:T(8,128)(2,1)} %bitcast.181, bf16[256,4480]{1,0:T(8,128)(2,1)} %get-tuple-element.164.refs_1_), custom_call_target="tpu_custom_call" | custom-call | tf_op jit(solution)/shard_map/wb/pallas_call | solution.py:131
  149.2 2.1 copy.117.refs_2_
  151.3 7.0 %collective-permute-done.1 = bf16[16,144,1120]{2,1,0:T(8,128)(2,1)} collective-permute-done((bf16[16,144,1120]{2,1,0:T(8,128)(2,1)}, bf16[16,144,1120]{2,1,0:T(8,128)(2,1)}, u32[]{:S(2)}, u32[]{:S(2)}) %collective-permute-start.1) | collective-permute-done | bytes 5160992 | tf_op jit(solution)/shard_map/ppermute | solution.py:35
  158.3 4.8 fusion.1
  163.1 10.3 %convert_reduce_fusion = (f32[4480]{0:T(1024)}, bf16[256,4480]{1,0:T(8,128)(2,1)S(1)}) fusion(f32[256,4480]{1,0:T(8,128)} %get-tuple-element.165, bf16[256,1120]{1,0:T(8,128)(2,1)S(1)} %bitcast.182, bf16[4480,1120]{0,1:T(8,128)(2,1)} %param.38), kind=kOutput, calls=%fused_computation.18 | convolution fusion | flops 2594237952 | bytes 17507840 | tf_op jit(solution)/shard_map/nd,fd->nf/dot_general | solution.py:558
  173.4 4.5 fusion.73
  177.9 2.7 copy.116
  180.6 2.1 multiply_reduce_fusion
  185.5 24.3 %wb.3 = (bf16[2,8,288,700]{3,2,1,0:T(8,128)(2,1)}, bf16[2,8,288,700]{3,2,1,0:T(8,128)(2,1)}) custom-call(s32[4]{0:T(128)} %broadcast_xor_fusion.right_at.left_at, s32[8]{0:T(128)} %fusion.56.left_at.right_at, bf16[256,1120]{1,0:T(8,128)(2,1)} %copy-done.17, bf16[256,4480]{1,0:T(8,128)(2,1)} %copy-done.18, bf16[256,1120]{1,0:T(8,128)(2,1)} %copy.117.refs_2_, ...), custom_call_target="tpu_custom_call" | custom-call | tf_op jit(solution)/shard_map/wb/pallas_call | solution.py:131
  211.7 2.0 collective-permute-start.4
  213.8 2.4 collective-permute-start.5
  217.5 2.8 convolution_convert_fusion
  220.3 18.6 %collective-permute-done.3 = bf16[1152,256]{1,0:T(8,128)(2,1)} collective-permute-done((bf16[1152,256]{1,0:T(8,128)(2,1)}, bf16[1152,256]{1,0:T(8,128)(2,1)}, u32[]{:S(2)}, u32[]{:S(2)}) %collective-permute-start.3) | collective-permute-done | bytes 589856 | tf_op jit(solution)/shard_map/ppermute | solution.py:35
  238.9 15.6 %collective-permute-done.4 = bf16[1152,256]{1,0:T(8,128)(2,1)} collective-permute-done((bf16[1152,256]{1,0:T(8,128)(2,1)}, bf16[1152,256]{1,0:T(8,128)(2,1)}, u32[]{:S(2)}, u32[]{:S(2)}) %collective-permute-start.4) | collective-permute-done | bytes 589856 | tf_op jit(solution)/shard_map/ppermute | solution.py:35
  254.5 13.6 %all-to-all-start.3 = ((bf16[4,1,256,280]{2,3,1,0:T(8,128)(2,1)}), bf16[4,1,256,280]{2,3,1,0:T(8,128)(2,1)S(1)}, u32[]{:S(2)}, u32[]{:S(2)}) async-start(bf16[4,1,256,280]{2,3,1,0:T(8,128)(2,1)} %bitcast.210), calls=%async_computation.3 | async-start | bytes 1146880 | tf_op jit(solution)/shard_map/all_to_all | solution.py:516
  282.8 3.2 pad_maximum_fusion.near_ref
  286.0 7.1 %collective-permute-start.12 = (bf16[4,1152,256]{2,1,0:T(8,128)(2,1)}, bf16[4,1152,256]{2,1,0:T(8,128)(2,1)}, u32[]{:S(2)}, u32[]{:S(2)}) collective-permute-start(bf16[4,1152,256]{2,1,0:T(8,128)(2,1)} %pad_maximum_fusion.near_ref), channel_id=1, source_target_pairs={{0,1},{1,0},{2,3},{3,2},{4,5},{5,4},{6,7},{7,6},{8,9},{9,8},{10,11... | collective-permute-start | bytes 7077896 | tf_op jit(solution)/shard_map/ppermute | solution.py:35
  294.3 3.7 fusion.15
  298.0 5.7 fusion
  303.7 33.3 %attend_back.1 = (bf16[1024,280]{1,0:T(8,128)(2,1)}, bf16[1024,560]{1,0:T(8,128)(2,1)}, bf16[1024,560]{1,0:T(8,128)(2,1)}) custom-call(s32[2]{0:T(128)} %pad_add_fusion.info, bf16[1024,280]{1,0:T(8,128)(2,1)} %bitcast.207, bf16[1024,560]{1,0:T(8,128)(2,1)} %bitcast.185, bf16[1024,560]{1,0:T(8,128)(2,1)} %bitcast.205, bf16[1024,280]{1,0:T(8,128)(2,1)} %bitcast.208, ...), custom_call_target="tpu_custom_call" | custom-call | flops 64424509440 | bytes 8388608 | tf_op jit(solution)/shard_map/attend_back/pallas_call | solution.py:422
  337.0 2.5 copy.119
  339.5 7.5 %collective-permute-start.6 = (bf16[1,1024,560]{1,2,0:T(8,128)(2,1)}, bf16[1,1024,560]{1,2,0:T(8,128)(2,1)}, u32[]{:S(2)}, u32[]{:S(2)}) collective-permute-start(bf16[1,1024,560]{1,2,0:T(8,128)(2,1)} %copy.119), channel_id=1, source_target_pairs={{0,1},{1,0},{2,3},{3,2},{4,5},{5,4},{6,7},{7,6},{8,9},{9,8},{10,11... | collective-permute-start | bytes 3440648 | tf_op jit(solution)/shard_map/ppermute | solution.py:35
  347.0 7.8 %fusion.18 = bf16[1,256,1120]{2,1,0:T(8,128)(2,1)S(1)} fusion(f32[256,1120]{1,0:T(8,128)S(1)} %copy-done.5, bf16[256,4480]{1,0:T(8,128)(2,1)} %get-tuple-element.164.refs_1_, bf16[4480,1120]{0,1:T(8,128)(2,1)} %param.38, f32[1120]{0:T(1024)S(1)} %copy-done.49), kind=kOutput, calls=%fused_computation.35 | convolution fusion | flops 2569871360 | bytes 14053760 | tf_op jit(solution)/shard_map/dot_general | solution.py:547
  355.9 5.3 all-to-all-start.4
  361.2 12.7 %collective-permute-done.21 = bf16[4,144,1120]{2,1,0:T(8,128)(2,1)} collective-permute-done((bf16[4,144,1120]{2,1,0:T(8,128)(2,1)}, bf16[4,144,1120]{2,1,0:T(8,128)(2,1)}, u32[]{:S(2)}, u32[]{:S(2)}) %collective-permute-start.21) | collective-permute-done | bytes 1290272 | tf_op jit(solution)/shard_map/ppermute | solution.py:35
  373.9 2.9 fusion.24
  376.8 2.9 collective-permute-start.22
  380.0 9.9 %qb.1 = bf16[4,288,840]{2,1,0:T(8,128)(2,1)} custom-call(s32[4]{0:T(128)} %gather_fusion, s32[4]{0:T(128)} %xor_multiply_fusion.row, bf16[4,1152,256]{2,1,0:T(8,128)(2,1)} %pad_maximum_fusion.near_ref, bf16[4,1152,256]{2,1,0:T(8,128)(2,1)} %collective-permute-done.12.far_ref, bf16[1024,280]{1,0:T(8,128)(2,1)} %get-tuple-element.57.dq_ref, ...), custom_call_target="tpu_custom_call" | custom-call | tf_op jit(solution)/shard_map/qb/pallas_call | solution.py:180
  389.8 2.3 slice.398
  392.1 4.7 collective-permute-done.6
  396.8 2.4 copy.120
  399.2 2.0 fusion.16
  402.7 4.9 all-to-all-start.5
  420.8 2.3 fusion.41
  423.1 2.0 collective-permute-start.23
  428.0 37.3 %collective-permute-done.14 = bf16[1,288,840]{2,1,0:T(8,128)(2,1)S(1)} collective-permute-done((bf16[1,288,840]{2,1,0:T(8,128)(2,1)S(1)}, bf16[1,288,840]{2,1,0:T(8,128)(2,1)S(1)}, u32[]{:S(2)}, u32[]{:S(2)}) %collective-permute-start.14) | collective-permute-done | bytes 483872 | tf_op jit(solution)/shard_map/ppermute | solution.py:35
  469.1 6.9 %fusion.72 = (f32[1120]{0:T(1024)S(1)}, f32[256,1120]{0,1:T(8,128)}) fusion(bf16[1120,3360]{1,0:T(8,128)(2,1)} %param.29, bf16[256,2240]{0,1:T(8,128)(2,1)S(1)} %bitcast.190, bf16[256,1120]{0,1:T(8,128)(2,1)S(1)} %bitcast.200), kind=kOutput, calls=%fused_computation.161 | convolution fusion | flops 1930484608 | bytes 10398080 | tf_op jit(solution)/shard_map/ne,de->nd/dot_general | solution.py:622
  478.7 4.6 fusion.11
  491.0 4.1 all-to-all-start.6
  495.2 23.2 %collective-permute-done.17 = bf16[4,288,700]{2,1,0:T(8,128)(2,1)} collective-permute-done((bf16[4,288,700]{2,1,0:T(8,128)(2,1)}, bf16[4,288,700]{2,1,0:T(8,128)(2,1)}, u32[]{:S(2)}, u32[]{:S(2)}) %collective-permute-start.17) | collective-permute-done | bytes 1612832 | tf_op jit(solution)/shard_map/ppermute | solution.py:35
  518.4 3.3 fusion.21
  522.8 2.1 fusion.46
  528.5 2.3 collective-permute-done.9
  532.9 26.0 %collective-permute-done.10 = f32[1,32,280]{2,1,0:T(8,128)S(1)} collective-permute-done((f32[1,32,280]{2,1,0:T(8,128)S(1)}, f32[1,32,280]{2,1,0:T(8,128)S(1)}, u32[]{:S(2)}, u32[]{:S(2)}) %collective-permute-start.10) | collective-permute-done | bytes 35872 | tf_op jit(solution)/shard_map/ppermute | solution.py:35
  560.8 2.1 collective-permute-start.19
  570.1 2.5 collective-permute-done.19
  (243 shorter events, 77.1 us)
Async XLA Ops:
  0.6 124.2 %copy-start = (bf16[1120,1120]{1,0:T(8,128)(2,1)S(1)}, bf16[1120,1120]{1,0:T(8,128)(2,1)}, u32[]{:S(2)}) copy-start(bf16[1120,1120]{1,0:T(8,128)(2,1)} %param.32) | copy-start | bytes 7526404
  0.7 4.3 copy-start.44
  0.7 4.3 copy-start.45
  0.7 4.4 copy-start.28
  0.7 4.4 copy-start.42
  4.1 54.2 %copy-start.31 = (f32[256]{0:T(256)}, f32[256]{0:T(256)S(1)}, u32[]{:S(2)}) copy-start(f32[256]{0:T(256)S(1)} %broadcast_multiply_fusion.1) | copy-start | bytes 3076
  4.9 53.4 %copy-start.36 = (f32[256]{0:T(256)}, f32[256]{0:T(256)S(1)}, u32[]{:S(2)}) copy-start(f32[256]{0:T(256)S(1)} %fusion.52) | copy-start | bytes 3076
  13.5 34.3 %all-to-all-start = ((bf16[4,1,256,560]{2,3,1,0:T(8,128)(2,1)}), bf16[4,1,256,560]{2,3,1,0:T(8,128)(2,1)}, u32[]{:S(2)}, u32[]{:S(2)}) async-start(bf16[4,1,256,560]{2,3,1,0:T(8,128)(2,1)} %bitcast.192), calls=%async_computation | async-start | bytes 2293760 | tf_op jit(solution)/shard_map/all_to_all | solution.py:516
  52.6 26.6 %collective-permute-start = (bf16[1,1024,560]{1,2,0:T(8,128)(2,1)}, bf16[1,1024,560]{1,2,0:T(8,128)(2,1)}, u32[]{:S(2)}, u32[]{:S(2)}) collective-permute-start(bf16[1,1024,560]{1,2,0:T(8,128)(2,1)} %copy.110), channel_id=1, source_target_pairs={{0,1},{1,0},{2,3},{3,2},{4,5},{5,4},{6,7},{7,6},{8,9},{9,8},{10,11... | collective-permute-start | bytes 3440648 | tf_op jit(solution)/shard_map/ppermute | solution.py:35
  54.1 19.0 %all-to-all-start.1 = ((bf16[4,1,256,280]{2,3,1,0:T(8,128)(2,1)}), bf16[4,1,256,280]{2,3,1,0:T(8,128)(2,1)}, u32[]{:S(2)}, u32[]{:S(2)}) async-start(bf16[4,1,256,280]{2,3,1,0:T(8,128)(2,1)} %bitcast.202), calls=%async_computation.1 | async-start | bytes 1146880 | tf_op jit(solution)/shard_map/all_to_all | solution.py:516
  104.2 9.3 %copy-start.2 = (s32[4]{0:T(128)S(1)}, s32[4]{0:T(128)}, u32[]{:S(2)}) copy-start(s32[4]{0:T(128)} %constant.127.clone) | copy-start | bytes 52
  104.2 20.6 %copy-start.48 = (f32[1120]{0:T(1024)S(1)}, f32[1120]{0:T(1024)}, u32[]{:S(2)}) copy-start(f32[1120]{0:T(1024)} %param.33) | copy-start | bytes 13444
  106.4 18.4 %all-to-all-start.2 = ((bf16[4,1,256,280]{2,3,1,0:T(8,128)(2,1)}), bf16[4,1,256,280]{2,3,1,0:T(8,128)(2,1)}, u32[]{:S(2)}, u32[]{:S(2)}) async-start(bf16[4,1,256,280]{2,3,1,0:T(8,128)(2,1)} %copy.112), calls=%async_computation.2 | async-start | bytes 1146880 | tf_op jit(solution)/shard_map/all_to_all | solution.py:522
  128.4 9.9 %copy-start.17 = (bf16[256,1120]{1,0:T(8,128)(2,1)}, bf16[256,1120]{1,0:T(8,128)(2,1)S(1)}, u32[]{:S(2)}) copy-start(bf16[256,1120]{1,0:T(8,128)(2,1)S(1)} %add_convert_fusion.refs_0_) | copy-start | bytes 1720324
  149.2 9.1 %collective-permute-start.1 = (bf16[16,144,1120]{2,1,0:T(8,128)(2,1)}, bf16[16,144,1120]{2,1,0:T(8,128)(2,1)}, u32[]{:S(2)}, u32[]{:S(2)}) collective-permute-start(bf16[16,144,1120]{2,1,0:T(8,128)(2,1)} %bitcast.215), channel_id=1, source_target_pairs={{0,8},{8,0},{16,24},{24,16},{1,9},{9,1},{17,25},{25,17},{2,10},{10... | collective-permute-start | bytes 15482888 | tf_op jit(solution)/shard_map/ppermute | solution.py:35
  158.3 4.8 copy-start.9
  158.3 15.1 %slice-start.1 = ((s8[10035200]{0:T(1024)(128)(4,1)}), s8[4194304]{0:T(1024)(128)(4,1)S(1)}, s32[]{:S(2)}) async-start(s8[10035200]{0:T(1024)(128)(4,1)} %bitcast.212), calls=%async_computation.8 | async-start | bytes 8388608
  163.1 10.3 %slice-start.2 = ((s8[10035200]{0:T(1024)(128)(4,1)}), s8[4194304]{0:T(1024)(128)(4,1)S(1)}, s32[]{:S(2)}) async-start(s8[10035200]{0:T(1024)(128)(4,1)} %bitcast.212), calls=%async_computation.9 | async-start | bytes 8388608
  163.1 10.3 %slice-start.3 = ((s8[10035200]{0:T(1024)(128)(4,1)}), s8[1646592]{0:T(1024)(128)(4,1)S(1)}, s32[]{:S(2)}) async-start(s8[10035200]{0:T(1024)(128)(4,1)} %bitcast.212), calls=%async_computation.10 | async-start | bytes 3293184
  173.4 4.5 copy-start.18
  183.4 26.4 %copy-start.40 = (f32[256]{0:T(256)}, f32[256]{0:T(256)S(1)}, u32[]{:S(2)}) copy-start(f32[256]{0:T(256)S(1)} %negate_multiply_fusion.1) | copy-start | bytes 3076
  209.8 88.2 %collective-permute-start.2 = (bf16[16,288,700]{2,1,0:T(8,128)(2,1)}, bf16[16,288,700]{2,1,0:T(8,128)(2,1)}, u32[]{:S(2)}, u32[]{:S(2)}) collective-permute-start(bf16[16,288,700]{2,1,0:T(8,128)(2,1)} %bitcast.214), channel_id=1, source_target_pairs={{0,8},{8,0},{16,24},{24,16},{1,9},{9,1},{17,25},{25,17},{2,10},{10... | collective-permute-start | bytes 19353608 | tf_op jit(solution)/shard_map/ppermute | solution.py:35
  209.9 84.3 %collective-permute-start.20 = (bf16[8,144,1120]{2,1,0:T(8,128)(2,1)}, bf16[8,144,1120]{2,1,0:T(8,128)(2,1)}, u32[]{:S(2)}, u32[]{:S(2)}) collective-permute-start(bf16[8,144,1120]{2,1,0:T(8,128)(2,1)} %fusion.1), channel_id=1, source_target_pairs={{0,16},{8,24},{16,0},{24,8},{1,17},{9,25},{17,1},{25,9},{2,18},{10... | collective-permute-start | bytes 7741448 | tf_op jit(solution)/shard_map/ppermute | solution.py:35
  211.7 27.1 %collective-permute-start.3 = (bf16[1152,256]{1,0:T(8,128)(2,1)}, bf16[1152,256]{1,0:T(8,128)(2,1)}, u32[]{:S(2)}, u32[]{:S(2)}) collective-permute-start(bf16[1152,256]{1,0:T(8,128)(2,1)} %bitcast.195), channel_id=1, source_target_pairs={{0,2},{2,0},{4,6},{6,4},{1,3},{3,1},{5,7},{7,5},{8,10},{10,8},{12,... | collective-permute-start | bytes 1769480 | tf_op jit(solution)/shard_map/ppermute | solution.py:35
  211.7 42.7 %collective-permute-start.4 = (bf16[1152,256]{1,0:T(8,128)(2,1)}, bf16[1152,256]{1,0:T(8,128)(2,1)}, u32[]{:S(2)}, u32[]{:S(2)}) collective-permute-start(bf16[1152,256]{1,0:T(8,128)(2,1)} %bitcast.196), channel_id=1, source_target_pairs={{0,4},{2,6},{4,0},{6,2},{1,5},{3,7},{5,1},{7,3},{8,12},{10,14},{12... | collective-permute-start | bytes 1769480 | tf_op jit(solution)/shard_map/ppermute | solution.py:35
  213.8 40.7 %collective-permute-start.5 = (bf16[1152,256]{1,0:T(8,128)(2,1)}, bf16[1152,256]{1,0:T(8,128)(2,1)}, u32[]{:S(2)}, u32[]{:S(2)}) collective-permute-start(bf16[1152,256]{1,0:T(8,128)(2,1)} %bitcast.197), channel_id=1, source_target_pairs={{0,6},{2,4},{4,2},{6,0},{1,7},{3,5},{5,3},{7,1},{8,14},{10,12},{12... | collective-permute-start | bytes 1769480 | tf_op jit(solution)/shard_map/ppermute | solution.py:35
  220.3 62.5 %copy-start.16 = (bf16[4,288,256]{2,1,0:T(8,128)(2,1)S(1)}, bf16[4,288,256]{2,1,0:T(8,128)(2,1)}, u32[]{:S(2)}) copy-start(bf16[4,288,256]{2,1,0:T(8,128)(2,1)} %pad.4) | copy-start | bytes 1769476
  254.5 38.6 %all-to-all-start.3 = ((bf16[4,1,256,280]{2,3,1,0:T(8,128)(2,1)}), bf16[4,1,256,280]{2,3,1,0:T(8,128)(2,1)S(1)}, u32[]{:S(2)}, u32[]{:S(2)}) async-start(bf16[4,1,256,280]{2,3,1,0:T(8,128)(2,1)} %bitcast.210), calls=%async_computation.3 | async-start | bytes 1146880 | tf_op jit(solution)/shard_map/all_to_all | solution.py:516
  286.0 94.0 %collective-permute-start.12 = (bf16[4,1152,256]{2,1,0:T(8,128)(2,1)}, bf16[4,1152,256]{2,1,0:T(8,128)(2,1)}, u32[]{:S(2)}, u32[]{:S(2)}) collective-permute-start(bf16[4,1152,256]{2,1,0:T(8,128)(2,1)} %pad_maximum_fusion.near_ref), channel_id=1, source_target_pairs={{0,1},{1,0},{2,3},{3,2},{4,5},{5,4},{6,7},{7,6},{8,9},{9,8},{10,11... | collective-permute-start | bytes 7077896 | tf_op jit(solution)/shard_map/ppermute | solution.py:35
  298.0 75.9 %collective-permute-start.21 = (bf16[4,144,1120]{2,1,0:T(8,128)(2,1)}, bf16[4,144,1120]{2,1,0:T(8,128)(2,1)}, u32[]{:S(2)}, u32[]{:S(2)}) collective-permute-start(bf16[4,144,1120]{2,1,0:T(8,128)(2,1)} %fusion.15), channel_id=1, source_target_pairs={{0,1},{1,0},{2,3},{3,2},{4,5},{5,4},{6,7},{7,6},{8,9},{9,8},{10,11... | collective-permute-start | bytes 3870728 | tf_op jit(solution)/shard_map/ppermute | solution.py:35
  337.0 10.0 %copy-start.5 = (f32[256,1120]{1,0:T(8,128)S(1)}, f32[256,1120]{1,0:T(8,128)}, u32[]{:S(2)}) copy-start(f32[256,1120]{1,0:T(8,128)} %copy-done.3) | copy-start | bytes 3440644
  337.0 10.0 %copy-start.49 = (f32[1120]{0:T(1024)S(1)}, f32[1120]{0:T(1024)}, u32[]{:S(2)}) copy-start(f32[1120]{0:T(1024)} %param.39) | copy-start | bytes 13444
  339.5 15.3 %copy-start.15 = (bf16[1024,280]{1,0:T(8,128)(2,1)S(1)}, bf16[1024,280]{1,0:T(8,128)(2,1)}, u32[]{:S(2)}) copy-start(bf16[1024,280]{1,0:T(8,128)(2,1)} %get-tuple-element.57.dq_ref) | copy-start | bytes 1720324
  339.5 57.3 %collective-permute-start.6 = (bf16[1,1024,560]{1,2,0:T(8,128)(2,1)}, bf16[1,1024,560]{1,2,0:T(8,128)(2,1)}, u32[]{:S(2)}, u32[]{:S(2)}) collective-permute-start(bf16[1,1024,560]{1,2,0:T(8,128)(2,1)} %copy.119), channel_id=1, source_target_pairs={{0,1},{1,0},{2,3},{3,2},{4,5},{5,4},{6,7},{7,6},{8,9},{9,8},{10,11... | collective-permute-start | bytes 3440648 | tf_op jit(solution)/shard_map/ppermute | solution.py:35
  355.9 45.4 %all-to-all-start.4 = ((bf16[4,1,256,280]{2,3,1,0:T(8,128)(2,1)}), bf16[4,1,256,280]{2,3,1,0:T(8,128)(2,1)S(1)}, u32[]{:S(2)}, u32[]{:S(2)}) async-start(bf16[4,1,256,280]{2,3,1,0:T(8,128)(2,1)} %copy.121), calls=%async_computation.4 | async-start | bytes 1146880 | tf_op jit(solution)/shard_map/all_to_all | solution.py:522
  376.8 44.0 %collective-permute-start.22 = (bf16[2,144,1120]{2,1,0:T(8,128)(2,1)}, bf16[2,144,1120]{2,1,0:T(8,128)(2,1)}, u32[]{:S(2)}, u32[]{:S(2)}) collective-permute-start(bf16[2,144,1120]{2,1,0:T(8,128)(2,1)} %fusion.24), channel_id=1, source_target_pairs={{0,4},{2,6},{4,0},{6,2},{1,5},{3,7},{5,1},{7,3},{8,12},{10,14},{12... | collective-permute-start | bytes 1935368 | tf_op jit(solution)/shard_map/ppermute | solution.py:35
  379.7 99.0 %collective-permute-start.16 = (bf16[8,288,700]{2,1,0:T(8,128)(2,1)}, bf16[8,288,700]{2,1,0:T(8,128)(2,1)}, u32[]{:S(2)}, u32[]{:S(2)}) collective-permute-start(bf16[8,288,700]{2,1,0:T(8,128)(2,1)} %fusion), channel_id=1, source_target_pairs={{0,16},{8,24},{16,0},{24,8},{1,17},{9,25},{17,1},{25,9},{2,18},{10... | collective-permute-start | bytes 9676808 | tf_op jit(solution)/shard_map/ppermute | solution.py:35
  392.1 26.9 %collective-permute-start.13 = (bf16[2,288,840]{2,1,0:T(8,128)(2,1)}, bf16[2,288,840]{2,1,0:T(8,128)(2,1)}, u32[]{:S(2)}, u32[]{:S(2)}) collective-permute-start(bf16[2,288,840]{2,1,0:T(8,128)(2,1)} %slice.398), channel_id=1, source_target_pairs={{0,8},{8,0},{16,24},{24,16},{1,9},{9,1},{17,25},{25,17},{2,10},{10... | collective-permute-start | bytes 2903048 | tf_op jit(solution)/shard_map/ppermute | solution.py:35
  402.7 9.2 %copy-start.35 = (f32[4480]{0:T(1024)S(1)}, f32[4480]{0:T(1024)}, u32[]{:S(2)}) copy-start(f32[4480]{0:T(1024)} %get-tuple-element.142) | copy-start | bytes 53764
  402.7 65.0 %all-to-all-start.5 = ((bf16[4,1,256,560]{2,3,1,0:T(8,128)(2,1)}), bf16[4,1,256,560]{2,3,1,0:T(8,128)(2,1)}, u32[]{:S(2)}, u32[]{:S(2)}) async-start(bf16[4,1,256,560]{2,3,1,0:T(8,128)(2,1)} %copy.122), calls=%async_computation.5 | async-start | bytes 2293760 | tf_op jit(solution)/shard_map/all_to_all | solution.py:522
  409.7 9.3 %copy-start.12 = (bf16[4,288,840]{2,1,0:T(8,128)(2,1)S(1)}, bf16[4,288,840]{2,1,0:T(8,128)(2,1)}, u32[]{:S(2)}) copy-start(bf16[4,288,840]{2,1,0:T(8,128)(2,1)} %qb.1) | copy-start | bytes 5806084
  420.2 45.1 %collective-permute-start.14 = (bf16[1,288,840]{2,1,0:T(8,128)(2,1)S(1)}, bf16[1,288,840]{2,1,0:T(8,128)(2,1)S(1)}, u32[]{:S(2)}, u32[]{:S(2)}) collective-permute-start(bf16[1,288,840]{2,1,0:T(8,128)(2,1)S(1)} %add_convert_fusion.2), channel_id=1, source_target_pairs={{0,16},{8,24},{16,0},{24,8},{1,17},{9,25},{17,1},{25,9},{2,18},{10... | collective-permute-start | bytes 1451528 | tf_op jit(solution)/shard_map/ppermute | solution.py:35
  423.1 42.2 %slice-start = ((bf16[4,288,840]{2,1,0:T(8,128)(2,1)}), bf16[1,288,840]{2,1,0:T(8,128)(2,1)S(1)}, s32[]{:S(2)}) async-start(bf16[4,288,840]{2,1,0:T(8,128)(2,1)} %qb.1), calls=%async_computation.7 | async-start | bytes 1032192 | tf_op jit(solution)/shard_map/slice | solution.py:208
  423.1 99.6 %collective-permute-start.23 = (bf16[1,144,1120]{2,1,0:T(8,128)(2,1)}, bf16[1,144,1120]{2,1,0:T(8,128)(2,1)}, u32[]{:S(2)}, u32[]{:S(2)}) collective-permute-start(bf16[1,144,1120]{2,1,0:T(8,128)(2,1)} %fusion.41), channel_id=1, source_target_pairs={{0,2},{2,0},{4,6},{6,4},{1,3},{3,1},{5,7},{7,5},{8,10},{10,8},{12,... | collective-permute-start | bytes 967688 | tf_op jit(solution)/shard_map/ppermute | solution.py:35
  427.9 41.1 %copy-start.20 = (bf16[4,1,256,280]{2,3,1,0:T(8,128)(2,1)S(1)}, bf16[4,1,256,280]{2,3,1,0:T(8,128)(2,1)}, u32[]{:S(2)}) copy-start(bf16[4,1,256,280]{2,3,1,0:T(8,128)(2,1)} %copy-done.19) | copy-start | bytes 1720324
  466.2 20.6 %collective-permute-start.15 = (bf16[280,840]{1,0:T(8,128)(2,1)}, bf16[280,840]{1,0:T(8,128)(2,1)}, u32[]{:S(2)}, u32[]{:S(2)}) collective-permute-start(bf16[280,840]{1,0:T(8,128)(2,1)} %fusion.47), channel_id=1, source_target_pairs={{0,1},{1,0},{2,3},{3,2},{4,5},{5,4},{6,7},{7,6},{8,9},{9,8},{10,11... | collective-permute-start | bytes 1411208 | tf_op jit(solution)/shard_map/ppermute | solution.py:35
  469.0 6.9 %copy-start.13 = (bf16[1,256,2,4,280]{1,4,3,2,0:T(8,128)(2,1)}, bf16[1,256,2,4,280]{1,4,3,2,0:T(8,128)(2,1)S(1)}, u32[]{:S(2)}) copy-start(bf16[1,256,2,4,280]{1,4,3,2,0:T(8,128)(2,1)S(1)} %copy.123) | copy-start | bytes 3440644
  478.7 5.2 copy-start.14
  478.7 5.2 copy-start.21
  478.7 5.7 copy-start.11
  483.3 35.1 %collective-permute-start.17 = (bf16[4,288,700]{2,1,0:T(8,128)(2,1)}, bf16[4,288,700]{2,1,0:T(8,128)(2,1)}, u32[]{:S(2)}, u32[]{:S(2)}) collective-permute-start(bf16[4,288,700]{2,1,0:T(8,128)(2,1)} %fusion.11), channel_id=1, source_target_pairs={{0,1},{1,0},{2,3},{3,2},{4,5},{5,4},{6,7},{7,6},{8,9},{9,8},{10,11... | collective-permute-start | bytes 4838408 | tf_op jit(solution)/shard_map/ppermute | solution.py:35
  486.0 9.1 %collective-permute-start.7 = (f32[2,32,280]{2,1,0:T(8,128)S(1)}, f32[2,32,280]{2,1,0:T(8,128)S(1)}, u32[]{:S(2)}, u32[]{:S(2)}) collective-permute-start(f32[2,32,280]{2,1,0:T(8,128)S(1)} %constant_dynamic-slice_fusion.6), channel_id=1, source_target_pairs={{0,16},{8,24},{16,0},{24,8},{1,17},{9,25},{17,1},{25,9},{2,18},{10... | collective-permute-start | bytes 215048 | tf_op jit(solution)/shard_map/ppermute | solution.py:35
  491.0 36.9 %all-to-all-start.6 = ((bf16[4,2,280,140]{2,1,3,0:T(2,128)(2,1)}), bf16[4,2,280,140]{2,1,3,0:T(2,128)(2,1)S(1)}, u32[]{:S(2)}, u32[]{:S(2)}) async-start(bf16[4,2,280,140]{2,1,3,0:T(2,128)(2,1)} %copy.129), calls=%async_computation.6 | async-start | bytes 1720320 | tf_op jit(solution)/shard_map/all_to_all | solution.py:609
  495.1 27.6 %copy-start.24 = (bf16[1,144,1120]{2,1,0:T(8,128)(2,1)S(1)}, bf16[1,144,1120]{2,1,0:T(8,128)(2,1)}, u32[]{:S(2)}) copy-start(bf16[1,144,1120]{2,1,0:T(8,128)(2,1)} %slice.432) | copy-start | bytes 967684
  495.1 27.6 %copy-start.25 = (bf16[1,144,1120]{2,1,0:T(8,128)(2,1)S(1)}, bf16[1,144,1120]{2,1,0:T(8,128)(2,1)}, u32[]{:S(2)}) copy-start(bf16[1,144,1120]{2,1,0:T(8,128)(2,1)} %slice.433) | copy-start | bytes 967684
  495.1 27.6 %copy-start.26 = (bf16[1,144,1120]{2,1,0:T(8,128)(2,1)S(1)}, bf16[1,144,1120]{2,1,0:T(8,128)(2,1)}, u32[]{:S(2)}) copy-start(bf16[1,144,1120]{2,1,0:T(8,128)(2,1)} %slice.436) | copy-start | bytes 967684
  495.2 27.6 %copy-start.27 = (bf16[1,144,1120]{2,1,0:T(8,128)(2,1)S(1)}, bf16[1,144,1120]{2,1,0:T(8,128)(2,1)}, u32[]{:S(2)}) copy-start(bf16[1,144,1120]{2,1,0:T(8,128)(2,1)} %slice.440) | copy-start | bytes 967684
  495.2 31.5 %collective-permute-start.8 = (f32[1,32,280]{2,1,0:T(8,128)S(1)}, f32[1,32,280]{2,1,0:T(8,128)S(1)}, u32[]{:S(2)}, u32[]{:S(2)}) collective-permute-start(f32[1,32,280]{2,1,0:T(8,128)S(1)} %constant_dynamic-slice_fusion.5), channel_id=1, source_target_pairs={{0,8},{8,0},{16,24},{24,16},{1,9},{9,1},{17,25},{25,17},{2,10},{10... | collective-permute-start | bytes 107528 | tf_op jit(solution)/shard_map/ppermute | solution.py:35
  521.7 37.2 %collective-permute-start.18 = (bf16[2,288,700]{2,1,0:T(8,128)(2,1)}, bf16[2,288,700]{2,1,0:T(8,128)(2,1)}, u32[]{:S(2)}, u32[]{:S(2)}) collective-permute-start(bf16[2,288,700]{2,1,0:T(8,128)(2,1)} %fusion.21), channel_id=1, source_target_pairs={{0,4},{2,6},{4,0},{6,2},{1,5},{3,7},{5,1},{7,3},{8,12},{10,14},{12... | collective-permute-start | bytes 2419208 | tf_op jit(solution)/shard_map/ppermute | solution.py:35
  526.7 4.2 collective-permute-start.9
  530.8 28.1 %collective-permute-start.10 = (f32[1,32,280]{2,1,0:T(8,128)S(1)}, f32[1,32,280]{2,1,0:T(8,128)S(1)}, u32[]{:S(2)}, u32[]{:S(2)}) collective-permute-start(f32[1,32,280]{2,1,0:T(8,128)S(1)} %add.337), channel_id=1, source_target_pairs={{0,4},{2,6},{4,0},{6,2},{1,5},{3,7},{5,1},{7,3},{8,12},{10,14},{12... | collective-permute-start | bytes 107528 | tf_op jit(solution)/shard_map/ppermute | solution.py:35
  558.9 6.1 %collective-permute-start.11 = (f32[1,32,280]{2,1,0:T(8,128)S(1)}, f32[1,32,280]{2,1,0:T(8,128)S(1)}, u32[]{:S(2)}, u32[]{:S(2)}) collective-permute-start(f32[1,32,280]{2,1,0:T(8,128)S(1)} %add.338), channel_id=1, source_target_pairs={{0,2},{2,0},{4,6},{6,4},{1,3},{3,1},{5,7},{7,5},{8,10},{10,8},{12,... | collective-permute-start | bytes 107528 | tf_op jit(solution)/shard_map/ppermute | solution.py:35
  560.8 11.8 %collective-permute-start.19 = (bf16[1,288,700]{2,1,0:T(8,128)(2,1)S(1)}, bf16[1,288,700]{2,1,0:T(8,128)(2,1)}, u32[]{:S(2)}, u32[]{:S(2)}) collective-permute-start(bf16[1,288,700]{2,1,0:T(8,128)(2,1)S(1)} %fusion.31), channel_id=1, source_target_pairs={{0,2},{2,0},{4,6},{6,4},{1,3},{3,1},{5,7},{7,5},{8,10},{10,8},{12,... | collective-permute-start | bytes 1209608 | tf_op jit(solution)/shard_map/ppermute | solution.py:35
  565.0 7.6 %copy-start.22 = (bf16[1,288,700]{2,1,0:T(8,128)(2,1)S(1)}, bf16[1,288,700]{2,1,0:T(8,128)(2,1)}, u32[]{:S(2)}) copy-start(bf16[1,288,700]{2,1,0:T(8,128)(2,1)} %slice_bitcast_fusion) | copy-start | bytes 1209604
  (21 other events, 36.7 us)
